TPU v7x, 32 devices: a whole 2x2x4 slice. The times are simulated.
32 devices in a mesh: rep: 2 (over x), tm: 16 (over z, y, core).
Axes of the slice: x: 2, y: 2, z: 4, core: 2. Of those that a mesh axis runs over, the one named last changes fastest.
Arguments:
- exo_tokens: bfloat16 [2048, 32, 1024], P('rep', 'tm'), parts along dimension 0, may hold values from -6 to 6
- queries: bfloat16 [2048, 1024], P(('rep', 'tm')), parts along dimension 0, may hold values from -80 to 80, as said below
- key_weight: bfloat16 [1024, 1024], replicated, may hold values from -0.1875 to 0.1875
- value_weight: bfloat16 [1024, 1024], replicated, may hold values from -0.1875 to 0.1875
- out_weight: bfloat16 [1024, 1024], replicated, may hold values from -0.1875 to 0.1875
- gaze_valid: int32 [2048], P(('rep', 'tm')), parts along dimension 0, may hold values 0 or 1
- window_offset: int32 [2048], P(('rep', 'tm')), parts along dimension 0, may hold values from 0 to 16
- cotangent: bfloat16 [2048, 1024], P(('rep', 'tm')), parts along dimension 0, may hold values from -6 to 6
Outputs:
- attended: bfloat16 [2048, 1024], P(('rep', 'tm')), parts along dimension 0
- d_queries: bfloat16 [2048, 1024], P(('rep', 'tm')), parts along dimension 0
- d_key_weight: float32 [2048, 1024], P(('rep', 'tm')), parts along dimension 0
- d_value_weight: float32 [2048, 1024], P(('rep', 'tm')), parts along dimension 0
- d_out_weight: float32 [2048, 1024], P(('rep', 'tm')), parts along dimension 0
There are 2 independent parts, one for each index of `rep`. A program takes and returns all parts, laid end to end along the dimension named above; an argument that names none is the same for every part. Nothing has to cross between parts.
Inputs may be any that keep to these rules, and one draw needn't show every extreme that they name: `queries`: ego gaze query vectors.
All inputs are finite; a program needn't handle non-finite values. No bound on the sum of `gaze_valid` on one device may be relied on, other than what follows from the above.
Results may differ from a plain program's by a relative error of at most 0.025.
The roundings to bfloat16 on the way count: a program that leaves them out, or rounds other values in their place, can miss the bound.
Values may be sent and summed in bfloat16 or wider, within the bound.
No kernel may reach another device: no remote copies, remote signals or barrier semaphores. Data moves between devices by JAX's collectives and lax.ppermute only.
A program may use at most 192 MiB of HBM per device.

v0:
```python
import jax
import jax.numpy as jnp
from jax import lax
from jax.sharding import PartitionSpec as P

H = 16
HD = 64
W = 16


def with_halo(block, sides, width):
    for axis, dim in sides:
        count = lax.axis_size(axis)
        forward = [(i, i + 1) for i in range(count - 1)]
        backward = [(target, source) for source, target in forward]
        low = lax.ppermute(
            lax.slice_in_dim(block, block.shape[dim] - width, None, axis=dim), axis, forward
        )
        high = lax.ppermute(lax.slice_in_dim(block, 0, width, axis=dim), axis, backward)
        block = jnp.concatenate([low, block, high], axis=dim)
    return block


def attend_block(
    q_rows, keys, values, grad_rows, valid_rows, offset_rows, out_weight, first, total
):
    n_query = q_rows.shape[0]
    n_frames = keys.shape[0]
    n_tok = keys.shape[1]
    width = q_rows.shape[1]
    scale = HD ** (-0.5)
    t_abs = first + jnp.arange(n_query, dtype=jnp.int32)
    f_abs = first - W + jnp.arange(n_frames, dtype=jnp.int32)
    lower = t_abs - W + offset_rows
    upper = t_abs + offset_rows
    allow = (f_abs[None, :] >= lower[:, None]) & (f_abs[None, :] <= upper[:, None])
    allow = allow & (f_abs[None, :] >= 0) & (f_abs[None, :] < total)
    allow_keys = jnp.repeat(allow, n_tok, axis=1)
    q_heads = q_rows.reshape(n_query, H, HD)
    k_heads = keys.reshape(n_frames * n_tok, H, HD)
    v_heads = values.reshape(n_frames * n_tok, H, HD)
    scores = (
        jnp.einsum("thd,khd->htk", q_heads, k_heads, preferred_element_type=jnp.float32) * scale
    )
    scores = jnp.where(allow_keys[None], scores, -1e30)
    top = jnp.max(scores, axis=-1, keepdims=True)
    expo = jnp.exp(scores - top)
    probs = expo / jnp.sum(expo, axis=-1, keepdims=True)
    probs_b = probs.astype(jnp.bfloat16)
    context = jnp.einsum("htk,khd->thd", probs_b, v_heads, preferred_element_type=jnp.float32)
    context = context.reshape(n_query, width).astype(jnp.bfloat16)
    valid_col = valid_rows.astype(jnp.float32)[:, None]
    attended = (
        jnp.dot(context, out_weight, preferred_element_type=jnp.float32) * valid_col
    ).astype(jnp.bfloat16)
    masked_grad = (grad_rows.astype(jnp.float32) * valid_col).astype(jnp.bfloat16)
    d_context = lax.dot_general(
        masked_grad, out_weight, (((1,), (1,)), ((), ())), preferred_element_type=jnp.float32
    )
    d_context = d_context.astype(jnp.bfloat16)
    d_heads = d_context.reshape(n_query, H, HD)
    d_probs = jnp.einsum("thd,khd->htk", d_heads, v_heads, preferred_element_type=jnp.float32)
    d_scores = probs * (d_probs - jnp.sum(probs * d_probs, axis=-1, keepdims=True)) * scale
    d_scores = d_scores.astype(jnp.bfloat16)
    d_query = jnp.einsum("htk,khd->thd", d_scores, k_heads, preferred_element_type=jnp.float32)
    d_query = d_query.reshape(n_query, width).astype(jnp.bfloat16)
    key_part = jnp.einsum("htk,thd->khd", d_scores, q_heads, preferred_element_type=jnp.float32)
    key_part = key_part.reshape(n_frames, n_tok, width).astype(jnp.bfloat16)
    value_part = jnp.einsum("htk,thd->khd", probs_b, d_heads, preferred_element_type=jnp.float32)
    value_part = value_part.reshape(n_frames, n_tok, width).astype(jnp.bfloat16)
    return (attended, d_query, key_part, value_part, context, masked_grad)


def shards(
    exo_tokens, queries, key_weight, value_weight, out_weight, gaze_valid, window_offset, cotangent
):
    rows_here = queries.shape[0]
    width = queries.shape[1]
    total = rows_here * lax.axis_size("tm")
    first = lax.axis_index("tm") * rows_here
    frame_block = lax.all_to_all(exo_tokens, "tm", split_axis=0, concat_axis=1, tiled=True)
    n_tok = frame_block.shape[1]
    tokens_wide = with_halo(frame_block, (("tm", 0),), W)
    flat = tokens_wide.reshape(-1, width)
    key_rows = jnp.dot(flat, key_weight, preferred_element_type=jnp.float32).astype(jnp.bfloat16)
    value_rows = jnp.dot(flat, value_weight, preferred_element_type=jnp.float32).astype(
        jnp.bfloat16
    )
    paired = jnp.stack([key_rows, value_rows], axis=1).reshape(
        tokens_wide.shape[0], n_tok, 2, width
    )
    attended, d_query, key_part, value_part, context, masked_grad = attend_block(
        queries,
        paired[:, :, 0],
        paired[:, :, 1],
        cotangent,
        gaze_valid,
        window_offset,
        out_weight,
        first,
        total,
    )
    grad_pairs = jnp.stack([key_part, value_part], axis=2)
    flat_sources = tokens_wide.reshape(-1, width)
    flat_grads = grad_pairs.reshape(-1, 2 * width)
    weight_share = lax.psum_scatter(
        lax.dot_general(
            flat_sources, flat_grads, (((0,), (0,)), ((), ())), preferred_element_type=jnp.float32
        ).astype(jnp.bfloat16),
        "tm",
        scatter_dimension=0,
        tiled=True,
    ).astype(jnp.float32)
    out_term = lax.dot_general(
        context, masked_grad, (((0,), (0,)), ((), ())), preferred_element_type=jnp.float32
    )
    d_out_weight = lax.psum_scatter(
        out_term.astype(jnp.bfloat16), "tm", scatter_dimension=0, tiled=True
    ).astype(jnp.float32)
    return (attended, d_query, weight_share[:, :width], weight_share[:, width:], d_out_weight)


def solution(mesh):
    in_specs = (
        P("rep", "tm", None),
        P(("rep", "tm"), None),
        P(),
        P(),
        P(),
        P(("rep", "tm")),
        P(("rep", "tm")),
        P(("rep", "tm"), None),
    )
    out_specs = (
        P(("rep", "tm"), None),
        P(("rep", "tm"), None),
        P(("rep", "tm"), None),
        P(("rep", "tm"), None),
        P(("rep", "tm"), None),
    )
    return jax.shard_map(shards, mesh=mesh, in_specs=in_specs, out_specs=out_specs, check_vma=False)
```

profile of v0, /device:TPU:0, one launch (start us, length us, event | category | flops | bytes accessed | tf_op | source)
XLA Modules:
  0.0 421.9 jit_solution(12475327256864713558)
XLA Ops:
  7.2 99.7 %all_to_all.18 = bf16[1024,2,1024]{2,1,0:T(2,128)(2,1)S(1)} all-to-all(bf16[1024,2,1024]{2,1,0:T(2,128)(2,1)} %param.8), channel_id=1, replica_groups=mesh['rep'=2,'tm'=16] {'tm'}, dimensions={0} | all-to-all | bytes 8388608 | tf_op jit(solution)/shard_map/all_to_all | solution.py:81
  106.9 1.3 copy.41
  108.2 1.9 copy-done.2
  111.5 1.1 copy.44
  112.6 1.3 collective-permute-start.1
  113.9 4.5 %collective-permute-start = (bf16[16,32,1024]{2,0,1:T(8,128)(2,1)}, bf16[16,32,1024]{2,0,1:T(8,128)(2,1)}, u32[]{:S(2)}, u32[]{:S(2)}) collective-permute-start(bf16[16,32,1024]{2,0,1:T(8,128)(2,1)} %bitcast.2), channel_id=1, source_target_pairs={{0,1},{1,2},{2,3},{3,4},{4,5},{5,6},{6,7},{7,8},{8,9},{9,10},{10,1... | collective-permute-start | bytes 3145736 | tf_op jit(solution)/shard_map/ppermute | solution.py:16
  118.4 2.4 convolution_convert_fusion.4
  121.9 2.6 copy.43
  124.6 3.0 pad_maximum_fusion.1
  127.6 3.5 copy.45
  131.1 8.9 %convolution_convert_fusion = bf16[3072,1024]{0,1:T(8,128)(2,1)} fusion(bf16[3072,1024]{1,0:T(8,128)(2,1)S(1)} %bitcast.63, bf16[1024,1024]{1,0:T(8,128)(2,1)S(1)} %copy-done), kind=kOutput, calls=%fused_computation.16 | convolution fusion | flops 6445596672 | bytes 14680064 | tf_op jit(solution)/shard_map/dot_general | solution.py:85
  140.1 7.5 %convolution_convert_fusion.1 = bf16[3072,1024]{0,1:T(8,128)(2,1)S(1)} fusion(bf16[3072,1024]{1,0:T(8,128)(2,1)S(1)} %bitcast.64, bf16[1024,1024]{1,0:T(8,128)(2,1)S(1)} %copy-done.8), kind=kOutput, calls=%fused_computation.17 | convolution fusion | flops 6445596672 | bytes 14680064 | tf_op jit(solution)/shard_map/dot_general | solution.py:86
  147.6 6.3 %fusion.36 = f32[16,64,3072]{2,1,0:T(8,128)} fusion(bf16[64,16,64]{0,2,1:T(8,128)(2,1)S(1)} %bitcast.66, bf16[3072,16,64]{0,2,1:T(8,128)(2,1)S(1)} %bitcast.60), kind=kOutput, calls=%fused_computation.47 | convolution fusion | flops 402653184 | bytes 19005440 | tf_op jit(solution)/shard_map/thd,khd->htk/dot_general | solution.py:62
  153.9 12.0 %fusion.35 = (f32[16,64]{1,0:T(8,128)S(1)}, f32[16,64,3072]{2,1,0:T(8,128)}) fusion(pred[64,3072]{1,0:T(8,128)(4,1)S(1)} %copy.46, bf16[64,16,64]{0,2,1:T(8,128)(2,1)S(1)} %bitcast.71, bf16[3072,16,64]{0,2,1:T(8,128)(2,1)} %bitcast.74), kind=kOutput, calls=%fused_computation.46 | convolution fusion | flops 415239168 | bytes 19206144 | tf_op jit(solution)/shard_map/sub | solution.py:47
  166.0 8.4 %fusion.20 = bf16[16,64,64]{2,1,0:T(8,128)(2,1)S(1)} fusion(bf16[3072,16,64]{0,2,1:T(8,128)(2,1)} %bitcast.61, f32[16,64,3072]{2,1,0:T(8,128)} %get-tuple-element.32, f32[16,64]{1,0:T(8,128)S(1)} %get-tuple-element.31), kind=kOutput, calls=%fused_computation.25 | convolution fusion | flops 409010176 | bytes 19009536 | tf_op jit(solution)/shard_map/htk,khd->thd/dot_general | solution.py:50
  174.4 1.6 copy-done.10
  176.0 3.7 convert_bitcast_fusion
  179.7 2.1 convolution_convert_fusion.3
  181.8 22.2 %convert_bitcast_fusion.1 = bf16[3072,16,64]{0,2,1:T(8,128)(2,1)} fusion(bf16[64,16,64]{0,2,1:T(8,128)(2,1)S(1)} %bitcast.72, f32[16,64,3072]{2,1,0:T(8,128)} %fusion.36, f32[16,64,3072]{2,1,0:T(8,128)} %get-tuple-element.32, f32[16,64]{1,0:T(8,128)S(1)} %get-tuple-element.31), kind=kOutput, calls=%fused_computation.11 | convolution fusion | flops 427823104 | bytes 31592448 | tf_op jit(solution)/shard_map/htk,thd->khd/dot_general | solution.py:67
  204.0 15.7 %copy.52 = bf16[3072,16,64]{2,1,0:T(8,128)(2,1)} copy(bf16[3072,16,64]{0,2,1:T(8,128)(2,1)} %convert_bitcast_fusion) | data formatting | bytes 12582912 | tf_op jit(solution)/shard_map/convert_element_type | solution.py:70
  219.7 17.3 %convert_element_type.109 = bf16[96,32,1,1024]{3,1,0,2:T(8,128)(2,1)} reshape(bf16[3072,16,64]{2,1,0:T(8,128)(2,1)} %copy.52) | data formatting | bytes 12582912 | tf_op jit(solution)/shard_map/convert_element_type | solution.py:70
  237.0 15.7 %copy.50 = bf16[3072,16,64]{2,1,0:T(8,128)(2,1)} copy(bf16[3072,16,64]{0,2,1:T(8,128)(2,1)} %convert_bitcast_fusion.1) | data formatting | bytes 12582912 | tf_op jit(solution)/shard_map/convert_element_type | solution.py:68
  252.7 17.3 %convert_element_type.106 = bf16[96,32,1,1024]{3,1,0,2:T(8,128)(2,1)} reshape(bf16[3072,16,64]{2,1,0:T(8,128)(2,1)} %copy.50) | data formatting | bytes 12582912 | tf_op jit(solution)/shard_map/convert_element_type | solution.py:68
  269.9 6.1 %pad_maximum_fusion = bf16[96,32,2,1024]{3,1,0,2:T(8,128)(2,1)S(1)} fusion(bf16[96,32,1,1024]{3,1,0,2:T(8,128)(2,1)} %convert_element_type.109, bf16[96,32,1,1024]{3,1,0,2:T(8,128)(2,1)} %convert_element_type.106), kind=kLoop, calls=%fused_computation.2 | loop fusion | flops 6291456 | bytes 25165824 | tf_op jit(solution)/shard_map/stack | solution.py:103
  276.1 28.3 %copy.53 = bf16[96,32,2,1024]{3,2,1,0:T(2,128)(2,1)S(1)} copy(bf16[96,32,2,1024]{3,1,0,2:T(8,128)(2,1)S(1)} %pad_maximum_fusion) | data formatting | bytes 25165824 | tf_op jit(solution)/shard_map/stack | solution.py:103
  304.3 3.2 copy.57
  307.5 16.2 %convolution_convert_fusion.2 = bf16[1024,2048]{1,0:T(8,128)(2,1)} fusion(bf16[3072,1024]{1,0:T(8,128)(2,1)} %bitcast.65, bf16[3072,2048]{1,0:T(8,128)(2,1)S(1)} %bitcast.62), kind=kOutput, calls=%fused_computation.19 | convolution fusion | flops 12886999040 | bytes 23068672 | tf_op jit(solution)/shard_map/dot_general | solution.py:107
  323.8 21.8 %fusion.17 = bf16[16,64,64]{2,1,0:T(8,128)(2,1)S(1)} fusion(bf16[3072,16,64]{0,2,1:T(8,128)(2,1)} %bitcast.75, f32[16,64,3072]{2,1,0:T(8,128)} %fusion.36, f32[16,64,3072]{2,1,0:T(8,128)} %get-tuple-element.32, f32[16,64]{1,0:T(8,128)S(1)} %get-tuple-element.31), kind=kOutput, calls=%fused_computation.24 | convolution fusion | flops 424742912 | bytes 31592448 | tf_op jit(solution)/shard_map/htk,khd->thd/dot_general | solution.py:65
  346.4 2.9 fusion.23
  349.3 1.6 convert_element_type.113
  350.9 62.3 %reduce-scatter.3.cloned.1.call-done = bf16[64,2048]{1,0:T(8,128)(2,1)} async-done(((bf16[1024,2048]{1,0:T(8,128)(2,1)}), bf16[64,2048]{1,0:T(8,128)(2,1)}) %reduce-scatter.3.cloned.1.call-update) | async-done | bytes 262160 | tf_op jit(solution)/shard_map/reduce_scatter | solution.py:106
  413.2 1.8 fusion.34
  (39 shorter events, 3.4 us)
Async XLA Ops:
  7.2 123.9 %copy-start = (bf16[1024,1024]{1,0:T(8,128)(2,1)S(1)}, bf16[1024,1024]{1,0:T(8,128)(2,1)}, u32[]{:S(2)}) copy-start(bf16[1024,1024]{1,0:T(8,128)(2,1)} %param.10) | copy-start | bytes 6291460
  7.2 342.1 %reduce-scatter.5.cloned.1.call-start = ((), (), s32[]{:S(2)}) async-start(), calls=%async_computation.4 | async-start | bytes 2228224 | tf_op jit(solution)/shard_map/reduce_scatter | solution.py:117
  106.9 11.5 %copy-start.9 = (s32[64]{0:T(128)S(1)}, s32[64]{0:T(128)}, u32[]{:S(2)}) copy-start(s32[64]{0:T(128)} %param.13) | copy-start | bytes 772
  106.9 11.5 %copy-start.5 = (bf16[64,1024]{1,0:T(8,128)(2,1)S(1)}, bf16[64,1024]{1,0:T(8,128)(2,1)}, u32[]{:S(2)}) copy-start(bf16[64,1024]{1,0:T(8,128)(2,1)} %param.15) | copy-start | bytes 393220
  106.9 14.0 %copy-start.6 = (bf16[64,1024]{1,0:T(8,128)(2,1)S(1)}, bf16[64,1024]{1,0:T(8,128)(2,1)}, u32[]{:S(2)}) copy-start(bf16[64,1024]{1,0:T(8,128)(2,1)} %param.9) | copy-start | bytes 393220
  106.9 14.3 %copy-start.7 = (s32[64]{0:T(128)S(1)}, s32[64]{0:T(128)}, u32[]{:S(2)}) copy-start(s32[64]{0:T(128)} %param.14) | copy-start | bytes 772
  108.2 1.9 copy-start.2
  112.6 12.0 %collective-permute-start.1 = (bf16[16,32,1024]{2,0,1:T(8,128)(2,1)}, bf16[16,32,1024]{2,0,1:T(8,128)(2,1)}, u32[]{:S(2)}, u32[]{:S(2)}) collective-permute-start(bf16[16,32,1024]{2,0,1:T(8,128)(2,1)} %bitcast.5), channel_id=1, source_target_pairs={{1,0},{2,1},{3,2},{4,3},{5,4},{6,5},{7,6},{8,7},{9,8},{10,9},{11,1... | collective-permute-start | bytes 3145736 | tf_op jit(solution)/shard_map/ppermute | solution.py:19
  113.9 10.7 %collective-permute-start = (bf16[16,32,1024]{2,0,1:T(8,128)(2,1)}, bf16[16,32,1024]{2,0,1:T(8,128)(2,1)}, u32[]{:S(2)}, u32[]{:S(2)}) collective-permute-start(bf16[16,32,1024]{2,0,1:T(8,128)(2,1)} %bitcast.2), channel_id=1, source_target_pairs={{0,1},{1,2},{2,3},{3,4},{4,5},{5,6},{6,7},{7,8},{8,9},{9,10},{10,1... | collective-permute-start | bytes 3145736 | tf_op jit(solution)/shard_map/ppermute | solution.py:16
  131.1 9.0 %copy-start.4 = (bf16[96,32,1024]{2,1,0:T(8,128)(2,1)}, bf16[96,32,1024]{2,1,0:T(8,128)(2,1)S(1)}, u32[]{:S(2)}) copy-start(bf16[96,32,1024]{2,1,0:T(8,128)(2,1)S(1)} %copy.45) | copy-start | bytes 18874372
  131.1 8.9 %copy-start.8 = (bf16[1024,1024]{1,0:T(8,128)(2,1)S(1)}, bf16[1024,1024]{1,0:T(8,128)(2,1)}, u32[]{:S(2)}) copy-start(bf16[1024,1024]{1,0:T(8,128)(2,1)} %param.11) | copy-start | bytes 6291460
  147.6 6.4 %copy-start.3 = (bf16[3072,1024]{0,1:T(8,128)(2,1)}, bf16[3072,1024]{0,1:T(8,128)(2,1)S(1)}, u32[]{:S(2)}) copy-start(bf16[3072,1024]{0,1:T(8,128)(2,1)S(1)} %convolution_convert_fusion.1) | copy-start | bytes 18874372
  166.0 10.0 %copy-start.10 = (f32[16,64,3072]{2,1,0:T(8,128)S(1)}, f32[16,64,3072]{2,1,0:T(8,128)}, u32[]{:S(2)}) copy-start(f32[16,64,3072]{2,1,0:T(8,128)} %get-tuple-element.32) | copy-start | bytes 37748740
  181.8 231.5 %reduce-scatter.3.cloned.1.call-start = ((), (), s32[]{:S(2)}) async-start(), calls=%async_computation.3 | async-start | bytes 4456448 | tf_op jit(solution)/shard_map/reduce_scatter | solution.py:106
  323.8 91.2 %copy-start.1 = (bf16[1024,1024]{1,0:T(8,128)(2,1)S(1)}, bf16[1024,1024]{1,0:T(8,128)(2,1)}, u32[]{:S(2)}) copy-start(bf16[1024,1024]{1,0:T(8,128)(2,1)} %param.10) | copy-start | bytes 6291460
Sparse Core Ops, SparseCore 0:
  181.9 78.3 reduce-scatter.4
  323.9 89.2 reduce-scatter.2
where the time goes:
time: 424 us; the launch traced here: 422 us
  matrix products  115 us (27%)
  local copies, waits for them, and re-layouts  114 us (27%)
  blocking collectives  99.7 us (24%)
  waiting for transfers between devices  62.3 us (15%)
  between operations  14.3 us (3%)
  other arithmetic  10.9 us (3%)
  starting transfers between devices  5.87 us (1%)
    all_to_all x1, blocking collectives, shards(): lax.all_to_all(exo_tokens, 'tm', split_axis=0, concat_axis=1, tiled=True)  99.7 us
    reduce_scatter x1, waiting for transfers between devices, shards(): lax.psum_scatter(lax.dot_general(flat_sources, flat_grads, (((0,), (0,)),...  62.3 us
    convert_element_type x2, local copies, waits for them, and re-layouts, attend_block(): value_part = value_part.reshape(n_frames, n_tok, width).astype(jnp.bfloat16)  33 us
    convert_element_type x2, local copies, waits for them, and re-layouts, attend_block(): key_part = key_part.reshape(n_frames, n_tok, width).astype(jnp.bfloat16)  32.9 us
    another operation x1, local copies, waits for them, and re-layouts, shards(): grad_pairs = jnp.stack([key_part, value_part], axis=2)  28.3 us
    dot_general x1, matrix products, attend_block(): jnp.einsum('htk,thd->khd', d_scores, q_heads, preferred_element_type=jnp....  22.2 us
    dot_general x1, matrix products, attend_block(): jnp.einsum('htk,khd->thd', d_scores, k_heads, preferred_element_type=jnp....  21.8 us
    dot_general x1, matrix products, shards(): lax.dot_general(flat_sources, flat_grads, (((0,), (0,)), ((), ())), prefe...  16.2 us
  transfers between devices with their start and end apart: 4, of which 1 were waited for; matrix products, arithmetic and copies ran while one was open for 42% of the time, Pallas kernels for 0%

commit v1 on v0

v1 whole, which is shorter than its diff:
```python
import functools

import jax
import jax.numpy as jnp
from jax import lax
from jax.experimental import pallas as pl
from jax.experimental.pallas import tpu as pltpu
from jax.sharding import PartitionSpec as P

H = 16
HD = 64
W = 16
GROUP = 4
LANES = GROUP * HD
CHUNK = 256
F32 = jnp.float32
BF16 = jnp.bfloat16


def tn_dot(a, b):
    return lax.dot_general(a, b, (((0,), (0,)), ((), ())), preferred_element_type=F32)


def nt_dot(a, b):
    return lax.dot_general(a, b, (((1,), (1,)), ((), ())), preferred_element_type=F32)


def nn_dot(a, b):
    return jnp.dot(a, b, preferred_element_type=F32)


def attention_kernel(
    tok, n_query, n_main, n_halo,
    lo_ref, hi_ref, q_ref, g_ref, km_ref, kh_ref, vm_ref, vh_ref,
    ctx_ref, dq_ref, kpm_ref, kph_ref, vpm_ref, vph_ref,
    s_ref, dp_ref, bq_ref, bg_ref, acc_ctx, acc_dq,
):
    scale = HD ** (-0.5)
    wide = GROUP * n_query
    row_head = lax.broadcasted_iota(jnp.int32, (wide, LANES), 0) // n_query
    col_head = lax.broadcasted_iota(jnp.int32, (wide, LANES), 1) // HD
    own = row_head == col_head
    zero = jnp.zeros((wide, LANES), BF16)
    bq_ref[...] = jnp.where(own, jnp.concatenate([q_ref[...]] * GROUP, axis=0), zero)
    bg_ref[...] = jnp.where(own, jnp.concatenate([g_ref[...]] * GROUP, axis=0), zero)
    lo = lo_ref[...]
    hi = hi_ref[...]
    rows = lax.broadcasted_iota(jnp.int32, (CHUNK, wide), 0)
    halo_rows = n_halo // 2

    def score(k_ref, v_ref, at, out_at, period, base, top):
        frame = (rows + at) % period // tok + base
        seen = (frame >= lo) & (frame <= hi)
        s = nt_dot(k_ref[pl.ds(at, CHUNK), :], bq_ref[...]) * scale
        s = jnp.where(seen, s, -1e30)
        s_ref[pl.ds(out_at, CHUNK), :] = s
        dp_ref[pl.ds(out_at, CHUNK), :] = nt_dot(v_ref[pl.ds(at, CHUNK), :], bg_ref[...])
        return jnp.maximum(top, jnp.max(s.reshape(CHUNK // 8, 8, wide), axis=0))

    top = jnp.full((8, wide), -1e30, F32)

    def main_score(c, top):
        at = pl.multiple_of(c * CHUNK, CHUNK)
        return score(km_ref, vm_ref, at, at, n_query * tok, 0, top)

    def halo_score(c, top):
        at = pl.multiple_of(c * CHUNK, CHUNK)
        base = jnp.where(at < halo_rows, -W, n_query)
        return score(kh_ref, vh_ref, at, n_main + at, W * tok, base, top)

    top = lax.fori_loop(0, n_main // CHUNK, main_score, top)
    top = lax.fori_loop(0, n_halo // CHUNK, halo_score, top)
    top = jnp.max(top, axis=0, keepdims=True)

    def expo(c, sums):
        total, weighted = sums
        at = pl.ds(pl.multiple_of(c * CHUNK, CHUNK), CHUNK)
        e = jnp.exp(s_ref[at, :] - top)
        s_ref[at, :] = e
        t = e * dp_ref[at, :]
        total = total + jnp.sum(e.reshape(CHUNK // 8, 8, wide), axis=0)
        weighted = weighted + jnp.sum(t.reshape(CHUNK // 8, 8, wide), axis=0)
        return total, weighted

    none = jnp.zeros((8, wide), F32)
    total, weighted = lax.fori_loop(0, (n_main + n_halo) // CHUNK, expo, (none, none))
    inverse = 1.0 / jnp.sum(total, axis=0, keepdims=True)
    mean = jnp.sum(weighted, axis=0, keepdims=True) * inverse

    acc_ctx[...] = jnp.zeros_like(acc_ctx)
    acc_dq[...] = jnp.zeros_like(acc_dq)

    def back(k_ref, v_ref, kp_ref, vp_ref, at, in_at):
        here = pl.ds(at, CHUNK)
        p = s_ref[pl.ds(in_at, CHUNK), :] * inverse
        ds = (p * (dp_ref[pl.ds(in_at, CHUNK), :] - mean) * scale).astype(BF16)
        pb = p.astype(BF16)
        acc_ctx[...] += tn_dot(pb, v_ref[here, :])
        acc_dq[...] += tn_dot(ds, k_ref[here, :])
        kp_ref[here, :] = nn_dot(ds, bq_ref[...]).astype(BF16)
        vp_ref[here, :] = nn_dot(pb, bg_ref[...]).astype(BF16)

    def main_back(c, carry):
        at = pl.multiple_of(c * CHUNK, CHUNK)
        back(km_ref, vm_ref, kpm_ref, vpm_ref, at, at)
        return carry

    def halo_back(c, carry):
        at = pl.multiple_of(c * CHUNK, CHUNK)
        back(kh_ref, vh_ref, kph_ref, vph_ref, at, n_main + at)
        return carry

    lax.fori_loop(0, n_main // CHUNK, main_back, 0)
    lax.fori_loop(0, n_halo // CHUNK, halo_back, 0)

    def diagonal(acc):
        kept = jnp.where(own, acc, 0.0)
        out = kept[:n_query]
        for h in range(1, GROUP):
            out = out + kept[h * n_query : (h + 1) * n_query]
        return out.astype(BF16)

    ctx_ref[...] = diagonal(acc_ctx[...])
    dq_ref[...] = diagonal(acc_dq[...])


def attention(tok, lo, hi, queries, d_context, k_main, k_halo, v_main, v_halo):
    n_query, width = queries.shape
    n_main, n_halo = k_main.shape[0], k_halo.shape[0]
    wide = GROUP * n_query
    flat = pl.BlockSpec((1, wide), lambda g: (0, 0))

    def cols(n):
        return pl.BlockSpec((n, LANES), lambda g: (0, g))

    def shape(n):
        return jax.ShapeDtypeStruct((n, width), BF16)

    n_keys = n_main + n_halo
    return pl.pallas_call(
        functools.partial(attention_kernel, tok, n_query, n_main, n_halo),
        grid=(width // LANES,),
        in_specs=[flat, flat, cols(n_query), cols(n_query)]
        + [cols(n_main), cols(n_halo), cols(n_main), cols(n_halo)],
        out_specs=[cols(n_query), cols(n_query)]
        + [cols(n_main), cols(n_halo), cols(n_main), cols(n_halo)],
        out_shape=[shape(n_query), shape(n_query)]
        + [shape(n_main), shape(n_halo), shape(n_main), shape(n_halo)],
        scratch_shapes=[
            pltpu.VMEM((n_keys, wide), F32),
            pltpu.VMEM((n_keys, wide), F32),
            pltpu.VMEM((wide, LANES), BF16),
            pltpu.VMEM((wide, LANES), BF16),
            pltpu.VMEM((wide, LANES), F32),
            pltpu.VMEM((wide, LANES), F32),
        ],
        compiler_params=pltpu.CompilerParams(dimension_semantics=("arbitrary",)),
        cost_estimate=pl.CostEstimate(
            flops=12 * n_keys * wide * width,
            bytes_accessed=8 * n_keys * width,
            transcendentals=n_keys * H * n_query,
        ),
        name="banded_attention",
    )(lo, hi, queries, d_context, k_main, k_halo, v_main, v_halo)


def scatter_sum(term, bits, order):
    n_dev = 1 << bits
    me = lax.axis_index("tm")
    rows, cols = term.shape
    left = list(range(bits - 1, -1, -1))
    block = term.reshape([2] * bits + [rows // n_dev, cols])
    for bit in order:
        axis = left.index(bit)
        left.remove(bit)
        mine = (me >> bit) & 1
        away = lax.dynamic_index_in_dim(block, 1 - mine, axis, keepdims=False)
        keep = lax.dynamic_index_in_dim(block, mine, axis, keepdims=False)
        come = lax.ppermute(away, "tm", [(i, i ^ (1 << bit)) for i in range(n_dev)])
        block = keep.astype(F32) + come.astype(F32)
        if left:
            block = block.astype(BF16)
    return block


def shards(
    exo_tokens, queries, key_weight, value_weight, out_weight, gaze_valid, window_offset, cotangent
):
    n_query, width = queries.shape
    tok = exo_tokens.shape[1]
    n_dev = lax.axis_size("tm")
    bits = n_dev.bit_length() - 1
    total = n_query * n_dev
    first = lax.axis_index("tm") * n_query
    own_rows = lax.all_to_all(
        exo_tokens.reshape(-1, width), "tm", split_axis=0, concat_axis=0, tiled=True
    )
    by_source = own_rows.reshape(n_dev, n_query * tok, width)
    edge = W * tok
    up = [(i, i + 1) for i in range(n_dev - 1)]
    down = [(target, source) for source, target in up]
    low = lax.ppermute(by_source[:, -edge:].reshape(-1, width), "tm", up)
    high = lax.ppermute(by_source[:, :edge].reshape(-1, width), "tm", down)
    halo = jnp.concatenate([low, high], axis=0)

    valid_col = gaze_valid.astype(F32)[:, None]
    masked_grad = (cotangent.astype(F32) * valid_col).astype(BF16)
    d_context = nt_dot(masked_grad, out_weight).astype(BF16)
    at = jnp.arange(n_query, dtype=jnp.int32)
    lower = jnp.maximum(at - W + window_offset, -first)
    upper = jnp.minimum(at + window_offset, total - 1 - first)
    lo = jnp.tile(lower[None, :], (1, GROUP))
    hi = jnp.tile(upper[None, :], (1, GROUP))

    k_main = nn_dot(own_rows, key_weight).astype(BF16)
    v_main = nn_dot(own_rows, value_weight).astype(BF16)
    k_halo = nn_dot(halo, key_weight).astype(BF16)
    v_halo = nn_dot(halo, value_weight).astype(BF16)
    context, d_query, kp_main, kp_halo, vp_main, vp_halo = attention(
        tok, lo, hi, queries, d_context, k_main, k_halo, v_main, v_halo
    )
    attended = (nn_dot(context, out_weight) * valid_col).astype(BF16)

    ascending = list(range(bits))
    rotated = [0] + list(range(2, bits)) + [1] if bits > 1 else ascending
    half = width // 2
    out_term = tn_dot(context, masked_grad).astype(BF16)
    d_out = jnp.concatenate(
        [
            scatter_sum(out_term[:, :half], bits, ascending),
            scatter_sum(out_term[:, half:], bits, rotated),
        ],
        axis=1,
    )
    d_key = scatter_sum(
        (tn_dot(own_rows, kp_main) + tn_dot(halo, kp_halo)).astype(BF16), bits, ascending
    )
    d_value = scatter_sum(
        (tn_dot(own_rows, vp_main) + tn_dot(halo, vp_halo)).astype(BF16), bits, rotated
    )
    return (attended, d_query, d_key, d_value, d_out)


def solution(mesh):
    in_specs = (
        P("rep", "tm", None),
        P(("rep", "tm"), None),
        P(),
        P(),
        P(),
        P(("rep", "tm")),
        P(("rep", "tm")),
        P(("rep", "tm"), None),
    )
    out_specs = (
        P(("rep", "tm"), None),
        P(("rep", "tm"), None),
        P(("rep", "tm"), None),
        P(("rep", "tm"), None),
        P(("rep", "tm"), None),
    )
    return jax.shard_map(shards, mesh=mesh, in_specs=in_specs, out_specs=out_specs, check_vma=False)
```

time: 424 us -> 269 us (0.63)
  local copies, waits for them, and re-layouts: 114 us -> 12.1 us
  blocking collectives: 99.7 us -> 0 us
  matrix products: 115 us -> 48.1 us
  starting transfers between devices: 5.87 us -> 61 us
  waiting for transfers between devices: 62.3 us -> 102 us
  Pallas kernels: 0 us -> 39.4 us
  between operations: 14.3 us -> 1.19 us
  other arithmetic: 10.9 us -> 4.07 us
    all_to_all x1 -> x0, blocking collectives: 99.7 us -> none  [shards(): lax.all_to_all(exo_tokens, 'tm', split_axis=0, concat_axis=1, tiled=True)]
    all_to_all x0 -> x1, waiting for transfers between devices: none -> 73.2 us  [shards(): lax.all_to_all(exo_tokens.reshape(-1, width), 'tm', split_axis=0, concat_...]
    convert_element_type x4 -> x0, local copies, waits for them, and re-layouts: 65.9 us -> none  [the longest x2 33 us: attend_block(): value_part = value_part.reshape(n_frames, n_tok, width).astype(jnp.bfloat16)]
    reduce_scatter x2 -> x0, waiting for transfers between devices: 62.3 us -> none  [the longest x1 62.3 us: shards(): lax.psum_scatter(lax.dot_general(flat_sources, flat_grads, (((0,), (0,)),...]
    dot_general x11, matrix products: 102 us -> 48.1 us  [the longest x5 25.4 us: nn_dot(): return jnp.dot(a, b, preferred_element_type=F32)]
    ppermute x2 -> x18, starting transfers between devices: 5.79 us -> 53.4 us  [the longest x16 49.2 us: scatter_sum(): come = lax.ppermute(away, 'tm', [(i, i ^ 1 << bit) for i in range(n_dev)])]
    pallas_call x0 -> x1, Pallas kernels: none -> 39.4 us  [attention(): pl.pallas_call(functools.partial(attention_kernel, tok, n_query, n_main,...]
    ppermute x2 -> x18, waiting for transfers between devices: 0.01 us -> 29.2 us  [the longest x16 29.2 us: scatter_sum(): come = lax.ppermute(away, 'tm', [(i, i ^ 1 << bit) for i in range(n_dev)])]
  transfers between devices with their start and end apart: 4 -> 19, of which waited for: 1 -> 7; matrix products, arithmetic and copies ran while one was open for 42% -> 17% of each run, Pallas kernels for 0% -> 0%
where the time goes in v1:
time: 269 us; the launch traced here: 268 us
  waiting for transfers between devices  102 us (38%)
  starting transfers between devices  61 us (23%)
  matrix products  48.1 us (18%)
  Pallas kernels  39.4 us (15%)
  local copies, waits for them, and re-layouts  12.1 us (4%)
  other arithmetic  4.07 us (2%)
    all_to_all x1, waiting for transfers between devices, shards(): lax.all_to_all(exo_tokens.reshape(-1, width), 'tm', split_axis=0, concat_...  73.2 us
    ppermute x16, starting transfers between devices, scatter_sum(): come = lax.ppermute(away, 'tm', [(i, i ^ 1 << bit) for i in range(n_dev)])  49.2 us
    pallas_call x1, Pallas kernels, attention(): pl.pallas_call(functools.partial(attention_kernel, tok, n_query, n_main,...  39.4 us
    ppermute x16, waiting for transfers between devices, scatter_sum(): come = lax.ppermute(away, 'tm', [(i, i ^ 1 << bit) for i in range(n_dev)])  29.2 us
    dot_general x5, matrix products, nn_dot(): return jnp.dot(a, b, preferred_element_type=F32)  25.4 us
    dot_general x5, matrix products, tn_dot(): lax.dot_general(a, b, (((0,), (0,)), ((), ())), preferred_element_type=F32)  19.7 us
    all_to_all x1, starting transfers between devices, shards(): lax.all_to_all(exo_tokens.reshape(-1, width), 'tm', split_axis=0, concat_...  7.6 us
    all_to_all x1, local copies, waits for them, and re-layouts, shards(): lax.all_to_all(exo_tokens.reshape(-1, width), 'tm', split_axis=0, concat_...  7.38 us
  transfers between devices with their start and end apart: 19, of which 7 were waited for; matrix products, arithmetic and copies ran while one was open for 17% of the time, Pallas kernels for 0%

profile of v1, /device:TPU:0, one launch (start us, length us, event | category | flops | bytes accessed | tf_op | source)
XLA Modules:
  0.0 268.3 jit_solution(17422110903288965652)
XLA Ops:
  0.6 7.4 %all_to_all.8 = bf16[16,128,1024]{2,1,0:T(8,128)(2,1)} reshape(bf16[1024,2,1024]{2,1,0:T(2,128)(2,1)} %param.8) | data formatting | bytes 8388608 | tf_op jit(solution)/shard_map/all_to_all | solution.py:195
  8.0 7.6 %all-to-all-start = ((bf16[16,128,1024]{2,1,0:T(8,128)(2,1)}), bf16[16,128,1024]{2,1,0:T(8,128)(2,1)}, u32[]{:S(2)}, u32[]{:S(2)}) async-start(bf16[16,128,1024]{2,1,0:T(8,128)(2,1)} %all_to_all.8), calls=%async_computation | async-start | bytes 8388608 | tf_op jit(solution)/shard_map/all_to_all | solution.py:195
  17.0 3.0 %convolution_convert_fusion.5.g_ref = bf16[64,1024]{1,0:T(8,128)(2,1)} fusion(bf16[1024,1024]{1,0:T(8,128)(2,1)} %param.12, bf16[64,1024]{1,0:T(8,128)(2,1)S(1)} %copy-done.3, f32[64]{0:T(128)S(1)} %convert_element_type.217), kind=kOutput, calls=%fused_computation.15 | convolution fusion | flops 134479872 | bytes 2359552 | tf_op jit(solution)/shard_map/dot_general | solution.py:25
  20.0 73.2 %all-to-all-done = bf16[16,128,1024]{2,1,0:T(8,128)(2,1)} async-done(((bf16[16,128,1024]{2,1,0:T(8,128)(2,1)}), bf16[16,128,1024]{2,1,0:T(8,128)(2,1)}, u32[]{:S(2)}, u32[]{:S(2)}) %all-to-all-start) | async-done | bytes 4194336 | tf_op jit(solution)/shard_map/all_to_all | solution.py:195
  93.2 1.7 fusion.15
  94.9 2.9 %collective-permute-start = (bf16[512,1024]{1,0:T(8,128)(2,1)S(1)}, bf16[512,1024]{1,0:T(8,128)(2,1)S(1)}, u32[]{:S(2)}, u32[]{:S(2)}) collective-permute-start(bf16[512,1024]{1,0:T(8,128)(2,1)S(1)} %bitcast.134), channel_id=1, source_target_pairs={{0,1},{1,2},{2,3},{3,4},{4,5},{5,6},{6,7},{7,8},{8,9},{9,10},{10,1... | collective-permute-start | bytes 3145736 | tf_op jit(solution)/shard_map/ppermute | solution.py:202
  99.2 8.4 %convolution_convert_fusion.vm_ref = bf16[2048,1024]{1,0:T(8,128)(2,1)} fusion(bf16[2048,1024]{1,0:T(8,128)(2,1)} %bitcast, bf16[1024,1024]{1,0:T(8,128)(2,1)S(1)} %copy-done), kind=kOutput, calls=%fused_computation.4 | convolution fusion | flops 4297064448 | bytes 10485760 | tf_op jit(solution)/shard_map/dot_general | solution.py:29
  107.6 8.4 %convolution_convert_fusion.1.km_ref = bf16[2048,1024]{1,0:T(8,128)(2,1)} fusion(bf16[2048,1024]{1,0:T(8,128)(2,1)} %bitcast, bf16[1024,1024]{1,0:T(8,128)(2,1)S(1)} %copy-done.8), kind=kOutput, calls=%fused_computation.5 | convolution fusion | flops 4297064448 | bytes 10485760 | tf_op jit(solution)/shard_map/dot_general | solution.py:29
  116.2 3.7 %convolution_convert_fusion.3.vh_ref = bf16[1024,1024]{1,0:T(8,128)(2,1)} fusion(bf16[1024,1024]{1,0:T(8,128)(2,1)S(1)} %constant_dynamic-update-slice_fusion, bf16[1024,1024]{1,0:T(8,128)(2,1)S(1)} %copy-done), kind=kOutput, calls=%fused_computation.11 | convolution fusion | flops 2148532224 | bytes 6291456 | tf_op jit(solution)/shard_map/dot_general | solution.py:29
  119.9 3.7 %convolution_convert_fusion.4.kh_ref = bf16[1024,1024]{1,0:T(8,128)(2,1)} fusion(bf16[1024,1024]{1,0:T(8,128)(2,1)S(1)} %constant_dynamic-update-slice_fusion, bf16[1024,1024]{1,0:T(8,128)(2,1)S(1)} %copy-done.8), kind=kOutput, calls=%fused_computation.12 | convolution fusion | flops 2148532224 | bytes 6291456 | tf_op jit(solution)/shard_map/dot_general | solution.py:29
  123.6 39.4 %banded_attention.1 = (bf16[64,1024]{1,0:T(8,128)(2,1)}, bf16[64,1024]{1,0:T(8,128)(2,1)}, bf16[2048,1024]{1,0:T(8,128)(2,1)}, bf16[1024,1024]{1,0:T(8,128)(2,1)...) custom-call(s32[1,256]{1,0:T(1,128)} %tile.17.lo_ref, s32[1,256]{1,0:T(1,128)} %tile.19.hi_ref, ...), custom_call_target="tpu_custom_call" | custom-call | flops 9663676416 | bytes 25165824 | tf_op jit(solution)/shard_map/banded_attention/pallas_call | solution.py:140
  163.0 1.7 convolution_convert_fusion.2
  165.1 6.0 %collective-permute-start.10 = (bf16[2,2,2,64,512]{4,3,0,1,2:T(8,128)(2,1)S(1)}, bf16[2,2,2,64,512]{4,3,0,1,2:T(8,128)(2,1)S(1)}, u32[]{:S(2)}, u32[]{:S(2)}) collective-permute-start(bf16[2,2,2,64,512]{4,3,0,1,2:T(8,128)(2,1)S(1)} %bitcast.136), channel_id=1, source_target_pairs={{0,1},{1,0},{2,3},{3,2},{4,5},{5,4},{6,7},{7,6},{8,9},{9,8},{10,11... | collective-permute-start | bytes 1572872 | tf_op jit(solution)/shard_map/ppermute | solution.py:179
  171.2 6.7 %fusion.17 = f32[1024,1024]{0,1:T(8,128)S(1)} fusion(bf16[2048,1024]{1,0:T(8,128)(2,1)S(1)} %copy-done.13, bf16[2048,1024]{1,0:T(8,128)(2,1)} %bitcast), kind=kOutput, calls=%fused_computation.76 | convolution fusion | flops 4294967296 | bytes 12582912 | tf_op jit(solution)/shard_map/dot_general | solution.py:21
  177.9 6.5 %fusion.18 = f32[1024,1024]{0,1:T(8,128)S(1)} fusion(bf16[2048,1024]{1,0:T(8,128)(2,1)S(1)} %copy-done.12, bf16[2048,1024]{1,0:T(8,128)(2,1)} %bitcast), kind=kOutput, calls=%fused_computation.77 | convolution fusion | flops 4294967296 | bytes 12582912 | tf_op jit(solution)/shard_map/dot_general | solution.py:21
  184.5 2.4 fusion.1
  186.9 2.4 fusion
  191.3 1.6 collective-permute-start.6
  193.3 10.5 %collective-permute-start.11 = (bf16[2,2,64,512]{3,2,0,1:T(8,128)(2,1)S(1)}, bf16[2,2,64,512]{3,2,0,1:T(8,128)(2,1)S(1)}, u32[]{:S(2)}, u32[]{:S(2)}) collective-permute-start(bf16[2,2,64,512]{3,2,0,1:T(8,128)(2,1)S(1)} %dynamic-slice_bitcast_fusion.3), channel_id=1, source_target_pairs={{0,2},{1,3},{2,0},{3,1},{4,6},{5,7},{6,4},{7,5},{8,10},{9,11},{10,... | collective-permute-start | bytes 786440 | tf_op jit(solution)/shard_map/ppermute | solution.py:179
  203.9 8.5 %collective-permute-start.15 = (bf16[2,2,64,512]{3,2,1,0:T(8,128)(2,1)S(1)}, bf16[2,2,64,512]{3,2,1,0:T(8,128)(2,1)S(1)}, u32[]{:S(2)}, u32[]{:S(2)}) collective-permute-start(bf16[2,2,64,512]{3,2,1,0:T(8,128)(2,1)S(1)} %dynamic-slice_bitcast_fusion.2), channel_id=1, source_target_pairs={{0,4},{1,5},{2,6},{3,7},{4,0},{5,1},{6,2},{7,3},{8,12},{9,13},{10,... | collective-permute-start | bytes 786440 | tf_op jit(solution)/shard_map/ppermute | solution.py:179
  212.5 6.3 %collective-permute-start.12 = (bf16[2,64,512]{2,1,0:T(8,128)(2,1)S(1)}, bf16[2,64,512]{2,1,0:T(8,128)(2,1)S(1)}, u32[]{:S(2)}, u32[]{:S(2)}) collective-permute-start(bf16[2,64,512]{2,1,0:T(8,128)(2,1)S(1)} %dynamic-slice_bitcast_fusion.7), channel_id=1, source_target_pairs={{0,4},{1,5},{2,6},{3,7},{4,0},{5,1},{6,2},{7,3},{8,12},{9,13},{10,... | collective-permute-start | bytes 393224 | tf_op jit(solution)/shard_map/ppermute | solution.py:179
  218.9 2.4 collective-permute-start.16
  221.3 2.0 collective-permute-done.12
  223.4 4.2 %collective-permute-start.13 = (bf16[64,512]{1,0:T(8,128)(2,1)S(1)}, bf16[64,512]{1,0:T(8,128)(2,1)S(1)}, u32[]{:S(2)}, u32[]{:S(2)}) collective-permute-start(bf16[64,512]{1,0:T(8,128)(2,1)S(1)} %dynamic-slice_bitcast_fusion.11), channel_id=1, source_target_pairs={{0,8},{1,9},{2,10},{3,11},{4,12},{5,13},{6,14},{7,15},{8,0},{9,1},... | collective-permute-start | bytes 196616 | tf_op jit(solution)/shard_map/ppermute | solution.py:179
  227.6 3.7 %collective-permute-start.17 = (bf16[64,512]{1,0:T(8,128)(2,1)S(1)}, bf16[64,512]{1,0:T(8,128)(2,1)S(1)}, u32[]{:S(2)}, u32[]{:S(2)}) collective-permute-start(bf16[64,512]{1,0:T(8,128)(2,1)S(1)} %dynamic-slice_bitcast_fusion.10), channel_id=1, source_target_pairs={{0,2},{1,3},{2,0},{3,1},{4,6},{5,7},{6,4},{7,5},{8,10},{9,11},{10,... | collective-permute-start | bytes 196616 | tf_op jit(solution)/shard_map/ppermute | solution.py:179
  234.6 10.0 %collective-permute-done.7 = bf16[2,2,64,1024]{3,2,1,0:T(8,128)(2,1)S(1)} collective-permute-done((bf16[2,2,64,1024]{3,2,1,0:T(8,128)(2,1)S(1)}, bf16[2,2,64,1024]{3,2,1,0:T(8,128)(2,1)S(1)}, u32[]{:S(2)}, u32[]{:S(2)}) %collective-permute-start.7) | collective-permute-done | bytes 524320 | tf_op jit(solution)/shard_map/ppermute | solution.py:179
  244.8 1.7 collective-permute-start.8
  246.8 1.8 collective-permute-start.4
  248.6 9.0 %collective-permute-done.8 = bf16[2,64,1024]{2,1,0:T(8,128)(2,1)S(1)} collective-permute-done((bf16[2,64,1024]{2,1,0:T(8,128)(2,1)S(1)}, bf16[2,64,1024]{2,1,0:T(8,128)(2,1)S(1)}, u32[]{:S(2)}, u32[]{:S(2)}) %collective-permute-start.8) | collective-permute-done | bytes 262176 | tf_op jit(solution)/shard_map/ppermute | solution.py:179
  257.7 1.5 collective-permute-start.9
  259.5 3.4 %collective-permute-done.9 = bf16[64,1024]{1,0:T(8,128)(2,1)S(1)} collective-permute-done((bf16[64,1024]{1,0:T(8,128)(2,1)S(1)}, bf16[64,1024]{1,0:T(8,128)(2,1)S(1)}, u32[]{:S(2)}, u32[]{:S(2)}) %collective-permute-start.9) | collective-permute-done | bytes 131104 | tf_op jit(solution)/shard_map/ppermute | solution.py:179
  263.6 3.9 %collective-permute-done.5 = bf16[64,1024]{1,0:T(8,128)(2,1)S(1)} collective-permute-done((bf16[64,1024]{1,0:T(8,128)(2,1)S(1)}, bf16[64,1024]{1,0:T(8,128)(2,1)S(1)}, u32[]{:S(2)}, u32[]{:S(2)}) %collective-permute-start.5) | collective-permute-done | bytes 131104 | tf_op jit(solution)/shard_map/ppermute | solution.py:179
  (92 shorter events, 11.3 us)
Async XLA Ops:
  0.6 98.5 %copy-start = (bf16[1024,1024]{1,0:T(8,128)(2,1)S(1)}, bf16[1024,1024]{1,0:T(8,128)(2,1)}, u32[]{:S(2)}) copy-start(bf16[1024,1024]{1,0:T(8,128)(2,1)} %param.11) | copy-start | bytes 6291460
  8.0 7.6 %copy-start.7 = (s32[64]{0:T(128)S(1)}, s32[64]{0:T(128)}, u32[]{:S(2)}) copy-start(s32[64]{0:T(128)} %param.14) | copy-start | bytes 772
  8.0 9.0 %copy-start.9 = (s32[64]{0:T(128)S(1)}, s32[64]{0:T(128)}, u32[]{:S(2)}) copy-start(s32[64]{0:T(128)} %param.13) | copy-start | bytes 772
  8.0 9.0 %copy-start.3 = (bf16[64,1024]{1,0:T(8,128)(2,1)S(1)}, bf16[64,1024]{1,0:T(8,128)(2,1)}, u32[]{:S(2)}) copy-start(bf16[64,1024]{1,0:T(8,128)(2,1)} %param.15) | copy-start | bytes 393220
  8.0 85.2 %all-to-all-start = ((bf16[16,128,1024]{2,1,0:T(8,128)(2,1)}), bf16[16,128,1024]{2,1,0:T(8,128)(2,1)}, u32[]{:S(2)}, u32[]{:S(2)}) async-start(bf16[16,128,1024]{2,1,0:T(8,128)(2,1)} %all_to_all.8), calls=%async_computation | async-start | bytes 8388608 | tf_op jit(solution)/shard_map/all_to_all | solution.py:195
  94.9 21.1 %collective-permute-start = (bf16[512,1024]{1,0:T(8,128)(2,1)S(1)}, bf16[512,1024]{1,0:T(8,128)(2,1)S(1)}, u32[]{:S(2)}, u32[]{:S(2)}) collective-permute-start(bf16[512,1024]{1,0:T(8,128)(2,1)S(1)} %bitcast.134), channel_id=1, source_target_pairs={{0,1},{1,2},{2,3},{3,4},{4,5},{5,6},{6,7},{7,8},{8,9},{9,10},{10,1... | collective-permute-start | bytes 3145736 | tf_op jit(solution)/shard_map/ppermute | solution.py:202
  97.9 18.3 %collective-permute-start.1 = (bf16[512,1024]{1,0:T(8,128)(2,1)S(1)}, bf16[512,1024]{1,0:T(8,128)(2,1)S(1)}, u32[]{:S(2)}, u32[]{:S(2)}) collective-permute-start(bf16[512,1024]{1,0:T(8,128)(2,1)S(1)} %bitcast.133), channel_id=1, source_target_pairs={{1,0},{2,1},{3,2},{4,3},{5,4},{6,5},{7,6},{8,7},{9,8},{10,9},{11,1... | collective-permute-start | bytes 3145736 | tf_op jit(solution)/shard_map/ppermute | solution.py:203
  99.2 8.5 %copy-start.8 = (bf16[1024,1024]{1,0:T(8,128)(2,1)S(1)}, bf16[1024,1024]{1,0:T(8,128)(2,1)}, u32[]{:S(2)}) copy-start(bf16[1024,1024]{1,0:T(8,128)(2,1)} %param.10) | copy-start | bytes 6291460
  116.2 3.7 %copy-start.5 = (bf16[1024,1024]{1,0:T(8,128)(2,1)}, bf16[1024,1024]{1,0:T(8,128)(2,1)S(1)}, u32[]{:S(2)}) copy-start(bf16[1024,1024]{1,0:T(8,128)(2,1)S(1)} %constant_dynamic-update-slice_fusion) | copy-start | bytes 6291460
  164.8 6.3 %copy-start.13 = (bf16[2048,1024]{1,0:T(8,128)(2,1)S(1)}, bf16[2048,1024]{1,0:T(8,128)(2,1)}, u32[]{:S(2)}) copy-start(bf16[2048,1024]{1,0:T(8,128)(2,1)} %get-tuple-element.13) | copy-start | bytes 12582916
  165.1 28.0 %collective-permute-start.10 = (bf16[2,2,2,64,512]{4,3,0,1,2:T(8,128)(2,1)S(1)}, bf16[2,2,2,64,512]{4,3,0,1,2:T(8,128)(2,1)S(1)}, u32[]{:S(2)}, u32[]{:S(2)}) collective-permute-start(bf16[2,2,2,64,512]{4,3,0,1,2:T(8,128)(2,1)S(1)} %bitcast.136), channel_id=1, source_target_pairs={{0,1},{1,0},{2,3},{3,2},{4,5},{5,4},{6,7},{7,6},{8,9},{9,8},{10,11... | collective-permute-start | bytes 1572872 | tf_op jit(solution)/shard_map/ppermute | solution.py:179
  171.1 32.7 %collective-permute-start.14 = (bf16[2,2,2,64,512]{4,3,2,0,1:T(8,128)(2,1)S(1)}, bf16[2,2,2,64,512]{4,3,2,0,1:T(8,128)(2,1)S(1)}, u32[]{:S(2)}, u32[]{:S(2)}) collective-permute-start(bf16[2,2,2,64,512]{4,3,2,0,1:T(8,128)(2,1)S(1)} %bitcast.135), channel_id=1, source_target_pairs={{0,1},{1,0},{2,3},{3,2},{4,5},{5,4},{6,7},{7,6},{8,9},{9,8},{10,11... | collective-permute-start | bytes 1572872 | tf_op jit(solution)/shard_map/ppermute | solution.py:179
  171.2 6.7 %copy-start.12 = (bf16[2048,1024]{1,0:T(8,128)(2,1)S(1)}, bf16[2048,1024]{1,0:T(8,128)(2,1)}, u32[]{:S(2)}) copy-start(bf16[2048,1024]{1,0:T(8,128)(2,1)} %get-tuple-element.15) | copy-start | bytes 12582916
  177.9 6.5 %copy-start.6 = (bf16[1024,1024]{1,0:T(8,128)(2,1)S(1)}, bf16[1024,1024]{1,0:T(8,128)(2,1)}, u32[]{:S(2)}) copy-start(bf16[1024,1024]{1,0:T(8,128)(2,1)} %copy-done.5) | copy-start | bytes 6291460
  177.9 6.5 %copy-start.11 = (bf16[1024,1024]{1,0:T(8,128)(2,1)S(1)}, bf16[1024,1024]{1,0:T(8,128)(2,1)}, u32[]{:S(2)}) copy-start(bf16[1024,1024]{1,0:T(8,128)(2,1)} %get-tuple-element.14) | copy-start | bytes 6291460
  186.9 2.5 copy-start.2
  186.9 2.5 copy-start.4
  191.3 40.1 %collective-permute-start.6 = (bf16[2,2,2,64,1024]{4,3,2,0,1:T(8,128)(2,1)S(1)}, bf16[2,2,2,64,1024]{4,3,2,0,1:T(8,128)(2,1)S(1)}, u32[]{:S(2)}, u32[]{:S(2)}) collective-permute-start(bf16[2,2,2,64,1024]{4,3,2,0,1:T(8,128)(2,1)S(1)} %bitcast.132), channel_id=1, source_target_pairs={{0,1},{1,0},{2,3},{3,2},{4,5},{5,4},{6,7},{7,6},{8,9},{9,8},{10,11... | collective-permute-start | bytes 3145736 | tf_op jit(solution)/shard_map/ppermute | solution.py:179
  193.0 38.9 %collective-permute-start.2 = (bf16[2,2,2,64,1024]{4,3,0,1,2:T(8,128)(2,1)S(1)}, bf16[2,2,2,64,1024]{4,3,0,1,2:T(8,128)(2,1)S(1)}, u32[]{:S(2)}, u32[]{:S(2)}) collective-permute-start(bf16[2,2,2,64,1024]{4,3,0,1,2:T(8,128)(2,1)S(1)} %bitcast.131), channel_id=1, source_target_pairs={{0,1},{1,0},{2,3},{3,2},{4,5},{5,4},{6,7},{7,6},{8,9},{9,8},{10,11... | collective-permute-start | bytes 3145736 | tf_op jit(solution)/shard_map/ppermute | solution.py:179
  193.3 19.1 %collective-permute-start.11 = (bf16[2,2,64,512]{3,2,0,1:T(8,128)(2,1)S(1)}, bf16[2,2,64,512]{3,2,0,1:T(8,128)(2,1)S(1)}, u32[]{:S(2)}, u32[]{:S(2)}) collective-permute-start(bf16[2,2,64,512]{3,2,0,1:T(8,128)(2,1)S(1)} %dynamic-slice_bitcast_fusion.3), channel_id=1, source_target_pairs={{0,2},{1,3},{2,0},{3,1},{4,6},{5,7},{6,4},{7,5},{8,10},{9,11},{10,... | collective-permute-start | bytes 786440 | tf_op jit(solution)/shard_map/ppermute | solution.py:179
  203.9 14.9 %collective-permute-start.15 = (bf16[2,2,64,512]{3,2,1,0:T(8,128)(2,1)S(1)}, bf16[2,2,64,512]{3,2,1,0:T(8,128)(2,1)S(1)}, u32[]{:S(2)}, u32[]{:S(2)}) collective-permute-start(bf16[2,2,64,512]{3,2,1,0:T(8,128)(2,1)S(1)} %dynamic-slice_bitcast_fusion.2), channel_id=1, source_target_pairs={{0,4},{1,5},{2,6},{3,7},{4,0},{5,1},{6,2},{7,3},{8,12},{9,13},{10,... | collective-permute-start | bytes 786440 | tf_op jit(solution)/shard_map/ppermute | solution.py:179
  212.5 10.8 %collective-permute-start.12 = (bf16[2,64,512]{2,1,0:T(8,128)(2,1)S(1)}, bf16[2,64,512]{2,1,0:T(8,128)(2,1)S(1)}, u32[]{:S(2)}, u32[]{:S(2)}) collective-permute-start(bf16[2,64,512]{2,1,0:T(8,128)(2,1)S(1)} %dynamic-slice_bitcast_fusion.7), channel_id=1, source_target_pairs={{0,4},{1,5},{2,6},{3,7},{4,0},{5,1},{6,2},{7,3},{8,12},{9,13},{10,... | collective-permute-start | bytes 393224 | tf_op jit(solution)/shard_map/ppermute | solution.py:179
  218.9 8.6 %collective-permute-start.16 = (bf16[2,64,512]{2,1,0:T(8,128)(2,1)S(1)}, bf16[2,64,512]{2,1,0:T(8,128)(2,1)S(1)}, u32[]{:S(2)}, u32[]{:S(2)}) collective-permute-start(bf16[2,64,512]{2,1,0:T(8,128)(2,1)S(1)} %dynamic-slice_bitcast_fusion.6), channel_id=1, source_target_pairs={{0,8},{1,9},{2,10},{3,11},{4,12},{5,13},{6,14},{7,15},{8,0},{9,1},... | collective-permute-start | bytes 393224 | tf_op jit(solution)/shard_map/ppermute | solution.py:179
  223.4 8.0 %collective-permute-start.13 = (bf16[64,512]{1,0:T(8,128)(2,1)S(1)}, bf16[64,512]{1,0:T(8,128)(2,1)S(1)}, u32[]{:S(2)}, u32[]{:S(2)}) collective-permute-start(bf16[64,512]{1,0:T(8,128)(2,1)S(1)} %dynamic-slice_bitcast_fusion.11), channel_id=1, source_target_pairs={{0,8},{1,9},{2,10},{3,11},{4,12},{5,13},{6,14},{7,15},{8,0},{9,1},... | collective-permute-start | bytes 196616 | tf_op jit(solution)/shard_map/ppermute | solution.py:179
  227.6 6.2 %collective-permute-start.17 = (bf16[64,512]{1,0:T(8,128)(2,1)S(1)}, bf16[64,512]{1,0:T(8,128)(2,1)S(1)}, u32[]{:S(2)}, u32[]{:S(2)}) collective-permute-start(bf16[64,512]{1,0:T(8,128)(2,1)S(1)} %dynamic-slice_bitcast_fusion.10), channel_id=1, source_target_pairs={{0,2},{1,3},{2,0},{3,1},{4,6},{5,7},{6,4},{7,5},{8,10},{9,11},{10,... | collective-permute-start | bytes 196616 | tf_op jit(solution)/shard_map/ppermute | solution.py:179
  231.8 12.7 %collective-permute-start.7 = (bf16[2,2,64,1024]{3,2,1,0:T(8,128)(2,1)S(1)}, bf16[2,2,64,1024]{3,2,1,0:T(8,128)(2,1)S(1)}, u32[]{:S(2)}, u32[]{:S(2)}) collective-permute-start(bf16[2,2,64,1024]{3,2,1,0:T(8,128)(2,1)S(1)} %dynamic-slice_bitcast_fusion), channel_id=1, source_target_pairs={{0,4},{1,5},{2,6},{3,7},{4,0},{5,1},{6,2},{7,3},{8,12},{9,13},{10,... | collective-permute-start | bytes 1572872 | tf_op jit(solution)/shard_map/ppermute | solution.py:179
  232.4 14.1 %collective-permute-start.3 = (bf16[2,2,64,1024]{3,2,0,1:T(8,128)(2,1)S(1)}, bf16[2,2,64,1024]{3,2,0,1:T(8,128)(2,1)S(1)}, u32[]{:S(2)}, u32[]{:S(2)}) collective-permute-start(bf16[2,2,64,1024]{3,2,0,1:T(8,128)(2,1)S(1)} %dynamic-slice_bitcast_fusion.1), channel_id=1, source_target_pairs={{0,2},{1,3},{2,0},{3,1},{4,6},{5,7},{6,4},{7,5},{8,10},{9,11},{10,... | collective-permute-start | bytes 1572872 | tf_op jit(solution)/shard_map/ppermute | solution.py:179
  244.8 12.8 %collective-permute-start.8 = (bf16[2,64,1024]{2,1,0:T(8,128)(2,1)S(1)}, bf16[2,64,1024]{2,1,0:T(8,128)(2,1)S(1)}, u32[]{:S(2)}, u32[]{:S(2)}) collective-permute-start(bf16[2,64,1024]{2,1,0:T(8,128)(2,1)S(1)} %dynamic-slice_bitcast_fusion.4), channel_id=1, source_target_pairs={{0,8},{1,9},{2,10},{3,11},{4,12},{5,13},{6,14},{7,15},{8,0},{9,1},... | collective-permute-start | bytes 786440 | tf_op jit(solution)/shard_map/ppermute | solution.py:179
  246.5 21.8 %copy-start.1 = (bf16[1024,1024]{1,0:T(8,128)(2,1)S(1)}, bf16[1024,1024]{1,0:T(8,128)(2,1)}, u32[]{:S(2)}) copy-start(bf16[1024,1024]{1,0:T(8,128)(2,1)} %param.11) | copy-start | bytes 6291460
  246.8 12.5 %collective-permute-start.4 = (bf16[2,64,1024]{2,1,0:T(8,128)(2,1)S(1)}, bf16[2,64,1024]{2,1,0:T(8,128)(2,1)S(1)}, u32[]{:S(2)}, u32[]{:S(2)}) collective-permute-start(bf16[2,64,1024]{2,1,0:T(8,128)(2,1)S(1)} %dynamic-slice_bitcast_fusion.5), channel_id=1, source_target_pairs={{0,4},{1,5},{2,6},{3,7},{4,0},{5,1},{6,2},{7,3},{8,12},{9,13},{10,... | collective-permute-start | bytes 786440 | tf_op jit(solution)/shard_map/ppermute | solution.py:179
  257.7 5.2 %collective-permute-start.9 = (bf16[64,1024]{1,0:T(8,128)(2,1)S(1)}, bf16[64,1024]{1,0:T(8,128)(2,1)S(1)}, u32[]{:S(2)}, u32[]{:S(2)}) collective-permute-start(bf16[64,1024]{1,0:T(8,128)(2,1)S(1)} %dynamic-slice_bitcast_fusion.8), channel_id=1, source_target_pairs={{0,2},{1,3},{2,0},{3,1},{4,6},{5,7},{6,4},{7,5},{8,10},{9,11},{10,... | collective-permute-start | bytes 393224 | tf_op jit(solution)/shard_map/ppermute | solution.py:179
  259.4 8.2 %collective-permute-start.5 = (bf16[64,1024]{1,0:T(8,128)(2,1)S(1)}, bf16[64,1024]{1,0:T(8,128)(2,1)S(1)}, u32[]{:S(2)}, u32[]{:S(2)}) collective-permute-start(bf16[64,1024]{1,0:T(8,128)(2,1)S(1)} %dynamic-slice_bitcast_fusion.9), channel_id=1, source_target_pairs={{0,8},{1,9},{2,10},{3,11},{4,12},{5,13},{6,14},{7,15},{8,0},{9,1},... | collective-permute-start | bytes 393224 | tf_op jit(solution)/shard_map/ppermute | solution.py:179
  (1 other events, 2.4 us)

commit v2 on v0

v2 whole, which is shorter than its diff:
```python
import functools

import jax
import jax.numpy as jnp
from jax import lax
from jax.experimental import pallas as pl
from jax.experimental.pallas import tpu as pltpu
from jax.sharding import PartitionSpec as P

H = 16
HD = 64
W = 16
GROUP = 4
LANES = GROUP * HD
CALLS = 2
CHUNK = 256
F32 = jnp.float32
BF16 = jnp.bfloat16


def tn_dot(a, b):
    return lax.dot_general(a, b, (((0,), (0,)), ((), ())), preferred_element_type=F32)


def nt_dot(a, b):
    return lax.dot_general(a, b, (((1,), (1,)), ((), ())), preferred_element_type=F32)


def nn_dot(a, b):
    return jnp.dot(a, b, preferred_element_type=F32)


def own_head(n_query):
    wide = GROUP * n_query
    row_head = lax.broadcasted_iota(jnp.int32, (wide, LANES), 0) // (n_query // 2) % GROUP
    col_head = lax.broadcasted_iota(jnp.int32, (wide, LANES), 1) // HD
    return row_head == col_head


def spread(x, own):
    part = x.shape[0] // 2
    rows = jnp.concatenate([x[:part]] * GROUP + [x[part:]] * GROUP, 0)
    return jnp.where(own, rows, jnp.zeros_like(rows))


def scaled(x):
    return (x.astype(F32) * HD ** (-0.5)).astype(BF16)


def fill_bias(lo_ref, hi_ref, bias_ref, n_query):
    wide = GROUP * n_query
    lo = lo_ref[...]
    hi = hi_ref[...]
    rows = lax.broadcasted_iota(jnp.int32, (CHUNK, wide), 0)
    near = rows % W
    far = rows % (2 * W)
    second = lax.broadcasted_iota(jnp.int32, (CHUNK, wide), 1) >= wide // 2
    frames = (
        near + jnp.where(second, n_query - W, 0),
        far + W,
        near + jnp.where(second, n_query, -W),
    )
    for i, frame in enumerate(frames):
        bias_ref[i] = jnp.where((frame >= lo) & (frame <= hi), 0.0, -1e30)


def load_edge(ref, side):
    return ref[:, :, side].reshape(CHUNK, LANES)


def load_halo(ref, side):
    return ref[side].reshape(CHUNK, LANES)


def load_mid(ref, c):
    runs = ref.shape[0] // 2
    return ref[pl.ds(c * runs, runs)].reshape(CHUNK, LANES)


def pair_dot(ref, load, x_ref):
    mid = x_ref.shape[0] // 2
    return jnp.concatenate(
        [nt_dot(load(ref, 0), x_ref[:mid, :]), nt_dot(load(ref, 1), x_ref[mid:, :])], 1
    )


def fold(x):
    return x.reshape(CHUNK // 8, 8, x.shape[1])


def stats_kernel(
    lo_ref, hi_ref, q_ref, g_ref, ke_ref, km_ref, kh_ref, ve_ref, vm_ref, vh_ref,
    out_ref, s_ref, bias_ref, bq_ref, bg_ref,
):
    n_query = q_ref.shape[0]
    wide = GROUP * n_query
    own = own_head(n_query)
    bq_ref[...] = scaled(spread(q_ref[...], own))
    bg_ref[...] = scaled(spread(g_ref[...], own))

    @pl.when(pl.program_id(1) == 0)
    def _():
        fill_bias(lo_ref, hi_ref, bias_ref, n_query)

    def score(at, table, s, top):
        s = s + bias_ref[table]
        s_ref[at] = s
        return jnp.maximum(top, jnp.max(fold(s), axis=0))

    top = jnp.full((8, wide), -1e30, F32)
    top = score(0, 0, pair_dot(ke_ref, load_edge, bq_ref), top)
    for c in range(2):
        top = score(1 + c, 1, nt_dot(load_mid(km_ref, c), bq_ref[...]), top)
    top = score(3, 2, pair_dot(kh_ref, load_halo, bq_ref), top)
    top = jnp.max(top, axis=0, keepdims=True)

    total = jnp.zeros((8, wide), F32)
    weighted = jnp.zeros((8, wide), F32)
    for c in range(4):
        if c == 0:
            dp = pair_dot(ve_ref, load_edge, bg_ref)
        elif c == 3:
            dp = pair_dot(vh_ref, load_halo, bg_ref)
        else:
            dp = nt_dot(load_mid(vm_ref, c - 1), bg_ref[...])
        e = jnp.exp(s_ref[c] - top)
        total = total + jnp.sum(fold(e), axis=0)
        weighted = weighted + jnp.sum(fold(e * dp), axis=0)
    out_ref[0:1, :] = top
    out_ref[1:2, :] = jnp.sum(total, axis=0, keepdims=True)
    out_ref[2:3, :] = jnp.sum(weighted, axis=0, keepdims=True)


def grads_kernel(
    lo_ref, hi_ref, one_ref, two_ref, q_ref, g_ref,
    ke_ref, km_ref, kh_ref, ve_ref, vm_ref, vh_ref,
    ctx_ref, dq_ref, pe_ref, pm_ref, ph_ref,
    bias_ref, bq_ref, bg_ref, bqs_ref, bgs_ref, acc_ctx, acc_dq,
):
    n_query = q_ref.shape[0]
    part = n_query // 2
    wide = GROUP * n_query
    mid = wide // 2
    own = own_head(n_query)
    bq_ref[...] = spread(q_ref[...], own)
    bg_ref[...] = spread(g_ref[...], own)
    bqs_ref[...] = scaled(bq_ref[...])
    bgs_ref[...] = scaled(bg_ref[...])

    @pl.when(pl.program_id(1) == 0)
    def _():
        fill_bias(lo_ref, hi_ref, bias_ref, n_query)

    top = jnp.maximum(one_ref[0:1, :], two_ref[0:1, :])
    one = jnp.exp(one_ref[0:1, :] - top)
    two = jnp.exp(two_ref[0:1, :] - top)
    inverse = 1.0 / (one_ref[1:2, :] * one + two_ref[1:2, :] * two)
    mean = (one_ref[2:3, :] * one + two_ref[2:3, :] * two) * inverse
    acc_ctx[...] = jnp.zeros_like(acc_ctx)
    acc_dq[...] = jnp.zeros_like(acc_dq)

    def soft(table, s, dp):
        p = jnp.exp(s + bias_ref[table] - top) * inverse
        return p.astype(BF16), (p * (dp - mean)).astype(BF16)

    def pair(k_ref, v_ref, load, table, store):
        pb, ds = soft(table, pair_dot(k_ref, load, bqs_ref), pair_dot(v_ref, load, bgs_ref))
        for side, lanes in ((0, slice(0, mid)), (1, slice(mid, wide))):
            acc_ctx[lanes, :] += tn_dot(pb[:, lanes], load(v_ref, side))
            acc_dq[lanes, :] += tn_dot(ds[:, lanes], load(k_ref, side))
            store(side, slice(0, LANES), nn_dot(ds[:, lanes], bq_ref[lanes, :]))
            store(side, slice(LANES, 2 * LANES), nn_dot(pb[:, lanes], bg_ref[lanes, :]))

    def store_edge(side, cols, x):
        shape = pe_ref.shape
        pe_ref[:, :, side, :, cols] = x.astype(BF16).reshape(shape[0], shape[1], W, LANES)

    def store_halo(side, cols, x):
        shape = ph_ref.shape
        ph_ref[side, :, :, :, cols] = x.astype(BF16).reshape(shape[1], shape[2], W, LANES)

    pair(ke_ref, ve_ref, load_edge, 0, store_edge)

    def middle(c, carry):
        runs = pm_ref.shape[0] // 2
        k = load_mid(km_ref, c)
        v = load_mid(vm_ref, c)
        pb, ds = soft(1, nt_dot(k, bqs_ref[...]), nt_dot(v, bgs_ref[...]))
        acc_ctx[...] += tn_dot(pb, v)
        acc_dq[...] += tn_dot(ds, k)
        shape = (runs, pm_ref.shape[1], 2 * W, LANES)
        here = pl.ds(c * runs, runs)
        pm_ref[here, :, :, :LANES] = nn_dot(ds, bq_ref[...]).astype(BF16).reshape(shape)
        pm_ref[here, :, :, LANES:] = nn_dot(pb, bg_ref[...]).astype(BF16).reshape(shape)
        return carry

    lax.fori_loop(0, 2, middle, 0)
    pair(kh_ref, vh_ref, load_halo, 2, store_halo)

    def diagonal(acc, out_ref):
        kept = jnp.where(own, acc, 0.0)
        for i in range(2):
            rows = [kept[(i * GROUP + h) * part : (i * GROUP + h + 1) * part] for h in range(GROUP)]
            out_ref[i * part : (i + 1) * part, :] = functools.reduce(jnp.add, rows)

    diagonal(acc_ctx[...], ctx_ref)
    diagonal(acc_dq[...], dq_ref)


def attention(first_group, groups, lo, hi, stats, queries, d_context, keys, values):
    n_query = queries.shape[1]
    src, tok = keys[0].shape[0], keys[0].shape[2]
    wide = GROUP * n_query
    flat = pl.BlockSpec((None, 1, wide), lambda b, g: (b, 0, 0))
    rows = pl.BlockSpec((None, n_query, LANES), lambda b, g: (b, 0, first_group + g))
    table = pl.BlockSpec((None, None, 3, wide), lambda b, g: (b, g, 0, 0))

    def edge(first, k=1):
        shape = (src, None, tok, 2, W, k * LANES)
        return pl.BlockSpec(shape, lambda b, g: (0, b, 0, 0, 0, first + g))

    def mid(first, k=1):
        shape = (src, None, tok, 2 * W, k * LANES)
        return pl.BlockSpec(shape, lambda b, g: (0, b, 0, 0, first + g))

    def halo(first, k=1):
        shape = (2, src, None, tok, W, k * LANES)
        return pl.BlockSpec(shape, lambda b, g: (0, 0, b, 0, 0, first + g))

    sections = [edge(first_group), mid(first_group), halo(first_group)]
    operand = pltpu.VMEM((wide, LANES), BF16)
    total = pltpu.VMEM((wide, LANES), F32)
    bias = pltpu.VMEM((3, CHUNK, wide), F32)
    scores = 8 * CHUNK * wide * groups
    common = dict(
        grid=(2, groups),
        compiler_params=pltpu.CompilerParams(dimension_semantics=("arbitrary", "arbitrary")),
    )
    if stats is None:
        return pl.pallas_call(
            stats_kernel,
            in_specs=[flat, flat, rows, rows] + sections * 2,
            out_specs=table,
            out_shape=jax.ShapeDtypeStruct((2, groups, 3, wide), F32),
            scratch_shapes=[pltpu.VMEM((4, CHUNK, wide), F32), bias, operand, operand],
            cost_estimate=pl.CostEstimate(
                flops=4 * scores * LANES, bytes_accessed=6 * scores, transcendentals=scores
            ),
            name="softmax_stats",
            **common,
        )(lo, hi, queries, d_context, *keys, *values)

    def shape(x):
        return jax.ShapeDtypeStruct(x.shape[:-1] + (2 * groups * LANES,), BF16)

    partial = jax.ShapeDtypeStruct((2, n_query, groups * LANES), F32)
    partial_spec = pl.BlockSpec((None, n_query, LANES), lambda b, g: (b, 0, g))
    return pl.pallas_call(
        grads_kernel,
        in_specs=[flat, flat, table, table, rows, rows] + sections * 2,
        out_specs=[partial_spec, partial_spec, edge(0, 2), mid(0, 2), halo(0, 2)],
        out_shape=[partial, partial] + [shape(x) for x in keys],
        scratch_shapes=[bias] + [operand] * 4 + [total] * 2,
        cost_estimate=pl.CostEstimate(
            flops=12 * scores * LANES, bytes_accessed=12 * scores, transcendentals=scores
        ),
        name="banded_grads",
        **common,
    )(lo, hi, *stats, queries, d_context, *keys, *values)


class ScatterSum:
    def __init__(self, term, bits, order):
        self.order = list(order)
        self.left = list(range(bits - 1, -1, -1))
        self.block = term.reshape([2] * bits + [term.shape[0] >> bits, term.shape[1]])

    def send(self):
        bit = self.order.pop(0)
        axis = self.left.index(bit)
        self.left.remove(bit)
        mine = (lax.axis_index("tm") >> bit) & 1
        away = lax.dynamic_index_in_dim(self.block, 1 - mine, axis, keepdims=False)
        self.keep = lax.dynamic_index_in_dim(self.block, mine, axis, keepdims=False)
        return away, 1 << bit

    def receive(self, come):
        block = self.keep.astype(F32) + come.astype(F32)
        self.block = block.astype(BF16) if self.left else block


class Gather:
    def __init__(self, block, bits):
        self.block = block
        self.order = list(range(bits - 1, -1, -1))

    def send(self):
        return self.block, 1 << self.order.pop(0)

    def receive(self, come):
        self.block = jnp.concatenate([self.block, come], axis=0)


class Swap:
    def __init__(self, block, bit):
        self.block = block
        self.order = [bit]

    def send(self):
        return self.block, 1 << self.order.pop(0)

    def receive(self, come):
        self.come = come


def beside(moving, work, *args):
    n_dev = lax.axis_size("tm")
    moving = [m for m in moving if m.order]
    sends = [m.send() for m in moving]
    args, aways = lax.optimization_barrier((args, [away for away, _ in sends]))
    comes = [
        lax.ppermute(away, "tm", [(i, i ^ step) for i in range(n_dev)])
        for away, (_, step) in zip(aways, sends)
    ]
    result, comes = lax.optimization_barrier((work(*args), comes))
    for m, come in zip(moving, comes):
        m.receive(come)
    return result


def shards(
    exo_tokens, queries, key_weight, value_weight, out_weight, gaze_valid, window_offset, cotangent
):
    n_query, width = queries.shape
    tok = exo_tokens.shape[1]
    n_dev = lax.axis_size("tm")
    bits = n_dev.bit_length() - 1
    src = n_dev // 2
    total = n_query * n_dev
    me = lax.axis_index("tm")
    upper_half = me >= src
    spot = me % src

    by_block = exo_tokens.reshape(2, src, n_query, tok, width)
    halves = [list(range(src)), list(range(src, n_dev))]
    outer = jnp.stack([by_block[:, :, :W], by_block[:, :, -W:]], axis=2)
    outer = outer.transpose(1, 0, 4, 2, 3, 5)
    inner = by_block[:, :, W:-W].transpose(1, 0, 3, 2, 4)
    edge = lax.all_to_all(outer, "tm", 0, 0, axis_index_groups=halves, tiled=True)
    middle = lax.all_to_all(inner, "tm", 0, 0, axis_index_groups=halves, tiled=True)
    ring = [(i, i // src * src + (i + 1) % src) for i in range(n_dev)]
    low = lax.ppermute(edge[:, :, :, 1], "tm", ring)
    high = lax.ppermute(edge[:, :, :, 0], "tm", [(target, source) for source, target in ring])
    low = jnp.where(spot == 0, jnp.flip(low, 1), low)
    high = jnp.where(spot == src - 1, jnp.flip(high, 1), high)
    halo = jnp.stack([low, high], axis=0)

    valid_col = gaze_valid.astype(F32)[:, None]
    masked_grad = (cotangent.astype(F32) * valid_col).astype(BF16)
    far = bits - 1
    gather = Gather(masked_grad, bits)
    swap_q, swap_o = Swap(queries, far), Swap(window_offset, far)
    beside([gather, swap_q, swap_o], lambda: ())

    def both(own, other):
        return jnp.where(upper_half, jnp.stack([other, own]), jnp.stack([own, other]))

    q_pair = both(queries, swap_q.come)
    d_context = nt_dot(gather.block, out_weight).astype(BF16)
    g_pair = both(d_context[:n_query], d_context[n_query:])
    offsets = both(window_offset, swap_o.come)
    at = jnp.arange(n_query, dtype=jnp.int32)
    first = (spot + jnp.array([0, src], jnp.int32))[:, None] * n_query
    lower = jnp.maximum(at - W + offsets, -first)
    upper = jnp.minimum(at + offsets, total - 1 - first)

    def lanes(x):
        return jnp.tile(x.reshape(2, 2, 1, n_query // 2), (1, 1, GROUP, 1)).reshape(2, 1, -1)

    lo, hi = lanes(lower), lanes(upper)

    def project(x):
        flat = x.reshape(-1, width)
        return (
            nn_dot(flat, key_weight).astype(BF16).reshape(x.shape),
            nn_dot(flat, value_weight).astype(BF16).reshape(x.shape),
        )

    ke, ve = project(edge)
    km, vm = beside([gather], project, middle)
    kh, vh = project(halo)
    keys, values = (ke, km, kh), (ve, vm, vh)
    sources = [x.reshape(-1, width) for x in (edge, middle, halo)]

    groups = width // LANES // CALLS

    def measure(call, moving):
        work = functools.partial(attention, call * groups, groups, lo, hi, None)
        return Swap(beside(moving, work, q_pair, g_pair, keys, values), far)

    swaps = [measure(0, [gather])]
    for call in range(1, CALLS):
        swaps.append(measure(call, [gather, swaps[-1]]))

    def own_part(x):
        return jnp.where(upper_half, x[1], x[0])

    def other_part(x):
        return jnp.where(upper_half, x[0], x[1])

    moving = [gather] + swaps
    owns, trades, shares = [], [], []
    if CALLS == 1:
        beside(moving, lambda: ())
    for call in range(CALLS):
        stats = (swaps[call].block, swaps[call].come)
        work = functools.partial(attention, call * groups, groups, lo, hi, stats)
        context, d_query, *grads = beside(moving, work, q_pair, g_pair, keys, values)
        owns.append(jnp.stack([own_part(context), own_part(d_query)]))
        trades.append(Swap(jnp.stack([other_part(context), other_part(d_query)]), far))
        moving.append(trades[-1])

        def weigh(*parts):
            terms = [tn_dot(x, g.reshape(x.shape[0], -1)) for x, g in zip(sources, parts)]
            return functools.reduce(jnp.add, terms).astype(BF16)

        term = beside(moving, weigh, *grads)
        cut = term.shape[1] // 2
        orders = [list(range(bits)), [0] + list(range(2, bits)) + [1]]
        for i, order in enumerate(orders):
            shares.append(ScatterSum(term[:, i * cut : (i + 1) * cut], bits, order))
            moving.append(shares[-1])

    pairs = [own + trade.come for own, trade in zip(owns, trades)]
    context = jnp.concatenate([x[0] for x in pairs], axis=1).astype(BF16)
    d_query = jnp.concatenate([x[1] for x in pairs], axis=1).astype(BF16)

    def finish(context):
        attended = (nn_dot(context, out_weight) * valid_col).astype(BF16)
        columns = context.reshape(n_query, n_dev, -1).swapaxes(0, 1)
        return attended, lax.all_to_all(columns, "tm", split_axis=0, concat_axis=0, tiled=True)

    attended, columns = beside(moving, finish, context)
    columns = columns.reshape([2] * bits + [n_query, -1])
    for bit in range(bits):
        axis = bits - 1 - bit
        columns = jnp.where((me >> bit) & 1 == 1, jnp.flip(columns, axis), columns)
    columns = columns.transpose(list(range(bits - 1, -1, -1)) + [bits, bits + 1])
    d_out = beside(moving, lambda c: tn_dot(c.reshape(total, -1), gather.block), columns)
    while any(m.order for m in moving):
        beside(moving, lambda: ())
    blocks = [s.block.reshape(s.block.shape[0], -1, 2, LANES) for s in shares]
    return (
        attended,
        d_query,
        jnp.concatenate([b[:, i, 0] for b in blocks for i in range(b.shape[1])], axis=1),
        jnp.concatenate([b[:, i, 1] for b in blocks for i in range(b.shape[1])], axis=1),
        d_out,
    )


def solution(mesh):
    in_specs = (
        P("rep", "tm", None),
        P(("rep", "tm"), None),
        P(),
        P(),
        P(),
        P(("rep", "tm")),
        P(("rep", "tm")),
        P(("rep", "tm"), None),
    )
    out_specs = (
        P(("rep", "tm"), None),
        P(("rep", "tm"), None),
        P(("rep", "tm"), None),
        P(("rep", "tm"), None),
        P(("rep", "tm"), None),
    )
    return jax.shard_map(shards, mesh=mesh, in_specs=in_specs, out_specs=out_specs, check_vma=False)
```

time: 424 us -> 278 us (0.66)
  blocking collectives: 99.7 us -> 0 us
  local copies, waits for them, and re-layouts: 114 us -> 30.6 us
  matrix products: 115 us -> 57.7 us
  starting transfers between devices: 5.87 us -> 51.6 us
  Pallas kernels: 0 us -> 41.2 us
  other arithmetic: 10.9 us -> 23.9 us
  between operations: 14.3 us -> 1.78 us
  waiting for transfers between devices: 62.3 us -> 66.8 us
    all_to_all x1 -> x0, blocking collectives: 99.7 us -> none  [shards(): lax.all_to_all(exo_tokens, 'tm', split_axis=0, concat_axis=1, tiled=True)]
    convert_element_type x4 -> x0, local copies, waits for them, and re-layouts: 65.9 us -> none  [the longest x2 33 us: attend_block(): value_part = value_part.reshape(n_frames, n_tok, width).astype(jnp.bfloat16)]
    reduce_scatter x2 -> x0, waiting for transfers between devices: 62.3 us -> none  [the longest x1 62.3 us: shards(): lax.psum_scatter(lax.dot_general(flat_sources, flat_grads, (((0,), (0,)),...]
    dot_general x11 -> x15, matrix products: 102 us -> 57.7 us  [the longest x7 29.9 us: nn_dot(): return jnp.dot(a, b, preferred_element_type=F32)]
    ppermute x2 -> x28, waiting for transfers between devices: 0.01 us -> 42.1 us  [the longest x26 42.1 us: beside(): lax.ppermute(away, 'tm', [(i, i ^ step) for i in range(n_dev)])]
    pallas_call x0 -> x4, Pallas kernels: none -> 41.2 us  [the longest x2 28.5 us: attention(): pl.pallas_call(grads_kernel, in_specs=[flat, flat, table, table, rows, ro...]
    ppermute x2 -> x28, starting transfers between devices: 5.79 us -> 37.8 us  [the longest x26 32.4 us: beside(): lax.ppermute(away, 'tm', [(i, i ^ step) for i in range(n_dev)])]
    another operation x1 -> x8, local copies, waits for them, and re-layouts: 28.3 us -> 1.85 us  [the longest x4 1.37 us: lanes(): jnp.tile(x.reshape(2, 2, 1, n_query // 2), (1, 1, GROUP, 1))]
  transfers between devices with their start and end apart: 4 -> 31, of which waited for: 1 -> 13; matrix products, arithmetic and copies ran while one was open for 42% -> 26% of each run, Pallas kernels for 0% -> 15%
where the time goes in v2:
time: 278 us; the launch traced here: 274 us
  waiting for transfers between devices  66.8 us (24%)
  matrix products  57.7 us (21%)
  starting transfers between devices  51.6 us (19%)
  Pallas kernels  41.2 us (15%)
  local copies, waits for them, and re-layouts  30.6 us (11%)
  other arithmetic  23.9 us (9%)
    ppermute x26, waiting for transfers between devices, beside(): lax.ppermute(away, 'tm', [(i, i ^ step) for i in range(n_dev)])  42.1 us
    ppermute x26, starting transfers between devices, beside(): lax.ppermute(away, 'tm', [(i, i ^ step) for i in range(n_dev)])  32.4 us
    dot_general x7, matrix products, nn_dot(): return jnp.dot(a, b, preferred_element_type=F32)  29.9 us
    pallas_call x2, Pallas kernels, attention(): pl.pallas_call(grads_kernel, in_specs=[flat, flat, table, table, rows, ro...  28.5 us
    dot_general x7, matrix products, tn_dot(): lax.dot_general(a, b, (((0,), (0,)), ((), ())), preferred_element_type=F32)  25.4 us
    all_to_all x1, waiting for transfers between devices, shards(): lax.all_to_all(outer, 'tm', 0, 0, axis_index_groups=halves, tiled=True)  22.5 us
    pallas_call x2, Pallas kernels, attention(): pl.pallas_call(stats_kernel, in_specs=[flat, flat, rows, rows] + sections...  12.7 us
    unnamed x81, local copies, waits for them, and re-layouts  9.46 us
  transfers between devices with their start and end apart: 31, of which 13 were waited for; matrix products, arithmetic and copies ran while one was open for 26% of the time, Pallas kernels for 15%

profile of v2, /device:TPU:0, one launch (start us, length us, event | category | flops | bytes accessed | tf_op | source)
XLA Modules:
  0.0 273.5 jit_solution(17361770996556741649)
XLA Ops:
  0.6 3.6 %copy.39 = bf16[1024,2,1024]{2,0,1:T(8,128)(2,1)S(1)} copy(bf16[1024,2,1024]{2,1,0:T(2,128)(2,1)} %param.9) | data formatting | bytes 8388608 | tf_op args[0]
  8.1 5.3 %all-to-all-start = ((bf16[8,2,2,2,16,1024]{5,4,3,2,1,0:T(8,128)(2,1)}), bf16[8,2,2,2,16,1024]{5,4,3,2,1,0:T(8,128)(2,1)}, u32[]{:S(2)}, u32[]{:S(2)}) async-start(bf16[8,2,2,2,16,1024]{5,4,3,2,1,0:T(8,128)(2,1)} %maximum_bitcast_fusion), calls=%async_computation | async-start | bytes 4194304 | tf_op jit(solution)/shard_map/all_to_all | solution.py:349
  13.4 3.3 %copy_bitcast_fusion = bf16[8,2,2,32,1024]{4,3,2,1,0:T(8,128)(2,1)} fusion(bf16[2,8,64,2,1024]{4,2,1,0,3:T(8,128)(2,1)} %bitcast.258), kind=kLoop, calls=%fused_computation.8 | loop fusion | bytes 4194304 | tf_op jit(solution)/shard_map/transpose | solution.py:348
  16.7 22.5 %all-to-all-done = bf16[8,2,2,2,16,1024]{5,4,3,2,1,0:T(8,128)(2,1)} async-done(((bf16[8,2,2,2,16,1024]{5,4,3,2,1,0:T(8,128)(2,1)}), bf16[8,2,2,2,16,1024]{5,4,3,2,1,0:T(8,128)(2,1)}, u32[]{:S(2)}, u32[]{:S(2)}) %all-to-all-start) | async-done | bytes 2097184 | tf_op jit(solution)/shard_map/all_to_all | solution.py:349
  39.2 4.4 %all-to-all-start.1 = ((bf16[8,2,2,32,1024]{4,3,2,1,0:T(8,128)(2,1)}), bf16[8,2,2,32,1024]{4,3,2,1,0:T(8,128)(2,1)}, u32[]{:S(2)}, u32[]{:S(2)}) async-start(bf16[8,2,2,32,1024]{4,3,2,1,0:T(8,128)(2,1)} %copy_bitcast_fusion), calls=%async_computation.1 | async-start | bytes 4194304 | tf_op jit(solution)/shard_map/all_to_all | solution.py:350
  44.4 3.1 %collective-permute-start = (bf16[64,1024]{1,0:T(8,128)(2,1)S(1)}, bf16[64,1024]{1,0:T(8,128)(2,1)S(1)}, u32[]{:S(2)}, u32[]{:S(2)}) collective-permute-start(bf16[64,1024]{1,0:T(8,128)(2,1)S(1)} %get-tuple-element.127), channel_id=1, source_target_pairs={{0,8},{1,9},{2,10},{3,11},{4,12},{5,13},{6,14},{7,15},{8,0},{9,1},... | collective-permute-start | bytes 393224 | tf_op jit(solution)/shard_map/ppermute | solution.py:322
  47.4 2.9 %collective-permute-start.2 = (s32[64]{0:T(128)S(1)}, s32[64]{0:T(128)S(1)}, u32[]{:S(2)}, u32[]{:S(2)}) collective-permute-start(s32[64]{0:T(128)S(1)} %copy-done.33), channel_id=1, source_target_pairs={{0,8},{1,9},{2,10},{3,11},{4,12},{5,13},{6,14},{7,15},{8,0},{9,1},... | collective-permute-start | bytes 776 | tf_op jit(solution)/shard_map/ppermute | solution.py:322
  50.5 22.3 %collective-permute-done.2 = s32[64]{0:T(128)S(1)} collective-permute-done((s32[64]{0:T(128)S(1)}, s32[64]{0:T(128)S(1)}, u32[]{:S(2)}, u32[]{:S(2)}) %collective-permute-start.2) | collective-permute-done | bytes 288 | tf_op jit(solution)/shard_map/ppermute | solution.py:322
  76.9 2.8 %slice_bitcast_fusion.1 = (bf16[8,2,2,16,1024]{4,3,2,1,0:T(8,128)(2,1)S(1)}, bf16[8,2,2,16,1024]{4,3,2,1,0:T(8,128)(2,1)}) fusion(bf16[8,2,2,2,16,1024]{5,4,3,2,1,0:T(8,128)(2,1)} %all-to-all-done), kind=kLoop, calls=%fused_computation.23 | loop fusion | bytes 4194304 | tf_op jit(solution)/shard_map/squeeze | solution.py:352
  79.6 5.3 %collective-permute-start.5 = (bf16[8,2,2,16,1024]{4,3,2,1,0:T(8,128)(2,1)}, bf16[8,2,2,16,1024]{4,3,2,1,0:T(8,128)(2,1)}, u32[]{:S(2)}, u32[]{:S(2)}) collective-permute-start(bf16[8,2,2,16,1024]{4,3,2,1,0:T(8,128)(2,1)} %get-tuple-element.258), channel_id=1, source_target_pairs={{1,0},{2,1},{3,2},{4,3},{5,4},{6,5},{7,6},{0,7},{9,8},{10,9},{11,1... | collective-permute-start | bytes 3145736 | tf_op jit(solution)/shard_map/ppermute | solution.py:353
  85.0 5.5 %convolution_convert_fusion.4 = bf16[1024,1024]{1,0:T(8,128)(2,1)} fusion(bf16[1024,1024]{1,0:T(8,128)(2,1)} %bitcast.11, bf16[1024,1024]{1,0:T(8,128)(2,1)S(1)} %copy-done), kind=kOutput, calls=%fused_computation.13 | convolution fusion | flops 2148532224 | bytes 6291456 | tf_op jit(solution)/shard_map/dot_general | solution.py:30
  90.5 5.4 %convolution_convert_fusion.3 = bf16[1024,1024]{1,0:T(8,128)(2,1)} fusion(bf16[1024,1024]{1,0:T(8,128)(2,1)} %bitcast.11, bf16[1024,1024]{1,0:T(8,128)(2,1)S(1)} %copy-done.26), kind=kOutput, calls=%fused_computation.12 | convolution fusion | flops 2148532224 | bytes 6291456 | tf_op jit(solution)/shard_map/dot_general | solution.py:30
  95.9 2.7 collective-permute-start.3
  98.6 5.2 %convolution_convert_fusion.1 = bf16[1024,1024]{1,0:T(8,128)(2,1)} fusion(bf16[1024,1024]{1,0:T(8,128)(2,1)} %bitcast.8, bf16[1024,1024]{1,0:T(8,128)(2,1)S(1)} %copy-done.26), kind=kOutput, calls=%fused_computation.10 | convolution fusion | flops 2148532224 | bytes 6291456 | tf_op jit(solution)/shard_map/dot_general | solution.py:30
  103.8 5.3 %convolution_convert_fusion.5 = bf16[1024,1024]{1,0:T(8,128)(2,1)} fusion(bf16[1024,1024]{1,0:T(8,128)(2,1)} %bitcast.8, bf16[1024,1024]{1,0:T(8,128)(2,1)S(1)} %copy-done), kind=kOutput, calls=%fused_computation.14 | convolution fusion | flops 2148532224 | bytes 6291456 | tf_op jit(solution)/shard_map/dot_general | solution.py:30
  115.0 3.7 %convolution_convert_fusion.2 = bf16[1024,1024]{1,0:T(8,128)(2,1)} fusion(bf16[1024,1024]{1,0:T(8,128)(2,1)S(1)} %bitcast.263, bf16[1024,1024]{1,0:T(8,128)(2,1)S(1)} %copy-done), kind=kOutput, calls=%fused_computation.11 | convolution fusion | flops 2148532224 | bytes 6291456 | tf_op jit(solution)/shard_map/dot_general | solution.py:30
  118.7 3.7 %convolution_convert_fusion = bf16[1024,1024]{1,0:T(8,128)(2,1)} fusion(bf16[1024,1024]{1,0:T(8,128)(2,1)S(1)} %bitcast.264, bf16[1024,1024]{1,0:T(8,128)(2,1)S(1)} %copy-done.26), kind=kOutput, calls=%fused_computation.9 | convolution fusion | flops 2148532224 | bytes 6291456 | tf_op jit(solution)/shard_map/dot_general | solution.py:30
  124.5 6.5 %softmax_stats.2.one_ref = f32[2,2,3,256]{3,2,1,0:T(4,128)} custom-call(s32[2,1,256]{2,1,0:T(1,128)} %tile.15.lo_ref, s32[2,1,256]{2,1,0:T(1,128)} %tile.17.hi_ref, bf16[2,64,1024]{2,1,0:T(8,128)(2,1)} %get-tuple-element.187.q_ref, bf16[2,64,1024]{2,1,0:T(8,128)(2,1)} %get-tuple-element.188.g_ref, bf16[8,2,2,2,16,1024]{5,4,3,2,1,0:T(8,128)(2,1)} %bitcast.245, ...), custom_call_target="tpu_custom_call" | custom-call | flops 1073741824 | bytes 6291456 | tf_op jit(solution)/shard_map/softmax_stats/pallas_call | solution.py:240
  130.9 4.2 %collective-permute-done.6 = bf16[256,1024]{1,0:T(8,128)(2,1)S(1)} collective-permute-done((bf16[256,1024]{1,0:T(8,128)(2,1)}, bf16[256,1024]{1,0:T(8,128)(2,1)S(1)}, u32[]{:S(2)}, u32[]{:S(2)}) %collective-permute-start.6) | collective-permute-done | bytes 524320 | tf_op jit(solution)/shard_map/ppermute | solution.py:322
  138.4 6.2 %softmax_stats.3.one_ref = f32[2,2,3,256]{3,2,1,0:T(4,128)} custom-call(s32[2,1,256]{2,1,0:T(1,128)} %tile.15.lo_ref, s32[2,1,256]{2,1,0:T(1,128)} %tile.17.hi_ref, bf16[2,64,1024]{2,1,0:T(8,128)(2,1)} %get-tuple-element.187.q_ref, bf16[2,64,1024]{2,1,0:T(8,128)(2,1)} %get-tuple-element.188.g_ref, bf16[8,2,2,2,16,1024]{5,4,3,2,1,0:T(8,128)(2,1)} %bitcast.246, ...), custom_call_target="tpu_custom_call" | custom-call | flops 1073741824 | bytes 6291456 | tf_op jit(solution)/shard_map/softmax_stats/pallas_call | solution.py:240
  144.7 3.0 %collective-permute-start.9 = (f32[2,2,3,256]{3,2,1,0:T(4,128)}, f32[2,2,3,256]{3,2,1,0:T(4,128)S(1)}, u32[]{:S(2)}, u32[]{:S(2)}) collective-permute-start(f32[2,2,3,256]{3,2,1,0:T(4,128)} %softmax_stats.3.one_ref), channel_id=1, source_target_pairs={{0,8},{1,9},{2,10},{3,11},{4,12},{5,13},{6,14},{7,15},{8,0},{9,1},... | collective-permute-start | bytes 36872 | tf_op jit(solution)/shard_map/ppermute | solution.py:322
  147.7 14.0 %banded_grads.2 = (f32[2,64,512]{2,1,0:T(8,128)}, f32[2,64,512]{2,1,0:T(8,128)}, bf16[8,2,2,2,16,1024]{5,4,3,2,1,0:T(8,128)(2,1)}, bf16[8,2,2,32,1024]{4,3,2,1,0:T(8,128)(2,1)}, bf16[2,8,2,2,16,1024]{5,4,3,2,1,0:T(8,128)(2,1)}) custom-call(s32[2,1,256]{2,1,0:T(1,128)} %tile.15.lo_ref, s32[2,1,256]{2,1,0:T(1,128)} %tile.17.hi_ref, ...), custom_call_target="tpu_custom_call" | custom-call | flops 3221225472 | bytes 12582912 | tf_op jit(solution)/shard_map/banded_grads/pallas_call | solution.py:258
  164.3 4.7 %fusion.28 = f32[1024,1024,1,1,1,1]{1,0,5,4,3,2:T(8,128)S(1)} fusion(bf16[8,2,2,2,16,1024]{5,4,3,2,1,0:T(8,128)(2,1)} %all-to-all-done, bf16[8,2,2,2,16,1024]{5,4,3,2,1,0:T(8,128)(2,1)} %get-tuple-element.180), kind=kOutput, calls=%fused_computation.146 | convolution fusion | flops 2147483648 | bytes 8388608 | tf_op jit(solution)/shard_map/dot_general | solution.py:22
  169.0 4.2 %fusion.29 = f32[1024,1024,1,1,1]{0,1,4,3,2:T(8,128)S(1)} fusion(bf16[8,2,2,32,1024]{4,3,2,1,0:T(8,128)(2,1)S(1)} %copy-done.31, bf16[8,2,2,32,1024]{4,3,2,1,0:T(8,128)(2,1)} %all-to-all-done.1), kind=kOutput, calls=%fused_computation.147 | convolution fusion | flops 2147483648 | bytes 8388608 | tf_op jit(solution)/shard_map/dot_general | solution.py:22
  173.3 2.7 fusion.1
  183.3 14.5 %banded_grads.3 = (f32[2,64,512]{2,1,0:T(8,128)}, f32[2,64,512]{2,1,0:T(8,128)}, bf16[8,2,2,2,16,1024]{5,4,3,2,1,0:T(8,128)(2,1)}, bf16[8,2,2,32,1024]{4,3,2,1,0:T(8,128)(2,1)}, bf16[2,8,2,2,16,1024]{5,4,3,2,1,0:T(8,128)(2,1)}) custom-call(s32[2,1,256]{2,1,0:T(1,128)} %tile.15.lo_ref, s32[2,1,256]{2,1,0:T(1,128)} %tile.17.hi_ref, ...), custom_call_target="tpu_custom_call" | custom-call | flops 3221225472 | bytes 12582912 | tf_op jit(solution)/shard_map/banded_grads/pallas_call | solution.py:258
  205.2 4.0 %fusion.30 = f32[1024,1024,1,1,1,1]{1,0,5,4,3,2:T(8,128)S(1)} fusion(bf16[8,2,2,2,16,1024]{5,4,3,2,1,0:T(8,128)(2,1)} %all-to-all-done, bf16[8,2,2,2,16,1024]{5,4,3,2,1,0:T(8,128)(2,1)S(1)} %copy-done.29), kind=kOutput, calls=%fused_computation.148 | convolution fusion | flops 2147483648 | bytes 8388608 | tf_op jit(solution)/shard_map/dot_general | solution.py:22
  209.2 4.2 %fusion.31 = f32[1024,1024,1,1,1]{0,1,4,3,2:T(8,128)S(1)} fusion(bf16[8,2,2,32,1024]{4,3,2,1,0:T(8,128)(2,1)S(1)} %copy-done.28, bf16[8,2,2,32,1024]{4,3,2,1,0:T(8,128)(2,1)} %all-to-all-done.1), kind=kOutput, calls=%fused_computation.149 | convolution fusion | flops 2147483648 | bytes 8388608 | tf_op jit(solution)/shard_map/dot_general | solution.py:22
  213.5 2.7 fusion
  226.4 4.2 %all-to-all-start.2 = ((bf16[16,2,2048]{2,1,0:T(2,128)(2,1)}), bf16[16,2,2048]{2,1,0:T(2,128)(2,1)S(1)}, u32[]{:S(2)}, u32[]{:S(2)}) async-start(bf16[16,2,2048]{2,1,0:T(2,128)(2,1)} %reshape.268), calls=%async_computation.2 | async-start | bytes 262144 | tf_op jit(solution)/shard_map/all_to_all | solution.py:441
  252.4 2.8 %fusion.32 = f32[64,1024]{1,0:T(8,128)} fusion(bf16[1024,64]{0,1:T(8,128)(2,1)S(1)} %reshape.241, bf16[1024,1024]{1,0:T(8,128)(2,1)} %constant_dynamic-update-slice_fusion), kind=kOutput, calls=%fused_computation.150 | convolution fusion | flops 134217728 | bytes 2490368 | tf_op jit(solution)/shard_map/dot_general | solution.py:22
  261.1 2.5 collective-permute-done.24
  (226 shorter events, 84.5 us)
Async XLA Ops:
  0.6 84.4 %copy-start = (bf16[1024,1024]{1,0:T(8,128)(2,1)S(1)}, bf16[1024,1024]{1,0:T(8,128)(2,1)}, u32[]{:S(2)}) copy-start(bf16[1024,1024]{1,0:T(8,128)(2,1)} %param.11) | copy-start | bytes 6291460
  8.1 31.1 %all-to-all-start = ((bf16[8,2,2,2,16,1024]{5,4,3,2,1,0:T(8,128)(2,1)}), bf16[8,2,2,2,16,1024]{5,4,3,2,1,0:T(8,128)(2,1)}, u32[]{:S(2)}, u32[]{:S(2)}) async-start(bf16[8,2,2,2,16,1024]{5,4,3,2,1,0:T(8,128)(2,1)} %maximum_bitcast_fusion), calls=%async_computation | async-start | bytes 4194304 | tf_op jit(solution)/shard_map/all_to_all | solution.py:349
  39.2 45.8 %all-to-all-start.1 = ((bf16[8,2,2,32,1024]{4,3,2,1,0:T(8,128)(2,1)}), bf16[8,2,2,32,1024]{4,3,2,1,0:T(8,128)(2,1)}, u32[]{:S(2)}, u32[]{:S(2)}) async-start(bf16[8,2,2,32,1024]{4,3,2,1,0:T(8,128)(2,1)} %copy_bitcast_fusion), calls=%async_computation.1 | async-start | bytes 4194304 | tf_op jit(solution)/shard_map/all_to_all | solution.py:350
  44.4 28.4 %collective-permute-start = (bf16[64,1024]{1,0:T(8,128)(2,1)S(1)}, bf16[64,1024]{1,0:T(8,128)(2,1)S(1)}, u32[]{:S(2)}, u32[]{:S(2)}) collective-permute-start(bf16[64,1024]{1,0:T(8,128)(2,1)S(1)} %get-tuple-element.127), channel_id=1, source_target_pairs={{0,8},{1,9},{2,10},{3,11},{4,12},{5,13},{6,14},{7,15},{8,0},{9,1},... | collective-permute-start | bytes 393224 | tf_op jit(solution)/shard_map/ppermute | solution.py:322
  47.4 25.3 %collective-permute-start.1 = (bf16[64,1024]{1,0:T(8,128)(2,1)S(1)}, bf16[64,1024]{1,0:T(8,128)(2,1)S(1)}, u32[]{:S(2)}, u32[]{:S(2)}) collective-permute-start(bf16[64,1024]{1,0:T(8,128)(2,1)S(1)} %copy-done.20), channel_id=1, source_target_pairs={{0,8},{1,9},{2,10},{3,11},{4,12},{5,13},{6,14},{7,15},{8,0},{9,1},... | collective-permute-start | bytes 393224 | tf_op jit(solution)/shard_map/ppermute | solution.py:322
  47.4 25.3 %collective-permute-start.2 = (s32[64]{0:T(128)S(1)}, s32[64]{0:T(128)S(1)}, u32[]{:S(2)}, u32[]{:S(2)}) collective-permute-start(s32[64]{0:T(128)S(1)} %copy-done.33), channel_id=1, source_target_pairs={{0,8},{1,9},{2,10},{3,11},{4,12},{5,13},{6,14},{7,15},{8,0},{9,1},... | collective-permute-start | bytes 776 | tf_op jit(solution)/shard_map/ppermute | solution.py:322
  79.6 30.3 %collective-permute-start.4 = (bf16[8,2,2,16,1024]{4,3,2,1,0:T(8,128)(2,1)S(1)}, bf16[8,2,2,16,1024]{4,3,2,1,0:T(8,128)(2,1)}, u32[]{:S(2)}, u32[]{:S(2)}) collective-permute-start(bf16[8,2,2,16,1024]{4,3,2,1,0:T(8,128)(2,1)S(1)} %get-tuple-element.257), channel_id=1, source_target_pairs={{0,1},{1,2},{2,3},{3,4},{4,5},{5,6},{6,7},{7,0},{8,9},{9,10},{10,1... | collective-permute-start | bytes 3145736 | tf_op jit(solution)/shard_map/ppermute | solution.py:352
  79.6 32.3 %collective-permute-start.5 = (bf16[8,2,2,16,1024]{4,3,2,1,0:T(8,128)(2,1)}, bf16[8,2,2,16,1024]{4,3,2,1,0:T(8,128)(2,1)}, u32[]{:S(2)}, u32[]{:S(2)}) collective-permute-start(bf16[8,2,2,16,1024]{4,3,2,1,0:T(8,128)(2,1)} %get-tuple-element.258), channel_id=1, source_target_pairs={{1,0},{2,1},{3,2},{4,3},{5,4},{6,5},{7,6},{0,7},{9,8},{10,9},{11,1... | collective-permute-start | bytes 3145736 | tf_op jit(solution)/shard_map/ppermute | solution.py:353
  95.9 13.2 %collective-permute-start.3 = (bf16[128,1024]{1,0:T(8,128)(2,1)S(1)}, bf16[128,1024]{1,0:T(8,128)(2,1)S(1)}, u32[]{:S(2)}, u32[]{:S(2)}) collective-permute-start(bf16[128,1024]{1,0:T(8,128)(2,1)S(1)} %copy-done.16), channel_id=1, source_target_pairs={{0,4},{1,5},{2,6},{3,7},{4,0},{5,1},{6,2},{7,3},{8,12},{9,13},{10,... | collective-permute-start | bytes 786440 | tf_op jit(solution)/shard_map/ppermute | solution.py:322
  122.4 12.7 %collective-permute-start.6 = (bf16[256,1024]{1,0:T(8,128)(2,1)}, bf16[256,1024]{1,0:T(8,128)(2,1)S(1)}, u32[]{:S(2)}, u32[]{:S(2)}) collective-permute-start(bf16[256,1024]{1,0:T(8,128)(2,1)} %pad_maximum_fusion.2), channel_id=1, source_target_pairs={{0,2},{1,3},{2,0},{3,1},{4,6},{5,7},{6,4},{7,5},{8,10},{9,11},{10,... | collective-permute-start | bytes 1572872 | tf_op jit(solution)/shard_map/ppermute | solution.py:322
  136.2 8.5 %collective-permute-start.7 = (bf16[512,1024]{1,0:T(8,128)(2,1)}, bf16[512,1024]{1,0:T(8,128)(2,1)S(1)}, u32[]{:S(2)}, u32[]{:S(2)}) collective-permute-start(bf16[512,1024]{1,0:T(8,128)(2,1)} %pad_maximum_fusion.1), channel_id=1, source_target_pairs={{0,1},{1,0},{2,3},{3,2},{4,5},{5,4},{6,7},{7,6},{8,9},{9,8},{10,11... | collective-permute-start | bytes 3145736 | tf_op jit(solution)/shard_map/ppermute | solution.py:322
  137.6 7.1 %collective-permute-start.8 = (f32[2,2,3,256]{3,2,1,0:T(4,128)S(1)}, f32[2,2,3,256]{3,2,1,0:T(4,128)S(1)}, u32[]{:S(2)}, u32[]{:S(2)}) collective-permute-start(f32[2,2,3,256]{3,2,1,0:T(4,128)S(1)} %copy-done.21), channel_id=1, source_target_pairs={{0,8},{1,9},{2,10},{3,11},{4,12},{5,13},{6,14},{7,15},{8,0},{9,1},... | collective-permute-start | bytes 36872 | tf_op jit(solution)/shard_map/ppermute | solution.py:322
  144.7 17.0 %collective-permute-start.9 = (f32[2,2,3,256]{3,2,1,0:T(4,128)}, f32[2,2,3,256]{3,2,1,0:T(4,128)S(1)}, u32[]{:S(2)}, u32[]{:S(2)}) collective-permute-start(f32[2,2,3,256]{3,2,1,0:T(4,128)} %softmax_stats.3.one_ref), channel_id=1, source_target_pairs={{0,8},{1,9},{2,10},{3,11},{4,12},{5,13},{6,14},{7,15},{8,0},{9,1},... | collective-permute-start | bytes 36872 | tf_op jit(solution)/shard_map/ppermute | solution.py:322
  163.7 14.7 %collective-permute-start.10 = (f32[2,64,512]{2,1,0:T(8,128)S(1)}, f32[2,64,512]{2,1,0:T(8,128)S(1)}, u32[]{:S(2)}, u32[]{:S(2)}) collective-permute-start(f32[2,64,512]{2,1,0:T(8,128)S(1)} %pad_maximum_fusion.4), channel_id=1, source_target_pairs={{0,8},{1,9},{2,10},{3,11},{4,12},{5,13},{6,14},{7,15},{8,0},{9,1},... | collective-permute-start | bytes 786440 | tf_op jit(solution)/shard_map/ppermute | solution.py:322
  182.1 15.7 %collective-permute-start.11 = (bf16[2,2,2,64,512]{4,3,0,1,2:T(8,128)(2,1)}, bf16[2,2,2,64,512]{4,3,0,1,2:T(8,128)(2,1)}, u32[]{:S(2)}, u32[]{:S(2)}) collective-permute-start(bf16[2,2,2,64,512]{4,3,0,1,2:T(8,128)(2,1)} %bitcast.223), channel_id=1, source_target_pairs={{0,1},{1,0},{2,3},{3,2},{4,5},{5,4},{6,7},{7,6},{8,9},{9,8},{10,11... | collective-permute-start | bytes 1572872 | tf_op jit(solution)/shard_map/ppermute | solution.py:322
  182.1 15.7 %collective-permute-start.12 = (bf16[2,2,2,64,512]{4,3,2,0,1:T(8,128)(2,1)}, bf16[2,2,2,64,512]{4,3,2,0,1:T(8,128)(2,1)}, u32[]{:S(2)}, u32[]{:S(2)}) collective-permute-start(bf16[2,2,2,64,512]{4,3,2,0,1:T(8,128)(2,1)} %bitcast.222), channel_id=1, source_target_pairs={{0,1},{1,0},{2,3},{3,2},{4,5},{5,4},{6,7},{7,6},{8,9},{9,8},{10,11... | collective-permute-start | bytes 1572872 | tf_op jit(solution)/shard_map/ppermute | solution.py:322
  202.5 13.7 %collective-permute-start.13 = (bf16[2,2,64,512]{3,2,0,1:T(8,128)(2,1)S(1)}, bf16[2,2,64,512]{3,2,0,1:T(8,128)(2,1)S(1)}, u32[]{:S(2)}, u32[]{:S(2)}) collective-permute-start(bf16[2,2,64,512]{3,2,0,1:T(8,128)(2,1)S(1)} %dynamic-slice_bitcast_fusion.3), channel_id=1, source_target_pairs={{0,2},{1,3},{2,0},{3,1},{4,6},{5,7},{6,4},{7,5},{8,10},{9,11},{10,... | collective-permute-start | bytes 786440 | tf_op jit(solution)/shard_map/ppermute | solution.py:322
  202.9 13.3 %collective-permute-start.14 = (bf16[2,2,64,512]{3,2,1,0:T(8,128)(2,1)S(1)}, bf16[2,2,64,512]{3,2,1,0:T(8,128)(2,1)S(1)}, u32[]{:S(2)}, u32[]{:S(2)}) collective-permute-start(bf16[2,2,64,512]{3,2,1,0:T(8,128)(2,1)S(1)} %dynamic-slice_bitcast_fusion.2), channel_id=1, source_target_pairs={{0,4},{1,5},{2,6},{3,7},{4,0},{5,1},{6,2},{7,3},{8,12},{9,13},{10,... | collective-permute-start | bytes 786440 | tf_op jit(solution)/shard_map/ppermute | solution.py:322
  202.9 14.6 %collective-permute-start.15 = (f32[2,64,512]{2,1,0:T(8,128)S(1)}, f32[2,64,512]{2,1,0:T(8,128)S(1)}, u32[]{:S(2)}, u32[]{:S(2)}) collective-permute-start(f32[2,64,512]{2,1,0:T(8,128)S(1)} %pad_maximum_fusion.5), channel_id=1, source_target_pairs={{0,8},{1,9},{2,10},{3,11},{4,12},{5,13},{6,14},{7,15},{8,0},{9,1},... | collective-permute-start | bytes 786440 | tf_op jit(solution)/shard_map/ppermute | solution.py:322
  221.9 19.6 %collective-permute-start.18 = (bf16[2,2,2,64,512]{4,3,0,1,2:T(8,128)(2,1)}, bf16[2,2,2,64,512]{4,3,0,1,2:T(8,128)(2,1)}, u32[]{:S(2)}, u32[]{:S(2)}) collective-permute-start(bf16[2,2,2,64,512]{4,3,0,1,2:T(8,128)(2,1)} %bitcast.221), channel_id=1, source_target_pairs={{0,1},{1,0},{2,3},{3,2},{4,5},{5,4},{6,7},{7,6},{8,9},{9,8},{10,11... | collective-permute-start | bytes 1572872 | tf_op jit(solution)/shard_map/ppermute | solution.py:322
  222.0 19.5 %collective-permute-start.19 = (bf16[2,2,2,64,512]{4,3,2,0,1:T(8,128)(2,1)}, bf16[2,2,2,64,512]{4,3,2,0,1:T(8,128)(2,1)}, u32[]{:S(2)}, u32[]{:S(2)}) collective-permute-start(bf16[2,2,2,64,512]{4,3,2,0,1:T(8,128)(2,1)} %bitcast.220), channel_id=1, source_target_pairs={{0,1},{1,0},{2,3},{3,2},{4,5},{5,4},{6,7},{7,6},{8,9},{9,8},{10,11... | collective-permute-start | bytes 1572872 | tf_op jit(solution)/shard_map/ppermute | solution.py:322
  226.4 12.6 %all-to-all-start.2 = ((bf16[16,2,2048]{2,1,0:T(2,128)(2,1)}), bf16[16,2,2048]{2,1,0:T(2,128)(2,1)S(1)}, u32[]{:S(2)}, u32[]{:S(2)}) async-start(bf16[16,2,2048]{2,1,0:T(2,128)(2,1)} %reshape.268), calls=%async_computation.2 | async-start | bytes 262144 | tf_op jit(solution)/shard_map/all_to_all | solution.py:441
  230.6 10.9 %collective-permute-start.16 = (bf16[2,64,512]{2,1,0:T(8,128)(2,1)}, bf16[2,64,512]{2,1,0:T(8,128)(2,1)}, u32[]{:S(2)}, u32[]{:S(2)}) collective-permute-start(bf16[2,64,512]{2,1,0:T(8,128)(2,1)} %dynamic-slice_bitcast_fusion.7), channel_id=1, source_target_pairs={{0,4},{1,5},{2,6},{3,7},{4,0},{5,1},{6,2},{7,3},{8,12},{9,13},{10,... | collective-permute-start | bytes 393224 | tf_op jit(solution)/shard_map/ppermute | solution.py:322
  232.7 8.9 %collective-permute-start.17 = (bf16[2,64,512]{2,1,0:T(8,128)(2,1)}, bf16[2,64,512]{2,1,0:T(8,128)(2,1)}, u32[]{:S(2)}, u32[]{:S(2)}) collective-permute-start(bf16[2,64,512]{2,1,0:T(8,128)(2,1)} %dynamic-slice_bitcast_fusion.6), channel_id=1, source_target_pairs={{0,8},{1,9},{2,10},{3,11},{4,12},{5,13},{6,14},{7,15},{8,0},{9,1},... | collective-permute-start | bytes 393224 | tf_op jit(solution)/shard_map/ppermute | solution.py:322
  246.7 10.3 %collective-permute-start.22 = (bf16[2,2,64,512]{3,2,0,1:T(8,128)(2,1)S(1)}, bf16[2,2,64,512]{3,2,0,1:T(8,128)(2,1)S(1)}, u32[]{:S(2)}, u32[]{:S(2)}) collective-permute-start(bf16[2,2,64,512]{3,2,0,1:T(8,128)(2,1)S(1)} %dynamic-slice_bitcast_fusion.1), channel_id=1, source_target_pairs={{0,2},{1,3},{2,0},{3,1},{4,6},{5,7},{6,4},{7,5},{8,10},{9,11},{10,... | collective-permute-start | bytes 786440 | tf_op jit(solution)/shard_map/ppermute | solution.py:322
  248.3 9.4 %collective-permute-start.23 = (bf16[2,2,64,512]{3,2,1,0:T(8,128)(2,1)S(1)}, bf16[2,2,64,512]{3,2,1,0:T(8,128)(2,1)S(1)}, u32[]{:S(2)}, u32[]{:S(2)}) collective-permute-start(bf16[2,2,64,512]{3,2,1,0:T(8,128)(2,1)S(1)} %dynamic-slice_bitcast_fusion), channel_id=1, source_target_pairs={{0,4},{1,5},{2,6},{3,7},{4,0},{5,1},{6,2},{7,3},{8,12},{9,13},{10,... | collective-permute-start | bytes 786440 | tf_op jit(solution)/shard_map/ppermute | solution.py:322
  250.6 6.4 %collective-permute-start.20 = (bf16[64,512]{1,0:T(8,128)(2,1)S(1)}, bf16[64,512]{1,0:T(8,128)(2,1)S(1)}, u32[]{:S(2)}, u32[]{:S(2)}) collective-permute-start(bf16[64,512]{1,0:T(8,128)(2,1)S(1)} %dynamic-slice_bitcast_fusion.11), channel_id=1, source_target_pairs={{0,8},{1,9},{2,10},{3,11},{4,12},{5,13},{6,14},{7,15},{8,0},{9,1},... | collective-permute-start | bytes 196616 | tf_op jit(solution)/shard_map/ppermute | solution.py:322
  251.8 5.1 %collective-permute-start.21 = (bf16[64,512]{1,0:T(8,128)(2,1)S(1)}, bf16[64,512]{1,0:T(8,128)(2,1)S(1)}, u32[]{:S(2)}, u32[]{:S(2)}) collective-permute-start(bf16[64,512]{1,0:T(8,128)(2,1)S(1)} %dynamic-slice_bitcast_fusion.10), channel_id=1, source_target_pairs={{0,2},{1,3},{2,0},{3,1},{4,6},{5,7},{6,4},{7,5},{8,10},{9,11},{10,... | collective-permute-start | bytes 196616 | tf_op jit(solution)/shard_map/ppermute | solution.py:322
  258.1 5.4 %collective-permute-start.24 = (bf16[2,64,512]{2,1,0:T(8,128)(2,1)S(1)}, bf16[2,64,512]{2,1,0:T(8,128)(2,1)S(1)}, u32[]{:S(2)}, u32[]{:S(2)}) collective-permute-start(bf16[2,64,512]{2,1,0:T(8,128)(2,1)S(1)} %dynamic-slice_bitcast_fusion.5), channel_id=1, source_target_pairs={{0,4},{1,5},{2,6},{3,7},{4,0},{5,1},{6,2},{7,3},{8,12},{9,13},{10,... | collective-permute-start | bytes 393224 | tf_op jit(solution)/shard_map/ppermute | solution.py:322
  259.3 6.0 %collective-permute-start.25 = (bf16[2,64,512]{2,1,0:T(8,128)(2,1)S(1)}, bf16[2,64,512]{2,1,0:T(8,128)(2,1)S(1)}, u32[]{:S(2)}, u32[]{:S(2)}) collective-permute-start(bf16[2,64,512]{2,1,0:T(8,128)(2,1)S(1)} %dynamic-slice_bitcast_fusion.4), channel_id=1, source_target_pairs={{0,8},{1,9},{2,10},{3,11},{4,12},{5,13},{6,14},{7,15},{8,0},{9,1},... | collective-permute-start | bytes 393224 | tf_op jit(solution)/shard_map/ppermute | solution.py:322
  265.4 5.2 %collective-permute-start.26 = (bf16[64,512]{1,0:T(8,128)(2,1)S(1)}, bf16[64,512]{1,0:T(8,128)(2,1)S(1)}, u32[]{:S(2)}, u32[]{:S(2)}) collective-permute-start(bf16[64,512]{1,0:T(8,128)(2,1)S(1)} %dynamic-slice_bitcast_fusion.9), channel_id=1, source_target_pairs={{0,8},{1,9},{2,10},{3,11},{4,12},{5,13},{6,14},{7,15},{8,0},{9,1},... | collective-permute-start | bytes 196616 | tf_op jit(solution)/shard_map/ppermute | solution.py:322
  267.1 4.3 %collective-permute-start.27 = (bf16[64,512]{1,0:T(8,128)(2,1)S(1)}, bf16[64,512]{1,0:T(8,128)(2,1)S(1)}, u32[]{:S(2)}, u32[]{:S(2)}) collective-permute-start(bf16[64,512]{1,0:T(8,128)(2,1)S(1)} %dynamic-slice_bitcast_fusion.8), channel_id=1, source_target_pairs={{0,2},{1,3},{2,0},{3,1},{4,6},{5,7},{6,4},{7,5},{8,10},{9,11},{10,... | collective-permute-start | bytes 196616 | tf_op jit(solution)/shard_map/ppermute | solution.py:322
  (33 other events, 326.5 us)

commit v3 on v2

--- a/solution.py
+++ b/solution.py
@@ -7,7 +7,7 @@
 from jax.experimental.pallas import tpu as pltpu
 from jax.sharding import PartitionSpec as P
 
-H = 16
+
 HD = 64
 W = 16
 GROUP = 4
@@ -53,31 +53,22 @@
     hi = hi_ref[...]
     rows = lax.broadcasted_iota(jnp.int32, (CHUNK, wide), 0)
     near = rows % W
-    far = rows % (2 * W)
     second = lax.broadcasted_iota(jnp.int32, (CHUNK, wide), 1) >= wide // 2
     frames = (
         near + jnp.where(second, n_query - W, 0),
-        far + W,
+        near + W,
+        near + 2 * W,
         near + jnp.where(second, n_query, -W),
     )
     for i, frame in enumerate(frames):
         bias_ref[i] = jnp.where((frame >= lo) & (frame <= hi), 0.0, -1e30)
 
 
-def load_edge(ref, side):
-    return ref[:, :, side].reshape(CHUNK, LANES)
-
-
-def load_halo(ref, side):
-    return ref[side].reshape(CHUNK, LANES)
-
-
-def load_mid(ref, c):
-    runs = ref.shape[0] // 2
-    return ref[pl.ds(c * runs, runs)].reshape(CHUNK, LANES)
-
-
-def pair_dot(ref, load, x_ref):
+def load(ref, side):
+    return ref[:, side].reshape(CHUNK, LANES)
+
+
+def pair_dot(ref, x_ref):
     mid = x_ref.shape[0] // 2
     return jnp.concatenate(
         [nt_dot(load(ref, 0), x_ref[:mid, :]), nt_dot(load(ref, 1), x_ref[mid:, :])], 1
@@ -102,27 +93,27 @@
     def _():
         fill_bias(lo_ref, hi_ref, bias_ref, n_query)
 
-    def score(at, table, s, top):
-        s = s + bias_ref[table]
+    def score(at, s, top):
+        s = s + bias_ref[at]
         s_ref[at] = s
         return jnp.maximum(top, jnp.max(fold(s), axis=0))
 
     top = jnp.full((8, wide), -1e30, F32)
-    top = score(0, 0, pair_dot(ke_ref, load_edge, bq_ref), top)
+    top = score(0, pair_dot(ke_ref, bq_ref), top)
     for c in range(2):
-        top = score(1 + c, 1, nt_dot(load_mid(km_ref, c), bq_ref[...]), top)
-    top = score(3, 2, pair_dot(kh_ref, load_halo, bq_ref), top)
+        top = score(1 + c, nt_dot(load(km_ref, c), bq_ref[...]), top)
+    top = score(3, pair_dot(kh_ref, bq_ref), top)
     top = jnp.max(top, axis=0, keepdims=True)
 
     total = jnp.zeros((8, wide), F32)
     weighted = jnp.zeros((8, wide), F32)
     for c in range(4):
         if c == 0:
-            dp = pair_dot(ve_ref, load_edge, bg_ref)
+            dp = pair_dot(ve_ref, bg_ref)
         elif c == 3:
-            dp = pair_dot(vh_ref, load_halo, bg_ref)
+            dp = pair_dot(vh_ref, bg_ref)
         else:
-            dp = nt_dot(load_mid(vm_ref, c - 1), bg_ref[...])
+            dp = nt_dot(load(vm_ref, c - 1), bg_ref[...])
         e = jnp.exp(s_ref[c] - top)
         total = total + jnp.sum(fold(e), axis=0)
         weighted = weighted + jnp.sum(fold(e * dp), axis=0)
@@ -134,7 +125,7 @@
 def grads_kernel(
     lo_ref, hi_ref, one_ref, two_ref, q_ref, g_ref,
     ke_ref, km_ref, kh_ref, ve_ref, vm_ref, vh_ref,
-    ctx_ref, dq_ref, pe_ref, pm_ref, ph_ref,
+    ctx_ref, dq_ref, part_ref,
     bias_ref, bq_ref, bg_ref, bqs_ref, bgs_ref, acc_ctx, acc_dq,
 ):
     n_query = q_ref.shape[0]
@@ -163,39 +154,35 @@
         p = jnp.exp(s + bias_ref[table] - top) * inverse
         return p.astype(BF16), (p * (dp - mean)).astype(BF16)
 
-    def pair(k_ref, v_ref, load, table, store):
-        pb, ds = soft(table, pair_dot(k_ref, load, bqs_ref), pair_dot(v_ref, load, bgs_ref))
+    shape = part_ref.shape[1:2] + part_ref.shape[3:5] + (LANES,)
+
+    def keep(section, side, kp, vp):
+        part_ref[section, :, side, :, :, :LANES] = kp.astype(BF16).reshape(shape)
+        part_ref[section, :, side, :, :, LANES:] = vp.astype(BF16).reshape(shape)
+
+    def pair(k_ref, v_ref, section, table):
+        pb, ds = soft(table, pair_dot(k_ref, bqs_ref), pair_dot(v_ref, bgs_ref))
         for side, lanes in ((0, slice(0, mid)), (1, slice(mid, wide))):
             acc_ctx[lanes, :] += tn_dot(pb[:, lanes], load(v_ref, side))
             acc_dq[lanes, :] += tn_dot(ds[:, lanes], load(k_ref, side))
-            store(side, slice(0, LANES), nn_dot(ds[:, lanes], bq_ref[lanes, :]))
-            store(side, slice(LANES, 2 * LANES), nn_dot(pb[:, lanes], bg_ref[lanes, :]))
-
-    def store_edge(side, cols, x):
-        shape = pe_ref.shape
-        pe_ref[:, :, side, :, cols] = x.astype(BF16).reshape(shape[0], shape[1], W, LANES)
-
-    def store_halo(side, cols, x):
-        shape = ph_ref.shape
-        ph_ref[side, :, :, :, cols] = x.astype(BF16).reshape(shape[1], shape[2], W, LANES)
-
-    pair(ke_ref, ve_ref, load_edge, 0, store_edge)
+            keep(
+                section, side,
+                nn_dot(ds[:, lanes], bq_ref[lanes, :]), nn_dot(pb[:, lanes], bg_ref[lanes, :]),
+            )
+
+    pair(ke_ref, ve_ref, 0, 0)
 
     def middle(c, carry):
-        runs = pm_ref.shape[0] // 2
-        k = load_mid(km_ref, c)
-        v = load_mid(vm_ref, c)
-        pb, ds = soft(1, nt_dot(k, bqs_ref[...]), nt_dot(v, bgs_ref[...]))
+        k = load(km_ref, c)
+        v = load(vm_ref, c)
+        pb, ds = soft(1 + c, nt_dot(k, bqs_ref[...]), nt_dot(v, bgs_ref[...]))
         acc_ctx[...] += tn_dot(pb, v)
         acc_dq[...] += tn_dot(ds, k)
-        shape = (runs, pm_ref.shape[1], 2 * W, LANES)
-        here = pl.ds(c * runs, runs)
-        pm_ref[here, :, :, :LANES] = nn_dot(ds, bq_ref[...]).astype(BF16).reshape(shape)
-        pm_ref[here, :, :, LANES:] = nn_dot(pb, bg_ref[...]).astype(BF16).reshape(shape)
+        keep(1, c, nn_dot(ds, bq_ref[...]), nn_dot(pb, bg_ref[...]))
         return carry
 
     lax.fori_loop(0, 2, middle, 0)
-    pair(kh_ref, vh_ref, load_halo, 2, store_halo)
+    pair(kh_ref, vh_ref, 2, 3)
 
     def diagonal(acc, out_ref):
         kept = jnp.where(own, acc, 0.0)
@@ -207,30 +194,22 @@
     diagonal(acc_dq[...], dq_ref)
 
 
-def attention(first_group, groups, lo, hi, stats, queries, d_context, keys, values):
-    n_query = queries.shape[1]
-    src, tok = keys[0].shape[0], keys[0].shape[2]
+def attention(first_group, groups, lo, hi, stats, queries, d_context, tokens):
+    n_query, width = queries.shape[1:]
+    src, _, tok = tokens[0].shape[:3]
     wide = GROUP * n_query
     flat = pl.BlockSpec((None, 1, wide), lambda b, g: (b, 0, 0))
     rows = pl.BlockSpec((None, n_query, LANES), lambda b, g: (b, 0, first_group + g))
-    table = pl.BlockSpec((None, None, 3, wide), lambda b, g: (b, g, 0, 0))
-
-    def edge(first, k=1):
-        shape = (src, None, tok, 2, W, k * LANES)
-        return pl.BlockSpec(shape, lambda b, g: (0, b, 0, 0, 0, first + g))
-
-    def mid(first, k=1):
-        shape = (src, None, tok, 2 * W, k * LANES)
-        return pl.BlockSpec(shape, lambda b, g: (0, b, 0, 0, first + g))
-
-    def halo(first, k=1):
-        shape = (2, src, None, tok, W, k * LANES)
-        return pl.BlockSpec(shape, lambda b, g: (0, 0, b, 0, 0, first + g))
-
-    sections = [edge(first_group), mid(first_group), halo(first_group)]
+    table = pl.BlockSpec((None, None, 3, wide), lambda b, g: (b, first_group + g, 0, 0))
+
+    def section(first):
+        shape = (src, 2, tok, None, W, LANES)
+        return pl.BlockSpec(shape, lambda b, g: (0, 0, 0, b, 0, first + g))
+
+    sections = [section(first_group)] * 3 + [section(width // LANES + first_group)] * 3
     operand = pltpu.VMEM((wide, LANES), BF16)
     total = pltpu.VMEM((wide, LANES), F32)
-    bias = pltpu.VMEM((3, CHUNK, wide), F32)
+    bias = pltpu.VMEM((4, CHUNK, wide), F32)
     scores = 8 * CHUNK * wide * groups
     common = dict(
         grid=(2, groups),
@@ -239,7 +218,7 @@
     if stats is None:
         return pl.pallas_call(
             stats_kernel,
-            in_specs=[flat, flat, rows, rows] + sections * 2,
+            in_specs=[flat, flat, rows, rows] + sections,
             out_specs=table,
             out_shape=jax.ShapeDtypeStruct((2, groups, 3, wide), F32),
             scratch_shapes=[pltpu.VMEM((4, CHUNK, wide), F32), bias, operand, operand],
@@ -248,25 +227,29 @@
             ),
             name="softmax_stats",
             **common,
-        )(lo, hi, queries, d_context, *keys, *values)
-
-    def shape(x):
-        return jax.ShapeDtypeStruct(x.shape[:-1] + (2 * groups * LANES,), BF16)
-
+        )(lo, hi, queries, d_context, *tokens, *tokens)
+
+    parts = pl.BlockSpec(
+        (3, src, 2, tok, None, W, 2 * LANES), lambda b, g: (0, 0, 0, 0, b, 0, g)
+    )
     partial = jax.ShapeDtypeStruct((2, n_query, groups * LANES), F32)
     partial_spec = pl.BlockSpec((None, n_query, LANES), lambda b, g: (b, 0, g))
     return pl.pallas_call(
         grads_kernel,
-        in_specs=[flat, flat, table, table, rows, rows] + sections * 2,
-        out_specs=[partial_spec, partial_spec, edge(0, 2), mid(0, 2), halo(0, 2)],
-        out_shape=[partial, partial] + [shape(x) for x in keys],
+        in_specs=[flat, flat, table, table, rows, rows] + sections,
+        out_specs=[partial_spec, partial_spec, parts],
+        out_shape=[
+            partial,
+            partial,
+            jax.ShapeDtypeStruct((3, src, 2, tok, 2, W, 2 * groups * LANES), BF16),
+        ],
         scratch_shapes=[bias] + [operand] * 4 + [total] * 2,
         cost_estimate=pl.CostEstimate(
             flops=12 * scores * LANES, bytes_accessed=12 * scores, transcendentals=scores
         ),
         name="banded_grads",
         **common,
-    )(lo, hi, *stats, queries, d_context, *keys, *values)
+    )(lo, hi, *stats, queries, d_context, *tokens, *tokens)
 
 
 class ScatterSum:
@@ -341,26 +324,25 @@
     upper_half = me >= src
     spot = me % src
 
-    by_block = exo_tokens.reshape(2, src, n_query, tok, width)
-    halves = [list(range(src)), list(range(src, n_dev))]
-    outer = jnp.stack([by_block[:, :, :W], by_block[:, :, -W:]], axis=2)
-    outer = outer.transpose(1, 0, 4, 2, 3, 5)
-    inner = by_block[:, :, W:-W].transpose(1, 0, 3, 2, 4)
-    edge = lax.all_to_all(outer, "tm", 0, 0, axis_index_groups=halves, tiled=True)
-    middle = lax.all_to_all(inner, "tm", 0, 0, axis_index_groups=halves, tiled=True)
-    ring = [(i, i // src * src + (i + 1) % src) for i in range(n_dev)]
-    low = lax.ppermute(edge[:, :, :, 1], "tm", ring)
-    high = lax.ppermute(edge[:, :, :, 0], "tm", [(target, source) for source, target in ring])
-    low = jnp.where(spot == 0, jnp.flip(low, 1), low)
-    high = jnp.where(spot == src - 1, jnp.flip(high, 1), high)
-    halo = jnp.stack([low, high], axis=0)
-
+    fence = lax.optimization_barrier
     valid_col = gaze_valid.astype(F32)[:, None]
     masked_grad = (cotangent.astype(F32) * valid_col).astype(BF16)
     far = bits - 1
     gather = Gather(masked_grad, bits)
     swap_q, swap_o = Swap(queries, far), Swap(window_offset, far)
-    beside([gather, swap_q, swap_o], lambda: ())
+
+    def frames(exo, *cuts):
+        by_block = exo.reshape(2, src, n_query, tok, width)
+        runs = jnp.stack([by_block[:, :, cut : cut + W] for cut in cuts], axis=2)
+        return runs.transpose(1, 2, 4, 0, 3, 5)
+
+    later = fence(exo_tokens)
+    outer = beside(
+        [gather, swap_q, swap_o], lambda exo: frames(exo, 0, n_query - W), exo_tokens
+    )
+    inner = frames(later, W, 2 * W)
+    halves = [list(range(src)), list(range(src, n_dev))]
+    edge = lax.all_to_all(outer, "tm", 0, 0, axis_index_groups=halves, tiled=True)
 
     def both(own, other):
         return jnp.where(upper_half, jnp.stack([other, own]), jnp.stack([own, other]))
@@ -378,29 +360,40 @@
         return jnp.tile(x.reshape(2, 2, 1, n_query // 2), (1, 1, GROUP, 1)).reshape(2, 1, -1)
 
     lo, hi = lanes(lower), lanes(upper)
+    weights = jnp.concatenate([key_weight, value_weight], axis=1)
+    edge, inner, q_pair, g_pair, lo, hi, weights = fence(
+        (edge, inner, q_pair, g_pair, lo, hi, weights)
+    )
 
     def project(x):
-        flat = x.reshape(-1, width)
-        return (
-            nn_dot(flat, key_weight).astype(BF16).reshape(x.shape),
-            nn_dot(flat, value_weight).astype(BF16).reshape(x.shape),
-        )
-
-    ke, ve = project(edge)
-    km, vm = beside([gather], project, middle)
-    kh, vh = project(halo)
-    keys, values = (ke, km, kh), (ve, vm, vh)
-    sources = [x.reshape(-1, width) for x in (edge, middle, halo)]
+        flat = nn_dot(x.reshape(-1, width), weights).astype(BF16)
+        return flat.reshape(x.shape[:-1] + (2 * width,))
+
+    low = jnp.where(spot == src - 1, jnp.flip(edge[:, 1], 2), edge[:, 1])
+    high = jnp.where(spot == 0, jnp.flip(edge[:, 0], 2), edge[:, 0])
+    low, high, inner = fence((low, high, inner))
+    ring = [(i, i // src * src + (i + 1) % src) for i in range(n_dev)]
+    low = lax.ppermute(low, "tm", ring)
+    high = lax.ppermute(high, "tm", [(target, source) for source, target in ring])
+    middle = lax.all_to_all(inner, "tm", 0, 0, axis_index_groups=halves, tiled=True)
+    edge_kv, low, high = fence((project(edge), low, high))
+    halo = jnp.stack([low, high], axis=1)
+    halo_kv, middle = fence((project(halo), middle))
+    middle_kv = beside([gather], project, middle)
+    tokens = (edge_kv, middle_kv, halo_kv)
 
     groups = width // LANES // CALLS
-
-    def measure(call, moving):
-        work = functools.partial(attention, call * groups, groups, lo, hi, None)
-        return Swap(beside(moving, work, q_pair, g_pair, keys, values), far)
-
-    swaps = [measure(0, [gather])]
-    for call in range(1, CALLS):
-        swaps.append(measure(call, [gather, swaps[-1]]))
+    stats = beside(
+        [gather],
+        functools.partial(attention, 0, width // LANES, lo, hi, None),
+        q_pair, g_pair, tokens,
+    )
+    swap = Swap(stats, far)
+    sources = beside(
+        [gather, swap],
+        lambda *x: jnp.concatenate([y.reshape(-1, width) for y in x], axis=0),
+        edge, middle, halo,
+    )
 
     def own_part(x):
         return jnp.where(upper_half, x[1], x[0])
@@ -408,28 +401,21 @@
     def other_part(x):
         return jnp.where(upper_half, x[0], x[1])
 
-    moving = [gather] + swaps
+    moving = [gather]
     owns, trades, shares = [], [], []
-    if CALLS == 1:
-        beside(moving, lambda: ())
     for call in range(CALLS):
-        stats = (swaps[call].block, swaps[call].come)
-        work = functools.partial(attention, call * groups, groups, lo, hi, stats)
-        context, d_query, *grads = beside(moving, work, q_pair, g_pair, keys, values)
+        work = functools.partial(attention, call * groups, groups, lo, hi, (swap.block, swap.come))
+        context, d_query, grads = beside(moving, work, q_pair, g_pair, tokens)
         owns.append(jnp.stack([own_part(context), own_part(d_query)]))
         trades.append(Swap(jnp.stack([other_part(context), other_part(d_query)]), far))
         moving.append(trades[-1])
-
-        def weigh(*parts):
-            terms = [tn_dot(x, g.reshape(x.shape[0], -1)) for x, g in zip(sources, parts)]
-            return functools.reduce(jnp.add, terms).astype(BF16)
-
-        term = beside(moving, weigh, *grads)
-        cut = term.shape[1] // 2
-        orders = [list(range(bits)), [0] + list(range(2, bits)) + [1]]
-        for i, order in enumerate(orders):
-            shares.append(ScatterSum(term[:, i * cut : (i + 1) * cut], bits, order))
-            moving.append(shares[-1])
+        term = beside(
+            moving,
+            lambda g: tn_dot(sources, g.reshape(sources.shape[0], -1)).astype(BF16),
+            grads,
+        )
+        shares.append(ScatterSum(term, bits, range(bits)))
+        moving.append(shares[-1])
 
     pairs = [own + trade.come for own, trade in zip(owns, trades)]
     context = jnp.concatenate([x[0] for x in pairs], axis=1).astype(BF16)
@@ -477,4 +463,5 @@
         P(("rep", "tm"), None),
         P(("rep", "tm"), None),
     )
+
     return jax.shard_map(shards, mesh=mesh, in_specs=in_specs, out_specs=out_specs, check_vma=False)

time: 278 us -> 288 us (1.036)
  waiting for transfers between devices: 66.8 us -> 78.4 us
  other arithmetic: 23.9 us -> 34.7 us
  matrix products: 57.7 us -> 50.8 us
  starting transfers between devices: 51.6 us -> 45.2 us
  local copies, waits for them, and re-layouts: 30.6 us -> 36.6 us
    ppermute x2, waiting for transfers between devices: 0.01 us -> 25.9 us  [the longest x1 25.9 us: shards(): low = lax.ppermute(low, 'tm', ring)]
    all_to_all x1, waiting for transfers between devices: 22.5 us -> 13.3 us  [shards(): lax.all_to_all(outer, 'tm', 0, 0, axis_index_groups=halves, tiled=True)]
    concatenate x0 -> x2, other arithmetic: none -> 8.37 us  [the longest x1 5.96 us: shards(): jnp.concatenate([y.reshape(-1, width) for y in x], axis=0)]
    ppermute x26 -> x17, waiting for transfers between devices: 42.1 us -> 33.9 us  [beside(): lax.ppermute(away, 'tm', [(i, i ^ step) for i in range(n_dev)])]
    optimization_barrier x0 -> x2, local copies, waits for them, and re-layouts: none -> 5.02 us  [the longest x1 3.49 us: shards(): later = fence(exo_tokens)]
    optimization_barrier x1 -> x2, local copies, waits for them, and re-layouts: 0.24 us -> 4.43 us  [beside(): args, aways = lax.optimization_barrier((args, [away for away, _ in sends]))]
    dot_general x7 -> x4, matrix products: 29.9 us -> 25.8 us  [nn_dot(): return jnp.dot(a, b, preferred_element_type=F32)]
    transpose x1 -> x0, local copies, waits for them, and re-layouts: 3.28 us -> none  [shards(): inner = by_block[:, :, W:-W].transpose(1, 0, 3, 2, 4)]
  transfers between devices with their start and end apart: 31 -> 22, of which waited for: 13 -> 12; matrix products, arithmetic and copies ran while one was open for 26% -> 29% of each run, Pallas kernels for 15% -> 9%
where the time goes in v3:
time: 288 us; the launch traced here: 286 us
  waiting for transfers between devices  78.4 us (27%)
  matrix products  50.8 us (18%)
  starting transfers between devices  45.2 us (16%)
  Pallas kernels  39.3 us (14%)
  local copies, waits for them, and re-layouts  36.6 us (13%)
  other arithmetic  34.7 us (12%)
    ppermute x17, waiting for transfers between devices, beside(): lax.ppermute(away, 'tm', [(i, i ^ step) for i in range(n_dev)])  33.9 us
    ppermute x17, starting transfers between devices, beside(): lax.ppermute(away, 'tm', [(i, i ^ step) for i in range(n_dev)])  30.1 us
    pallas_call x2, Pallas kernels, attention(): pl.pallas_call(grads_kernel, in_specs=[flat, flat, table, table, rows, ro...  28.3 us
    ppermute x1, waiting for transfers between devices, shards(): low = lax.ppermute(low, 'tm', ring)  25.9 us
    dot_general x4, matrix products, nn_dot(): return jnp.dot(a, b, preferred_element_type=F32)  25.8 us
    dot_general x3, matrix products, tn_dot(): lax.dot_general(a, b, (((0,), (0,)), ((), ())), preferred_element_type=F32)  24.1 us
    all_to_all x1, waiting for transfers between devices, shards(): lax.all_to_all(outer, 'tm', 0, 0, axis_index_groups=halves, tiled=True)  13.3 us
    pallas_call x1, Pallas kernels, attention(): pl.pallas_call(stats_kernel, in_specs=[flat, flat, rows, rows] + sections...  11 us
  transfers between devices with their start and end apart: 22, of which 12 were waited for; matrix products, arithmetic and copies ran while one was open for 29% of the time, Pallas kernels for 9%

profile of v3, /device:TPU:0, one launch (start us, length us, event | category | flops | bytes accessed | tf_op | source)
XLA Modules:
  0.0 286.3 jit_solution(15620650824575799554)
XLA Ops:
  3.1 4.1 %collective-permute-start.2 = (s32[64]{0:T(128)}, s32[64]{0:T(128)S(1)}, u32[]{:S(2)}, u32[]{:S(2)}) collective-permute-start(s32[64]{0:T(128)} %param.15), channel_id=1, source_target_pairs={{0,8},{1,9},{2,10},{3,11},{4,12},{5,13},{6,14},{7,15},{8,0},{9,1},... | collective-permute-start | bytes 776 | tf_op jit(solution)/shard_map/ppermute | solution.py:305
  7.2 2.9 %collective-permute-start.1 = (bf16[64,1024]{1,0:T(8,128)(2,1)}, bf16[64,1024]{1,0:T(8,128)(2,1)S(1)}, u32[]{:S(2)}, u32[]{:S(2)}) collective-permute-start(bf16[64,1024]{1,0:T(8,128)(2,1)} %param.10), channel_id=1, source_target_pairs={{0,8},{1,9},{2,10},{3,11},{4,12},{5,13},{6,14},{7,15},{8,0},{9,1},... | collective-permute-start | bytes 393224 | tf_op jit(solution)/shard_map/ppermute | solution.py:305
  10.1 3.5 %copy.49 = bf16[1024,2,1024]{2,0,1:T(8,128)(2,1)S(1)} copy(bf16[1024,2,1024]{2,1,0:T(2,128)(2,1)} %param.9) | data formatting | bytes 8388608 | tf_op jit(solution)/shard_map/optimization_barrier | solution.py:303
  14.0 5.8 %collective-permute-done = bf16[64,1024]{1,0:T(8,128)(2,1)S(1)} collective-permute-done((bf16[64,1024]{1,0:T(8,128)(2,1)S(1)}, bf16[64,1024]{1,0:T(8,128)(2,1)S(1)}, u32[]{:S(2)}, u32[]{:S(2)}) %collective-permute-start) | collective-permute-done | bytes 131104 | tf_op jit(solution)/shard_map/ppermute | solution.py:305
  22.9 4.5 %all-to-all-start = ((bf16[8,2,2,2,16,1024]{5,4,3,2,1,0:T(8,128)(2,1)}), bf16[8,2,2,2,16,1024]{5,4,3,2,1,0:T(8,128)(2,1)}, u32[]{:S(2)}, u32[]{:S(2)}) async-start(bf16[8,2,2,2,16,1024]{5,4,3,2,1,0:T(8,128)(2,1)} %copy.50), calls=%async_computation | async-start | bytes 4194304 | tf_op jit(solution)/shard_map/all_to_all | solution.py:345
  27.5 3.5 %copy.51 = bf16[1024,2,1024]{2,0,1:T(8,128)(2,1)S(1)} copy(bf16[1024,2,1024]{2,1,0:T(2,128)(2,1)} %param.9) | data formatting | bytes 8388608 | tf_op jit(solution)/shard_map/optimization_barrier | solution.py:339
  34.2 2.4 pad_maximum_fusion.1
  39.9 13.3 %all-to-all-done = bf16[8,2,2,2,16,1024]{5,4,3,2,1,0:T(8,128)(2,1)} async-done(((bf16[8,2,2,2,16,1024]{5,4,3,2,1,0:T(8,128)(2,1)}), bf16[8,2,2,2,16,1024]{5,4,3,2,1,0:T(8,128)(2,1)}, u32[]{:S(2)}, u32[]{:S(2)}) %all-to-all-start) | async-done | bytes 2097184 | tf_op jit(solution)/shard_map/all_to_all | solution.py:345
  59.0 4.3 %all-to-all-start.1 = ((bf16[8,2,2,2,16,1024]{5,4,3,2,1,0:T(8,128)(2,1)}), bf16[8,2,2,2,16,1024]{5,4,3,2,1,0:T(8,128)(2,1)}, u32[]{:S(2)}, u32[]{:S(2)}) async-start(bf16[8,2,2,2,16,1024]{5,4,3,2,1,0:T(8,128)(2,1)} %copy.54), calls=%async_computation.1 | async-start | bytes 4194304 | tf_op jit(solution)/shard_map/all_to_all | solution.py:378
  63.7 2.3 collective-permute-start.4
  66.0 9.3 %convolution_convert_fusion.2 = bf16[1024,2048]{1,0:T(8,128)(2,1)} fusion(bf16[1024,1024]{1,0:T(8,128)(2,1)} %bitcast.12, bf16[1024,2048]{1,0:T(8,128)(2,1)} %pad_maximum_fusion.1), kind=kOutput, calls=%fused_computation.4 | convolution fusion | flops 4297064448 | bytes 10485760 | tf_op jit(solution)/shard_map/dot_general | solution.py:30
  75.3 25.9 %collective-permute-done.3 = bf16[8,2,2,16,1024]{4,3,2,1,0:T(8,128)(2,1)S(1)} collective-permute-done((bf16[8,2,2,16,1024]{4,3,2,1,0:T(8,128)(2,1)}, bf16[8,2,2,16,1024]{4,3,2,1,0:T(8,128)(2,1)S(1)}, u32[]{:S(2)}, u32[]{:S(2)}) %collective-permute-start.3) | collective-permute-done | bytes 1048608 | tf_op jit(solution)/shard_map/ppermute | solution.py:376
  104.1 6.1 %convolution_convert_fusion.1 = bf16[1024,2048]{1,0:T(8,128)(2,1)} fusion(bf16[1024,1024]{1,0:T(8,128)(2,1)S(1)} %bitcast.164, bf16[1024,2048]{1,0:T(8,128)(2,1)S(1)} %copy-done.5), kind=kOutput, calls=%fused_computation.3 | convolution fusion | flops 4297064448 | bytes 10485760 | tf_op jit(solution)/shard_map/dot_general | solution.py:30
  110.8 9.3 %convolution_convert_fusion = bf16[1024,2048]{1,0:T(8,128)(2,1)} fusion(bf16[1024,1024]{1,0:T(8,128)(2,1)} %bitcast.20, bf16[1024,2048]{1,0:T(8,128)(2,1)} %pad_maximum_fusion.1), kind=kOutput, calls=%fused_computation.2 | convolution fusion | flops 4297064448 | bytes 10485760 | tf_op jit(solution)/shard_map/dot_general | solution.py:30
  120.9 11.7 %collective-permute-start.6 = (bf16[256,1024]{1,0:T(8,128)(2,1)}, bf16[256,1024]{1,0:T(8,128)(2,1)S(1)}, u32[]{:S(2)}, u32[]{:S(2)}) collective-permute-start(bf16[256,1024]{1,0:T(8,128)(2,1)} %pad_maximum_fusion.4), channel_id=1, source_target_pairs={{0,2},{1,3},{2,0},{3,1},{4,6},{5,7},{6,4},{7,5},{8,10},{9,11},{10,... | collective-permute-start | bytes 1572872 | tf_op jit(solution)/shard_map/ppermute | solution.py:305
  132.6 11.0 %softmax_stats.1.one_ref = f32[2,4,3,256]{3,2,1,0:T(4,128)} custom-call(s32[2,1,256]{2,1,0:T(1,128)} %tile.15.lo_ref, s32[2,1,256]{2,1,0:T(1,128)} %tile.17.hi_ref, bf16[2,64,1024]{2,1,0:T(8,128)(2,1)} %get-tuple-element.146.q_ref, bf16[2,64,1024]{2,1,0:T(8,128)(2,1)} %get-tuple-element.147.g_ref, bf16[8,2,2,2,16,2048]{5,4,3,2,1,0:T(8,128)(2,1)} %bitcast.144, ...), custom_call_target="tpu_custom_call" | custom-call | flops 2147483648 | bytes 12582912 | tf_op jit(solution)/shard_map/softmax_stats/pallas_call | solution.py:219
  146.8 6.0 %pad_maximum_fusion = bf16[3072,1024]{1,0:T(8,128)(2,1)} fusion(bf16[1024,1024]{1,0:T(8,128)(2,1)} %bitcast.165, bf16[1024,1024]{1,0:T(8,128)(2,1)} %bitcast.23, bf16[1024,1024]{1,0:T(8,128)(2,1)} %bitcast.22), kind=kLoop, calls=%fused_computation | loop fusion | flops 18874368 | bytes 12582912 | tf_op jit(solution)/shard_map/concatenate | solution.py:394
  153.4 14.1 %banded_grads.2 = (f32[2,64,512]{2,1,0:T(8,128)}, f32[2,64,512]{2,1,0:T(8,128)}, bf16[3,8,2,2,2,16,1024]{6,5,4,3,2,1,0:T(8,128)(2,1)}) custom-call(s32[2,1,256]{2,1,0:T(1,128)} %tile.15.lo_ref, s32[2,1,256]{2,1,0:T(1,128)} %tile.17.hi_ref, f32[2,4,3,256]{3,2,1,0:T(4,128)} %softmax_stats.1.one_ref, f32[2,4,3,256]{3,2,1,0:T(4,128)} %copy-done.21, ...), custom_call_target="tpu_custom_call" | custom-call | flops 3221225472 | bytes 12582912 | tf_op jit(solution)/shard_map/banded_grads/pallas_call | solution.py:237
  170.8 3.0 %collective-permute-start.9 = (f32[2,64,512]{2,1,0:T(8,128)S(1)}, f32[2,64,512]{2,1,0:T(8,128)S(1)}, u32[]{:S(2)}, u32[]{:S(2)}) collective-permute-start(f32[2,64,512]{2,1,0:T(8,128)S(1)} %pad_maximum_fusion.6), channel_id=1, source_target_pairs={{0,8},{1,9},{2,10},{3,11},{4,12},{5,13},{6,14},{7,15},{8,0},{9,1},... | collective-permute-start | bytes 786440 | tf_op jit(solution)/shard_map/ppermute | solution.py:305
  173.8 10.7 %convolution_convert_fusion.4 = bf16[1024,1024]{1,0:T(8,128)(2,1)S(1)} fusion(bf16[3072,1024]{1,0:T(8,128)(2,1)} %pad_maximum_fusion, bf16[3072,1024]{1,0:T(8,128)(2,1)} %bitcast.183), kind=kOutput, calls=%fused_computation.13 | convolution fusion | flops 6443499520 | bytes 14680064 | tf_op jit(solution)/shard_map/dot_general | solution.py:22
  189.1 14.3 %banded_grads.3 = (f32[2,64,512]{2,1,0:T(8,128)}, f32[2,64,512]{2,1,0:T(8,128)}, bf16[3,8,2,2,2,16,1024]{6,5,4,3,2,1,0:T(8,128)(2,1)}) custom-call(s32[2,1,256]{2,1,0:T(1,128)} %tile.15.lo_ref, s32[2,1,256]{2,1,0:T(1,128)} %tile.17.hi_ref, f32[2,4,3,256]{3,2,1,0:T(4,128)} %softmax_stats.1.one_ref, f32[2,4,3,256]{3,2,1,0:T(4,128)} %copy-done.21, ...), custom_call_target="tpu_custom_call" | custom-call | flops 3221225472 | bytes 12582912 | tf_op jit(solution)/shard_map/banded_grads/pallas_call | solution.py:237
  208.0 10.7 %convolution_convert_fusion.3 = bf16[1024,1024]{1,0:T(8,128)(2,1)S(1)} fusion(bf16[3072,1024]{1,0:T(8,128)(2,1)} %pad_maximum_fusion, bf16[3072,1024]{1,0:T(8,128)(2,1)} %bitcast.182), kind=kOutput, calls=%fused_computation.12 | convolution fusion | flops 6443499520 | bytes 14680064 | tf_op jit(solution)/shard_map/dot_general | solution.py:22
  218.7 3.7 %collective-permute-done.12 = f32[2,64,512]{2,1,0:T(8,128)S(1)} collective-permute-done((f32[2,64,512]{2,1,0:T(8,128)S(1)}, f32[2,64,512]{2,1,0:T(8,128)S(1)}, u32[]{:S(2)}, u32[]{:S(2)}) %collective-permute-start.12) | collective-permute-done | bytes 262176 | tf_op jit(solution)/shard_map/ppermute | solution.py:305
  231.3 3.6 %all-to-all-start.2 = ((bf16[16,2,2048]{2,1,0:T(2,128)(2,1)}), bf16[16,2,2048]{2,1,0:T(2,128)(2,1)S(1)}, u32[]{:S(2)}, u32[]{:S(2)}) async-start(bf16[16,2,2048]{2,1,0:T(2,128)(2,1)} %reshape.225), calls=%async_computation.2 | async-start | bytes 262144 | tf_op jit(solution)/shard_map/all_to_all | solution.py:427
  238.0 5.4 %all-to-all-done.2 = bf16[16,2,2048]{2,1,0:T(2,128)(2,1)S(1)} async-done(((bf16[16,2,2048]{2,1,0:T(2,128)(2,1)}), bf16[16,2,2048]{2,1,0:T(2,128)(2,1)S(1)}, u32[]{:S(2)}, u32[]{:S(2)}) %all-to-all-start.2) | async-done | bytes 131104 | tf_op jit(solution)/shard_map/all_to_all | solution.py:427
  243.6 2.4 collective-permute-done.13
  252.1 2.3 constant_dynamic-update-slice_fusion
  256.5 2.4 collective-permute-start.15
  259.0 2.8 fusion.13
  261.7 3.2 %collective-permute-done.15 = bf16[64,1024]{1,0:T(8,128)(2,1)S(1)} collective-permute-done((bf16[64,1024]{1,0:T(8,128)(2,1)S(1)}, bf16[64,1024]{1,0:T(8,128)(2,1)S(1)}, u32[]{:S(2)}, u32[]{:S(2)}) %collective-permute-start.15) | collective-permute-done | bytes 131104 | tf_op jit(solution)/shard_map/ppermute | solution.py:305
  268.1 7.1 %collective-permute-done.17 = bf16[2,64,1024]{2,1,0:T(8,128)(2,1)S(1)} collective-permute-done((bf16[2,64,1024]{2,1,0:T(8,128)(2,1)S(1)}, bf16[2,64,1024]{2,1,0:T(8,128)(2,1)S(1)}, u32[]{:S(2)}, u32[]{:S(2)}) %collective-permute-start.17) | collective-permute-done | bytes 262176 | tf_op jit(solution)/shard_map/ppermute | solution.py:305
  277.4 6.9 %collective-permute-done.18 = bf16[64,1024]{1,0:T(8,128)(2,1)S(1)} collective-permute-done((bf16[64,1024]{1,0:T(8,128)(2,1)S(1)}, bf16[64,1024]{1,0:T(8,128)(2,1)S(1)}, u32[]{:S(2)}, u32[]{:S(2)}) %collective-permute-start.18) | collective-permute-done | bytes 131104 | tf_op jit(solution)/shard_map/ppermute | solution.py:305
  (161 shorter events, 67.0 us)
Async XLA Ops:
  0.6 37.5 %copy-start = (bf16[1024,1024]{1,0:T(8,128)(2,1)S(1)}, bf16[1024,1024]{1,0:T(8,128)(2,1)}, u32[]{:S(2)}) copy-start(bf16[1024,1024]{1,0:T(8,128)(2,1)} %param.13) | copy-start | bytes 6291460
  3.1 10.9 %collective-permute-start.2 = (s32[64]{0:T(128)}, s32[64]{0:T(128)S(1)}, u32[]{:S(2)}, u32[]{:S(2)}) collective-permute-start(s32[64]{0:T(128)} %param.15), channel_id=1, source_target_pairs={{0,8},{1,9},{2,10},{3,11},{4,12},{5,13},{6,14},{7,15},{8,0},{9,1},... | collective-permute-start | bytes 776 | tf_op jit(solution)/shard_map/ppermute | solution.py:305
  7.2 12.6 %collective-permute-start = (bf16[64,1024]{1,0:T(8,128)(2,1)S(1)}, bf16[64,1024]{1,0:T(8,128)(2,1)S(1)}, u32[]{:S(2)}, u32[]{:S(2)}) collective-permute-start(bf16[64,1024]{1,0:T(8,128)(2,1)S(1)} %get-tuple-element.93), channel_id=1, source_target_pairs={{0,8},{1,9},{2,10},{3,11},{4,12},{5,13},{6,14},{7,15},{8,0},{9,1},... | collective-permute-start | bytes 393224 | tf_op jit(solution)/shard_map/ppermute | solution.py:305
  7.2 14.3 %collective-permute-start.1 = (bf16[64,1024]{1,0:T(8,128)(2,1)}, bf16[64,1024]{1,0:T(8,128)(2,1)S(1)}, u32[]{:S(2)}, u32[]{:S(2)}) collective-permute-start(bf16[64,1024]{1,0:T(8,128)(2,1)} %param.10), channel_id=1, source_target_pairs={{0,8},{1,9},{2,10},{3,11},{4,12},{5,13},{6,14},{7,15},{8,0},{9,1},... | collective-permute-start | bytes 393224 | tf_op jit(solution)/shard_map/ppermute | solution.py:305
  22.9 4.5 %copy-start.23 = (s32[64]{0:T(128)S(1)}, s32[64]{0:T(128)}, u32[]{:S(2)}) copy-start(s32[64]{0:T(128)} %param.15) | copy-start | bytes 772
  22.9 30.2 %all-to-all-start = ((bf16[8,2,2,2,16,1024]{5,4,3,2,1,0:T(8,128)(2,1)}), bf16[8,2,2,2,16,1024]{5,4,3,2,1,0:T(8,128)(2,1)}, u32[]{:S(2)}, u32[]{:S(2)}) async-start(bf16[8,2,2,2,16,1024]{5,4,3,2,1,0:T(8,128)(2,1)} %copy.50), calls=%async_computation | async-start | bytes 4194304 | tf_op jit(solution)/shard_map/all_to_all | solution.py:345
  59.0 51.2 %all-to-all-start.1 = ((bf16[8,2,2,2,16,1024]{5,4,3,2,1,0:T(8,128)(2,1)}), bf16[8,2,2,2,16,1024]{5,4,3,2,1,0:T(8,128)(2,1)}, u32[]{:S(2)}, u32[]{:S(2)}) async-start(bf16[8,2,2,2,16,1024]{5,4,3,2,1,0:T(8,128)(2,1)} %copy.54), calls=%async_computation.1 | async-start | bytes 4194304 | tf_op jit(solution)/shard_map/all_to_all | solution.py:378
  63.3 37.9 %collective-permute-start.3 = (bf16[8,2,2,16,1024]{4,3,2,1,0:T(8,128)(2,1)}, bf16[8,2,2,16,1024]{4,3,2,1,0:T(8,128)(2,1)S(1)}, u32[]{:S(2)}, u32[]{:S(2)}) collective-permute-start(bf16[8,2,2,16,1024]{4,3,2,1,0:T(8,128)(2,1)} %reverse_select_fusion.1), channel_id=1, source_target_pairs={{0,1},{1,2},{2,3},{3,4},{4,5},{5,6},{6,7},{7,0},{8,9},{9,10},{10,1... | collective-permute-start | bytes 3145736 | tf_op jit(solution)/shard_map/ppermute | solution.py:376
  63.7 37.5 %collective-permute-start.4 = (bf16[8,2,2,16,1024]{4,3,2,1,0:T(8,128)(2,1)}, bf16[8,2,2,16,1024]{4,3,2,1,0:T(8,128)(2,1)S(1)}, u32[]{:S(2)}, u32[]{:S(2)}) collective-permute-start(bf16[8,2,2,16,1024]{4,3,2,1,0:T(8,128)(2,1)} %reverse_select_fusion), channel_id=1, source_target_pairs={{1,0},{2,1},{3,2},{4,3},{5,4},{6,5},{7,6},{0,7},{9,8},{10,9},{11,1... | collective-permute-start | bytes 3145736 | tf_op jit(solution)/shard_map/ppermute | solution.py:377
  110.2 9.9 %collective-permute-start.5 = (bf16[128,1024]{1,0:T(8,128)(2,1)S(1)}, bf16[128,1024]{1,0:T(8,128)(2,1)S(1)}, u32[]{:S(2)}, u32[]{:S(2)}) collective-permute-start(bf16[128,1024]{1,0:T(8,128)(2,1)S(1)} %pad_maximum_fusion.5), channel_id=1, source_target_pairs={{0,4},{1,5},{2,6},{3,7},{4,0},{5,1},{6,2},{7,3},{8,12},{9,13},{10,... | collective-permute-start | bytes 786440 | tf_op jit(solution)/shard_map/ppermute | solution.py:305
  120.9 24.6 %collective-permute-start.6 = (bf16[256,1024]{1,0:T(8,128)(2,1)}, bf16[256,1024]{1,0:T(8,128)(2,1)S(1)}, u32[]{:S(2)}, u32[]{:S(2)}) collective-permute-start(bf16[256,1024]{1,0:T(8,128)(2,1)} %pad_maximum_fusion.4), channel_id=1, source_target_pairs={{0,2},{1,3},{2,0},{3,1},{4,6},{5,7},{6,4},{7,5},{8,10},{9,11},{10,... | collective-permute-start | bytes 1572872 | tf_op jit(solution)/shard_map/ppermute | solution.py:305
  143.6 3.3 %copy-start.16 = (f32[2,4,3,256]{3,2,1,0:T(4,128)S(1)}, f32[2,4,3,256]{3,2,1,0:T(4,128)}, u32[]{:S(2)}) copy-start(f32[2,4,3,256]{3,2,1,0:T(4,128)} %softmax_stats.1.one_ref) | copy-start | bytes 73732
  145.6 7.2 %copy-start.9 = (bf16[256,1024]{1,0:T(8,128)(2,1)}, bf16[256,1024]{1,0:T(8,128)(2,1)S(1)}, u32[]{:S(2)}) copy-start(bf16[256,1024]{1,0:T(8,128)(2,1)S(1)} %collective-permute-done.6) | copy-start | bytes 1572868
  146.7 6.1 %collective-permute-start.7 = (bf16[512,1024]{1,0:T(8,128)(2,1)}, bf16[512,1024]{1,0:T(8,128)(2,1)}, u32[]{:S(2)}, u32[]{:S(2)}) collective-permute-start(bf16[512,1024]{1,0:T(8,128)(2,1)} %pad_maximum_fusion.3), channel_id=1, source_target_pairs={{0,1},{1,0},{2,3},{3,2},{4,5},{5,4},{6,7},{7,6},{8,9},{9,8},{10,11... | collective-permute-start | bytes 3145736 | tf_op jit(solution)/shard_map/ppermute | solution.py:305
  146.8 6.0 %collective-permute-start.8 = (f32[2,4,3,256]{3,2,1,0:T(4,128)S(1)}, f32[2,4,3,256]{3,2,1,0:T(4,128)S(1)}, u32[]{:S(2)}, u32[]{:S(2)}) collective-permute-start(f32[2,4,3,256]{3,2,1,0:T(4,128)S(1)} %copy-done.16), channel_id=1, source_target_pairs={{0,8},{1,9},{2,10},{3,11},{4,12},{5,13},{6,14},{7,15},{8,0},{9,1},... | collective-permute-start | bytes 73736 | tf_op jit(solution)/shard_map/ppermute | solution.py:305
  170.8 14.8 %collective-permute-start.9 = (f32[2,64,512]{2,1,0:T(8,128)S(1)}, f32[2,64,512]{2,1,0:T(8,128)S(1)}, u32[]{:S(2)}, u32[]{:S(2)}) collective-permute-start(f32[2,64,512]{2,1,0:T(8,128)S(1)} %pad_maximum_fusion.6), channel_id=1, source_target_pairs={{0,8},{1,9},{2,10},{3,11},{4,12},{5,13},{6,14},{7,15},{8,0},{9,1},... | collective-permute-start | bytes 786440 | tf_op jit(solution)/shard_map/ppermute | solution.py:305
  187.3 16.1 %collective-permute-start.10 = (bf16[2,2,2,64,1024]{4,3,0,1,2:T(8,128)(2,1)}, bf16[2,2,2,64,1024]{4,3,0,1,2:T(8,128)(2,1)}, u32[]{:S(2)}, u32[]{:S(2)}) collective-permute-start(bf16[2,2,2,64,1024]{4,3,0,1,2:T(8,128)(2,1)} %bitcast.134), channel_id=1, source_target_pairs={{0,1},{1,0},{2,3},{3,2},{4,5},{5,4},{6,7},{7,6},{8,9},{9,8},{10,11... | collective-permute-start | bytes 3145736 | tf_op jit(solution)/shard_map/ppermute | solution.py:305
  207.1 15.2 %collective-permute-start.12 = (f32[2,64,512]{2,1,0:T(8,128)S(1)}, f32[2,64,512]{2,1,0:T(8,128)S(1)}, u32[]{:S(2)}, u32[]{:S(2)}) collective-permute-start(f32[2,64,512]{2,1,0:T(8,128)S(1)} %pad_maximum_fusion.7), channel_id=1, source_target_pairs={{0,8},{1,9},{2,10},{3,11},{4,12},{5,13},{6,14},{7,15},{8,0},{9,1},... | collective-permute-start | bytes 786440 | tf_op jit(solution)/shard_map/ppermute | solution.py:305
  207.2 15.2 %collective-permute-start.11 = (bf16[2,2,64,1024]{3,2,0,1:T(8,128)(2,1)S(1)}, bf16[2,2,64,1024]{3,2,0,1:T(8,128)(2,1)S(1)}, u32[]{:S(2)}, u32[]{:S(2)}) collective-permute-start(bf16[2,2,64,1024]{3,2,0,1:T(8,128)(2,1)S(1)} %dynamic-slice_bitcast_fusion.1), channel_id=1, source_target_pairs={{0,2},{1,3},{2,0},{3,1},{4,6},{5,7},{6,4},{7,5},{8,10},{9,11},{10,... | collective-permute-start | bytes 1572872 | tf_op jit(solution)/shard_map/ppermute | solution.py:305
  226.2 19.9 %collective-permute-start.14 = (bf16[2,2,2,64,1024]{4,3,0,1,2:T(8,128)(2,1)}, bf16[2,2,2,64,1024]{4,3,0,1,2:T(8,128)(2,1)}, u32[]{:S(2)}, u32[]{:S(2)}) collective-permute-start(bf16[2,2,2,64,1024]{4,3,0,1,2:T(8,128)(2,1)} %bitcast.133), channel_id=1, source_target_pairs={{0,1},{1,0},{2,3},{3,2},{4,5},{5,4},{6,7},{7,6},{8,9},{9,8},{10,11... | collective-permute-start | bytes 3145736 | tf_op jit(solution)/shard_map/ppermute | solution.py:305
  226.9 10.0 %copy-start.13 = (bf16[64,1024]{1,0:T(8,128)(2,1)S(1)}, bf16[64,1024]{1,0:T(8,128)(2,1)}, u32[]{:S(2)}) copy-start(bf16[64,1024]{1,0:T(8,128)(2,1)} %pad_maximum_fusion.10) | copy-start | bytes 393220
  231.3 12.1 %all-to-all-start.2 = ((bf16[16,2,2048]{2,1,0:T(2,128)(2,1)}), bf16[16,2,2048]{2,1,0:T(2,128)(2,1)S(1)}, u32[]{:S(2)}, u32[]{:S(2)}) async-start(bf16[16,2,2048]{2,1,0:T(2,128)(2,1)} %reshape.225), calls=%async_computation.2 | async-start | bytes 262144 | tf_op jit(solution)/shard_map/all_to_all | solution.py:427
  234.9 11.1 %collective-permute-start.13 = (bf16[2,64,1024]{2,1,0:T(8,128)(2,1)}, bf16[2,64,1024]{2,1,0:T(8,128)(2,1)}, u32[]{:S(2)}, u32[]{:S(2)}) collective-permute-start(bf16[2,64,1024]{2,1,0:T(8,128)(2,1)} %dynamic-slice_bitcast_fusion.3), channel_id=1, source_target_pairs={{0,4},{1,5},{2,6},{3,7},{4,0},{5,1},{6,2},{7,3},{8,12},{9,13},{10,... | collective-permute-start | bytes 786440 | tf_op jit(solution)/shard_map/ppermute | solution.py:305
  247.7 3.6 %copy-start.10 = (bf16[256,1024]{1,0:T(8,128)(2,1)S(1)}, bf16[256,1024]{1,0:T(8,128)(2,1)}, u32[]{:S(2)}) copy-start(bf16[256,1024]{1,0:T(8,128)(2,1)} %copy-done.9) | copy-start | bytes 1572868
  249.9 15.0 %collective-permute-start.16 = (bf16[2,2,64,1024]{3,2,0,1:T(8,128)(2,1)}, bf16[2,2,64,1024]{3,2,0,1:T(8,128)(2,1)}, u32[]{:S(2)}, u32[]{:S(2)}) collective-permute-start(bf16[2,2,64,1024]{3,2,0,1:T(8,128)(2,1)} %dynamic-slice_bitcast_fusion), channel_id=1, source_target_pairs={{0,2},{1,3},{2,0},{3,1},{4,6},{5,7},{6,4},{7,5},{8,10},{9,11},{10,... | collective-permute-start | bytes 1572872 | tf_op jit(solution)/shard_map/ppermute | solution.py:305
  254.4 10.6 %copy-start.4 = (bf16[2,2,2,64,1024]{4,3,0,1,2:T(8,128)(2,1)S(1)}, bf16[2,2,2,64,1024]{4,3,0,1,2:T(8,128)(2,1)}, u32[]{:S(2)}) copy-start(bf16[2,2,2,64,1024]{4,3,0,1,2:T(8,128)(2,1)} %copy-done.3) | copy-start | bytes 3145732
  256.5 10.6 %copy-start.18 = (bf16[64,512]{1,0:T(8,128)(2,1)S(1)}, bf16[64,512]{1,0:T(8,128)(2,1)}, u32[]{:S(2)}) copy-start(bf16[64,512]{1,0:T(8,128)(2,1)} %get-tuple-element.209) | copy-start | bytes 196612
  256.5 10.6 %copy-start.19 = (bf16[64,512]{1,0:T(8,128)(2,1)S(1)}, bf16[64,512]{1,0:T(8,128)(2,1)}, u32[]{:S(2)}) copy-start(bf16[64,512]{1,0:T(8,128)(2,1)} %get-tuple-element.211) | copy-start | bytes 196612
  256.5 11.3 %copy-start.15 = (bf16[2,64,1024]{2,1,0:T(8,128)(2,1)S(1)}, bf16[2,64,1024]{2,1,0:T(8,128)(2,1)}, u32[]{:S(2)}) copy-start(bf16[2,64,1024]{2,1,0:T(8,128)(2,1)} %copy-done.14) | copy-start | bytes 786436
  256.5 8.4 %collective-permute-start.15 = (bf16[64,1024]{1,0:T(8,128)(2,1)S(1)}, bf16[64,1024]{1,0:T(8,128)(2,1)S(1)}, u32[]{:S(2)}, u32[]{:S(2)}) collective-permute-start(bf16[64,1024]{1,0:T(8,128)(2,1)S(1)} %dynamic-slice_bitcast_fusion.5), channel_id=1, source_target_pairs={{0,8},{1,9},{2,10},{3,11},{4,12},{5,13},{6,14},{7,15},{8,0},{9,1},... | collective-permute-start | bytes 393224 | tf_op jit(solution)/shard_map/ppermute | solution.py:305
  267.1 8.1 %collective-permute-start.17 = (bf16[2,64,1024]{2,1,0:T(8,128)(2,1)S(1)}, bf16[2,64,1024]{2,1,0:T(8,128)(2,1)S(1)}, u32[]{:S(2)}, u32[]{:S(2)}) collective-permute-start(bf16[2,64,1024]{2,1,0:T(8,128)(2,1)S(1)} %dynamic-slice_bitcast_fusion.2), channel_id=1, source_target_pairs={{0,4},{1,5},{2,6},{3,7},{4,0},{5,1},{6,2},{7,3},{8,12},{9,13},{10,... | collective-permute-start | bytes 786440 | tf_op jit(solution)/shard_map/ppermute | solution.py:305
  276.2 8.1 %collective-permute-start.18 = (bf16[64,1024]{1,0:T(8,128)(2,1)S(1)}, bf16[64,1024]{1,0:T(8,128)(2,1)S(1)}, u32[]{:S(2)}, u32[]{:S(2)}) collective-permute-start(bf16[64,1024]{1,0:T(8,128)(2,1)S(1)} %dynamic-slice_bitcast_fusion.4), channel_id=1, source_target_pairs={{0,8},{1,9},{2,10},{3,11},{4,12},{5,13},{6,14},{7,15},{8,0},{9,1},... | collective-permute-start | bytes 393224 | tf_op jit(solution)/shard_map/ppermute | solution.py:305
  (14 other events, 25.5 us)

commit v4 on v3

--- a/solution.py
+++ b/solution.py
@@ -68,11 +68,21 @@
     return ref[:, side].reshape(CHUNK, LANES)
 
 
-def pair_dot(ref, x_ref):
+def sides(ref):
+    return load(ref, 0), load(ref, 1)
+
+
+def halo_sides(near_ref, far_ref):
+    lower = pl.program_id(0) == 0
+    return (
+        jnp.where(lower, load(far_ref, 0), load(near_ref, 1)),
+        jnp.where(lower, load(near_ref, 0), load(far_ref, 1)),
+    )
+
+
+def pair_dot(rows, x_ref):
     mid = x_ref.shape[0] // 2
-    return jnp.concatenate(
-        [nt_dot(load(ref, 0), x_ref[:mid, :]), nt_dot(load(ref, 1), x_ref[mid:, :])], 1
-    )
+    return jnp.concatenate([nt_dot(rows[0], x_ref[:mid, :]), nt_dot(rows[1], x_ref[mid:, :])], 1)
 
 
 def fold(x):
@@ -80,7 +90,8 @@
 
 
 def stats_kernel(
-    lo_ref, hi_ref, q_ref, g_ref, ke_ref, km_ref, kh_ref, ve_ref, vm_ref, vh_ref,
+    lo_ref, hi_ref, q_ref, g_ref,
+    ke_ref, km_ref, kn_ref, kf_ref, ve_ref, vm_ref, vn_ref, vf_ref,
     out_ref, s_ref, bias_ref, bq_ref, bg_ref,
 ):
     n_query = q_ref.shape[0]
@@ -99,19 +110,19 @@
         return jnp.maximum(top, jnp.max(fold(s), axis=0))
 
     top = jnp.full((8, wide), -1e30, F32)
-    top = score(0, pair_dot(ke_ref, bq_ref), top)
+    top = score(0, pair_dot(sides(ke_ref), bq_ref), top)
     for c in range(2):
         top = score(1 + c, nt_dot(load(km_ref, c), bq_ref[...]), top)
-    top = score(3, pair_dot(kh_ref, bq_ref), top)
+    top = score(3, pair_dot(halo_sides(kn_ref, kf_ref), bq_ref), top)
     top = jnp.max(top, axis=0, keepdims=True)
 
     total = jnp.zeros((8, wide), F32)
     weighted = jnp.zeros((8, wide), F32)
     for c in range(4):
         if c == 0:
-            dp = pair_dot(ve_ref, bg_ref)
+            dp = pair_dot(sides(ve_ref), bg_ref)
         elif c == 3:
-            dp = pair_dot(vh_ref, bg_ref)
+            dp = pair_dot(halo_sides(vn_ref, vf_ref), bg_ref)
         else:
             dp = nt_dot(load(vm_ref, c - 1), bg_ref[...])
         e = jnp.exp(s_ref[c] - top)
@@ -124,8 +135,8 @@
 
 def grads_kernel(
     lo_ref, hi_ref, one_ref, two_ref, q_ref, g_ref,
-    ke_ref, km_ref, kh_ref, ve_ref, vm_ref, vh_ref,
-    ctx_ref, dq_ref, part_ref,
+    ke_ref, km_ref, kn_ref, kf_ref, ve_ref, vm_ref, vn_ref, vf_ref,
+    out_ref, part_ref,
     bias_ref, bq_ref, bg_ref, bqs_ref, bgs_ref, acc_ctx, acc_dq,
 ):
     n_query = q_ref.shape[0]
@@ -160,17 +171,17 @@
         part_ref[section, :, side, :, :, :LANES] = kp.astype(BF16).reshape(shape)
         part_ref[section, :, side, :, :, LANES:] = vp.astype(BF16).reshape(shape)
 
-    def pair(k_ref, v_ref, section, table):
-        pb, ds = soft(table, pair_dot(k_ref, bqs_ref), pair_dot(v_ref, bgs_ref))
+    def pair(k, v, section, table):
+        pb, ds = soft(table, pair_dot(k, bqs_ref), pair_dot(v, bgs_ref))
         for side, lanes in ((0, slice(0, mid)), (1, slice(mid, wide))):
-            acc_ctx[lanes, :] += tn_dot(pb[:, lanes], load(v_ref, side))
-            acc_dq[lanes, :] += tn_dot(ds[:, lanes], load(k_ref, side))
+            acc_ctx[lanes, :] += tn_dot(pb[:, lanes], v[side])
+            acc_dq[lanes, :] += tn_dot(ds[:, lanes], k[side])
             keep(
                 section, side,
                 nn_dot(ds[:, lanes], bq_ref[lanes, :]), nn_dot(pb[:, lanes], bg_ref[lanes, :]),
             )
 
-    pair(ke_ref, ve_ref, 0, 0)
+    pair(sides(ke_ref), sides(ve_ref), 0, 0)
 
     def middle(c, carry):
         k = load(km_ref, c)
@@ -182,16 +193,16 @@
         return carry
 
     lax.fori_loop(0, 2, middle, 0)
-    pair(kh_ref, vh_ref, 2, 3)
-
-    def diagonal(acc, out_ref):
+    pair(halo_sides(kn_ref, kf_ref), halo_sides(vn_ref, vf_ref), 2, 3)
+
+    def diagonal(acc, which):
         kept = jnp.where(own, acc, 0.0)
         for i in range(2):
             rows = [kept[(i * GROUP + h) * part : (i * GROUP + h + 1) * part] for h in range(GROUP)]
-            out_ref[i * part : (i + 1) * part, :] = functools.reduce(jnp.add, rows)
-
-    diagonal(acc_ctx[...], ctx_ref)
-    diagonal(acc_dq[...], dq_ref)
+            out_ref[which, i * part : (i + 1) * part, :] = functools.reduce(jnp.add, rows)
+
+    diagonal(acc_ctx[...], 0)
+    diagonal(acc_dq[...], 1)
 
 
 def attention(first_group, groups, lo, hi, stats, queries, d_context, tokens):
@@ -202,11 +213,17 @@
     rows = pl.BlockSpec((None, n_query, LANES), lambda b, g: (b, 0, first_group + g))
     table = pl.BlockSpec((None, None, 3, wide), lambda b, g: (b, first_group + g, 0, 0))
 
-    def section(first):
+    def section(first, block):
         shape = (src, 2, tok, None, W, LANES)
-        return pl.BlockSpec(shape, lambda b, g: (0, 0, 0, b, 0, first + g))
-
-    sections = [section(first_group)] * 3 + [section(width // LANES + first_group)] * 3
+        return pl.BlockSpec(shape, lambda b, g: (0, 0, 0, block(b), 0, first + g))
+
+    def sections(first):
+        far = pl.BlockSpec((src, 2, tok, W, LANES), lambda b, g: (0, 0, 0, 0, first + g))
+        return [section(first, lambda b: b)] * 2 + [section(first, lambda b: 1 - b), far]
+
+    edge, middle, ext = tokens
+    tokens = (edge, middle, edge, ext)
+    sections = sections(first_group) + sections(width // LANES + first_group)
     operand = pltpu.VMEM((wide, LANES), BF16)
     total = pltpu.VMEM((wide, LANES), F32)
     bias = pltpu.VMEM((4, CHUNK, wide), F32)
@@ -232,15 +249,15 @@
     parts = pl.BlockSpec(
         (3, src, 2, tok, None, W, 2 * LANES), lambda b, g: (0, 0, 0, 0, b, 0, g)
     )
-    partial = jax.ShapeDtypeStruct((2, n_query, groups * LANES), F32)
-    partial_spec = pl.BlockSpec((None, n_query, LANES), lambda b, g: (b, 0, g))
     return pl.pallas_call(
         grads_kernel,
         in_specs=[flat, flat, table, table, rows, rows] + sections,
-        out_specs=[partial_spec, partial_spec, parts],
+        out_specs=[
+            pl.BlockSpec((None, 2, n_query, LANES), lambda b, g: (b, 0, 0, g)),
+            parts,
+        ],
         out_shape=[
-            partial,
-            partial,
+            jax.ShapeDtypeStruct((2, 2, n_query, groups * LANES), F32),
             jax.ShapeDtypeStruct((3, src, 2, tok, 2, W, 2 * groups * LANES), BF16),
         ],
         scratch_shapes=[bias] + [operand] * 4 + [total] * 2,
@@ -252,10 +269,15 @@
     )(lo, hi, *stats, queries, d_context, *tokens, *tokens)
 
 
+def flips(n_dev, bit):
+    return [(i, i ^ (1 << bit)) for i in range(n_dev)]
+
+
 class ScatterSum:
-    def __init__(self, term, bits, order):
-        self.order = list(order)
+    def __init__(self, term, bits):
+        self.order = list(range(bits))
         self.left = list(range(bits - 1, -1, -1))
+        self.n_dev = 1 << bits
         self.block = term.reshape([2] * bits + [term.shape[0] >> bits, term.shape[1]])
 
     def send(self):
@@ -265,7 +287,7 @@
         mine = (lax.axis_index("tm") >> bit) & 1
         away = lax.dynamic_index_in_dim(self.block, 1 - mine, axis, keepdims=False)
         self.keep = lax.dynamic_index_in_dim(self.block, mine, axis, keepdims=False)
-        return away, 1 << bit
+        return away, flips(self.n_dev, bit)
 
     def receive(self, come):
         block = self.keep.astype(F32) + come.astype(F32)
@@ -275,36 +297,33 @@
 class Gather:
     def __init__(self, block, bits):
         self.block = block
+        self.n_dev = 1 << bits
         self.order = list(range(bits - 1, -1, -1))
 
     def send(self):
-        return self.block, 1 << self.order.pop(0)
+        return self.block, flips(self.n_dev, self.order.pop(0))
 
     def receive(self, come):
         self.block = jnp.concatenate([self.block, come], axis=0)
 
 
-class Swap:
-    def __init__(self, block, bit):
+class Move:
+    def __init__(self, block, perm):
         self.block = block
-        self.order = [bit]
+        self.order = [perm]
 
     def send(self):
-        return self.block, 1 << self.order.pop(0)
+        return self.block, self.order.pop(0)
 
     def receive(self, come):
         self.come = come
 
 
 def beside(moving, work, *args):
-    n_dev = lax.axis_size("tm")
     moving = [m for m in moving if m.order]
     sends = [m.send() for m in moving]
     args, aways = lax.optimization_barrier((args, [away for away, _ in sends]))
-    comes = [
-        lax.ppermute(away, "tm", [(i, i ^ step) for i in range(n_dev)])
-        for away, (_, step) in zip(aways, sends)
-    ]
+    comes = [lax.ppermute(away, "tm", perm) for away, (_, perm) in zip(aways, sends)]
     result, comes = lax.optimization_barrier((work(*args), comes))
     for m, come in zip(moving, comes):
         m.receive(come)
@@ -323,36 +342,38 @@
     me = lax.axis_index("tm")
     upper_half = me >= src
     spot = me % src
-
     fence = lax.optimization_barrier
+
+    owner_one = [(s, 2 * s) for s in range(src)] + [(src + s, 2 * s + 1) for s in range(src)]
+    owner_two = [(s, 2 * s + 1) for s in range(src)] + [(src + s, 2 * s) for s in range(src)]
     valid_col = gaze_valid.astype(F32)[:, None]
     masked_grad = (cotangent.astype(F32) * valid_col).astype(BF16)
-    far = bits - 1
-    gather = Gather(masked_grad, bits)
-    swap_q, swap_o = Swap(queries, far), Swap(window_offset, far)
+    note = jnp.zeros((W, width), BF16).at[0, :n_query].set(window_offset.astype(BF16))
+    letter = jnp.concatenate([queries, masked_grad, note], axis=0)
+    one = lax.ppermute(letter, "tm", [(b, a) for a, b in owner_one])
+    two = lax.ppermute(letter, "tm", [(b, a) for a, b in owner_two])
 
     def frames(exo, *cuts):
-        by_block = exo.reshape(2, src, n_query, tok, width)
-        runs = jnp.stack([by_block[:, :, cut : cut + W] for cut in cuts], axis=2)
-        return runs.transpose(1, 2, 4, 0, 3, 5)
+        by_block = exo.reshape(src, 2, n_query, tok, width)
+        runs = jnp.stack([by_block[:, :, cut : cut + W] for cut in cuts], axis=1)
+        return runs.transpose(0, 1, 4, 2, 3, 5)
 
     later = fence(exo_tokens)
-    outer = beside(
-        [gather, swap_q, swap_o], lambda exo: frames(exo, 0, n_query - W), exo_tokens
-    )
+    outer = frames(exo_tokens, 0, n_query - W)
     inner = frames(later, W, 2 * W)
     halves = [list(range(src)), list(range(src, n_dev))]
     edge = lax.all_to_all(outer, "tm", 0, 0, axis_index_groups=halves, tiled=True)
-
-    def both(own, other):
-        return jnp.where(upper_half, jnp.stack([other, own]), jnp.stack([own, other]))
-
-    q_pair = both(queries, swap_q.come)
-    d_context = nt_dot(gather.block, out_weight).astype(BF16)
-    g_pair = both(d_context[:n_query], d_context[n_query:])
-    offsets = both(window_offset, swap_o.come)
+    weights = jnp.concatenate([key_weight, value_weight], axis=1)
+    edge, inner, weights = fence((edge, inner, weights))
+    middle = lax.all_to_all(inner, "tm", 0, 0, axis_index_groups=halves, tiled=True)
+
+    pair = jnp.where(upper_half, jnp.stack([two, one]), jnp.stack([one, two]))
+    q_pair = pair[:, :n_query]
+    g_pair = nt_dot(pair[:, n_query : 2 * n_query].reshape(-1, width), out_weight)
+    g_pair = g_pair.astype(BF16).reshape(q_pair.shape)
+    offsets = pair[:, 2 * n_query, :n_query].astype(jnp.int32)
     at = jnp.arange(n_query, dtype=jnp.int32)
-    first = (spot + jnp.array([0, src], jnp.int32))[:, None] * n_query
+    first = (2 * spot + jnp.arange(2, dtype=jnp.int32))[:, None] * n_query
     lower = jnp.maximum(at - W + offsets, -first)
     upper = jnp.minimum(at + offsets, total - 1 - first)
 
@@ -360,27 +381,23 @@
         return jnp.tile(x.reshape(2, 2, 1, n_query // 2), (1, 1, GROUP, 1)).reshape(2, 1, -1)
 
     lo, hi = lanes(lower), lanes(upper)
-    weights = jnp.concatenate([key_weight, value_weight], axis=1)
-    edge, inner, q_pair, g_pair, lo, hi, weights = fence(
-        (edge, inner, q_pair, g_pair, lo, hi, weights)
-    )
 
     def project(x):
         flat = nn_dot(x.reshape(-1, width), weights).astype(BF16)
         return flat.reshape(x.shape[:-1] + (2 * width,))
 
-    low = jnp.where(spot == src - 1, jnp.flip(edge[:, 1], 2), edge[:, 1])
-    high = jnp.where(spot == 0, jnp.flip(edge[:, 0], 2), edge[:, 0])
-    low, high, inner = fence((low, high, inner))
-    ring = [(i, i // src * src + (i + 1) % src) for i in range(n_dev)]
-    low = lax.ppermute(low, "tm", ring)
-    high = lax.ppermute(high, "tm", [(target, source) for source, target in ring])
-    middle = lax.all_to_all(inner, "tm", 0, 0, axis_index_groups=halves, tiled=True)
-    edge_kv, low, high = fence((project(edge), low, high))
-    halo = jnp.stack([low, high], axis=1)
-    halo_kv, middle = fence((project(halo), middle))
-    middle_kv = beside([gather], project, middle)
-    tokens = (edge_kv, middle_kv, halo_kv)
+    edge_kv = project(edge)
+    up = [(i, i + 1) for i in range(n_dev - 1) if (i + 1) % src]
+    low = Move(edge[:, 1, :, 1], up)
+    high = Move(edge[:, 0, :, 0], [(target, source) for source, target in up])
+    gather = Gather(masked_grad, bits)
+    middle, edge_kv, q_pair, g_pair, lo, hi, low.block, high.block = fence(
+        (middle, edge_kv, q_pair, g_pair, lo, hi, low.block, high.block)
+    )
+    middle_kv = beside([low, high, gather], project, middle)
+    ext = jnp.stack([low.come, high.come], axis=1)
+    ext_kv = beside([gather], project, ext)
+    tokens = (edge_kv, middle_kv, ext_kv)
 
     groups = width // LANES // CALLS
     stats = beside(
@@ -388,38 +405,42 @@
         functools.partial(attention, 0, width // LANES, lo, hi, None),
         q_pair, g_pair, tokens,
     )
-    swap = Swap(stats, far)
-    sources = beside(
-        [gather, swap],
-        lambda *x: jnp.concatenate([y.reshape(-1, width) for y in x], axis=0),
-        edge, middle, halo,
-    )
-
-    def own_part(x):
-        return jnp.where(upper_half, x[1], x[0])
-
-    def other_part(x):
-        return jnp.where(upper_half, x[0], x[1])
+    swap = Move(stats, flips(n_dev, bits - 1))
+
+    def all_sources(edge, middle, ext):
+        below = jnp.stack([ext[:, 0], edge[:, 1, :, 0]], axis=2)
+        above = jnp.stack([edge[:, 0, :, 1], ext[:, 1]], axis=2)
+        halo = jnp.stack([below, above], axis=1)
+        return jnp.concatenate([x.reshape(-1, width) for x in (edge, middle, halo)], axis=0)
+
+    sources = beside([gather, swap], all_sources, edge, middle, ext)
 
     moving = [gather]
-    owns, trades, shares = [], [], []
+    trades, shares = [], []
     for call in range(CALLS):
         work = functools.partial(attention, call * groups, groups, lo, hi, (swap.block, swap.come))
-        context, d_query, grads = beside(moving, work, q_pair, g_pair, tokens)
-        owns.append(jnp.stack([own_part(context), own_part(d_query)]))
-        trades.append(Swap(jnp.stack([other_part(context), other_part(d_query)]), far))
-        moving.append(trades[-1])
+        partial, grads = beside(moving, work, q_pair, g_pair, tokens)
+        half = upper_half.astype(jnp.int32)
+        trade = [
+            Move(lax.dynamic_index_in_dim(partial, half, 0, keepdims=False), owner_one),
+            Move(lax.dynamic_index_in_dim(partial, 1 - half, 0, keepdims=False), owner_two),
+        ]
+        trades.append(trade)
+        moving += trade
         term = beside(
             moving,
             lambda g: tn_dot(sources, g.reshape(sources.shape[0], -1)).astype(BF16),
             grads,
         )
-        shares.append(ScatterSum(term, bits, range(bits)))
+        shares.append(ScatterSum(term, bits))
         moving.append(shares[-1])
 
-    pairs = [own + trade.come for own, trade in zip(owns, trades)]
-    context = jnp.concatenate([x[0] for x in pairs], axis=1).astype(BF16)
-    d_query = jnp.concatenate([x[1] for x in pairs], axis=1).astype(BF16)
+    def assemble(*parts):
+        sums = [(a + b).astype(BF16) for a, b in zip(parts[::2], parts[1::2])]
+        return jnp.concatenate(sums, axis=2)
+
+    own = beside(moving, assemble, *[move.come for trade in trades for move in trade])
+    context, d_query = own[0], own[1]
 
     def finish(context):
         attended = (nn_dot(context, out_weight) * valid_col).astype(BF16)

time: 288 us -> 297 us (1.031)
  starting transfers between devices: 45.2 us -> 56.8 us
  other arithmetic: 34.7 us -> 24.6 us
  local copies, waits for them, and re-layouts: 36.6 us -> 42.5 us
  waiting for transfers between devices: 78.4 us -> 81.6 us
  matrix products: 50.8 us -> 47.7 us
    ppermute x19 -> x21, starting transfers between devices: 32.8 us -> 42.1 us  [the longest x19 36.8 us: beside(): lax.ppermute(away, 'tm', perm)]
    select_n x7 -> x1, other arithmetic: 8.73 us -> 1.14 us  [shards(): pair = jnp.where(upper_half, jnp.stack([two, one]), jnp.stack([one, two]))]
    unnamed x60 -> x61, local copies, waits for them, and re-layouts: 9.4 us -> 13.7 us
    optimization_barrier x2 -> x1, local copies, waits for them, and re-layouts: 4.43 us -> 0.24 us  [beside(): args, aways = lax.optimization_barrier((args, [away for away, _ in sends]))]
    dot_general x4, matrix products: 25.8 us -> 22.1 us  [nn_dot(): return jnp.dot(a, b, preferred_element_type=F32)]
    all_to_all x1, waiting for transfers between devices: 13.3 us -> 16.7 us  [shards(): lax.all_to_all(outer, 'tm', 0, 0, axis_index_groups=halves, tiled=True)]
    ppermute x19 -> x21, waiting for transfers between devices: 59.7 us -> 60.4 us  [the longest x19 36.8 us: beside(): lax.ppermute(away, 'tm', perm)]
  transfers between devices with their start and end apart: 22 -> 24, of which waited for: 12 -> 12; matrix products, arithmetic and copies ran while one was open for 29% -> 27% of each run, Pallas kernels for 9% -> 9%
where the time goes in v4:
time: 297 us; the launch traced here: 296 us
  waiting for transfers between devices  81.6 us (27%)
  starting transfers between devices  56.8 us (19%)
  matrix products  47.7 us (16%)
  local copies, waits for them, and re-layouts  42.5 us (14%)
  Pallas kernels  41.1 us (14%)
  other arithmetic  24.6 us (8%)
    ppermute x19, starting transfers between devices, beside(): lax.ppermute(away, 'tm', perm)  36.8 us
    ppermute x19, waiting for transfers between devices, beside(): lax.ppermute(away, 'tm', perm)  36.8 us
    pallas_call x2, Pallas kernels, attention(): pl.pallas_call(grads_kernel, in_specs=[flat, flat, table, table, rows, ro...  28.9 us
    dot_general x3, matrix products, tn_dot(): lax.dot_general(a, b, (((0,), (0,)), ((), ())), preferred_element_type=F32)  24.1 us
    ppermute x1, waiting for transfers between devices, shards(): two = lax.ppermute(letter, 'tm', [(b, a) for a, b in owner_two])  23.6 us
    dot_general x4, matrix products, nn_dot(): return jnp.dot(a, b, preferred_element_type=F32)  22.1 us
    all_to_all x1, waiting for transfers between devices, shards(): lax.all_to_all(outer, 'tm', 0, 0, axis_index_groups=halves, tiled=True)  16.7 us
    unnamed x61, local copies, waits for them, and re-layouts  13.7 us
  transfers between devices with their start and end apart: 24, of which 12 were waited for; matrix products, arithmetic and copies ran while one was open for 27% of the time, Pallas kernels for 9%

profile of v4, /device:TPU:0, one launch (start us, length us, event | category | flops | bytes accessed | tf_op | source)
XLA Modules:
  0.0 295.7 jit_solution(5421253989989332008)
XLA Ops:
  0.6 3.6 %copy.78 = bf16[1024,2,1024]{2,0,1:T(8,128)(2,1)S(1)} copy(bf16[1024,2,1024]{2,1,0:T(2,128)(2,1)} %param.10) | data formatting | bytes 8388608 | tf_op args[0]
  6.2 5.3 %all-to-all-start = ((bf16[8,2,2,2,16,1024]{5,4,3,2,1,0:T(8,128)(2,1)}), bf16[8,2,2,2,16,1024]{5,4,3,2,1,0:T(8,128)(2,1)}, u32[]{:S(2)}, u32[]{:S(2)}) async-start(bf16[8,2,2,2,16,1024]{5,4,3,2,1,0:T(8,128)(2,1)} %copy.79), calls=%async_computation | async-start | bytes 4194304 | tf_op jit(solution)/shard_map/all_to_all | solution.py:365
  11.5 3.5 %copy.80 = bf16[1024,2,1024]{2,0,1:T(8,128)(2,1)S(1)} copy(bf16[1024,2,1024]{2,1,0:T(2,128)(2,1)} %param.10) | data formatting | bytes 8388608 | tf_op jit(solution)/shard_map/optimization_barrier | solution.py:361
  20.6 16.7 %all-to-all-done = bf16[8,2,2,2,16,1024]{5,4,3,2,1,0:T(8,128)(2,1)} async-done(((bf16[8,2,2,2,16,1024]{5,4,3,2,1,0:T(8,128)(2,1)}), bf16[8,2,2,2,16,1024]{5,4,3,2,1,0:T(8,128)(2,1)}, u32[]{:S(2)}, u32[]{:S(2)}) %all-to-all-start) | async-done | bytes 2097184 | tf_op jit(solution)/shard_map/all_to_all | solution.py:365
  37.3 3.3 %copy.81 = bf16[8,2,2,2,16,1024]{5,4,3,2,1,0:T(8,128)(2,1)} copy(bf16[8,2,2,2,16,1024]{5,4,3,0,2,1:T(8,128)(2,1)} %maximum_bitcast_fusion.1) | data formatting | bytes 4194304 | tf_op jit(solution)/shard_map/optimization_barrier | solution.py:367
  40.6 4.5 %all-to-all-start.1 = ((bf16[8,2,2,2,16,1024]{5,4,3,2,1,0:T(8,128)(2,1)}), bf16[8,2,2,2,16,1024]{5,4,3,2,1,0:T(8,128)(2,1)}, u32[]{:S(2)}, u32[]{:S(2)}) async-start(bf16[8,2,2,2,16,1024]{5,4,3,2,1,0:T(8,128)(2,1)} %copy.81), calls=%async_computation.1 | async-start | bytes 4194304 | tf_op jit(solution)/shard_map/all_to_all | solution.py:368
  46.6 4.6 %collective-permute-start = (bf16[144,1024]{1,0:T(8,128)(2,1)S(1)}, bf16[144,1024]{1,0:T(8,128)(2,1)S(1)}, u32[]{:S(2)}, u32[]{:S(2)}) collective-permute-start(bf16[144,1024]{1,0:T(8,128)(2,1)S(1)} %fusion.8), channel_id=1, source_target_pairs={{1,0},{3,1},{5,2},{7,3},{9,4},{11,5},{13,6},{15,7},{0,8},{2,9},{4,... | collective-permute-start | bytes 884744 | tf_op jit(solution)/shard_map/ppermute | solution.py:354
  51.3 23.6 %collective-permute-done = bf16[144,1024]{1,0:T(8,128)(2,1)S(1)} collective-permute-done((bf16[144,1024]{1,0:T(8,128)(2,1)S(1)}, bf16[144,1024]{1,0:T(8,128)(2,1)S(1)}, u32[]{:S(2)}, u32[]{:S(2)}) %collective-permute-start) | collective-permute-done | bytes 294944 | tf_op jit(solution)/shard_map/ppermute | solution.py:354
  81.9 7.7 %convolution_convert_fusion.1 = bf16[1024,2048]{1,0:T(8,128)(2,1)} fusion(bf16[1024,1024]{1,0:T(8,128)(2,1)} %bitcast.8, bf16[1024,2048]{1,0:T(8,128)(2,1)S(1)} %copy-done.3), kind=kOutput, calls=%fused_computation.3 | convolution fusion | flops 4297064448 | bytes 10485760 | tf_op jit(solution)/shard_map/dot_general | solution.py:30
  89.6 3.4 %collective-permute-start.4 = (bf16[64,1024]{1,0:T(8,128)(2,1)S(1)}, bf16[64,1024]{1,0:T(8,128)(2,1)S(1)}, u32[]{:S(2)}, u32[]{:S(2)}) collective-permute-start(bf16[64,1024]{1,0:T(8,128)(2,1)S(1)} %get-tuple-element.117), channel_id=1, source_target_pairs={{0,8},{1,9},{2,10},{3,11},{4,12},{5,13},{6,14},{7,15},{8,0},{9,1},... | collective-permute-start | bytes 393224 | tf_op jit(solution)/shard_map/ppermute | solution.py:326
  93.0 8.5 %collective-permute-start.2 = (bf16[8,2,16,1024]{3,2,1,0:T(8,128)(2,1)S(1)}, bf16[8,2,16,1024]{3,2,1,0:T(8,128)(2,1)S(1)}, u32[]{:S(2)}, u32[]{:S(2)}) collective-permute-start(bf16[8,2,16,1024]{3,2,1,0:T(8,128)(2,1)S(1)} %get-tuple-element.115), channel_id=1, source_target_pairs={{0,1},{1,2},{2,3},{3,4},{4,5},{5,6},{6,7},{8,9},{9,10},{10,11},{11... | collective-permute-start | bytes 1572872 | tf_op jit(solution)/shard_map/ppermute | solution.py:326
  103.0 9.5 %convolution_convert_fusion = bf16[1024,2048]{1,0:T(8,128)(2,1)} fusion(bf16[1024,1024]{1,0:T(8,128)(2,1)} %bitcast.17, bf16[1024,2048]{1,0:T(8,128)(2,1)} %pad_maximum_fusion.1), kind=kOutput, calls=%fused_computation.2 | convolution fusion | flops 4297064448 | bytes 10485760 | tf_op jit(solution)/shard_map/dot_general | solution.py:30
  112.6 3.8 %collective-permute-start.5 = (bf16[128,1024]{1,0:T(8,128)(2,1)S(1)}, bf16[128,1024]{1,0:T(8,128)(2,1)S(1)}, u32[]{:S(2)}, u32[]{:S(2)}) collective-permute-start(bf16[128,1024]{1,0:T(8,128)(2,1)S(1)} %pad_maximum_fusion.6), channel_id=1, source_target_pairs={{0,4},{1,5},{2,6},{3,7},{4,0},{5,1},{6,2},{7,3},{8,12},{9,13},{10,... | collective-permute-start | bytes 786440 | tf_op jit(solution)/shard_map/ppermute | solution.py:326
  116.4 3.8 %convolution_convert_fusion.2 = bf16[512,2048]{1,0:T(8,128)(2,1)} fusion(bf16[512,1024]{1,0:T(8,128)(2,1)S(1)} %bitcast.189, bf16[1024,2048]{1,0:T(8,128)(2,1)S(1)} %copy-done.4), kind=kOutput, calls=%fused_computation.4 | convolution fusion | flops 2148532224 | bytes 7340032 | tf_op jit(solution)/shard_map/dot_general | solution.py:30
  120.1 3.4 %collective-permute-done.5 = bf16[128,1024]{1,0:T(8,128)(2,1)S(1)} collective-permute-done((bf16[128,1024]{1,0:T(8,128)(2,1)S(1)}, bf16[128,1024]{1,0:T(8,128)(2,1)S(1)}, u32[]{:S(2)}, u32[]{:S(2)}) %collective-permute-start.5) | collective-permute-done | bytes 262176 | tf_op jit(solution)/shard_map/ppermute | solution.py:326
  124.4 12.1 %softmax_stats.1.one_ref = f32[2,4,3,256]{3,2,1,0:T(4,128)} custom-call(s32[2,1,256]{2,1,0:T(1,128)} %tile.15.lo_ref, s32[2,1,256]{2,1,0:T(1,128)} %tile.17.hi_ref, bf16[2,64,1024]{2,1,0:T(8,128)(2,1)} %get-tuple-element.159.q_ref, bf16[2,64,1024]{2,1,0:T(8,128)(2,1)} %bitcast.186, bf16[8,2,2,2,16,2048]{5,4,3,2,1,0:T(8,128)(2,1)} %bitcast.159, ...), custom_call_target="tpu_custom_call" | custom-call | flops 2147483648 | bytes 12582912 | tf_op jit(solution)/shard_map/softmax_stats/pallas_call | solution.py:236
  142.0 5.5 %pad_maximum_fusion = bf16[3072,1024]{1,0:T(8,128)(2,1)} fusion(bf16[1024,1024]{1,0:T(8,128)(2,1)S(1)} %bitcast.185, bf16[1024,1024]{1,0:T(8,128)(2,1)} %bitcast.24, bf16[1024,1024]{1,0:T(8,128)(2,1)} %bitcast.23), kind=kLoop, calls=%fused_computation | loop fusion | flops 18874368 | bytes 12582912 | tf_op jit(solution)/shard_map/concatenate | solution.py:414
  148.1 14.5 %banded_grads.2 = (f32[2,2,64,512]{3,2,1,0:T(8,128)}, bf16[3,8,2,2,2,16,1024]{6,5,4,3,2,1,0:T(8,128)(2,1)}) custom-call(s32[2,1,256]{2,1,0:T(1,128)} %tile.15.lo_ref, s32[2,1,256]{2,1,0:T(1,128)} %tile.17.hi_ref, f32[2,4,3,256]{3,2,1,0:T(4,128)} %softmax_stats.1.one_ref, f32[2,4,3,256]{3,2,1,0:T(4,128)} %copy-done.21, ...), custom_call_target="tpu_custom_call" | custom-call | flops 3221225472 | bytes 12582912 | tf_op jit(solution)/shard_map/banded_grads/pallas_call | solution.py:252
  166.4 10.7 %convolution_convert_fusion.4 = bf16[1024,1024]{1,0:T(8,128)(2,1)S(1)} fusion(bf16[3072,1024]{1,0:T(8,128)(2,1)} %pad_maximum_fusion, bf16[3072,1024]{1,0:T(8,128)(2,1)} %bitcast.208), kind=kOutput, calls=%fused_computation.13 | convolution fusion | flops 6443499520 | bytes 14680064 | tf_op jit(solution)/shard_map/dot_general | solution.py:22
  177.0 4.0 %collective-permute-done.10 = f32[2,64,512]{2,1,0:T(8,128)S(1)} collective-permute-done((f32[2,64,512]{2,1,0:T(8,128)S(1)}, f32[2,64,512]{2,1,0:T(8,128)S(1)}, u32[]{:S(2)}, u32[]{:S(2)}) %collective-permute-start.10) | collective-permute-done | bytes 262176 | tf_op jit(solution)/shard_map/ppermute | solution.py:326
  182.8 14.5 %banded_grads.3 = (f32[2,2,64,512]{3,2,1,0:T(8,128)}, bf16[3,8,2,2,2,16,1024]{6,5,4,3,2,1,0:T(8,128)(2,1)}) custom-call(s32[2,1,256]{2,1,0:T(1,128)} %tile.15.lo_ref, s32[2,1,256]{2,1,0:T(1,128)} %tile.17.hi_ref, f32[2,4,3,256]{3,2,1,0:T(4,128)} %softmax_stats.1.one_ref, f32[2,4,3,256]{3,2,1,0:T(4,128)} %copy-done.21, ...), custom_call_target="tpu_custom_call" | custom-call | flops 3221225472 | bytes 12582912 | tf_op jit(solution)/shard_map/banded_grads/pallas_call | solution.py:252
  206.2 10.7 %convolution_convert_fusion.3 = bf16[1024,1024]{1,0:T(8,128)(2,1)S(1)} fusion(bf16[3072,1024]{1,0:T(8,128)(2,1)} %pad_maximum_fusion, bf16[3072,1024]{1,0:T(8,128)(2,1)} %bitcast.207), kind=kOutput, calls=%fused_computation.12 | convolution fusion | flops 6443499520 | bytes 14680064 | tf_op jit(solution)/shard_map/dot_general | solution.py:22
  217.7 5.6 %collective-permute-done.12 = bf16[2,2,64,1024]{3,2,0,1:T(8,128)(2,1)S(1)} collective-permute-done((bf16[2,2,64,1024]{3,2,0,1:T(8,128)(2,1)S(1)}, bf16[2,2,64,1024]{3,2,0,1:T(8,128)(2,1)S(1)}, u32[]{:S(2)}, u32[]{:S(2)}) %collective-permute-start.12) | collective-permute-done | bytes 524320 | tf_op jit(solution)/shard_map/ppermute | solution.py:326
  226.3 3.0 %collective-permute-start.16 = (bf16[2,2,2,64,1024]{4,3,0,1,2:T(8,128)(2,1)}, bf16[2,2,2,64,1024]{4,3,0,1,2:T(8,128)(2,1)}, u32[]{:S(2)}, u32[]{:S(2)}) collective-permute-start(bf16[2,2,2,64,1024]{4,3,0,1,2:T(8,128)(2,1)} %bitcast.149), channel_id=1, source_target_pairs={{0,1},{1,0},{2,3},{3,2},{4,5},{5,4},{6,7},{7,6},{8,9},{9,8},{10,11... | collective-permute-start | bytes 3145736 | tf_op jit(solution)/shard_map/ppermute | solution.py:326
  230.7 4.0 %collective-permute-start.15 = (bf16[2,64,1024]{2,1,0:T(8,128)(2,1)}, bf16[2,64,1024]{2,1,0:T(8,128)(2,1)S(1)}, u32[]{:S(2)}, u32[]{:S(2)}) collective-permute-start(bf16[2,64,1024]{2,1,0:T(8,128)(2,1)} %dynamic-slice_bitcast_fusion.3), channel_id=1, source_target_pairs={{0,4},{1,5},{2,6},{3,7},{4,0},{5,1},{6,2},{7,3},{8,12},{9,13},{10,... | collective-permute-start | bytes 786440 | tf_op jit(solution)/shard_map/ppermute | solution.py:326
  236.9 5.0 %collective-permute-done.15 = bf16[2,64,1024]{2,1,0:T(8,128)(2,1)S(1)} collective-permute-done((bf16[2,64,1024]{2,1,0:T(8,128)(2,1)}, bf16[2,64,1024]{2,1,0:T(8,128)(2,1)S(1)}, u32[]{:S(2)}, u32[]{:S(2)}) %collective-permute-start.15) | collective-permute-done | bytes 262176 | tf_op jit(solution)/shard_map/ppermute | solution.py:326
  254.6 4.9 %all-to-all-start.2 = ((bf16[16,2,2048]{2,1,0:T(2,128)(2,1)}), bf16[16,2,2048]{2,1,0:T(2,128)(2,1)S(1)}, u32[]{:S(2)}, u32[]{:S(2)}) async-start(bf16[16,2,2048]{2,1,0:T(2,128)(2,1)} %reshape.234), calls=%async_computation.2 | async-start | bytes 262144 | tf_op jit(solution)/shard_map/all_to_all | solution.py:448
  259.5 2.9 collective-permute-start.17
  263.6 4.4 %all-to-all-done.2 = bf16[16,2,2048]{2,1,0:T(2,128)(2,1)S(1)} async-done(((bf16[16,2,2048]{2,1,0:T(2,128)(2,1)}), bf16[16,2,2048]{2,1,0:T(2,128)(2,1)S(1)}, u32[]{:S(2)}, u32[]{:S(2)}) %all-to-all-start.2) | async-done | bytes 131104 | tf_op jit(solution)/shard_map/all_to_all | solution.py:448
  268.2 3.8 %collective-permute-done.17 = bf16[64,1024]{1,0:T(8,128)(2,1)} collective-permute-done((bf16[64,1024]{1,0:T(8,128)(2,1)}, bf16[64,1024]{1,0:T(8,128)(2,1)}, u32[]{:S(2)}, u32[]{:S(2)}) %collective-permute-start.17) | collective-permute-done | bytes 131104 | tf_op jit(solution)/shard_map/ppermute | solution.py:326
  280.6 5.2 %collective-permute-done.19 = bf16[2,64,1024]{2,1,0:T(8,128)(2,1)S(1)} collective-permute-done((bf16[2,64,1024]{2,1,0:T(8,128)(2,1)}, bf16[2,64,1024]{2,1,0:T(8,128)(2,1)S(1)}, u32[]{:S(2)}, u32[]{:S(2)}) %collective-permute-start.19) | collective-permute-done | bytes 262176 | tf_op jit(solution)/shard_map/ppermute | solution.py:326
  286.9 6.9 %collective-permute-done.20 = bf16[64,1024]{1,0:T(8,128)(2,1)S(1)} collective-permute-done((bf16[64,1024]{1,0:T(8,128)(2,1)S(1)}, bf16[64,1024]{1,0:T(8,128)(2,1)S(1)}, u32[]{:S(2)}, u32[]{:S(2)}) %collective-permute-start.20) | collective-permute-done | bytes 131104 | tf_op jit(solution)/shard_map/ppermute | solution.py:326
  (164 shorter events, 71.6 us)
Async XLA Ops:
  0.6 78.4 %copy-start = (bf16[1024,1024]{1,0:T(8,128)(2,1)S(1)}, bf16[1024,1024]{1,0:T(8,128)(2,1)}, u32[]{:S(2)}) copy-start(bf16[1024,1024]{1,0:T(8,128)(2,1)} %param.14) | copy-start | bytes 6291460
  6.2 31.1 %all-to-all-start = ((bf16[8,2,2,2,16,1024]{5,4,3,2,1,0:T(8,128)(2,1)}), bf16[8,2,2,2,16,1024]{5,4,3,2,1,0:T(8,128)(2,1)}, u32[]{:S(2)}, u32[]{:S(2)}) async-start(bf16[8,2,2,2,16,1024]{5,4,3,2,1,0:T(8,128)(2,1)} %copy.79), calls=%async_computation | async-start | bytes 4194304 | tf_op jit(solution)/shard_map/all_to_all | solution.py:365
  40.6 49.0 %all-to-all-start.1 = ((bf16[8,2,2,2,16,1024]{5,4,3,2,1,0:T(8,128)(2,1)}), bf16[8,2,2,2,16,1024]{5,4,3,2,1,0:T(8,128)(2,1)}, u32[]{:S(2)}, u32[]{:S(2)}) async-start(bf16[8,2,2,2,16,1024]{5,4,3,2,1,0:T(8,128)(2,1)} %copy.81), calls=%async_computation.1 | async-start | bytes 4194304 | tf_op jit(solution)/shard_map/all_to_all | solution.py:368
  45.9 5.4 %collective-permute-start.1 = (bf16[144,1024]{1,0:T(8,128)(2,1)S(1)}, bf16[144,1024]{1,0:T(8,128)(2,1)S(1)}, u32[]{:S(2)}, u32[]{:S(2)}) collective-permute-start(bf16[144,1024]{1,0:T(8,128)(2,1)S(1)} %fusion.8), channel_id=1, source_target_pairs={{0,0},{2,1},{4,2},{6,3},{8,4},{10,5},{12,6},{14,7},{1,8},{3,9},{5,... | collective-permute-start | bytes 884744 | tf_op jit(solution)/shard_map/ppermute | solution.py:353
  46.6 28.3 %collective-permute-start = (bf16[144,1024]{1,0:T(8,128)(2,1)S(1)}, bf16[144,1024]{1,0:T(8,128)(2,1)S(1)}, u32[]{:S(2)}, u32[]{:S(2)}) collective-permute-start(bf16[144,1024]{1,0:T(8,128)(2,1)S(1)} %fusion.8), channel_id=1, source_target_pairs={{1,0},{3,1},{5,2},{7,3},{9,4},{11,5},{13,6},{15,7},{0,8},{2,9},{4,... | collective-permute-start | bytes 884744 | tf_op jit(solution)/shard_map/ppermute | solution.py:354
  89.6 22.9 %collective-permute-start.4 = (bf16[64,1024]{1,0:T(8,128)(2,1)S(1)}, bf16[64,1024]{1,0:T(8,128)(2,1)S(1)}, u32[]{:S(2)}, u32[]{:S(2)}) collective-permute-start(bf16[64,1024]{1,0:T(8,128)(2,1)S(1)} %get-tuple-element.117), channel_id=1, source_target_pairs={{0,8},{1,9},{2,10},{3,11},{4,12},{5,13},{6,14},{7,15},{8,0},{9,1},... | collective-permute-start | bytes 393224 | tf_op jit(solution)/shard_map/ppermute | solution.py:326
  93.0 19.5 %collective-permute-start.2 = (bf16[8,2,16,1024]{3,2,1,0:T(8,128)(2,1)S(1)}, bf16[8,2,16,1024]{3,2,1,0:T(8,128)(2,1)S(1)}, u32[]{:S(2)}, u32[]{:S(2)}) collective-permute-start(bf16[8,2,16,1024]{3,2,1,0:T(8,128)(2,1)S(1)} %get-tuple-element.115), channel_id=1, source_target_pairs={{0,1},{1,2},{2,3},{3,4},{4,5},{5,6},{6,7},{8,9},{9,10},{10,11},{11... | collective-permute-start | bytes 1572872 | tf_op jit(solution)/shard_map/ppermute | solution.py:326
  101.5 11.0 %collective-permute-start.3 = (bf16[8,2,16,1024]{3,2,1,0:T(8,128)(2,1)S(1)}, bf16[8,2,16,1024]{3,2,1,0:T(8,128)(2,1)S(1)}, u32[]{:S(2)}, u32[]{:S(2)}) collective-permute-start(bf16[8,2,16,1024]{3,2,1,0:T(8,128)(2,1)S(1)} %get-tuple-element.116), channel_id=1, source_target_pairs={{1,0},{2,1},{3,2},{4,3},{5,4},{6,5},{7,6},{9,8},{10,9},{11,10},{12... | collective-permute-start | bytes 1572872 | tf_op jit(solution)/shard_map/ppermute | solution.py:326
  103.0 13.4 %copy-start.4 = (bf16[1024,2048]{1,0:T(8,128)(2,1)S(1)}, bf16[1024,2048]{1,0:T(8,128)(2,1)}, u32[]{:S(2)}) copy-start(bf16[1024,2048]{1,0:T(8,128)(2,1)} %pad_maximum_fusion.1) | copy-start | bytes 12582916
  112.5 11.1 %copy-start.10 = (bf16[64,1024]{1,0:T(8,128)(2,1)}, bf16[64,1024]{1,0:T(8,128)(2,1)S(1)}, u32[]{:S(2)}) copy-start(bf16[64,1024]{1,0:T(8,128)(2,1)S(1)} %collective-permute-done.4) | copy-start | bytes 393220
  112.6 10.9 %collective-permute-start.5 = (bf16[128,1024]{1,0:T(8,128)(2,1)S(1)}, bf16[128,1024]{1,0:T(8,128)(2,1)S(1)}, u32[]{:S(2)}, u32[]{:S(2)}) collective-permute-start(bf16[128,1024]{1,0:T(8,128)(2,1)S(1)} %pad_maximum_fusion.6), channel_id=1, source_target_pairs={{0,4},{1,5},{2,6},{3,7},{4,0},{5,1},{6,2},{7,3},{8,12},{9,13},{10,... | collective-permute-start | bytes 786440 | tf_op jit(solution)/shard_map/ppermute | solution.py:326
  124.4 14.3 %collective-permute-start.6 = (bf16[256,1024]{1,0:T(8,128)(2,1)}, bf16[256,1024]{1,0:T(8,128)(2,1)}, u32[]{:S(2)}, u32[]{:S(2)}) collective-permute-start(bf16[256,1024]{1,0:T(8,128)(2,1)} %pad_maximum_fusion.5), channel_id=1, source_target_pairs={{0,2},{1,3},{2,0},{3,1},{4,6},{5,7},{6,4},{7,5},{8,10},{9,11},{10,... | collective-permute-start | bytes 1572872 | tf_op jit(solution)/shard_map/ppermute | solution.py:326
  139.8 7.8 %collective-permute-start.8 = (f32[2,4,3,256]{3,2,1,0:T(4,128)S(1)}, f32[2,4,3,256]{3,2,1,0:T(4,128)S(1)}, u32[]{:S(2)}, u32[]{:S(2)}) collective-permute-start(f32[2,4,3,256]{3,2,1,0:T(4,128)S(1)} %copy-done.14), channel_id=1, source_target_pairs={{0,8},{1,9},{2,10},{3,11},{4,12},{5,13},{6,14},{7,15},{8,0},{9,1},... | collective-permute-start | bytes 73736 | tf_op jit(solution)/shard_map/ppermute | solution.py:326
  141.2 6.3 %collective-permute-start.7 = (bf16[512,1024]{1,0:T(8,128)(2,1)S(1)}, bf16[512,1024]{1,0:T(8,128)(2,1)}, u32[]{:S(2)}, u32[]{:S(2)}) collective-permute-start(bf16[512,1024]{1,0:T(8,128)(2,1)S(1)} %pad_maximum_fusion.4), channel_id=1, source_target_pairs={{0,1},{1,0},{2,3},{3,2},{4,5},{5,4},{6,7},{7,6},{8,9},{9,8},{10,11... | collective-permute-start | bytes 3145736 | tf_op jit(solution)/shard_map/ppermute | solution.py:326
  163.7 13.4 %collective-permute-start.9 = (f32[2,64,512]{2,1,0:T(8,128)S(1)}, f32[2,64,512]{2,1,0:T(8,128)S(1)}, u32[]{:S(2)}, u32[]{:S(2)}) collective-permute-start(f32[2,64,512]{2,1,0:T(8,128)S(1)} %get-tuple-element.154), channel_id=1, source_target_pairs={{0,0},{1,2},{2,4},{3,6},{4,8},{5,10},{6,12},{7,14},{8,1},{9,3},{10... | collective-permute-start | bytes 786440 | tf_op jit(solution)/shard_map/ppermute | solution.py:326
  164.4 16.7 %collective-permute-start.10 = (f32[2,64,512]{2,1,0:T(8,128)S(1)}, f32[2,64,512]{2,1,0:T(8,128)S(1)}, u32[]{:S(2)}, u32[]{:S(2)}) collective-permute-start(f32[2,64,512]{2,1,0:T(8,128)S(1)} %get-tuple-element.155), channel_id=1, source_target_pairs={{0,1},{1,3},{2,5},{3,7},{4,9},{5,11},{6,13},{7,15},{8,0},{9,2},{10... | collective-permute-start | bytes 786440 | tf_op jit(solution)/shard_map/ppermute | solution.py:326
  182.8 14.5 %collective-permute-start.11 = (bf16[2,2,2,64,1024]{4,3,0,1,2:T(8,128)(2,1)}, bf16[2,2,2,64,1024]{4,3,0,1,2:T(8,128)(2,1)}, u32[]{:S(2)}, u32[]{:S(2)}) collective-permute-start(bf16[2,2,2,64,1024]{4,3,0,1,2:T(8,128)(2,1)} %bitcast.150), channel_id=1, source_target_pairs={{0,1},{1,0},{2,3},{3,2},{4,5},{5,4},{6,7},{7,6},{8,9},{9,8},{10,11... | collective-permute-start | bytes 3145736 | tf_op jit(solution)/shard_map/ppermute | solution.py:326
  200.0 16.8 %collective-permute-start.13 = (f32[2,64,512]{2,1,0:T(8,128)S(1)}, f32[2,64,512]{2,1,0:T(8,128)S(1)}, u32[]{:S(2)}, u32[]{:S(2)}) collective-permute-start(f32[2,64,512]{2,1,0:T(8,128)S(1)} %get-tuple-element.172), channel_id=1, source_target_pairs={{0,0},{1,2},{2,4},{3,6},{4,8},{5,10},{6,12},{7,14},{8,1},{9,3},{10... | collective-permute-start | bytes 786440 | tf_op jit(solution)/shard_map/ppermute | solution.py:326
  200.7 16.9 %collective-permute-start.14 = (f32[2,64,512]{2,1,0:T(8,128)S(1)}, f32[2,64,512]{2,1,0:T(8,128)S(1)}, u32[]{:S(2)}, u32[]{:S(2)}) collective-permute-start(f32[2,64,512]{2,1,0:T(8,128)S(1)} %get-tuple-element.173), channel_id=1, source_target_pairs={{0,1},{1,3},{2,5},{3,7},{4,9},{5,11},{6,13},{7,15},{8,0},{9,2},{10... | collective-permute-start | bytes 786440 | tf_op jit(solution)/shard_map/ppermute | solution.py:326
  203.3 19.9 %collective-permute-start.12 = (bf16[2,2,64,1024]{3,2,0,1:T(8,128)(2,1)S(1)}, bf16[2,2,64,1024]{3,2,0,1:T(8,128)(2,1)S(1)}, u32[]{:S(2)}, u32[]{:S(2)}) collective-permute-start(bf16[2,2,64,1024]{3,2,0,1:T(8,128)(2,1)S(1)} %dynamic-slice_bitcast_fusion.1), channel_id=1, source_target_pairs={{0,2},{1,3},{2,0},{3,1},{4,6},{5,7},{6,4},{7,5},{8,10},{9,11},{10,... | collective-permute-start | bytes 1572872 | tf_op jit(solution)/shard_map/ppermute | solution.py:326
  216.9 6.6 %copy-start.17 = (f32[2,64,512]{2,1,0:T(8,128)}, f32[2,64,512]{2,1,0:T(8,128)S(1)}, u32[]{:S(2)}) copy-start(f32[2,64,512]{2,1,0:T(8,128)S(1)} %collective-permute-done.13) | copy-start | bytes 786436
  217.7 5.8 %copy-start.18 = (f32[2,64,512]{2,1,0:T(8,128)}, f32[2,64,512]{2,1,0:T(8,128)S(1)}, u32[]{:S(2)}) copy-start(f32[2,64,512]{2,1,0:T(8,128)S(1)} %collective-permute-done.14) | copy-start | bytes 786436
  223.5 5.8 %copy-start.11 = (bf16[64,1024]{1,0:T(8,128)(2,1)S(1)}, bf16[64,1024]{1,0:T(8,128)(2,1)}, u32[]{:S(2)}) copy-start(bf16[64,1024]{1,0:T(8,128)(2,1)} %copy-done.10) | copy-start | bytes 393220
  226.3 15.6 %collective-permute-start.16 = (bf16[2,2,2,64,1024]{4,3,0,1,2:T(8,128)(2,1)}, bf16[2,2,2,64,1024]{4,3,0,1,2:T(8,128)(2,1)}, u32[]{:S(2)}, u32[]{:S(2)}) collective-permute-start(bf16[2,2,2,64,1024]{4,3,0,1,2:T(8,128)(2,1)} %bitcast.149), channel_id=1, source_target_pairs={{0,1},{1,0},{2,3},{3,2},{4,5},{5,4},{6,7},{7,6},{8,9},{9,8},{10,11... | collective-permute-start | bytes 3145736 | tf_op jit(solution)/shard_map/ppermute | solution.py:326
  230.7 11.2 %collective-permute-start.15 = (bf16[2,64,1024]{2,1,0:T(8,128)(2,1)}, bf16[2,64,1024]{2,1,0:T(8,128)(2,1)S(1)}, u32[]{:S(2)}, u32[]{:S(2)}) collective-permute-start(bf16[2,64,1024]{2,1,0:T(8,128)(2,1)} %dynamic-slice_bitcast_fusion.3), channel_id=1, source_target_pairs={{0,4},{1,5},{2,6},{3,7},{4,0},{5,1},{6,2},{7,3},{8,12},{9,13},{10,... | collective-permute-start | bytes 786440 | tf_op jit(solution)/shard_map/ppermute | solution.py:326
  247.6 24.5 %collective-permute-start.18 = (bf16[2,2,64,1024]{3,2,0,1:T(8,128)(2,1)}, bf16[2,2,64,1024]{3,2,0,1:T(8,128)(2,1)}, u32[]{:S(2)}, u32[]{:S(2)}) collective-permute-start(bf16[2,2,64,1024]{3,2,0,1:T(8,128)(2,1)} %dynamic-slice_bitcast_fusion), channel_id=1, source_target_pairs={{0,2},{1,3},{2,0},{3,1},{4,6},{5,7},{6,4},{7,5},{8,10},{9,11},{10,... | collective-permute-start | bytes 1572872 | tf_op jit(solution)/shard_map/ppermute | solution.py:326
  251.8 20.3 %copy-start.2 = (bf16[2,2,2,64,1024]{4,3,0,1,2:T(8,128)(2,1)S(1)}, bf16[2,2,2,64,1024]{4,3,0,1,2:T(8,128)(2,1)}, u32[]{:S(2)}) copy-start(bf16[2,2,2,64,1024]{4,3,0,1,2:T(8,128)(2,1)} %copy-done.1) | copy-start | bytes 3145732
  254.6 13.4 %all-to-all-start.2 = ((bf16[16,2,2048]{2,1,0:T(2,128)(2,1)}), bf16[16,2,2048]{2,1,0:T(2,128)(2,1)S(1)}, u32[]{:S(2)}, u32[]{:S(2)}) async-start(bf16[16,2,2048]{2,1,0:T(2,128)(2,1)} %reshape.234), calls=%async_computation.2 | async-start | bytes 262144 | tf_op jit(solution)/shard_map/all_to_all | solution.py:448
  259.5 12.5 %collective-permute-start.17 = (bf16[64,1024]{1,0:T(8,128)(2,1)}, bf16[64,1024]{1,0:T(8,128)(2,1)}, u32[]{:S(2)}, u32[]{:S(2)}) collective-permute-start(bf16[64,1024]{1,0:T(8,128)(2,1)} %dynamic-slice_bitcast_fusion.9), channel_id=1, source_target_pairs={{0,8},{1,9},{2,10},{3,11},{4,12},{5,13},{6,14},{7,15},{8,0},{9,1},... | collective-permute-start | bytes 393224 | tf_op jit(solution)/shard_map/ppermute | solution.py:326
  277.2 8.6 %copy-start.7 = (bf16[2,2,64,1024]{3,2,0,1:T(8,128)(2,1)S(1)}, bf16[2,2,64,1024]{3,2,0,1:T(8,128)(2,1)}, u32[]{:S(2)}) copy-start(bf16[2,2,64,1024]{3,2,0,1:T(8,128)(2,1)} %fusion.3) | copy-start | bytes 1572868
  277.7 8.0 %collective-permute-start.19 = (bf16[2,64,1024]{2,1,0:T(8,128)(2,1)}, bf16[2,64,1024]{2,1,0:T(8,128)(2,1)S(1)}, u32[]{:S(2)}, u32[]{:S(2)}) collective-permute-start(bf16[2,64,1024]{2,1,0:T(8,128)(2,1)} %dynamic-slice_bitcast_fusion.2), channel_id=1, source_target_pairs={{0,4},{1,5},{2,6},{3,7},{4,0},{5,1},{6,2},{7,3},{8,12},{9,13},{10,... | collective-permute-start | bytes 786440 | tf_op jit(solution)/shard_map/ppermute | solution.py:326
  285.9 7.9 %collective-permute-start.20 = (bf16[64,1024]{1,0:T(8,128)(2,1)S(1)}, bf16[64,1024]{1,0:T(8,128)(2,1)S(1)}, u32[]{:S(2)}, u32[]{:S(2)}) collective-permute-start(bf16[64,1024]{1,0:T(8,128)(2,1)S(1)} %dynamic-slice_bitcast_fusion.8), channel_id=1, source_target_pairs={{0,8},{1,9},{2,10},{3,11},{4,12},{5,13},{6,14},{7,15},{8,0},{9,1},... | collective-permute-start | bytes 393224 | tf_op jit(solution)/shard_map/ppermute | solution.py:326
  (16 other events, 42.6 us)

commit v5 on v4

--- a/solution.py
+++ b/solution.py
@@ -3,6 +3,7 @@
 import jax
 import jax.numpy as jnp
 from jax import lax
+from jax.experimental.layout import Layout, with_layout_constraint
 from jax.experimental import pallas as pl
 from jax.experimental.pallas import tpu as pltpu
 from jax.sharding import PartitionSpec as P
@@ -273,27 +274,6 @@
     return [(i, i ^ (1 << bit)) for i in range(n_dev)]
 
 
-class ScatterSum:
-    def __init__(self, term, bits):
-        self.order = list(range(bits))
-        self.left = list(range(bits - 1, -1, -1))
-        self.n_dev = 1 << bits
-        self.block = term.reshape([2] * bits + [term.shape[0] >> bits, term.shape[1]])
-
-    def send(self):
-        bit = self.order.pop(0)
-        axis = self.left.index(bit)
-        self.left.remove(bit)
-        mine = (lax.axis_index("tm") >> bit) & 1
-        away = lax.dynamic_index_in_dim(self.block, 1 - mine, axis, keepdims=False)
-        self.keep = lax.dynamic_index_in_dim(self.block, mine, axis, keepdims=False)
-        return away, flips(self.n_dev, bit)
-
-    def receive(self, come):
-        block = self.keep.astype(F32) + come.astype(F32)
-        self.block = block.astype(BF16) if self.left else block
-
-
 class Gather:
     def __init__(self, block, bits):
         self.block = block
@@ -301,10 +281,19 @@
         self.order = list(range(bits - 1, -1, -1))
 
     def send(self):
-        return self.block, flips(self.n_dev, self.order.pop(0))
+        self.bit = self.order.pop(0)
+        return self.block, flips(self.n_dev, self.bit)
 
     def receive(self, come):
-        self.block = jnp.concatenate([self.block, come], axis=0)
+        if self.bit == 0:
+            self.block = jnp.stack([self.block, come])
+            return
+        mine = (lax.axis_index("tm") >> self.bit) & 1
+        self.block = jnp.where(
+            mine == 0,
+            jnp.stack([self.block, come], axis=-3),
+            jnp.stack([come, self.block], axis=-3),
+        )
 
 
 class Move:
@@ -350,22 +339,29 @@
     masked_grad = (cotangent.astype(F32) * valid_col).astype(BF16)
     note = jnp.zeros((W, width), BF16).at[0, :n_query].set(window_offset.astype(BF16))
     letter = jnp.concatenate([queries, masked_grad, note], axis=0)
-    one = lax.ppermute(letter, "tm", [(b, a) for a, b in owner_one])
-    two = lax.ppermute(letter, "tm", [(b, a) for a, b in owner_two])
 
     def frames(exo, *cuts):
         by_block = exo.reshape(src, 2, n_query, tok, width)
         runs = jnp.stack([by_block[:, :, cut : cut + W] for cut in cuts], axis=1)
-        return runs.transpose(0, 1, 4, 2, 3, 5)
+        runs = runs.transpose(0, 1, 4, 2, 3, 5)
+        return with_layout_constraint(runs, Layout(tuple(range(6))))
 
     later = fence(exo_tokens)
     outer = frames(exo_tokens, 0, n_query - W)
     inner = frames(later, W, 2 * W)
     halves = [list(range(src)), list(range(src, n_dev))]
+    gather = Gather(masked_grad, bits)
     edge = lax.all_to_all(outer, "tm", 0, 0, axis_index_groups=halves, tiled=True)
+    one = lax.ppermute(letter, "tm", [(b, a) for a, b in owner_one])
+    two = lax.ppermute(letter, "tm", [(b, a) for a, b in owner_two])
+    away, perm = gather.send()
+    come = lax.ppermute(away, "tm", perm)
     weights = jnp.concatenate([key_weight, value_weight], axis=1)
-    edge, inner, weights = fence((edge, inner, weights))
+    edge, inner, weights, one, two, come = fence((edge, inner, weights, one, two, come))
+    gather.receive(come)
     middle = lax.all_to_all(inner, "tm", 0, 0, axis_index_groups=halves, tiled=True)
+    away, perm = gather.send()
+    come = lax.ppermute(away, "tm", perm)
 
     pair = jnp.where(upper_half, jnp.stack([two, one]), jnp.stack([one, two]))
     q_pair = pair[:, :n_query]
@@ -390,13 +386,13 @@
     up = [(i, i + 1) for i in range(n_dev - 1) if (i + 1) % src]
     low = Move(edge[:, 1, :, 1], up)
     high = Move(edge[:, 0, :, 0], [(target, source) for source, target in up])
-    gather = Gather(masked_grad, bits)
-    middle, edge_kv, q_pair, g_pair, lo, hi, low.block, high.block = fence(
-        (middle, edge_kv, q_pair, g_pair, lo, hi, low.block, high.block)
-    )
-    middle_kv = beside([low, high, gather], project, middle)
+    middle, come, edge_kv, q_pair, g_pair, lo, hi, low.block, high.block = fence(
+        (middle, come, edge_kv, q_pair, g_pair, lo, hi, low.block, high.block)
+    )
+    gather.receive(come)
+    middle_kv = beside([low, high], project, middle)
     ext = jnp.stack([low.come, high.come], axis=1)
-    ext_kv = beside([gather], project, ext)
+    ext_kv = project(ext)
     tokens = (edge_kv, middle_kv, ext_kv)
 
     groups = width // LANES // CALLS
@@ -414,56 +410,84 @@
         return jnp.concatenate([x.reshape(-1, width) for x in (edge, middle, halo)], axis=0)
 
     sources = beside([gather, swap], all_sources, edge, middle, ext)
-
-    moving = [gather]
-    trades, shares = [], []
-    for call in range(CALLS):
-        work = functools.partial(attention, call * groups, groups, lo, hi, (swap.block, swap.come))
-        partial, grads = beside(moving, work, q_pair, g_pair, tokens)
+    while gather.order:
+        beside([gather], lambda: ())
+
+    core = me & 1
+    chips = [[2 * k + c for k in range(src)] for c in range(2)]
+
+    def meet(term):
+        rows = term.reshape(src, 2, -1, term.shape[1])
+        away = lax.dynamic_index_in_dim(rows, 1 - core, 1, keepdims=False)
+        keep = lax.dynamic_index_in_dim(rows, core, 1, keepdims=False)
+        return Move(away, flips(n_dev, 0)), keep
+
+    def scatter(block):
+        return lax.all_to_all(block, "tm", 0, 0, axis_index_groups=chips, tiled=True)
+
+    def add(x, y):
+        return (x.astype(F32) + y.astype(F32)).astype(BF16)
+
+    def half_context(part):
         half = upper_half.astype(jnp.int32)
-        trade = [
-            Move(lax.dynamic_index_in_dim(partial, half, 0, keepdims=False), owner_one),
-            Move(lax.dynamic_index_in_dim(partial, 1 - half, 0, keepdims=False), owner_two),
+        return [
+            Move(lax.dynamic_index_in_dim(part, half, 0, keepdims=False), owner_one),
+            Move(lax.dynamic_index_in_dim(part, 1 - half, 0, keepdims=False), owner_two),
         ]
-        trades.append(trade)
-        moving += trade
-        term = beside(
-            moving,
-            lambda g: tn_dot(sources, g.reshape(sources.shape[0], -1)).astype(BF16),
-            grads,
-        )
-        shares.append(ScatterSum(term, bits))
-        moving.append(shares[-1])
+
+    def weigh(g):
+        return tn_dot(sources, g.reshape(sources.shape[0], -1)).astype(BF16)
 
     def assemble(*parts):
         sums = [(a + b).astype(BF16) for a, b in zip(parts[::2], parts[1::2])]
         return jnp.concatenate(sums, axis=2)
 
-    own = beside(moving, assemble, *[move.come for trade in trades for move in trade])
-    context, d_query = own[0], own[1]
-
-    def finish(context):
-        attended = (nn_dot(context, out_weight) * valid_col).astype(BF16)
-        columns = context.reshape(n_query, n_dev, -1).swapaxes(0, 1)
-        return attended, lax.all_to_all(columns, "tm", split_axis=0, concat_axis=0, tiled=True)
-
-    attended, columns = beside(moving, finish, context)
-    columns = columns.reshape([2] * bits + [n_query, -1])
-    for bit in range(bits):
-        axis = bits - 1 - bit
-        columns = jnp.where((me >> bit) & 1 == 1, jnp.flip(columns, axis), columns)
-    columns = columns.transpose(list(range(bits - 1, -1, -1)) + [bits, bits + 1])
-    d_out = beside(moving, lambda c: tn_dot(c.reshape(total, -1), gather.block), columns)
-    while any(m.order for m in moving):
-        beside(moving, lambda: ())
-    blocks = [s.block.reshape(s.block.shape[0], -1, 2, LANES) for s in shares]
-    return (
-        attended,
-        d_query,
-        jnp.concatenate([b[:, i, 0] for b in blocks for i in range(b.shape[1])], axis=1),
-        jnp.concatenate([b[:, i, 1] for b in blocks for i in range(b.shape[1])], axis=1),
-        d_out,
-    )
+    trades, shares, ready = [], [], None
+    for call in range(CALLS):
+        work = functools.partial(attention, call * groups, groups, lo, hi, (swap.block, swap.come))
+        if ready is not None:
+            ready, q_pair = fence((ready, q_pair))
+            share = scatter(ready)
+        partial, grads = work(q_pair, g_pair, tokens)
+        trade = half_context(partial)
+        trades += trade
+        term = beside(trade, weigh, grads)
+        if ready is not None:
+            share, term = fence((share, term))
+            shares.append(share)
+        if call < CALLS - 1:
+            away, keep = meet(term)
+            keep = beside([away], lambda x: x, keep)
+            ready = add(keep, away.come)
+
+    context, d_query = assemble(*[move.come for move in trades])
+    away, keep = meet(term)
+    partner = Move(context, flips(n_dev, 0))
+    keep, context = beside([away, partner], lambda *x: x, keep, context)
+    ready = add(keep, away.come)
+
+    columns = jnp.concatenate(
+        [x.reshape(n_query, src, -1).swapaxes(0, 1) for x in (context, partner.come)], axis=2
+    )
+    if ready.shape[1] == n_query:
+        packed = scatter(jnp.concatenate([ready, columns], axis=2))
+        share, columns = packed[:, :, : ready.shape[2]], packed[:, :, ready.shape[2] :]
+    else:
+        share, columns = scatter(ready), scatter(columns)
+    shares.append(share)
+    attended = (nn_dot(context, out_weight) * valid_col).astype(BF16)
+    columns = columns.reshape(src * n_query, -1)
+    all_grad = gather.block.reshape(2, src * n_query, width)
+    cut = columns.shape[1] // 2
+    d_out = tn_dot(columns[:, :cut], all_grad[0]) + tn_dot(columns[:, cut:], all_grad[1])
+    d_out = lax.dynamic_slice_in_dim(d_out, core * (cut // 2), cut // 2, 0)
+    sums = [jnp.sum(share.astype(F32), axis=0) for share in shares]
+
+    def heads(which):
+        at = [(2 * i + which) * LANES for i in range(groups)]
+        return jnp.concatenate([x[:, i : i + LANES] for x in sums for i in at], axis=1)
+
+    return attended, d_query, heads(0), heads(1), d_out
 
 
 def solution(mesh):

time: 297 us -> 277 us (0.933)
  local copies, waits for them, and re-layouts: 42.5 us -> 28.8 us
  waiting for transfers between devices: 81.6 us -> 73.4 us
  other arithmetic: 24.6 us -> 28.7 us
    all_to_all x1 -> x2, waiting for transfers between devices: 4.45 us -> 40.6 us  [scatter(): lax.all_to_all(block, 'tm', 0, 0, axis_index_groups=chips, tiled=True)]
    ppermute x19 -> x12, waiting for transfers between devices: 36.8 us -> 4.67 us  [beside(): lax.ppermute(away, 'tm', perm)]
    ppermute x0 -> x2, waiting for transfers between devices: none -> 28.1 us  [shards(): come = lax.ppermute(away, 'tm', perm)]
    ppermute x1, waiting for transfers between devices: 23.6 us -> 0.01 us  [shards(): two = lax.ppermute(letter, 'tm', [(b, a) for a, b in owner_two])]
    ppermute x19 -> x12, starting transfers between devices: 36.8 us -> 17.8 us  [beside(): lax.ppermute(away, 'tm', perm)]
    all_to_all x1, waiting for transfers between devices: 16.7 us -> 0.01 us  [shards(): lax.all_to_all(outer, 'tm', 0, 0, axis_index_groups=halves, tiled=True)]
    all_to_all x1, starting transfers between devices: 4.48 us -> 11.9 us  [shards(): lax.all_to_all(inner, 'tm', 0, 0, axis_index_groups=halves, tiled=True)]
    select_n x3 -> x6, other arithmetic: 0.18 us -> 7.35 us  [receive(): jnp.where(mine == 0, jnp.stack([self.block, come], axis=-3), jnp.stack([c...]
  transfers between devices with their start and end apart: 24 -> 20, of which waited for: 12 -> 6; matrix products, arithmetic and copies ran while one was open for 27% -> 27% of each run, Pallas kernels for 9% -> 4%
where the time goes in v5:
time: 277 us; the launch traced here: 276 us
  waiting for transfers between devices  73.4 us (26%)
  starting transfers between devices  54.9 us (20%)
  matrix products  47.8 us (17%)
  Pallas kernels  41.1 us (15%)
  local copies, waits for them, and re-layouts  28.8 us (10%)
  other arithmetic  28.7 us (10%)
    all_to_all x2, waiting for transfers between devices, scatter(): lax.all_to_all(block, 'tm', 0, 0, axis_index_groups=chips, tiled=True)  40.6 us
    pallas_call x2, Pallas kernels, attention(): pl.pallas_call(grads_kernel, in_specs=[flat, flat, table, table, rows, ro...  28.9 us
    ppermute x2, waiting for transfers between devices, shards(): come = lax.ppermute(away, 'tm', perm)  28.1 us
    dot_general x4, matrix products, tn_dot(): lax.dot_general(a, b, (((0,), (0,)), ((), ())), preferred_element_type=F32)  24.3 us
    dot_general x4, matrix products, nn_dot(): return jnp.dot(a, b, preferred_element_type=F32)  21.9 us
    ppermute x12, starting transfers between devices, beside(): lax.ppermute(away, 'tm', perm)  17.8 us
    pallas_call x1, Pallas kernels, attention(): pl.pallas_call(stats_kernel, in_specs=[flat, flat, rows, rows] + sections...  12.1 us
    all_to_all x1, starting transfers between devices, shards(): lax.all_to_all(inner, 'tm', 0, 0, axis_index_groups=halves, tiled=True)  11.9 us
  transfers between devices with their start and end apart: 20, of which 6 were waited for; matrix products, arithmetic and copies ran while one was open for 27% of the time, Pallas kernels for 4%

profile of v5, /device:TPU:0, one launch (start us, length us, event | category | flops | bytes accessed | tf_op | source)
XLA Modules:
  0.0 275.7 jit_solution(1276631533143262355)
XLA Ops:
  0.6 3.6 %copy.22 = bf16[1024,2,1024]{2,0,1:T(8,128)(2,1)S(1)} copy(bf16[1024,2,1024]{2,1,0:T(2,128)(2,1)} %param.10) | data formatting | bytes 8388608 | tf_op args[0]
  6.4 5.4 %all-to-all-start = ((bf16[8,2,2,2,16,1024]{5,4,3,2,1,0:T(8,128)(2,1)}), bf16[8,2,2,2,16,1024]{5,4,3,2,1,0:T(8,128)(2,1)}, u32[]{:S(2)}, u32[]{:S(2)}) async-start(bf16[8,2,2,2,16,1024]{5,4,3,2,1,0:T(8,128)(2,1)} %maximum_bitcast_fusion), calls=%async_computation | async-start | bytes 4194304 | tf_op jit(solution)/shard_map/all_to_all | solution.py:354
  12.7 4.9 %collective-permute-start.1 = (bf16[144,1024]{1,0:T(8,128)(2,1)S(1)}, bf16[144,1024]{1,0:T(8,128)(2,1)S(1)}, u32[]{:S(2)}, u32[]{:S(2)}) collective-permute-start(bf16[144,1024]{1,0:T(8,128)(2,1)S(1)} %fusion.2), channel_id=1, source_target_pairs={{1,0},{3,1},{5,2},{7,3},{9,4},{11,5},{13,6},{15,7},{0,8},{2,9},{4,... | collective-permute-start | bytes 884744 | tf_op jit(solution)/shard_map/ppermute | solution.py:356
  17.6 2.4 collective-permute-start.2
  20.0 3.5 %copy.25 = bf16[1024,2,1024]{2,0,1:T(8,128)(2,1)S(1)} copy(bf16[1024,2,1024]{2,1,0:T(2,128)(2,1)} %param.10) | data formatting | bytes 8388608 | tf_op jit(solution)/shard_map/optimization_barrier | solution.py:349
  26.0 2.4 pad_maximum_fusion.1
  30.0 14.6 %collective-permute-done.2 = bf16[64,1024]{1,0:T(8,128)(2,1)S(1)} collective-permute-done((bf16[64,1024]{1,0:T(8,128)(2,1)S(1)}, bf16[64,1024]{1,0:T(8,128)(2,1)S(1)}, u32[]{:S(2)}, u32[]{:S(2)}) %collective-permute-start.2) | collective-permute-done | bytes 131104 | tf_op jit(solution)/shard_map/ppermute | solution.py:358
  44.6 11.9 %all-to-all-start.1 = ((bf16[8,2,2,2,16,1024]{5,4,3,2,1,0:T(8,128)(2,1)}), bf16[8,2,2,2,16,1024]{5,4,3,2,1,0:T(8,128)(2,1)}, u32[]{:S(2)}, u32[]{:S(2)}) async-start(bf16[8,2,2,2,16,1024]{5,4,3,2,1,0:T(8,128)(2,1)} %maximum_bitcast_fusion.1), calls=%async_computation.1 | async-start | bytes 4194304 | tf_op jit(solution)/shard_map/all_to_all | solution.py:362
  59.4 3.1 %collective-permute-start.3 = (bf16[2,64,1024]{2,1,0:T(8,128)(2,1)S(1)}, bf16[2,64,1024]{2,1,0:T(8,128)(2,1)S(1)}, u32[]{:S(2)}, u32[]{:S(2)}) collective-permute-start(bf16[2,64,1024]{2,1,0:T(8,128)(2,1)S(1)} %maximum_select_fusion.6), channel_id=1, source_target_pairs={{0,4},{1,5},{2,6},{3,7},{4,0},{5,1},{6,2},{7,3},{8,12},{9,13},{10,... | collective-permute-start | bytes 786440 | tf_op jit(solution)/shard_map/ppermute | solution.py:364
  65.8 7.7 %convolution_convert_fusion.1 = bf16[1024,2048]{1,0:T(8,128)(2,1)} fusion(bf16[1024,1024]{1,0:T(8,128)(2,1)} %bitcast.11, bf16[1024,2048]{1,0:T(8,128)(2,1)S(1)} %copy-done.3), kind=kOutput, calls=%fused_computation.3 | convolution fusion | flops 4297064448 | bytes 10485760 | tf_op jit(solution)/shard_map/dot_general | solution.py:31
  74.7 13.5 %collective-permute-done.3 = bf16[2,64,1024]{2,1,0:T(8,128)(2,1)S(1)} collective-permute-done((bf16[2,64,1024]{2,1,0:T(8,128)(2,1)S(1)}, bf16[2,64,1024]{2,1,0:T(8,128)(2,1)S(1)}, u32[]{:S(2)}, u32[]{:S(2)}) %collective-permute-start.3) | collective-permute-done | bytes 262176 | tf_op jit(solution)/shard_map/ppermute | solution.py:364
  91.0 9.3 %convolution_convert_fusion = bf16[1024,2048]{1,0:T(8,128)(2,1)} fusion(bf16[1024,1024]{1,0:T(8,128)(2,1)} %bitcast.19, bf16[1024,2048]{1,0:T(8,128)(2,1)} %pad_maximum_fusion.1), kind=kOutput, calls=%fused_computation.2 | convolution fusion | flops 4297064448 | bytes 10485760 | tf_op jit(solution)/shard_map/dot_general | solution.py:31
  101.5 2.0 copy-done.4
  103.5 3.7 %convolution_convert_fusion.2 = bf16[512,2048]{1,0:T(8,128)(2,1)} fusion(bf16[512,1024]{1,0:T(8,128)(2,1)S(1)} %bitcast.158, bf16[1024,2048]{1,0:T(8,128)(2,1)S(1)} %copy-done.4), kind=kOutput, calls=%fused_computation.4 | convolution fusion | flops 2148532224 | bytes 7340032 | tf_op jit(solution)/shard_map/dot_general | solution.py:31
  107.2 4.2 %collective-permute-start.6 = (bf16[2,2,64,1024]{3,2,0,1:T(8,128)(2,1)}, bf16[2,2,64,1024]{3,2,0,1:T(8,128)(2,1)}, u32[]{:S(2)}, u32[]{:S(2)}) collective-permute-start(bf16[2,2,64,1024]{3,2,0,1:T(8,128)(2,1)} %maximum_select_fusion.4), channel_id=1, source_target_pairs={{0,2},{1,3},{2,0},{3,1},{4,6},{5,7},{6,4},{7,5},{8,10},{9,11},{10,... | collective-permute-start | bytes 1572872 | tf_op jit(solution)/shard_map/ppermute | solution.py:315
  111.3 1.9 maximum_select_fusion.3
  113.3 12.1 %softmax_stats.1.one_ref = f32[2,4,3,256]{3,2,1,0:T(4,128)} custom-call(s32[2,1,256]{2,1,0:T(1,128)} %tile.15.lo_ref, s32[2,1,256]{2,1,0:T(1,128)} %tile.17.hi_ref, bf16[2,64,1024]{2,1,0:T(8,128)(2,1)} %get-tuple-element.133.q_ref, bf16[2,64,1024]{2,1,0:T(8,128)(2,1)} %bitcast.147, bf16[8,2,2,2,16,2048]{5,4,3,2,1,0:T(8,128)(2,1)} %bitcast.120, ...), custom_call_target="tpu_custom_call" | custom-call | flops 2147483648 | bytes 12582912 | tf_op jit(solution)/shard_map/softmax_stats/pallas_call | solution.py:237
  131.0 5.5 %pad_maximum_fusion = bf16[3072,1024]{1,0:T(8,128)(2,1)} fusion(bf16[1024,1024]{1,0:T(8,128)(2,1)S(1)} %bitcast.146, bf16[1024,1024]{1,0:T(8,128)(2,1)} %bitcast.34, bf16[1024,1024]{1,0:T(8,128)(2,1)} %bitcast.33), kind=kLoop, calls=%fused_computation | loop fusion | flops 18874368 | bytes 12582912 | tf_op jit(solution)/shard_map/concatenate | solution.py:410
  137.1 14.5 %banded_grads.2 = (f32[2,2,64,512]{3,2,1,0:T(8,128)}, bf16[3,8,2,2,2,16,1024]{6,5,4,3,2,1,0:T(8,128)(2,1)}) custom-call(s32[2,1,256]{2,1,0:T(1,128)} %tile.15.lo_ref, s32[2,1,256]{2,1,0:T(1,128)} %tile.17.hi_ref, f32[2,4,3,256]{3,2,1,0:T(4,128)} %softmax_stats.1.one_ref, f32[2,4,3,256]{3,2,1,0:T(4,128)} %copy-done.18, ...), custom_call_target="tpu_custom_call" | custom-call | flops 3221225472 | bytes 12582912 | tf_op jit(solution)/shard_map/banded_grads/pallas_call | solution.py:253
  153.9 10.7 %convolution_convert_fusion.4 = bf16[1024,1024]{1,0:T(8,128)(2,1)S(1)} fusion(bf16[3072,1024]{1,0:T(8,128)(2,1)} %pad_maximum_fusion, bf16[3072,1024]{1,0:T(8,128)(2,1)} %bitcast.172), kind=kOutput, calls=%fused_computation.13 | convolution fusion | flops 6443499520 | bytes 14680064 | tf_op jit(solution)/shard_map/dot_general | solution.py:23
  164.8 3.2 %collective-permute-start.11 = (bf16[8,64,1024]{2,1,0:T(8,128)(2,1)S(1)}, bf16[8,64,1024]{2,1,0:T(8,128)(2,1)S(1)}, u32[]{:S(2)}, u32[]{:S(2)}) collective-permute-start(bf16[8,64,1024]{2,1,0:T(8,128)(2,1)S(1)} %get-tuple-element.129), channel_id=1, source_target_pairs={{0,1},{1,0},{2,3},{3,2},{4,5},{5,4},{6,7},{7,6},{8,9},{9,8},{10,11... | collective-permute-start | bytes 3145736 | tf_op jit(solution)/shard_map/ppermute | solution.py:315
  168.1 2.2 collective-permute-done.11
  171.8 14.5 %banded_grads.3 = (f32[2,2,64,512]{3,2,1,0:T(8,128)}, bf16[3,8,2,2,2,16,1024]{6,5,4,3,2,1,0:T(8,128)(2,1)}) custom-call(s32[2,1,256]{2,1,0:T(1,128)} %tile.15.lo_ref, s32[2,1,256]{2,1,0:T(1,128)} %tile.17.hi_ref, f32[2,4,3,256]{3,2,1,0:T(4,128)} %softmax_stats.1.one_ref, f32[2,4,3,256]{3,2,1,0:T(4,128)} %copy-done.18, ...), custom_call_target="tpu_custom_call" | custom-call | flops 3221225472 | bytes 12582912 | tf_op jit(solution)/shard_map/banded_grads/pallas_call | solution.py:253
  188.1 3.6 %collective-permute-start.12 = (f32[2,64,512]{2,1,0:T(8,128)}, f32[2,64,512]{2,1,0:T(8,128)}, u32[]{:S(2)}, u32[]{:S(2)}) collective-permute-start(f32[2,64,512]{2,1,0:T(8,128)} %get-tuple-element.137), channel_id=1, source_target_pairs={{0,0},{1,2},{2,4},{3,6},{4,8},{5,10},{6,12},{7,14},{8,1},{9,3},{10... | collective-permute-start | bytes 786440 | tf_op jit(solution)/shard_map/ppermute | solution.py:315
  192.9 3.9 %all-to-all-start.2 = ((bf16[8,64,1024]{2,1,0:T(8,128)(2,1)}), bf16[8,64,1024]{2,1,0:T(8,128)(2,1)S(1)}, u32[]{:S(2)}, u32[]{:S(2)}) async-start(bf16[8,64,1024]{2,1,0:T(8,128)(2,1)} %add_convert_fusion.1), calls=%async_computation.2 | async-start | bytes 2097152 | tf_op jit(solution)/shard_map/all_to_all | solution.py:426
  196.7 11.7 %convolution_convert_fusion.3 = bf16[1024,1024]{1,0:T(8,128)(2,1)} fusion(bf16[3072,1024]{1,0:T(8,128)(2,1)} %pad_maximum_fusion, bf16[3072,1024]{1,0:T(8,128)(2,1)} %bitcast.171), kind=kOutput, calls=%fused_computation.12 | convolution fusion | flops 6443499520 | bytes 14680064 | tf_op jit(solution)/shard_map/dot_general | solution.py:23
  210.2 16.9 %all-to-all-done.2 = bf16[8,64,1024]{2,1,0:T(8,128)(2,1)S(1)} async-done(((bf16[8,64,1024]{2,1,0:T(8,128)(2,1)}), bf16[8,64,1024]{2,1,0:T(8,128)(2,1)S(1)}, u32[]{:S(2)}, u32[]{:S(2)}) %all-to-all-start.2) | async-done | bytes 1048608 | tf_op jit(solution)/shard_map/all_to_all | solution.py:426
  227.0 2.1 dynamic-slice_bitcast_fusion
  230.4 2.4 collective-permute-done.15
  234.6 4.9 %all-to-all-start.3 = ((bf16[8,64,1280]{2,1,0:T(8,128)(2,1)}), bf16[8,64,1280]{2,1,0:T(8,128)(2,1)S(1)}, u32[]{:S(2)}, u32[]{:S(2)}) async-start(bf16[8,64,1280]{2,1,0:T(8,128)(2,1)} %pad_maximum_fusion.3), calls=%async_computation.3 | async-start | bytes 2621440 | tf_op jit(solution)/shard_map/all_to_all | solution.py:426
  243.3 2.3 copy.38
  247.6 23.7 %all-to-all-done.3 = bf16[8,64,1280]{2,1,0:T(8,128)(2,1)S(1)} async-done(((bf16[8,64,1280]{2,1,0:T(8,128)(2,1)}), bf16[8,64,1280]{2,1,0:T(8,128)(2,1)S(1)}, u32[]{:S(2)}, u32[]{:S(2)}) %all-to-all-start.3) | async-done | bytes 1310752 | tf_op jit(solution)/shard_map/all_to_all | solution.py:426
  (130 shorter events, 46.3 us)
Async XLA Ops:
  0.6 63.6 %copy-start = (bf16[1024,1024]{1,0:T(8,128)(2,1)S(1)}, bf16[1024,1024]{1,0:T(8,128)(2,1)}, u32[]{:S(2)}) copy-start(bf16[1024,1024]{1,0:T(8,128)(2,1)} %param.14) | copy-start | bytes 6291460
  6.4 5.4 %copy-start.19 = (s32[64]{0:T(128)S(1)}, s32[64]{0:T(128)}, u32[]{:S(2)}) copy-start(s32[64]{0:T(128)} %param.15) | copy-start | bytes 772
  6.4 5.5 %copy-start.20 = (s32[64]{0:T(128)S(1)}, s32[64]{0:T(128)}, u32[]{:S(2)}) copy-start(s32[64]{0:T(128)} %param.16) | copy-start | bytes 772
  6.4 5.5 %copy-start.9 = (bf16[64,1024]{1,0:T(8,128)(2,1)S(1)}, bf16[64,1024]{1,0:T(8,128)(2,1)}, u32[]{:S(2)}) copy-start(bf16[64,1024]{1,0:T(8,128)(2,1)} %param.17) | copy-start | bytes 393220
  6.4 5.6 %copy-start.17 = (bf16[64,1024]{1,0:T(8,128)(2,1)S(1)}, bf16[64,1024]{1,0:T(8,128)(2,1)}, u32[]{:S(2)}) copy-start(bf16[64,1024]{1,0:T(8,128)(2,1)} %param.11) | copy-start | bytes 393220
  6.4 38.2 %all-to-all-start = ((bf16[8,2,2,2,16,1024]{5,4,3,2,1,0:T(8,128)(2,1)}), bf16[8,2,2,2,16,1024]{5,4,3,2,1,0:T(8,128)(2,1)}, u32[]{:S(2)}, u32[]{:S(2)}) async-start(bf16[8,2,2,2,16,1024]{5,4,3,2,1,0:T(8,128)(2,1)} %maximum_bitcast_fusion), calls=%async_computation | async-start | bytes 4194304 | tf_op jit(solution)/shard_map/all_to_all | solution.py:354
  12.1 32.6 %collective-permute-start = (bf16[144,1024]{1,0:T(8,128)(2,1)S(1)}, bf16[144,1024]{1,0:T(8,128)(2,1)S(1)}, u32[]{:S(2)}, u32[]{:S(2)}) collective-permute-start(bf16[144,1024]{1,0:T(8,128)(2,1)S(1)} %fusion.2), channel_id=1, source_target_pairs={{0,0},{2,1},{4,2},{6,3},{8,4},{10,5},{12,6},{14,7},{1,8},{3,9},{5,... | collective-permute-start | bytes 884744 | tf_op jit(solution)/shard_map/ppermute | solution.py:355
  12.7 31.9 %collective-permute-start.1 = (bf16[144,1024]{1,0:T(8,128)(2,1)S(1)}, bf16[144,1024]{1,0:T(8,128)(2,1)S(1)}, u32[]{:S(2)}, u32[]{:S(2)}) collective-permute-start(bf16[144,1024]{1,0:T(8,128)(2,1)S(1)} %fusion.2), channel_id=1, source_target_pairs={{1,0},{3,1},{5,2},{7,3},{9,4},{11,5},{13,6},{15,7},{0,8},{2,9},{4,... | collective-permute-start | bytes 884744 | tf_op jit(solution)/shard_map/ppermute | solution.py:356
  17.6 27.0 %collective-permute-start.2 = (bf16[64,1024]{1,0:T(8,128)(2,1)S(1)}, bf16[64,1024]{1,0:T(8,128)(2,1)S(1)}, u32[]{:S(2)}, u32[]{:S(2)}) collective-permute-start(bf16[64,1024]{1,0:T(8,128)(2,1)S(1)} %multiply_convert_fusion), channel_id=1, source_target_pairs={{0,8},{1,9},{2,10},{3,11},{4,12},{5,13},{6,14},{7,15},{8,0},{9,1},... | collective-permute-start | bytes 393224 | tf_op jit(solution)/shard_map/ppermute | solution.py:358
  23.8 2.2 copy-start.8
  44.6 11.9 %copy-start.11 = (bf16[144,1024]{1,0:T(8,128)(2,1)}, bf16[144,1024]{1,0:T(8,128)(2,1)S(1)}, u32[]{:S(2)}) copy-start(bf16[144,1024]{1,0:T(8,128)(2,1)S(1)} %collective-permute-done.1) | copy-start | bytes 884740
  44.6 43.6 %all-to-all-start.1 = ((bf16[8,2,2,2,16,1024]{5,4,3,2,1,0:T(8,128)(2,1)}), bf16[8,2,2,2,16,1024]{5,4,3,2,1,0:T(8,128)(2,1)}, u32[]{:S(2)}, u32[]{:S(2)}) async-start(bf16[8,2,2,2,16,1024]{5,4,3,2,1,0:T(8,128)(2,1)} %maximum_bitcast_fusion.1), calls=%async_computation.1 | async-start | bytes 4194304 | tf_op jit(solution)/shard_map/all_to_all | solution.py:362
  59.4 28.8 %collective-permute-start.3 = (bf16[2,64,1024]{2,1,0:T(8,128)(2,1)S(1)}, bf16[2,64,1024]{2,1,0:T(8,128)(2,1)S(1)}, u32[]{:S(2)}, u32[]{:S(2)}) collective-permute-start(bf16[2,64,1024]{2,1,0:T(8,128)(2,1)S(1)} %maximum_select_fusion.6), channel_id=1, source_target_pairs={{0,4},{1,5},{2,6},{3,7},{4,0},{5,1},{6,2},{7,3},{8,12},{9,13},{10,... | collective-permute-start | bytes 786440 | tf_op jit(solution)/shard_map/ppermute | solution.py:364
  62.5 3.2 %copy-start.3 = (bf16[1024,2048]{1,0:T(8,128)(2,1)S(1)}, bf16[1024,2048]{1,0:T(8,128)(2,1)}, u32[]{:S(2)}) copy-start(bf16[1024,2048]{1,0:T(8,128)(2,1)} %pad_maximum_fusion.1) | copy-start | bytes 12582916
  88.2 23.1 %copy-start.6 = (bf16[2,64,1024]{2,1,0:T(8,128)(2,1)}, bf16[2,64,1024]{2,1,0:T(8,128)(2,1)S(1)}, u32[]{:S(2)}) copy-start(bf16[2,64,1024]{2,1,0:T(8,128)(2,1)S(1)} %collective-permute-done.3) | copy-start | bytes 786436
  88.2 13.0 %collective-permute-start.4 = (bf16[8,2,16,1024]{3,2,1,0:T(8,128)(2,1)S(1)}, bf16[8,2,16,1024]{3,2,1,0:T(8,128)(2,1)S(1)}, u32[]{:S(2)}, u32[]{:S(2)}) collective-permute-start(bf16[8,2,16,1024]{3,2,1,0:T(8,128)(2,1)S(1)} %get-tuple-element.96), channel_id=1, source_target_pairs={{0,1},{1,2},{2,3},{3,4},{4,5},{5,6},{6,7},{8,9},{9,10},{10,11},{11... | collective-permute-start | bytes 1572872 | tf_op jit(solution)/shard_map/ppermute | solution.py:315
  89.6 11.7 %collective-permute-start.5 = (bf16[8,2,16,1024]{3,2,1,0:T(8,128)(2,1)S(1)}, bf16[8,2,16,1024]{3,2,1,0:T(8,128)(2,1)S(1)}, u32[]{:S(2)}, u32[]{:S(2)}) collective-permute-start(bf16[8,2,16,1024]{3,2,1,0:T(8,128)(2,1)S(1)} %get-tuple-element.97), channel_id=1, source_target_pairs={{1,0},{2,1},{3,2},{4,3},{5,4},{6,5},{7,6},{9,8},{10,9},{11,10},{12... | collective-permute-start | bytes 1572872 | tf_op jit(solution)/shard_map/ppermute | solution.py:315
  91.0 9.3 %copy-start.10 = (bf16[2,1,64,1024]{3,2,0,1:T(8,128)(2,1)S(1)}, bf16[2,1,64,1024]{3,2,0,1:T(8,128)(2,1)}, u32[]{:S(2)}) copy-start(bf16[2,1,64,1024]{3,2,0,1:T(8,128)(2,1)} %get-tuple-element.174) | copy-start | bytes 786436
  101.3 2.2 copy-start.4
  107.2 18.2 %collective-permute-start.6 = (bf16[2,2,64,1024]{3,2,0,1:T(8,128)(2,1)}, bf16[2,2,64,1024]{3,2,0,1:T(8,128)(2,1)}, u32[]{:S(2)}, u32[]{:S(2)}) collective-permute-start(bf16[2,2,64,1024]{3,2,0,1:T(8,128)(2,1)} %maximum_select_fusion.4), channel_id=1, source_target_pairs={{0,2},{1,3},{2,0},{3,1},{4,6},{5,7},{6,4},{7,5},{8,10},{9,11},{10,... | collective-permute-start | bytes 1572872 | tf_op jit(solution)/shard_map/ppermute | solution.py:315
  128.4 8.1 %collective-permute-start.7 = (bf16[2,2,2,64,1024]{4,3,0,1,2:T(8,128)(2,1)S(1)}, bf16[2,2,2,64,1024]{4,3,0,1,2:T(8,128)(2,1)}, u32[]{:S(2)}, u32[]{:S(2)}) collective-permute-start(bf16[2,2,2,64,1024]{4,3,0,1,2:T(8,128)(2,1)S(1)} %maximum_select_fusion), channel_id=1, source_target_pairs={{0,1},{1,0},{2,3},{3,2},{4,5},{5,4},{6,7},{7,6},{8,9},{9,8},{10,11... | collective-permute-start | bytes 3145736 | tf_op jit(solution)/shard_map/ppermute | solution.py:315
  130.8 5.7 %collective-permute-start.8 = (f32[2,4,3,256]{3,2,1,0:T(4,128)S(1)}, f32[2,4,3,256]{3,2,1,0:T(4,128)S(1)}, u32[]{:S(2)}, u32[]{:S(2)}) collective-permute-start(f32[2,4,3,256]{3,2,1,0:T(4,128)S(1)} %copy-done.12), channel_id=1, source_target_pairs={{0,8},{1,9},{2,10},{3,11},{4,12},{5,13},{6,14},{7,15},{8,0},{9,1},... | collective-permute-start | bytes 73736 | tf_op jit(solution)/shard_map/ppermute | solution.py:315
  152.7 11.9 %collective-permute-start.10 = (f32[2,64,512]{2,1,0:T(8,128)S(1)}, f32[2,64,512]{2,1,0:T(8,128)S(1)}, u32[]{:S(2)}, u32[]{:S(2)}) collective-permute-start(f32[2,64,512]{2,1,0:T(8,128)S(1)} %get-tuple-element.126), channel_id=1, source_target_pairs={{0,1},{1,3},{2,5},{3,7},{4,9},{5,11},{6,13},{7,15},{8,0},{9,2},{10... | collective-permute-start | bytes 786440 | tf_op jit(solution)/shard_map/ppermute | solution.py:315
  153.0 11.6 %collective-permute-start.9 = (f32[2,64,512]{2,1,0:T(8,128)S(1)}, f32[2,64,512]{2,1,0:T(8,128)S(1)}, u32[]{:S(2)}, u32[]{:S(2)}) collective-permute-start(f32[2,64,512]{2,1,0:T(8,128)S(1)} %get-tuple-element.125), channel_id=1, source_target_pairs={{0,0},{1,2},{2,4},{3,6},{4,8},{5,10},{6,12},{7,14},{8,1},{9,3},{10... | collective-permute-start | bytes 786440 | tf_op jit(solution)/shard_map/ppermute | solution.py:315
  164.8 5.5 %collective-permute-start.11 = (bf16[8,64,1024]{2,1,0:T(8,128)(2,1)S(1)}, bf16[8,64,1024]{2,1,0:T(8,128)(2,1)S(1)}, u32[]{:S(2)}, u32[]{:S(2)}) collective-permute-start(bf16[8,64,1024]{2,1,0:T(8,128)(2,1)S(1)} %get-tuple-element.129), channel_id=1, source_target_pairs={{0,1},{1,0},{2,3},{3,2},{4,5},{5,4},{6,7},{7,6},{8,9},{9,8},{10,11... | collective-permute-start | bytes 3145736 | tf_op jit(solution)/shard_map/ppermute | solution.py:315
  188.1 20.3 %collective-permute-start.12 = (f32[2,64,512]{2,1,0:T(8,128)}, f32[2,64,512]{2,1,0:T(8,128)}, u32[]{:S(2)}, u32[]{:S(2)}) collective-permute-start(f32[2,64,512]{2,1,0:T(8,128)} %get-tuple-element.137), channel_id=1, source_target_pairs={{0,0},{1,2},{2,4},{3,6},{4,8},{5,10},{6,12},{7,14},{8,1},{9,3},{10... | collective-permute-start | bytes 786440 | tf_op jit(solution)/shard_map/ppermute | solution.py:315
  191.7 16.8 %collective-permute-start.13 = (f32[2,64,512]{2,1,0:T(8,128)S(1)}, f32[2,64,512]{2,1,0:T(8,128)}, u32[]{:S(2)}, u32[]{:S(2)}) collective-permute-start(f32[2,64,512]{2,1,0:T(8,128)S(1)} %get-tuple-element.138), channel_id=1, source_target_pairs={{0,1},{1,3},{2,5},{3,7},{4,9},{5,11},{6,13},{7,15},{8,0},{9,2},{10... | collective-permute-start | bytes 786440 | tf_op jit(solution)/shard_map/ppermute | solution.py:315
  192.9 34.2 %all-to-all-start.2 = ((bf16[8,64,1024]{2,1,0:T(8,128)(2,1)}), bf16[8,64,1024]{2,1,0:T(8,128)(2,1)S(1)}, u32[]{:S(2)}, u32[]{:S(2)}) async-start(bf16[8,64,1024]{2,1,0:T(8,128)(2,1)} %add_convert_fusion.1), calls=%async_computation.2 | async-start | bytes 2097152 | tf_op jit(solution)/shard_map/all_to_all | solution.py:426
  229.1 3.7 %collective-permute-start.14 = (bf16[8,64,1024]{2,1,0:T(8,128)(2,1)S(1)}, bf16[8,64,1024]{2,1,0:T(8,128)(2,1)S(1)}, u32[]{:S(2)}, u32[]{:S(2)}) collective-permute-start(bf16[8,64,1024]{2,1,0:T(8,128)(2,1)S(1)} %get-tuple-element.147), channel_id=1, source_target_pairs={{0,1},{1,0},{2,3},{3,2},{4,5},{5,4},{6,7},{7,6},{8,9},{9,8},{10,11... | collective-permute-start | bytes 3145736 | tf_op jit(solution)/shard_map/ppermute | solution.py:315
  230.4 2.5 collective-permute-start.15
  234.6 36.7 %all-to-all-start.3 = ((bf16[8,64,1280]{2,1,0:T(8,128)(2,1)}), bf16[8,64,1280]{2,1,0:T(8,128)(2,1)S(1)}, u32[]{:S(2)}, u32[]{:S(2)}) async-start(bf16[8,64,1280]{2,1,0:T(8,128)(2,1)} %pad_maximum_fusion.3), calls=%async_computation.3 | async-start | bytes 2621440 | tf_op jit(solution)/shard_map/all_to_all | solution.py:426
  242.2 3.4 %copy-start.2 = (bf16[8,64,1024]{2,1,0:T(8,128)(2,1)S(1)}, bf16[8,64,1024]{2,1,0:T(8,128)(2,1)}, u32[]{:S(2)}) copy-start(bf16[8,64,1024]{2,1,0:T(8,128)(2,1)} %copy-done.1) | copy-start | bytes 3145732
  (9 other events, 13.3 us)

commit v6 on v5

--- a/solution.py
+++ b/solution.py
@@ -13,7 +13,7 @@
 W = 16
 GROUP = 4
 LANES = GROUP * HD
-CALLS = 2
+SPLIT = (3, 1)
 CHUNK = 256
 F32 = jnp.float32
 BF16 = jnp.bfloat16
@@ -354,14 +354,9 @@
     edge = lax.all_to_all(outer, "tm", 0, 0, axis_index_groups=halves, tiled=True)
     one = lax.ppermute(letter, "tm", [(b, a) for a, b in owner_one])
     two = lax.ppermute(letter, "tm", [(b, a) for a, b in owner_two])
-    away, perm = gather.send()
-    come = lax.ppermute(away, "tm", perm)
     weights = jnp.concatenate([key_weight, value_weight], axis=1)
-    edge, inner, weights, one, two, come = fence((edge, inner, weights, one, two, come))
-    gather.receive(come)
+    edge, inner, weights, one, two = fence((edge, inner, weights, one, two))
     middle = lax.all_to_all(inner, "tm", 0, 0, axis_index_groups=halves, tiled=True)
-    away, perm = gather.send()
-    come = lax.ppermute(away, "tm", perm)
 
     pair = jnp.where(upper_half, jnp.stack([two, one]), jnp.stack([one, two]))
     q_pair = pair[:, :n_query]
@@ -386,16 +381,14 @@
     up = [(i, i + 1) for i in range(n_dev - 1) if (i + 1) % src]
     low = Move(edge[:, 1, :, 1], up)
     high = Move(edge[:, 0, :, 0], [(target, source) for source, target in up])
-    middle, come, edge_kv, q_pair, g_pair, lo, hi, low.block, high.block = fence(
-        (middle, come, edge_kv, q_pair, g_pair, lo, hi, low.block, high.block)
-    )
-    gather.receive(come)
+    middle, edge_kv, q_pair, g_pair, lo, hi, low.block, high.block = fence(
+        (middle, edge_kv, q_pair, g_pair, lo, hi, low.block, high.block)
+    )
     middle_kv = beside([low, high], project, middle)
     ext = jnp.stack([low.come, high.come], axis=1)
     ext_kv = project(ext)
     tokens = (edge_kv, middle_kv, ext_kv)
 
-    groups = width // LANES // CALLS
     stats = beside(
         [gather],
         functools.partial(attention, 0, width // LANES, lo, hi, None),
@@ -410,8 +403,6 @@
         return jnp.concatenate([x.reshape(-1, width) for x in (edge, middle, halo)], axis=0)
 
     sources = beside([gather, swap], all_sources, edge, middle, ext)
-    while gather.order:
-        beside([gather], lambda: ())
 
     core = me & 1
     chips = [[2 * k + c for k in range(src)] for c in range(2)]
@@ -442,29 +433,29 @@
         sums = [(a + b).astype(BF16) for a, b in zip(parts[::2], parts[1::2])]
         return jnp.concatenate(sums, axis=2)
 
-    trades, shares, ready = [], [], None
-    for call in range(CALLS):
-        work = functools.partial(attention, call * groups, groups, lo, hi, (swap.block, swap.come))
+    trades, shares, ready, start = [], [], None, 0
+    for call, groups in enumerate(SPLIT):
+        work = functools.partial(attention, start, groups, lo, hi, (swap.block, swap.come))
+        start += groups
         if ready is not None:
             ready, q_pair = fence((ready, q_pair))
             share = scatter(ready)
-        partial, grads = work(q_pair, g_pair, tokens)
+        partial, grads = beside([gather], work, q_pair, g_pair, tokens)
         trade = half_context(partial)
         trades += trade
-        term = beside(trade, weigh, grads)
+        term = beside(trade + [gather], weigh, grads)
         if ready is not None:
-            share, term = fence((share, term))
             shares.append(share)
-        if call < CALLS - 1:
+        if call < len(SPLIT) - 1:
             away, keep = meet(term)
-            keep = beside([away], lambda x: x, keep)
+            keep = beside([away, gather], lambda x: x, keep)
             ready = add(keep, away.come)
 
     context, d_query = assemble(*[move.come for move in trades])
     away, keep = meet(term)
     partner = Move(context, flips(n_dev, 0))
     keep, context = beside([away, partner], lambda *x: x, keep, context)
-    ready = add(keep, away.come)
+    ready, shares = fence((add(keep, away.come), shares))
 
     columns = jnp.concatenate(
         [x.reshape(n_query, src, -1).swapaxes(0, 1) for x in (context, partner.come)], axis=2
@@ -484,8 +475,8 @@
     sums = [jnp.sum(share.astype(F32), axis=0) for share in shares]
 
     def heads(which):
-        at = [(2 * i + which) * LANES for i in range(groups)]
-        return jnp.concatenate([x[:, i : i + LANES] for x in sums for i in at], axis=1)
+        cuts = [(x, (2 * i + which) * LANES) for x, n in zip(sums, SPLIT) for i in range(n)]
+        return jnp.concatenate([x[:, i : i + LANES] for x, i in cuts], axis=1)
 
     return attended, d_query, heads(0), heads(1), d_out
 

time: 277 us -> 266 us (0.960)
    ppermute x2 -> x0, waiting for transfers between devices: 28.1 us -> none  [shards(): come = lax.ppermute(away, 'tm', perm)]
    ppermute x12 -> x14, waiting for transfers between devices: 4.67 us -> 32 us  [beside(): lax.ppermute(away, 'tm', perm)]
    all_to_all x2, waiting for transfers between devices: 40.6 us -> 14.4 us  [scatter(): lax.all_to_all(block, 'tm', 0, 0, axis_index_groups=chips, tiled=True)]
    ppermute x1, waiting for transfers between devices: 0.01 us -> 14.7 us  [shards(): two = lax.ppermute(letter, 'tm', [(b, a) for a, b in owner_two])]
    all_to_all x1, waiting for transfers between devices: 0.01 us -> 11 us  [shards(): lax.all_to_all(inner, 'tm', 0, 0, axis_index_groups=halves, tiled=True)]
    ppermute x2 -> x0, starting transfers between devices: 5.48 us -> none  [shards(): come = lax.ppermute(away, 'tm', perm)]
    select_n x6, other arithmetic: 7.35 us -> 2.41 us  [receive(): jnp.where(mine == 0, jnp.stack([self.block, come], axis=-3), jnp.stack([c...]
    ppermute x12 -> x14, starting transfers between devices: 17.8 us -> 20 us  [beside(): lax.ppermute(away, 'tm', perm)]
  transfers between devices with their start and end apart: 20 -> 20, of which waited for: 6 -> 7; matrix products, arithmetic and copies ran while one was open for 27% -> 26% of each run, Pallas kernels for 4% -> 15%
where the time goes in v6:
time: 266 us; the launch traced here: 265 us
  waiting for transfers between devices  72.1 us (27%)
  starting transfers between devices  52.2 us (20%)
  matrix products  45.3 us (17%)
  Pallas kernels  40.6 us (15%)
  other arithmetic  27.2 us (10%)
  local copies, waits for them, and re-layouts  26.4 us (10%)
    ppermute x14, waiting for transfers between devices, beside(): lax.ppermute(away, 'tm', perm)  32 us
    pallas_call x2, Pallas kernels, attention(): pl.pallas_call(grads_kernel, in_specs=[flat, flat, table, table, rows, ro...  28.4 us
    dot_general x4, matrix products, tn_dot(): lax.dot_general(a, b, (((0,), (0,)), ((), ())), preferred_element_type=F32)  21.9 us
    dot_general x4, matrix products, nn_dot(): return jnp.dot(a, b, preferred_element_type=F32)  21.8 us
    ppermute x14, starting transfers between devices, beside(): lax.ppermute(away, 'tm', perm)  20 us
    ppermute x1, waiting for transfers between devices, shards(): two = lax.ppermute(letter, 'tm', [(b, a) for a, b in owner_two])  14.7 us
    all_to_all x2, waiting for transfers between devices, scatter(): lax.all_to_all(block, 'tm', 0, 0, axis_index_groups=chips, tiled=True)  14.4 us
    all_to_all x1, starting transfers between devices, shards(): lax.all_to_all(inner, 'tm', 0, 0, axis_index_groups=halves, tiled=True)  12.8 us
  transfers between devices with their start and end apart: 20, of which 7 were waited for; matrix products, arithmetic and copies ran while one was open for 26% of the time, Pallas kernels for 15%

profile of v6, /device:TPU:0, one launch (start us, length us, event | category | flops | bytes accessed | tf_op | source)
XLA Modules:
  0.0 265.0 jit_solution(14014319277053631002)
XLA Ops:
  0.6 3.6 %copy.22 = bf16[1024,2,1024]{2,0,1:T(8,128)(2,1)S(1)} copy(bf16[1024,2,1024]{2,1,0:T(2,128)(2,1)} %param.10) | data formatting | bytes 8388608 | tf_op args[0]
  4.9 1.6 maximum_bitcast_fusion
  6.5 5.4 %all-to-all-start = ((bf16[8,2,2,2,16,1024]{5,4,3,2,1,0:T(8,128)(2,1)}), bf16[8,2,2,2,16,1024]{5,4,3,2,1,0:T(8,128)(2,1)}, u32[]{:S(2)}, u32[]{:S(2)}) async-start(bf16[8,2,2,2,16,1024]{5,4,3,2,1,0:T(8,128)(2,1)} %maximum_bitcast_fusion), calls=%async_computation | async-start | bytes 4194304 | tf_op jit(solution)/shard_map/all_to_all | solution.py:354
  12.8 4.8 %collective-permute-start.1 = (bf16[144,1024]{1,0:T(8,128)(2,1)S(1)}, bf16[144,1024]{1,0:T(8,128)(2,1)}, u32[]{:S(2)}, u32[]{:S(2)}) collective-permute-start(bf16[144,1024]{1,0:T(8,128)(2,1)S(1)} %fusion.2), channel_id=1, source_target_pairs={{1,0},{3,1},{5,2},{7,3},{9,4},{11,5},{13,6},{15,7},{0,8},{2,9},{4,... | collective-permute-start | bytes 884744 | tf_op jit(solution)/shard_map/ppermute | solution.py:356
  17.6 3.5 %copy.25 = bf16[1024,2,1024]{2,0,1:T(8,128)(2,1)S(1)} copy(bf16[1024,2,1024]{2,1,0:T(2,128)(2,1)} %param.10) | data formatting | bytes 8388608 | tf_op jit(solution)/shard_map/optimization_barrier | solution.py:349
  24.7 2.4 pad_maximum_fusion.1
  27.1 14.7 %collective-permute-done.1 = bf16[144,1024]{1,0:T(8,128)(2,1)} collective-permute-done((bf16[144,1024]{1,0:T(8,128)(2,1)S(1)}, bf16[144,1024]{1,0:T(8,128)(2,1)}, u32[]{:S(2)}, u32[]{:S(2)}) %collective-permute-start.1) | collective-permute-done | bytes 294944 | tf_op jit(solution)/shard_map/ppermute | solution.py:356
  41.9 12.8 %all-to-all-start.1 = ((bf16[8,2,2,2,16,1024]{5,4,3,2,1,0:T(8,128)(2,1)}), bf16[8,2,2,2,16,1024]{5,4,3,2,1,0:T(8,128)(2,1)}, u32[]{:S(2)}, u32[]{:S(2)}) async-start(bf16[8,2,2,2,16,1024]{5,4,3,2,1,0:T(8,128)(2,1)} %maximum_bitcast_fusion.1), calls=%async_computation.1 | async-start | bytes 4194304 | tf_op jit(solution)/shard_map/all_to_all | solution.py:359
  61.8 7.7 %convolution_convert_fusion.2 = bf16[1024,2048]{1,0:T(8,128)(2,1)} fusion(bf16[1024,1024]{1,0:T(8,128)(2,1)} %bitcast.9, bf16[1024,2048]{1,0:T(8,128)(2,1)S(1)} %copy-done.1), kind=kOutput, calls=%fused_computation.4 | convolution fusion | flops 4297064448 | bytes 10485760 | tf_op jit(solution)/shard_map/dot_general | solution.py:31
  69.5 11.0 %all-to-all-done.1 = bf16[8,2,2,2,16,1024]{5,4,3,2,1,0:T(8,128)(2,1)} async-done(((bf16[8,2,2,2,16,1024]{5,4,3,2,1,0:T(8,128)(2,1)}), bf16[8,2,2,2,16,1024]{5,4,3,2,1,0:T(8,128)(2,1)}, u32[]{:S(2)}, u32[]{:S(2)}) %all-to-all-start.1) | async-done | bytes 2097184 | tf_op jit(solution)/shard_map/all_to_all | solution.py:359
  83.4 9.3 %convolution_convert_fusion.1 = bf16[1024,2048]{1,0:T(8,128)(2,1)} fusion(bf16[1024,1024]{1,0:T(8,128)(2,1)} %bitcast.17, bf16[1024,2048]{1,0:T(8,128)(2,1)} %pad_maximum_fusion.1), kind=kOutput, calls=%fused_computation.3 | convolution fusion | flops 4297064448 | bytes 10485760 | tf_op jit(solution)/shard_map/dot_general | solution.py:31
  92.9 2.0 copy-done.2
  94.9 3.8 %convolution_convert_fusion.3 = bf16[512,2048]{1,0:T(8,128)(2,1)} fusion(bf16[512,1024]{1,0:T(8,128)(2,1)S(1)} %bitcast.159, bf16[1024,2048]{1,0:T(8,128)(2,1)S(1)} %copy-done.2), kind=kOutput, calls=%fused_computation.7 | convolution fusion | flops 2148532224 | bytes 7340032 | tf_op jit(solution)/shard_map/dot_general | solution.py:31
  98.6 12.1 %softmax_stats.1.one_ref = f32[2,4,3,256]{3,2,1,0:T(4,128)} custom-call(s32[2,1,256]{2,1,0:T(1,128)} %tile.15.lo_ref, s32[2,1,256]{2,1,0:T(1,128)} %tile.17.hi_ref, bf16[2,64,1024]{2,1,0:T(8,128)(2,1)} %get-tuple-element.156.q_ref, bf16[2,64,1024]{2,1,0:T(8,128)(2,1)} %bitcast.147, bf16[8,2,2,2,16,2048]{5,4,3,2,1,0:T(8,128)(2,1)} %bitcast.120, ...), custom_call_target="tpu_custom_call" | custom-call | flops 2147483648 | bytes 12582912 | tf_op jit(solution)/shard_map/softmax_stats/pallas_call | solution.py:237
  113.9 5.2 %collective-permute-start.5 = (bf16[2,64,1024]{2,1,0:T(8,128)(2,1)S(1)}, bf16[2,64,1024]{2,1,0:T(8,128)(2,1)S(1)}, u32[]{:S(2)}, u32[]{:S(2)}) collective-permute-start(bf16[2,64,1024]{2,1,0:T(8,128)(2,1)S(1)} %maximum_select_fusion.6), channel_id=1, source_target_pairs={{0,4},{1,5},{2,6},{3,7},{4,0},{5,1},{6,2},{7,3},{8,12},{9,13},{10,... | collective-permute-start | bytes 786440 | tf_op jit(solution)/shard_map/ppermute | solution.py:315
  119.0 2.9 %collective-permute-start.6 = (f32[2,4,3,256]{3,2,1,0:T(4,128)S(1)}, f32[2,4,3,256]{3,2,1,0:T(4,128)S(1)}, u32[]{:S(2)}, u32[]{:S(2)}) collective-permute-start(f32[2,4,3,256]{3,2,1,0:T(4,128)S(1)} %copy-done.12), channel_id=1, source_target_pairs={{0,8},{1,9},{2,10},{3,11},{4,12},{5,13},{6,14},{7,15},{8,0},{9,1},... | collective-permute-start | bytes 73736 | tf_op jit(solution)/shard_map/ppermute | solution.py:315
  122.0 5.5 %pad_maximum_fusion = bf16[3072,1024]{1,0:T(8,128)(2,1)} fusion(bf16[1024,1024]{1,0:T(8,128)(2,1)S(1)} %bitcast.146, bf16[1024,1024]{1,0:T(8,128)(2,1)} %bitcast.26, bf16[1024,1024]{1,0:T(8,128)(2,1)} %bitcast.25), kind=kLoop, calls=%fused_computation | loop fusion | flops 18874368 | bytes 12582912 | tf_op jit(solution)/shard_map/concatenate | solution.py:403
  130.4 20.3 %banded_grads.2 = (f32[2,2,64,768]{3,2,1,0:T(8,128)}, bf16[3,8,2,2,2,16,1536]{6,5,4,3,2,1,0:T(8,128)(2,1)}) custom-call(s32[2,1,256]{2,1,0:T(1,128)} %tile.15.lo_ref, s32[2,1,256]{2,1,0:T(1,128)} %tile.17.hi_ref, f32[2,4,3,256]{3,2,1,0:T(4,128)} %softmax_stats.1.one_ref, f32[2,4,3,256]{3,2,1,0:T(4,128)} %copy-done.14, ...), custom_call_target="tpu_custom_call" | custom-call | flops 4831838208 | bytes 18874368 | tf_op jit(solution)/shard_map/banded_grads/pallas_call | solution.py:253
  152.7 3.0 %collective-permute-start.9 = (f32[2,64,768]{2,1,0:T(8,128)S(1)}, f32[2,64,768]{2,1,0:T(8,128)S(1)}, u32[]{:S(2)}, u32[]{:S(2)}) collective-permute-start(f32[2,64,768]{2,1,0:T(8,128)S(1)} %get-tuple-element.148), channel_id=1, source_target_pairs={{0,1},{1,3},{2,5},{3,7},{4,9},{5,11},{6,13},{7,15},{8,0},{9,2},{10... | collective-permute-start | bytes 1179656 | tf_op jit(solution)/shard_map/ppermute | solution.py:315
  155.7 14.1 %convolution_convert_fusion = bf16[1024,1536]{1,0:T(8,128)(2,1)S(1)} fusion(bf16[3072,1024]{1,0:T(8,128)(2,1)} %pad_maximum_fusion, bf16[3072,1536]{1,0:T(8,128)(2,1)} %bitcast.172), kind=kOutput, calls=%fused_computation.2 | convolution fusion | flops 9665249280 | bytes 18874368 | tf_op jit(solution)/shard_map/dot_general | solution.py:23
  169.8 5.2 %collective-permute-done.9 = f32[2,64,768]{2,1,0:T(8,128)S(1)} collective-permute-done((f32[2,64,768]{2,1,0:T(8,128)S(1)}, f32[2,64,768]{2,1,0:T(8,128)S(1)}, u32[]{:S(2)}, u32[]{:S(2)}) %collective-permute-start.9) | collective-permute-done | bytes 393248 | tf_op jit(solution)/shard_map/ppermute | solution.py:315
  176.1 3.4 %collective-permute-done.11 = bf16[8,64,1536]{2,1,0:T(8,128)(2,1)S(1)} collective-permute-done((bf16[8,64,1536]{2,1,0:T(8,128)(2,1)S(1)}, bf16[8,64,1536]{2,1,0:T(8,128)(2,1)S(1)}, u32[]{:S(2)}, u32[]{:S(2)}) %collective-permute-start.11) | collective-permute-done | bytes 1572896 | tf_op jit(solution)/shard_map/ppermute | solution.py:315
  181.1 4.3 %all-to-all-start.2 = ((bf16[8,64,1536]{2,1,0:T(8,128)(2,1)}), bf16[8,64,1536]{2,1,0:T(8,128)(2,1)}, u32[]{:S(2)}, u32[]{:S(2)}) async-start(bf16[8,64,1536]{2,1,0:T(8,128)(2,1)} %add_convert_fusion), calls=%async_computation.2 | async-start | bytes 3145728 | tf_op jit(solution)/shard_map/all_to_all | solution.py:417
  186.5 8.1 %banded_grads.3 = (f32[2,2,64,256]{3,2,1,0:T(8,128)}, bf16[3,8,2,2,2,16,512]{6,5,4,3,2,1,0:T(8,128)(2,1)}) custom-call(s32[2,1,256]{2,1,0:T(1,128)} %tile.15.lo_ref, s32[2,1,256]{2,1,0:T(1,128)} %tile.17.hi_ref, f32[2,4,3,256]{3,2,1,0:T(4,128)} %softmax_stats.1.one_ref, f32[2,4,3,256]{3,2,1,0:T(4,128)} %copy-done.14, ...), custom_call_target="tpu_custom_call" | custom-call | flops 1610612736 | bytes 6291456 | tf_op jit(solution)/shard_map/banded_grads/pallas_call | solution.py:253
  196.3 3.3 %collective-permute-start.13 = (f32[2,64,256]{2,1,0:T(8,128)S(1)}, f32[2,64,256]{2,1,0:T(8,128)S(1)}, u32[]{:S(2)}, u32[]{:S(2)}) collective-permute-start(f32[2,64,256]{2,1,0:T(8,128)S(1)} %get-tuple-element.165), channel_id=1, source_target_pairs={{0,1},{1,3},{2,5},{3,7},{4,9},{5,11},{6,13},{7,15},{8,0},{9,2},{10... | collective-permute-start | bytes 393224 | tf_op jit(solution)/shard_map/ppermute | solution.py:315
  199.6 7.1 %convolution_convert_fusion.4 = bf16[1024,512]{1,0:T(8,128)(2,1)S(1)} fusion(bf16[3072,1024]{1,0:T(8,128)(2,1)} %pad_maximum_fusion, bf16[3072,512]{1,0:T(8,128)(2,1)} %bitcast.173), kind=kOutput, calls=%fused_computation.13 | convolution fusion | flops 3221749760 | bytes 10485760 | tf_op jit(solution)/shard_map/dot_general | solution.py:23
  206.8 21.8 %collective-permute-done.13 = f32[2,64,256]{2,1,0:T(8,128)S(1)} collective-permute-done((f32[2,64,256]{2,1,0:T(8,128)S(1)}, f32[2,64,256]{2,1,0:T(8,128)S(1)}, u32[]{:S(2)}, u32[]{:S(2)}) %collective-permute-start.13) | collective-permute-done | bytes 131104 | tf_op jit(solution)/shard_map/ppermute | solution.py:315
  229.9 1.6 collective-permute-done.15
  233.0 1.9 pad_maximum_fusion.4
  234.9 4.2 %all-to-all-start.3 = ((bf16[8,64,768]{2,1,0:T(8,128)(2,1)}), bf16[8,64,768]{2,1,0:T(8,128)(2,1)}, u32[]{:S(2)}, u32[]{:S(2)}) async-start(bf16[8,64,768]{2,1,0:T(8,128)(2,1)} %pad_maximum_fusion.4), calls=%async_computation.3 | async-start | bytes 1572864 | tf_op jit(solution)/shard_map/all_to_all | solution.py:417
  243.8 1.7 convert_reduce_fusion
  245.5 14.4 %all-to-all-done.3 = bf16[8,64,768]{2,1,0:T(8,128)(2,1)} async-done(((bf16[8,64,768]{2,1,0:T(8,128)(2,1)}), bf16[8,64,768]{2,1,0:T(8,128)(2,1)}, u32[]{:S(2)}, u32[]{:S(2)}) %all-to-all-start.3) | async-done | bytes 786464 | tf_op jit(solution)/shard_map/all_to_all | solution.py:417
  (122 shorter events, 41.0 us)
Async XLA Ops:
  0.6 59.6 %copy-start = (bf16[1024,1024]{1,0:T(8,128)(2,1)S(1)}, bf16[1024,1024]{1,0:T(8,128)(2,1)}, u32[]{:S(2)}) copy-start(bf16[1024,1024]{1,0:T(8,128)(2,1)} %param.14) | copy-start | bytes 6291460
  6.5 5.4 %copy-start.15 = (s32[64]{0:T(128)S(1)}, s32[64]{0:T(128)}, u32[]{:S(2)}) copy-start(s32[64]{0:T(128)} %param.15) | copy-start | bytes 772
  6.5 5.5 %copy-start.16 = (s32[64]{0:T(128)S(1)}, s32[64]{0:T(128)}, u32[]{:S(2)}) copy-start(s32[64]{0:T(128)} %param.16) | copy-start | bytes 772
  6.5 5.5 %copy-start.6 = (bf16[64,1024]{1,0:T(8,128)(2,1)S(1)}, bf16[64,1024]{1,0:T(8,128)(2,1)}, u32[]{:S(2)}) copy-start(bf16[64,1024]{1,0:T(8,128)(2,1)} %param.17) | copy-start | bytes 393220
  6.5 5.6 %copy-start.13 = (bf16[64,1024]{1,0:T(8,128)(2,1)S(1)}, bf16[64,1024]{1,0:T(8,128)(2,1)}, u32[]{:S(2)}) copy-start(bf16[64,1024]{1,0:T(8,128)(2,1)} %param.11) | copy-start | bytes 393220
  6.5 35.4 %all-to-all-start = ((bf16[8,2,2,2,16,1024]{5,4,3,2,1,0:T(8,128)(2,1)}), bf16[8,2,2,2,16,1024]{5,4,3,2,1,0:T(8,128)(2,1)}, u32[]{:S(2)}, u32[]{:S(2)}) async-start(bf16[8,2,2,2,16,1024]{5,4,3,2,1,0:T(8,128)(2,1)} %maximum_bitcast_fusion), calls=%async_computation | async-start | bytes 4194304 | tf_op jit(solution)/shard_map/all_to_all | solution.py:354
  12.1 15.0 %collective-permute-start = (bf16[144,1024]{1,0:T(8,128)(2,1)S(1)}, bf16[144,1024]{1,0:T(8,128)(2,1)S(1)}, u32[]{:S(2)}, u32[]{:S(2)}) collective-permute-start(bf16[144,1024]{1,0:T(8,128)(2,1)S(1)} %fusion.2), channel_id=1, source_target_pairs={{0,0},{2,1},{4,2},{6,3},{8,4},{10,5},{12,6},{14,7},{1,8},{3,9},{5,... | collective-permute-start | bytes 884744 | tf_op jit(solution)/shard_map/ppermute | solution.py:355
  12.8 29.1 %collective-permute-start.1 = (bf16[144,1024]{1,0:T(8,128)(2,1)S(1)}, bf16[144,1024]{1,0:T(8,128)(2,1)}, u32[]{:S(2)}, u32[]{:S(2)}) collective-permute-start(bf16[144,1024]{1,0:T(8,128)(2,1)S(1)} %fusion.2), channel_id=1, source_target_pairs={{1,0},{3,1},{5,2},{7,3},{9,4},{11,5},{13,6},{15,7},{0,8},{2,9},{4,... | collective-permute-start | bytes 884744 | tf_op jit(solution)/shard_map/ppermute | solution.py:356
  21.8 2.4 copy-start.4
  21.8 3.0 %copy-start.5 = (bf16[1024,1024]{1,0:T(8,128)(2,1)S(1)}, bf16[1024,1024]{1,0:T(8,128)(2,1)}, u32[]{:S(2)}) copy-start(bf16[1024,1024]{1,0:T(8,128)(2,1)} %param.12) | copy-start | bytes 6291460
  41.9 38.6 %all-to-all-start.1 = ((bf16[8,2,2,2,16,1024]{5,4,3,2,1,0:T(8,128)(2,1)}), bf16[8,2,2,2,16,1024]{5,4,3,2,1,0:T(8,128)(2,1)}, u32[]{:S(2)}, u32[]{:S(2)}) async-start(bf16[8,2,2,2,16,1024]{5,4,3,2,1,0:T(8,128)(2,1)} %maximum_bitcast_fusion.1), calls=%async_computation.1 | async-start | bytes 4194304 | tf_op jit(solution)/shard_map/all_to_all | solution.py:359
  58.8 3.0 %copy-start.1 = (bf16[1024,2048]{1,0:T(8,128)(2,1)S(1)}, bf16[1024,2048]{1,0:T(8,128)(2,1)}, u32[]{:S(2)}) copy-start(bf16[1024,2048]{1,0:T(8,128)(2,1)} %pad_maximum_fusion.1) | copy-start | bytes 12582916
  80.5 12.2 %collective-permute-start.2 = (bf16[8,2,16,1024]{3,2,1,0:T(8,128)(2,1)S(1)}, bf16[8,2,16,1024]{3,2,1,0:T(8,128)(2,1)S(1)}, u32[]{:S(2)}, u32[]{:S(2)}) collective-permute-start(bf16[8,2,16,1024]{3,2,1,0:T(8,128)(2,1)S(1)} %get-tuple-element.109), channel_id=1, source_target_pairs={{0,1},{1,2},{2,3},{3,4},{4,5},{5,6},{6,7},{8,9},{9,10},{10,11},{11... | collective-permute-start | bytes 1572872 | tf_op jit(solution)/shard_map/ppermute | solution.py:315
  81.9 10.7 %collective-permute-start.3 = (bf16[8,2,16,1024]{3,2,1,0:T(8,128)(2,1)S(1)}, bf16[8,2,16,1024]{3,2,1,0:T(8,128)(2,1)S(1)}, u32[]{:S(2)}, u32[]{:S(2)}) collective-permute-start(bf16[8,2,16,1024]{3,2,1,0:T(8,128)(2,1)S(1)} %get-tuple-element.110), channel_id=1, source_target_pairs={{1,0},{2,1},{3,2},{4,3},{5,4},{6,5},{7,6},{9,8},{10,9},{11,10},{12... | collective-permute-start | bytes 1572872 | tf_op jit(solution)/shard_map/ppermute | solution.py:315
  92.7 2.2 copy-start.2
  98.6 12.2 %collective-permute-start.4 = (bf16[64,1024]{1,0:T(8,128)(2,1)S(1)}, bf16[64,1024]{1,0:T(8,128)(2,1)S(1)}, u32[]{:S(2)}, u32[]{:S(2)}) collective-permute-start(bf16[64,1024]{1,0:T(8,128)(2,1)S(1)} %multiply_convert_fusion), channel_id=1, source_target_pairs={{0,8},{1,9},{2,10},{3,11},{4,12},{5,13},{6,14},{7,15},{8,0},{9,1},... | collective-permute-start | bytes 393224 | tf_op jit(solution)/shard_map/ppermute | solution.py:315
  113.5 5.5 %copy-start.12 = (f32[2,4,3,256]{3,2,1,0:T(4,128)S(1)}, f32[2,4,3,256]{3,2,1,0:T(4,128)}, u32[]{:S(2)}) copy-start(f32[2,4,3,256]{3,2,1,0:T(4,128)} %softmax_stats.1.one_ref) | copy-start | bytes 73732
  113.9 14.4 %collective-permute-start.5 = (bf16[2,64,1024]{2,1,0:T(8,128)(2,1)S(1)}, bf16[2,64,1024]{2,1,0:T(8,128)(2,1)S(1)}, u32[]{:S(2)}, u32[]{:S(2)}) collective-permute-start(bf16[2,64,1024]{2,1,0:T(8,128)(2,1)S(1)} %maximum_select_fusion.6), channel_id=1, source_target_pairs={{0,4},{1,5},{2,6},{3,7},{4,0},{5,1},{6,2},{7,3},{8,12},{9,13},{10,... | collective-permute-start | bytes 786440 | tf_op jit(solution)/shard_map/ppermute | solution.py:315
  119.0 9.2 %collective-permute-start.6 = (f32[2,4,3,256]{3,2,1,0:T(4,128)S(1)}, f32[2,4,3,256]{3,2,1,0:T(4,128)S(1)}, u32[]{:S(2)}, u32[]{:S(2)}) collective-permute-start(f32[2,4,3,256]{3,2,1,0:T(4,128)S(1)} %copy-done.12), channel_id=1, source_target_pairs={{0,8},{1,9},{2,10},{3,11},{4,12},{5,13},{6,14},{7,15},{8,0},{9,1},... | collective-permute-start | bytes 73736 | tf_op jit(solution)/shard_map/ppermute | solution.py:315
  122.0 5.5 %copy-start.10 = (bf16[1,1,64,1024]{3,2,1,0:T(8,128)(2,1)S(1)}, bf16[1,1,64,1024]{3,2,1,0:T(8,128)(2,1)}, u32[]{:S(2)}) copy-start(bf16[1,1,64,1024]{3,2,1,0:T(8,128)(2,1)} %fusion.37) | copy-start | bytes 393220
  129.7 21.0 %collective-permute-start.7 = (bf16[2,2,64,1024]{3,2,0,1:T(8,128)(2,1)}, bf16[2,2,64,1024]{3,2,0,1:T(8,128)(2,1)S(1)}, u32[]{:S(2)}, u32[]{:S(2)}) collective-permute-start(bf16[2,2,64,1024]{3,2,0,1:T(8,128)(2,1)} %maximum_select_fusion.3), channel_id=1, source_target_pairs={{0,2},{1,3},{2,0},{3,1},{4,6},{5,7},{6,4},{7,5},{8,10},{9,11},{10,... | collective-permute-start | bytes 1572872 | tf_op jit(solution)/shard_map/ppermute | solution.py:315
  151.9 23.1 %collective-permute-start.10 = (bf16[2,2,2,64,1024]{4,3,0,1,2:T(8,128)(2,1)S(1)}, bf16[2,2,2,64,1024]{4,3,0,1,2:T(8,128)(2,1)S(1)}, u32[]{:S(2)}, u32[]{:S(2)}) collective-permute-start(bf16[2,2,2,64,1024]{4,3,0,1,2:T(8,128)(2,1)S(1)} %maximum_select_fusion), channel_id=1, source_target_pairs={{0,1},{1,0},{2,3},{3,2},{4,5},{5,4},{6,7},{7,6},{8,9},{9,8},{10,11... | collective-permute-start | bytes 3145736 | tf_op jit(solution)/shard_map/ppermute | solution.py:315
  152.0 17.9 %collective-permute-start.8 = (f32[2,64,768]{2,1,0:T(8,128)S(1)}, f32[2,64,768]{2,1,0:T(8,128)S(1)}, u32[]{:S(2)}, u32[]{:S(2)}) collective-permute-start(f32[2,64,768]{2,1,0:T(8,128)S(1)} %get-tuple-element.147), channel_id=1, source_target_pairs={{0,0},{1,2},{2,4},{3,6},{4,8},{5,10},{6,12},{7,14},{8,1},{9,3},{10... | collective-permute-start | bytes 1179656 | tf_op jit(solution)/shard_map/ppermute | solution.py:315
  152.7 22.4 %collective-permute-start.9 = (f32[2,64,768]{2,1,0:T(8,128)S(1)}, f32[2,64,768]{2,1,0:T(8,128)S(1)}, u32[]{:S(2)}, u32[]{:S(2)}) collective-permute-start(f32[2,64,768]{2,1,0:T(8,128)S(1)} %get-tuple-element.148), channel_id=1, source_target_pairs={{0,1},{1,3},{2,5},{3,7},{4,9},{5,11},{6,13},{7,15},{8,0},{9,2},{10... | collective-permute-start | bytes 1179656 | tf_op jit(solution)/shard_map/ppermute | solution.py:315
  176.1 3.4 %collective-permute-start.11 = (bf16[8,64,1536]{2,1,0:T(8,128)(2,1)S(1)}, bf16[8,64,1536]{2,1,0:T(8,128)(2,1)S(1)}, u32[]{:S(2)}, u32[]{:S(2)}) collective-permute-start(bf16[8,64,1536]{2,1,0:T(8,128)(2,1)S(1)} %get-tuple-element.152), channel_id=1, source_target_pairs={{0,1},{1,0},{2,3},{3,2},{4,5},{5,4},{6,7},{7,6},{8,9},{9,8},{10,11... | collective-permute-start | bytes 4718600 | tf_op jit(solution)/shard_map/ppermute | solution.py:315
  181.1 51.9 %all-to-all-start.2 = ((bf16[8,64,1536]{2,1,0:T(8,128)(2,1)}), bf16[8,64,1536]{2,1,0:T(8,128)(2,1)}, u32[]{:S(2)}, u32[]{:S(2)}) async-start(bf16[8,64,1536]{2,1,0:T(8,128)(2,1)} %add_convert_fusion), calls=%async_computation.2 | async-start | bytes 3145728 | tf_op jit(solution)/shard_map/all_to_all | solution.py:417
  195.6 11.1 %collective-permute-start.12 = (f32[2,64,256]{2,1,0:T(8,128)S(1)}, f32[2,64,256]{2,1,0:T(8,128)S(1)}, u32[]{:S(2)}, u32[]{:S(2)}) collective-permute-start(f32[2,64,256]{2,1,0:T(8,128)S(1)} %get-tuple-element.164), channel_id=1, source_target_pairs={{0,0},{1,2},{2,4},{3,6},{4,8},{5,10},{6,12},{7,14},{8,1},{9,3},{10... | collective-permute-start | bytes 393224 | tf_op jit(solution)/shard_map/ppermute | solution.py:315
  196.3 32.2 %collective-permute-start.13 = (f32[2,64,256]{2,1,0:T(8,128)S(1)}, f32[2,64,256]{2,1,0:T(8,128)S(1)}, u32[]{:S(2)}, u32[]{:S(2)}) collective-permute-start(f32[2,64,256]{2,1,0:T(8,128)S(1)} %get-tuple-element.165), channel_id=1, source_target_pairs={{0,1},{1,3},{2,5},{3,7},{4,9},{5,11},{6,13},{7,15},{8,0},{9,2},{10... | collective-permute-start | bytes 393224 | tf_op jit(solution)/shard_map/ppermute | solution.py:315
  229.3 2.2 collective-permute-start.14
  229.4 2.1 collective-permute-start.15
  234.9 25.0 %all-to-all-start.3 = ((bf16[8,64,768]{2,1,0:T(8,128)(2,1)}), bf16[8,64,768]{2,1,0:T(8,128)(2,1)}, u32[]{:S(2)}, u32[]{:S(2)}) async-start(bf16[8,64,768]{2,1,0:T(8,128)(2,1)} %pad_maximum_fusion.4), calls=%async_computation.3 | async-start | bytes 1572864 | tf_op jit(solution)/shard_map/all_to_all | solution.py:417
  259.9 1.4 copy-start.3
  (5 other events, 4.9 us)

commit v7 on v6

--- a/solution.py
+++ b/solution.py
@@ -13,7 +13,7 @@
 W = 16
 GROUP = 4
 LANES = GROUP * HD
-SPLIT = (3, 1)
+SPLIT = (2, 2)
 CHUNK = 256
 F32 = jnp.float32
 BF16 = jnp.bfloat16
@@ -57,46 +57,46 @@
     second = lax.broadcasted_iota(jnp.int32, (CHUNK, wide), 1) >= wide // 2
     frames = (
         near + jnp.where(second, n_query - W, 0),
+        near + jnp.where(second, n_query, -W),
         near + W,
         near + 2 * W,
-        near + jnp.where(second, n_query, -W),
     )
     for i, frame in enumerate(frames):
-        bias_ref[i] = jnp.where((frame >= lo) & (frame <= hi), 0.0, -1e30)
+        at = slice(i % 2 * CHUNK, (i % 2 + 1) * CHUNK)
+        bias_ref[i // 2, at, :] = jnp.where((frame >= lo) & (frame <= hi), 0.0, -1e30)
 
 
 def load(ref, side):
     return ref[:, side].reshape(CHUNK, LANES)
 
 
-def sides(ref):
-    return load(ref, 0), load(ref, 1)
-
-
-def halo_sides(near_ref, far_ref):
+def row_groups(edge_ref, mid_ref, near_ref, far_ref):
     lower = pl.program_id(0) == 0
+    below = jnp.where(lower, load(far_ref, 0), load(near_ref, 1))
+    above = jnp.where(lower, load(near_ref, 0), load(far_ref, 1))
     return (
-        jnp.where(lower, load(far_ref, 0), load(near_ref, 1)),
-        jnp.where(lower, load(near_ref, 0), load(far_ref, 1)),
-    )
-
-
-def pair_dot(rows, x_ref):
+        jnp.concatenate([load(edge_ref, 0), below], 0),
+        jnp.concatenate([load(edge_ref, 1), above], 0),
+        jnp.concatenate([load(mid_ref, 0), load(mid_ref, 1)], 0),
+    )
+
+
+def group_dots(rows, x_ref):
     mid = x_ref.shape[0] // 2
-    return jnp.concatenate([nt_dot(rows[0], x_ref[:mid, :]), nt_dot(rows[1], x_ref[mid:, :])], 1)
+    pair = jnp.concatenate([nt_dot(rows[0], x_ref[:mid, :]), nt_dot(rows[1], x_ref[mid:, :])], 1)
+    return pair, nt_dot(rows[2], x_ref[...])
 
 
 def fold(x):
-    return x.reshape(CHUNK // 8, 8, x.shape[1])
+    return x.reshape(x.shape[0] // 8, 8, x.shape[1])
 
 
 def stats_kernel(
     lo_ref, hi_ref, q_ref, g_ref,
     ke_ref, km_ref, kn_ref, kf_ref, ve_ref, vm_ref, vn_ref, vf_ref,
-    out_ref, s_ref, bias_ref, bq_ref, bg_ref,
+    out_ref, bias_ref, bq_ref, bg_ref,
 ):
     n_query = q_ref.shape[0]
-    wide = GROUP * n_query
     own = own_head(n_query)
     bq_ref[...] = scaled(spread(q_ref[...], own))
     bg_ref[...] = scaled(spread(g_ref[...], own))
@@ -105,40 +105,26 @@
     def _():
         fill_bias(lo_ref, hi_ref, bias_ref, n_query)
 
-    def score(at, s, top):
-        s = s + bias_ref[at]
-        s_ref[at] = s
-        return jnp.maximum(top, jnp.max(fold(s), axis=0))
-
-    top = jnp.full((8, wide), -1e30, F32)
-    top = score(0, pair_dot(sides(ke_ref), bq_ref), top)
-    for c in range(2):
-        top = score(1 + c, nt_dot(load(km_ref, c), bq_ref[...]), top)
-    top = score(3, pair_dot(halo_sides(kn_ref, kf_ref), bq_ref), top)
-    top = jnp.max(top, axis=0, keepdims=True)
-
-    total = jnp.zeros((8, wide), F32)
-    weighted = jnp.zeros((8, wide), F32)
-    for c in range(4):
-        if c == 0:
-            dp = pair_dot(sides(ve_ref), bg_ref)
-        elif c == 3:
-            dp = pair_dot(halo_sides(vn_ref, vf_ref), bg_ref)
-        else:
-            dp = nt_dot(load(vm_ref, c - 1), bg_ref[...])
-        e = jnp.exp(s_ref[c] - top)
-        total = total + jnp.sum(fold(e), axis=0)
-        weighted = weighted + jnp.sum(fold(e * dp), axis=0)
+    scores = group_dots(row_groups(ke_ref, km_ref, kn_ref, kf_ref), bq_ref)
+    d_probs = group_dots(row_groups(ve_ref, vm_ref, vn_ref, vf_ref), bg_ref)
+    scores = [s + bias_ref[i] for i, s in enumerate(scores)]
+    tops = [jnp.max(fold(s), axis=0) for s in scores]
+    top = jnp.max(jnp.maximum(*tops), axis=0, keepdims=True)
+    total, weighted = [], []
+    for s, dp in zip(scores, d_probs):
+        e = jnp.exp(s - top)
+        total.append(jnp.sum(fold(e), axis=0))
+        weighted.append(jnp.sum(fold(e * dp), axis=0))
     out_ref[0:1, :] = top
-    out_ref[1:2, :] = jnp.sum(total, axis=0, keepdims=True)
-    out_ref[2:3, :] = jnp.sum(weighted, axis=0, keepdims=True)
+    out_ref[1:2, :] = jnp.sum(total[0] + total[1], axis=0, keepdims=True)
+    out_ref[2:3, :] = jnp.sum(weighted[0] + weighted[1], axis=0, keepdims=True)
 
 
 def grads_kernel(
     lo_ref, hi_ref, one_ref, two_ref, q_ref, g_ref,
     ke_ref, km_ref, kn_ref, kf_ref, ve_ref, vm_ref, vn_ref, vf_ref,
     out_ref, part_ref,
-    bias_ref, bq_ref, bg_ref, bqs_ref, bgs_ref, acc_ctx, acc_dq,
+    bias_ref, bq_ref, bg_ref, bqs_ref, bgs_ref,
 ):
     n_query = q_ref.shape[0]
     part = n_query // 2
@@ -159,51 +145,38 @@
     two = jnp.exp(two_ref[0:1, :] - top)
     inverse = 1.0 / (one_ref[1:2, :] * one + two_ref[1:2, :] * two)
     mean = (one_ref[2:3, :] * one + two_ref[2:3, :] * two) * inverse
-    acc_ctx[...] = jnp.zeros_like(acc_ctx)
-    acc_dq[...] = jnp.zeros_like(acc_dq)
-
-    def soft(table, s, dp):
-        p = jnp.exp(s + bias_ref[table] - top) * inverse
-        return p.astype(BF16), (p * (dp - mean)).astype(BF16)
+    keys = row_groups(ke_ref, km_ref, kn_ref, kf_ref)
+    values = row_groups(ve_ref, vm_ref, vn_ref, vf_ref)
+    probs, d_scores = [], []
+    for i, (s, dp) in enumerate(zip(group_dots(keys, bqs_ref), group_dots(values, bgs_ref))):
+        p = jnp.exp(s + bias_ref[i] - top) * inverse
+        probs.append(p.astype(BF16))
+        d_scores.append((p * (dp - mean)).astype(BF16))
 
     shape = part_ref.shape[1:2] + part_ref.shape[3:5] + (LANES,)
-
-    def keep(section, side, kp, vp):
-        part_ref[section, :, side, :, :, :LANES] = kp.astype(BF16).reshape(shape)
-        part_ref[section, :, side, :, :, LANES:] = vp.astype(BF16).reshape(shape)
-
-    def pair(k, v, section, table):
-        pb, ds = soft(table, pair_dot(k, bqs_ref), pair_dot(v, bgs_ref))
-        for side, lanes in ((0, slice(0, mid)), (1, slice(mid, wide))):
-            acc_ctx[lanes, :] += tn_dot(pb[:, lanes], v[side])
-            acc_dq[lanes, :] += tn_dot(ds[:, lanes], k[side])
-            keep(
-                section, side,
-                nn_dot(ds[:, lanes], bq_ref[lanes, :]), nn_dot(pb[:, lanes], bg_ref[lanes, :]),
-            )
-
-    pair(sides(ke_ref), sides(ve_ref), 0, 0)
-
-    def middle(c, carry):
-        k = load(km_ref, c)
-        v = load(vm_ref, c)
-        pb, ds = soft(1 + c, nt_dot(k, bqs_ref[...]), nt_dot(v, bgs_ref[...]))
-        acc_ctx[...] += tn_dot(pb, v)
-        acc_dq[...] += tn_dot(ds, k)
-        keep(1, c, nn_dot(ds, bq_ref[...]), nn_dot(pb, bg_ref[...]))
-        return carry
-
-    lax.fori_loop(0, 2, middle, 0)
-    pair(halo_sides(kn_ref, kf_ref), halo_sides(vn_ref, vf_ref), 2, 3)
-
-    def diagonal(acc, which):
-        kept = jnp.where(own, acc, 0.0)
-        for i in range(2):
-            rows = [kept[(i * GROUP + h) * part : (i * GROUP + h + 1) * part] for h in range(GROUP)]
-            out_ref[which, i * part : (i + 1) * part, :] = functools.reduce(jnp.add, rows)
-
-    diagonal(acc_ctx[...], 0)
-    diagonal(acc_dq[...], 1)
+    low, high, both = slice(0, mid), slice(mid, wide), slice(0, wide)
+    places = (((0, 0), (2, 0)), ((0, 1), (2, 1)), ((1, 0), (1, 1)))
+
+    def back(weights, x_ref, cols):
+        for which, lanes, place in zip((0, 0, 1), (low, high, both), places):
+            x = nn_dot(weights[which][:, lanes], x_ref[lanes, :]).astype(BF16)
+            for i, (section, side) in enumerate(place):
+                rows = x[i * CHUNK : (i + 1) * CHUNK].reshape(shape)
+                part_ref[section, :, side, :, :, cols] = rows
+
+    back(d_scores, bq_ref, slice(0, LANES))
+    back(probs, bg_ref, slice(LANES, 2 * LANES))
+
+    def forward(which, weights, rows):
+        for i, lanes in enumerate((low, high)):
+            left = jnp.concatenate([w[:, lanes] for w in weights], 0)
+            acc = tn_dot(left, jnp.concatenate([rows[i], rows[2]], 0))
+            acc = jnp.where(own[lanes], acc, 0.0)
+            heads = [acc[h * part : (h + 1) * part] for h in range(GROUP)]
+            out_ref[which, i * part : (i + 1) * part, :] = functools.reduce(jnp.add, heads)
+
+    forward(0, probs, values)
+    forward(1, d_scores, keys)
 
 
 def attention(first_group, groups, lo, hi, stats, queries, d_context, tokens):
@@ -226,8 +199,7 @@
     tokens = (edge, middle, edge, ext)
     sections = sections(first_group) + sections(width // LANES + first_group)
     operand = pltpu.VMEM((wide, LANES), BF16)
-    total = pltpu.VMEM((wide, LANES), F32)
-    bias = pltpu.VMEM((4, CHUNK, wide), F32)
+    bias = pltpu.VMEM((2, 2 * CHUNK, wide), F32)
     scores = 8 * CHUNK * wide * groups
     common = dict(
         grid=(2, groups),
@@ -239,7 +211,7 @@
             in_specs=[flat, flat, rows, rows] + sections,
             out_specs=table,
             out_shape=jax.ShapeDtypeStruct((2, groups, 3, wide), F32),
-            scratch_shapes=[pltpu.VMEM((4, CHUNK, wide), F32), bias, operand, operand],
+            scratch_shapes=[bias, operand, operand],
             cost_estimate=pl.CostEstimate(
                 flops=4 * scores * LANES, bytes_accessed=6 * scores, transcendentals=scores
             ),
@@ -261,7 +233,7 @@
             jax.ShapeDtypeStruct((2, 2, n_query, groups * LANES), F32),
             jax.ShapeDtypeStruct((3, src, 2, tok, 2, W, 2 * groups * LANES), BF16),
         ],
-        scratch_shapes=[bias] + [operand] * 4 + [total] * 2,
+        scratch_shapes=[bias] + [operand] * 4,
         cost_estimate=pl.CostEstimate(
             flops=12 * scores * LANES, bytes_accessed=12 * scores, transcendentals=scores
         ),

time: 266 us -> 266 us (level)
  Pallas kernels: 40.6 us -> 32.1 us
  waiting for transfers between devices: 72.1 us -> 79.9 us
    all_to_all x2, waiting for transfers between devices: 14.4 us -> 43.3 us  [scatter(): lax.all_to_all(block, 'tm', 0, 0, axis_index_groups=chips, tiled=True)]
    ppermute x14, waiting for transfers between devices: 32 us -> 10.9 us  [beside(): lax.ppermute(away, 'tm', perm)]
    pallas_call x2, Pallas kernels: 28.4 us -> 19.7 us  [attention(): pl.pallas_call(grads_kernel, in_specs=[flat, flat, table, table, rows, ro...]
    unnamed x37 -> x43, local copies, waits for them, and re-layouts: 10.6 us -> 8.48 us
  transfers between devices with their start and end apart: 20 -> 20, of which waited for: 7 -> 8; matrix products, arithmetic and copies ran while one was open for 26% -> 28% of each run, Pallas kernels for 15% -> 8%
where the time goes in v7:
time: 266 us; the launch traced here: 265 us
  waiting for transfers between devices  79.9 us (30%)
  starting transfers between devices  51.6 us (19%)
  matrix products  47.6 us (18%)
  Pallas kernels  32.1 us (12%)
  other arithmetic  27.1 us (10%)
  local copies, waits for them, and re-layouts  25.4 us (10%)
    all_to_all x2, waiting for transfers between devices, scatter(): lax.all_to_all(block, 'tm', 0, 0, axis_index_groups=chips, tiled=True)  43.3 us
    dot_general x4, matrix products, tn_dot(): lax.dot_general(a, b, (((0,), (0,)), ((), ())), preferred_element_type=F32)  24.3 us
    dot_general x4, matrix products, nn_dot(): return jnp.dot(a, b, preferred_element_type=F32)  21.8 us
    pallas_call x2, Pallas kernels, attention(): pl.pallas_call(grads_kernel, in_specs=[flat, flat, table, table, rows, ro...  19.7 us
    ppermute x14, starting transfers between devices, beside(): lax.ppermute(away, 'tm', perm)  18.5 us
    ppermute x1, waiting for transfers between devices, shards(): two = lax.ppermute(letter, 'tm', [(b, a) for a, b in owner_two])  14.7 us
    all_to_all x1, starting transfers between devices, shards(): lax.all_to_all(inner, 'tm', 0, 0, axis_index_groups=halves, tiled=True)  12.8 us
    pallas_call x1, Pallas kernels, attention(): pl.pallas_call(stats_kernel, in_specs=[flat, flat, rows, rows] + sections...  12.4 us
  transfers between devices with their start and end apart: 20, of which 8 were waited for; matrix products, arithmetic and copies ran while one was open for 28% of the time, Pallas kernels for 8%

profile of v7, /device:TPU:0, one launch (start us, length us, event | category | flops | bytes accessed | tf_op | source)
XLA Modules:
  0.0 264.9 jit_solution(2807825476739020825)
XLA Ops:
  0.6 3.6 %copy.22 = bf16[1024,2,1024]{2,0,1:T(8,128)(2,1)S(1)} copy(bf16[1024,2,1024]{2,1,0:T(2,128)(2,1)} %param.10) | data formatting | bytes 8388608 | tf_op args[0]
  6.4 5.4 %all-to-all-start = ((bf16[8,2,2,2,16,1024]{5,4,3,2,1,0:T(8,128)(2,1)}), bf16[8,2,2,2,16,1024]{5,4,3,2,1,0:T(8,128)(2,1)}, u32[]{:S(2)}, u32[]{:S(2)}) async-start(bf16[8,2,2,2,16,1024]{5,4,3,2,1,0:T(8,128)(2,1)} %maximum_bitcast_fusion), calls=%async_computation | async-start | bytes 4194304 | tf_op jit(solution)/shard_map/all_to_all | solution.py:326
  12.7 4.9 %collective-permute-start.1 = (bf16[144,1024]{1,0:T(8,128)(2,1)S(1)}, bf16[144,1024]{1,0:T(8,128)(2,1)}, u32[]{:S(2)}, u32[]{:S(2)}) collective-permute-start(bf16[144,1024]{1,0:T(8,128)(2,1)S(1)} %fusion.2), channel_id=1, source_target_pairs={{1,0},{3,1},{5,2},{7,3},{9,4},{11,5},{13,6},{15,7},{0,8},{2,9},{4,... | collective-permute-start | bytes 884744 | tf_op jit(solution)/shard_map/ppermute | solution.py:328
  17.6 3.5 %copy.25 = bf16[1024,2,1024]{2,0,1:T(8,128)(2,1)S(1)} copy(bf16[1024,2,1024]{2,1,0:T(2,128)(2,1)} %param.10) | data formatting | bytes 8388608 | tf_op jit(solution)/shard_map/optimization_barrier | solution.py:321
  24.7 2.4 pad_maximum_fusion.1
  27.1 14.7 %collective-permute-done.1 = bf16[144,1024]{1,0:T(8,128)(2,1)} collective-permute-done((bf16[144,1024]{1,0:T(8,128)(2,1)S(1)}, bf16[144,1024]{1,0:T(8,128)(2,1)}, u32[]{:S(2)}, u32[]{:S(2)}) %collective-permute-start.1) | collective-permute-done | bytes 294944 | tf_op jit(solution)/shard_map/ppermute | solution.py:328
  41.8 12.8 %all-to-all-start.1 = ((bf16[8,2,2,2,16,1024]{5,4,3,2,1,0:T(8,128)(2,1)}), bf16[8,2,2,2,16,1024]{5,4,3,2,1,0:T(8,128)(2,1)}, u32[]{:S(2)}, u32[]{:S(2)}) async-start(bf16[8,2,2,2,16,1024]{5,4,3,2,1,0:T(8,128)(2,1)} %maximum_bitcast_fusion.1), calls=%async_computation.1 | async-start | bytes 4194304 | tf_op jit(solution)/shard_map/all_to_all | solution.py:331
  61.8 7.7 %convolution_convert_fusion.1 = bf16[1024,2048]{1,0:T(8,128)(2,1)} fusion(bf16[1024,1024]{1,0:T(8,128)(2,1)} %bitcast.9, bf16[1024,2048]{1,0:T(8,128)(2,1)S(1)} %copy-done.1), kind=kOutput, calls=%fused_computation.3 | convolution fusion | flops 4297064448 | bytes 10485760 | tf_op jit(solution)/shard_map/dot_general | solution.py:31
  69.4 11.0 %all-to-all-done.1 = bf16[8,2,2,2,16,1024]{5,4,3,2,1,0:T(8,128)(2,1)} async-done(((bf16[8,2,2,2,16,1024]{5,4,3,2,1,0:T(8,128)(2,1)}), bf16[8,2,2,2,16,1024]{5,4,3,2,1,0:T(8,128)(2,1)}, u32[]{:S(2)}, u32[]{:S(2)}) %all-to-all-start.1) | async-done | bytes 2097184 | tf_op jit(solution)/shard_map/all_to_all | solution.py:331
  83.3 9.3 %convolution_convert_fusion = bf16[1024,2048]{1,0:T(8,128)(2,1)} fusion(bf16[1024,1024]{1,0:T(8,128)(2,1)} %bitcast.17, bf16[1024,2048]{1,0:T(8,128)(2,1)} %pad_maximum_fusion.1), kind=kOutput, calls=%fused_computation.2 | convolution fusion | flops 4297064448 | bytes 10485760 | tf_op jit(solution)/shard_map/dot_general | solution.py:31
  92.9 2.0 copy-done.2
  94.8 3.7 %convolution_convert_fusion.2 = bf16[512,2048]{1,0:T(8,128)(2,1)} fusion(bf16[512,1024]{1,0:T(8,128)(2,1)S(1)} %bitcast.160, bf16[1024,2048]{1,0:T(8,128)(2,1)S(1)} %copy-done.2), kind=kOutput, calls=%fused_computation.4 | convolution fusion | flops 2148532224 | bytes 7340032 | tf_op jit(solution)/shard_map/dot_general | solution.py:31
  98.5 12.4 %softmax_stats.1.one_ref = f32[2,4,3,256]{3,2,1,0:T(4,128)} custom-call(s32[2,1,256]{2,1,0:T(1,128)} %tile.15.lo_ref, s32[2,1,256]{2,1,0:T(1,128)} %tile.17.hi_ref, bf16[2,64,1024]{2,1,0:T(8,128)(2,1)} %get-tuple-element.156.q_ref, bf16[2,64,1024]{2,1,0:T(8,128)(2,1)} %bitcast.147, bf16[8,2,2,2,16,2048]{5,4,3,2,1,0:T(8,128)(2,1)} %bitcast.120, ...), custom_call_target="tpu_custom_call" | custom-call | flops 2147483648 | bytes 12582912 | tf_op jit(solution)/shard_map/softmax_stats/pallas_call | solution.py:209
  114.0 5.2 %collective-permute-start.5 = (bf16[2,64,1024]{2,1,0:T(8,128)(2,1)S(1)}, bf16[2,64,1024]{2,1,0:T(8,128)(2,1)S(1)}, u32[]{:S(2)}, u32[]{:S(2)}) collective-permute-start(bf16[2,64,1024]{2,1,0:T(8,128)(2,1)S(1)} %maximum_select_fusion.6), channel_id=1, source_target_pairs={{0,4},{1,5},{2,6},{3,7},{4,0},{5,1},{6,2},{7,3},{8,12},{9,13},{10,... | collective-permute-start | bytes 786440 | tf_op jit(solution)/shard_map/ppermute | solution.py:287
  119.2 2.9 %collective-permute-start.6 = (f32[2,4,3,256]{3,2,1,0:T(4,128)S(1)}, f32[2,4,3,256]{3,2,1,0:T(4,128)S(1)}, u32[]{:S(2)}, u32[]{:S(2)}) collective-permute-start(f32[2,4,3,256]{3,2,1,0:T(4,128)S(1)} %copy-done.13), channel_id=1, source_target_pairs={{0,8},{1,9},{2,10},{3,11},{4,12},{5,13},{6,14},{7,15},{8,0},{9,1},... | collective-permute-start | bytes 73736 | tf_op jit(solution)/shard_map/ppermute | solution.py:287
  122.1 5.5 %pad_maximum_fusion = bf16[3072,1024]{1,0:T(8,128)(2,1)} fusion(bf16[1024,1024]{1,0:T(8,128)(2,1)S(1)} %bitcast.146, bf16[1024,1024]{1,0:T(8,128)(2,1)} %bitcast.26, bf16[1024,1024]{1,0:T(8,128)(2,1)} %bitcast.25), kind=kLoop, calls=%fused_computation | loop fusion | flops 18874368 | bytes 12582912 | tf_op jit(solution)/shard_map/concatenate | solution.py:375
  131.7 9.9 %banded_grads.2 = (f32[2,2,64,512]{3,2,1,0:T(8,128)}, bf16[3,8,2,2,2,16,1024]{6,5,4,3,2,1,0:T(8,128)(2,1)}) custom-call(s32[2,1,256]{2,1,0:T(1,128)} %tile.15.lo_ref, s32[2,1,256]{2,1,0:T(1,128)} %tile.17.hi_ref, f32[2,4,3,256]{3,2,1,0:T(4,128)} %softmax_stats.1.one_ref, f32[2,4,3,256]{3,2,1,0:T(4,128)} %copy-done.17, ...), custom_call_target="tpu_custom_call" | custom-call | flops 3221225472 | bytes 12582912 | tf_op jit(solution)/shard_map/banded_grads/pallas_call | solution.py:225
  141.6 2.4 collective-permute-done.7
  145.0 2.0 collective-permute-start.9
  147.0 10.7 %convolution_convert_fusion.4 = bf16[1024,1024]{1,0:T(8,128)(2,1)S(1)} fusion(bf16[3072,1024]{1,0:T(8,128)(2,1)} %pad_maximum_fusion, bf16[3072,1024]{1,0:T(8,128)(2,1)} %bitcast.173), kind=kOutput, calls=%fused_computation.13 | convolution fusion | flops 6443499520 | bytes 14680064 | tf_op jit(solution)/shard_map/dot_general | solution.py:23
  157.7 3.4 %collective-permute-done.9 = f32[2,64,512]{2,1,0:T(8,128)S(1)} collective-permute-done((f32[2,64,512]{2,1,0:T(8,128)S(1)}, f32[2,64,512]{2,1,0:T(8,128)S(1)}, u32[]{:S(2)}, u32[]{:S(2)}) %collective-permute-start.9) | collective-permute-done | bytes 262176 | tf_op jit(solution)/shard_map/ppermute | solution.py:287
  162.2 2.6 collective-permute-done.11
  166.3 9.9 %banded_grads.3 = (f32[2,2,64,512]{3,2,1,0:T(8,128)}, bf16[3,8,2,2,2,16,1024]{6,5,4,3,2,1,0:T(8,128)(2,1)}) custom-call(s32[2,1,256]{2,1,0:T(1,128)} %tile.15.lo_ref, s32[2,1,256]{2,1,0:T(1,128)} %tile.17.hi_ref, f32[2,4,3,256]{3,2,1,0:T(4,128)} %softmax_stats.1.one_ref, f32[2,4,3,256]{3,2,1,0:T(4,128)} %copy-done.17, ...), custom_call_target="tpu_custom_call" | custom-call | flops 3221225472 | bytes 12582912 | tf_op jit(solution)/shard_map/banded_grads/pallas_call | solution.py:225
  177.9 2.0 collective-permute-start.13
  179.9 11.7 %convolution_convert_fusion.3 = bf16[1024,1024]{1,0:T(8,128)(2,1)} fusion(bf16[3072,1024]{1,0:T(8,128)(2,1)} %pad_maximum_fusion, bf16[3072,1024]{1,0:T(8,128)(2,1)} %bitcast.172), kind=kOutput, calls=%fused_computation.12 | convolution fusion | flops 6443499520 | bytes 14680064 | tf_op jit(solution)/shard_map/dot_general | solution.py:23
  191.5 5.1 %all-to-all-start.2 = ((bf16[8,64,1024]{2,1,0:T(8,128)(2,1)}), bf16[8,64,1024]{2,1,0:T(8,128)(2,1)}, u32[]{:S(2)}, u32[]{:S(2)}) async-start(bf16[8,64,1024]{2,1,0:T(8,128)(2,1)} %add_convert_fusion.1), calls=%async_computation.2 | async-start | bytes 2097152 | tf_op jit(solution)/shard_map/all_to_all | solution.py:389
  197.4 1.7 dynamic-slice_bitcast_fusion
  200.5 2.4 collective-permute-done.15
  203.5 19.9 %all-to-all-done.2 = bf16[8,64,1024]{2,1,0:T(8,128)(2,1)} async-done(((bf16[8,64,1024]{2,1,0:T(8,128)(2,1)}), bf16[8,64,1024]{2,1,0:T(8,128)(2,1)}, u32[]{:S(2)}, u32[]{:S(2)}) %all-to-all-start.2) | async-done | bytes 1048608 | tf_op jit(solution)/shard_map/all_to_all | solution.py:389
  224.6 4.2 %all-to-all-start.3 = ((bf16[8,64,1280]{2,1,0:T(8,128)(2,1)}), bf16[8,64,1280]{2,1,0:T(8,128)(2,1)S(1)}, u32[]{:S(2)}, u32[]{:S(2)}) async-start(bf16[8,64,1280]{2,1,0:T(8,128)(2,1)} %pad_maximum_fusion.3), calls=%async_computation.3 | async-start | bytes 2621440 | tf_op jit(solution)/shard_map/all_to_all | solution.py:389
  237.0 23.5 %all-to-all-done.3 = bf16[8,64,1280]{2,1,0:T(8,128)(2,1)S(1)} async-done(((bf16[8,64,1280]{2,1,0:T(8,128)(2,1)}), bf16[8,64,1280]{2,1,0:T(8,128)(2,1)S(1)}, u32[]{:S(2)}, u32[]{:S(2)}) %all-to-all-start.3) | async-done | bytes 1310752 | tf_op jit(solution)/shard_map/all_to_all | solution.py:389
  260.5 1.6 fusion.7
  (128 shorter events, 43.8 us)
Async XLA Ops:
  0.6 59.6 %copy-start = (bf16[1024,1024]{1,0:T(8,128)(2,1)S(1)}, bf16[1024,1024]{1,0:T(8,128)(2,1)}, u32[]{:S(2)}) copy-start(bf16[1024,1024]{1,0:T(8,128)(2,1)} %param.14) | copy-start | bytes 6291460
  6.4 5.4 %copy-start.18 = (s32[64]{0:T(128)S(1)}, s32[64]{0:T(128)}, u32[]{:S(2)}) copy-start(s32[64]{0:T(128)} %param.15) | copy-start | bytes 772
  6.4 5.5 %copy-start.19 = (s32[64]{0:T(128)S(1)}, s32[64]{0:T(128)}, u32[]{:S(2)}) copy-start(s32[64]{0:T(128)} %param.16) | copy-start | bytes 772
  6.4 5.5 %copy-start.8 = (bf16[64,1024]{1,0:T(8,128)(2,1)S(1)}, bf16[64,1024]{1,0:T(8,128)(2,1)}, u32[]{:S(2)}) copy-start(bf16[64,1024]{1,0:T(8,128)(2,1)} %param.17) | copy-start | bytes 393220
  6.4 5.6 %copy-start.16 = (bf16[64,1024]{1,0:T(8,128)(2,1)S(1)}, bf16[64,1024]{1,0:T(8,128)(2,1)}, u32[]{:S(2)}) copy-start(bf16[64,1024]{1,0:T(8,128)(2,1)} %param.11) | copy-start | bytes 393220
  6.4 35.4 %all-to-all-start = ((bf16[8,2,2,2,16,1024]{5,4,3,2,1,0:T(8,128)(2,1)}), bf16[8,2,2,2,16,1024]{5,4,3,2,1,0:T(8,128)(2,1)}, u32[]{:S(2)}, u32[]{:S(2)}) async-start(bf16[8,2,2,2,16,1024]{5,4,3,2,1,0:T(8,128)(2,1)} %maximum_bitcast_fusion), calls=%async_computation | async-start | bytes 4194304 | tf_op jit(solution)/shard_map/all_to_all | solution.py:326
  12.0 15.1 %collective-permute-start = (bf16[144,1024]{1,0:T(8,128)(2,1)S(1)}, bf16[144,1024]{1,0:T(8,128)(2,1)S(1)}, u32[]{:S(2)}, u32[]{:S(2)}) collective-permute-start(bf16[144,1024]{1,0:T(8,128)(2,1)S(1)} %fusion.2), channel_id=1, source_target_pairs={{0,0},{2,1},{4,2},{6,3},{8,4},{10,5},{12,6},{14,7},{1,8},{3,9},{5,... | collective-permute-start | bytes 884744 | tf_op jit(solution)/shard_map/ppermute | solution.py:327
  12.7 29.1 %collective-permute-start.1 = (bf16[144,1024]{1,0:T(8,128)(2,1)S(1)}, bf16[144,1024]{1,0:T(8,128)(2,1)}, u32[]{:S(2)}, u32[]{:S(2)}) collective-permute-start(bf16[144,1024]{1,0:T(8,128)(2,1)S(1)} %fusion.2), channel_id=1, source_target_pairs={{1,0},{3,1},{5,2},{7,3},{9,4},{11,5},{13,6},{15,7},{0,8},{2,9},{4,... | collective-permute-start | bytes 884744 | tf_op jit(solution)/shard_map/ppermute | solution.py:328
  21.7 3.0 %copy-start.7 = (bf16[1024,1024]{1,0:T(8,128)(2,1)S(1)}, bf16[1024,1024]{1,0:T(8,128)(2,1)}, u32[]{:S(2)}) copy-start(bf16[1024,1024]{1,0:T(8,128)(2,1)} %param.12) | copy-start | bytes 6291460
  41.8 38.6 %all-to-all-start.1 = ((bf16[8,2,2,2,16,1024]{5,4,3,2,1,0:T(8,128)(2,1)}), bf16[8,2,2,2,16,1024]{5,4,3,2,1,0:T(8,128)(2,1)}, u32[]{:S(2)}, u32[]{:S(2)}) async-start(bf16[8,2,2,2,16,1024]{5,4,3,2,1,0:T(8,128)(2,1)} %maximum_bitcast_fusion.1), calls=%async_computation.1 | async-start | bytes 4194304 | tf_op jit(solution)/shard_map/all_to_all | solution.py:331
  58.8 3.0 %copy-start.1 = (bf16[1024,2048]{1,0:T(8,128)(2,1)S(1)}, bf16[1024,2048]{1,0:T(8,128)(2,1)}, u32[]{:S(2)}) copy-start(bf16[1024,2048]{1,0:T(8,128)(2,1)} %pad_maximum_fusion.1) | copy-start | bytes 12582916
  80.4 12.3 %collective-permute-start.2 = (bf16[8,2,16,1024]{3,2,1,0:T(8,128)(2,1)S(1)}, bf16[8,2,16,1024]{3,2,1,0:T(8,128)(2,1)S(1)}, u32[]{:S(2)}, u32[]{:S(2)}) collective-permute-start(bf16[8,2,16,1024]{3,2,1,0:T(8,128)(2,1)S(1)} %get-tuple-element.109), channel_id=1, source_target_pairs={{0,1},{1,2},{2,3},{3,4},{4,5},{5,6},{6,7},{8,9},{9,10},{10,11},{11... | collective-permute-start | bytes 1572872 | tf_op jit(solution)/shard_map/ppermute | solution.py:287
  81.8 10.8 %collective-permute-start.3 = (bf16[8,2,16,1024]{3,2,1,0:T(8,128)(2,1)S(1)}, bf16[8,2,16,1024]{3,2,1,0:T(8,128)(2,1)S(1)}, u32[]{:S(2)}, u32[]{:S(2)}) collective-permute-start(bf16[8,2,16,1024]{3,2,1,0:T(8,128)(2,1)S(1)} %get-tuple-element.110), channel_id=1, source_target_pairs={{1,0},{2,1},{3,2},{4,3},{5,4},{6,5},{7,6},{9,8},{10,9},{11,10},{12... | collective-permute-start | bytes 1572872 | tf_op jit(solution)/shard_map/ppermute | solution.py:287
  98.5 12.4 %collective-permute-start.4 = (bf16[64,1024]{1,0:T(8,128)(2,1)S(1)}, bf16[64,1024]{1,0:T(8,128)(2,1)S(1)}, u32[]{:S(2)}, u32[]{:S(2)}) collective-permute-start(bf16[64,1024]{1,0:T(8,128)(2,1)S(1)} %multiply_convert_fusion), channel_id=1, source_target_pairs={{0,8},{1,9},{2,10},{3,11},{4,12},{5,13},{6,14},{7,15},{8,0},{9,1},... | collective-permute-start | bytes 393224 | tf_op jit(solution)/shard_map/ppermute | solution.py:287
  113.7 5.5 %copy-start.13 = (f32[2,4,3,256]{3,2,1,0:T(4,128)S(1)}, f32[2,4,3,256]{3,2,1,0:T(4,128)}, u32[]{:S(2)}) copy-start(f32[2,4,3,256]{3,2,1,0:T(4,128)} %softmax_stats.1.one_ref) | copy-start | bytes 73732
  114.0 14.5 %collective-permute-start.5 = (bf16[2,64,1024]{2,1,0:T(8,128)(2,1)S(1)}, bf16[2,64,1024]{2,1,0:T(8,128)(2,1)S(1)}, u32[]{:S(2)}, u32[]{:S(2)}) collective-permute-start(bf16[2,64,1024]{2,1,0:T(8,128)(2,1)S(1)} %maximum_select_fusion.6), channel_id=1, source_target_pairs={{0,4},{1,5},{2,6},{3,7},{4,0},{5,1},{6,2},{7,3},{8,12},{9,13},{10,... | collective-permute-start | bytes 786440 | tf_op jit(solution)/shard_map/ppermute | solution.py:287
  119.2 9.3 %collective-permute-start.6 = (f32[2,4,3,256]{3,2,1,0:T(4,128)S(1)}, f32[2,4,3,256]{3,2,1,0:T(4,128)S(1)}, u32[]{:S(2)}, u32[]{:S(2)}) collective-permute-start(f32[2,4,3,256]{3,2,1,0:T(4,128)S(1)} %copy-done.13), channel_id=1, source_target_pairs={{0,8},{1,9},{2,10},{3,11},{4,12},{5,13},{6,14},{7,15},{8,0},{9,1},... | collective-permute-start | bytes 73736 | tf_op jit(solution)/shard_map/ppermute | solution.py:287
  122.1 5.5 %copy-start.12 = (bf16[1,1,64,1024]{3,2,1,0:T(8,128)(2,1)S(1)}, bf16[1,1,64,1024]{3,2,1,0:T(8,128)(2,1)}, u32[]{:S(2)}) copy-start(bf16[1,1,64,1024]{3,2,1,0:T(8,128)(2,1)} %fusion.37) | copy-start | bytes 393220
  128.5 13.1 %copy-start.4 = (bf16[2,64,1024]{2,1,0:T(8,128)(2,1)}, bf16[2,64,1024]{2,1,0:T(8,128)(2,1)S(1)}, u32[]{:S(2)}) copy-start(bf16[2,64,1024]{2,1,0:T(8,128)(2,1)S(1)} %collective-permute-done.5) | copy-start | bytes 786436
  130.0 14.1 %collective-permute-start.7 = (bf16[2,2,64,1024]{3,2,0,1:T(8,128)(2,1)}, bf16[2,2,64,1024]{3,2,0,1:T(8,128)(2,1)S(1)}, u32[]{:S(2)}, u32[]{:S(2)}) collective-permute-start(bf16[2,2,64,1024]{3,2,0,1:T(8,128)(2,1)} %maximum_select_fusion.3), channel_id=1, source_target_pairs={{0,2},{1,3},{2,0},{3,1},{4,6},{5,7},{6,4},{7,5},{8,10},{9,11},{10,... | collective-permute-start | bytes 1572872 | tf_op jit(solution)/shard_map/ppermute | solution.py:287
  141.6 2.6 copy-start.11
  144.0 13.7 %copy-start.5 = (bf16[2,2,64,1024]{3,2,0,1:T(8,128)(2,1)}, bf16[2,2,64,1024]{3,2,0,1:T(8,128)(2,1)S(1)}, u32[]{:S(2)}) copy-start(bf16[2,2,64,1024]{3,2,0,1:T(8,128)(2,1)S(1)} %collective-permute-done.7) | copy-start | bytes 1572868
  144.3 16.9 %collective-permute-start.10 = (bf16[2,2,2,64,1024]{4,3,0,1,2:T(8,128)(2,1)S(1)}, bf16[2,2,2,64,1024]{4,3,0,1,2:T(8,128)(2,1)S(1)}, u32[]{:S(2)}, u32[]{:S(2)}) collective-permute-start(bf16[2,2,2,64,1024]{4,3,0,1,2:T(8,128)(2,1)S(1)} %maximum_select_fusion), channel_id=1, source_target_pairs={{0,1},{1,0},{2,3},{3,2},{4,5},{5,4},{6,7},{7,6},{8,9},{9,8},{10,11... | collective-permute-start | bytes 3145736 | tf_op jit(solution)/shard_map/ppermute | solution.py:287
  144.4 13.4 %collective-permute-start.8 = (f32[2,64,512]{2,1,0:T(8,128)S(1)}, f32[2,64,512]{2,1,0:T(8,128)S(1)}, u32[]{:S(2)}, u32[]{:S(2)}) collective-permute-start(f32[2,64,512]{2,1,0:T(8,128)S(1)} %get-tuple-element.147), channel_id=1, source_target_pairs={{0,0},{1,2},{2,4},{3,6},{4,8},{5,10},{6,12},{7,14},{8,1},{9,3},{10... | collective-permute-start | bytes 786440 | tf_op jit(solution)/shard_map/ppermute | solution.py:287
  145.0 16.1 %collective-permute-start.9 = (f32[2,64,512]{2,1,0:T(8,128)S(1)}, f32[2,64,512]{2,1,0:T(8,128)S(1)}, u32[]{:S(2)}, u32[]{:S(2)}) collective-permute-start(f32[2,64,512]{2,1,0:T(8,128)S(1)} %get-tuple-element.148), channel_id=1, source_target_pairs={{0,1},{1,3},{2,5},{3,7},{4,9},{5,11},{6,13},{7,15},{8,0},{9,2},{10... | collective-permute-start | bytes 786440 | tf_op jit(solution)/shard_map/ppermute | solution.py:287
  162.2 2.7 %collective-permute-start.11 = (bf16[8,64,1024]{2,1,0:T(8,128)(2,1)S(1)}, bf16[8,64,1024]{2,1,0:T(8,128)(2,1)S(1)}, u32[]{:S(2)}, u32[]{:S(2)}) collective-permute-start(bf16[8,64,1024]{2,1,0:T(8,128)(2,1)S(1)} %get-tuple-element.152), channel_id=1, source_target_pairs={{0,1},{1,0},{2,3},{3,2},{4,5},{5,4},{6,7},{7,6},{8,9},{9,8},{10,11... | collective-permute-start | bytes 3145736 | tf_op jit(solution)/shard_map/ppermute | solution.py:287
  177.2 19.5 %collective-permute-start.12 = (f32[2,64,512]{2,1,0:T(8,128)S(1)}, f32[2,64,512]{2,1,0:T(8,128)S(1)}, u32[]{:S(2)}, u32[]{:S(2)}) collective-permute-start(f32[2,64,512]{2,1,0:T(8,128)S(1)} %get-tuple-element.164), channel_id=1, source_target_pairs={{0,0},{1,2},{2,4},{3,6},{4,8},{5,10},{6,12},{7,14},{8,1},{9,3},{10... | collective-permute-start | bytes 786440 | tf_op jit(solution)/shard_map/ppermute | solution.py:287
  177.9 18.8 %collective-permute-start.13 = (f32[2,64,512]{2,1,0:T(8,128)S(1)}, f32[2,64,512]{2,1,0:T(8,128)S(1)}, u32[]{:S(2)}, u32[]{:S(2)}) collective-permute-start(f32[2,64,512]{2,1,0:T(8,128)S(1)} %get-tuple-element.165), channel_id=1, source_target_pairs={{0,1},{1,3},{2,5},{3,7},{4,9},{5,11},{6,13},{7,15},{8,0},{9,2},{10... | collective-permute-start | bytes 786440 | tf_op jit(solution)/shard_map/ppermute | solution.py:287
  191.5 31.8 %all-to-all-start.2 = ((bf16[8,64,1024]{2,1,0:T(8,128)(2,1)}), bf16[8,64,1024]{2,1,0:T(8,128)(2,1)}, u32[]{:S(2)}, u32[]{:S(2)}) async-start(bf16[8,64,1024]{2,1,0:T(8,128)(2,1)} %add_convert_fusion.1), calls=%async_computation.2 | async-start | bytes 2097152 | tf_op jit(solution)/shard_map/all_to_all | solution.py:389
  199.1 3.8 %collective-permute-start.14 = (bf16[8,64,1024]{2,1,0:T(8,128)(2,1)S(1)}, bf16[8,64,1024]{2,1,0:T(8,128)(2,1)S(1)}, u32[]{:S(2)}, u32[]{:S(2)}) collective-permute-start(bf16[8,64,1024]{2,1,0:T(8,128)(2,1)S(1)} %get-tuple-element.173), channel_id=1, source_target_pairs={{0,1},{1,0},{2,3},{3,2},{4,5},{5,4},{6,7},{7,6},{8,9},{9,8},{10,11... | collective-permute-start | bytes 3145736 | tf_op jit(solution)/shard_map/ppermute | solution.py:287
  200.5 2.5 collective-permute-start.15
  224.6 35.9 %all-to-all-start.3 = ((bf16[8,64,1280]{2,1,0:T(8,128)(2,1)}), bf16[8,64,1280]{2,1,0:T(8,128)(2,1)S(1)}, u32[]{:S(2)}, u32[]{:S(2)}) async-start(bf16[8,64,1280]{2,1,0:T(8,128)(2,1)} %pad_maximum_fusion.3), calls=%async_computation.3 | async-start | bytes 2621440 | tf_op jit(solution)/shard_map/all_to_all | solution.py:389
  (8 other events, 12.9 us)

commit v8 on v7

--- a/solution.py
+++ b/solution.py
@@ -153,16 +153,22 @@
         probs.append(p.astype(BF16))
         d_scores.append((p * (dp - mean)).astype(BF16))
 
-    shape = part_ref.shape[1:2] + part_ref.shape[3:5] + (LANES,)
+    shape = part_ref.shape[1:4] + (LANES,)
     low, high, both = slice(0, mid), slice(mid, wide), slice(0, wide)
-    places = (((0, 0), (2, 0)), ((0, 1), (2, 1)), ((1, 0), (1, 1)))
+    first = pl.program_id(0) == 0
 
     def back(weights, x_ref, cols):
-        for which, lanes, place in zip((0, 0, 1), (low, high, both), places):
-            x = nn_dot(weights[which][:, lanes], x_ref[lanes, :]).astype(BF16)
-            for i, (section, side) in enumerate(place):
-                rows = x[i * CHUNK : (i + 1) * CHUNK].reshape(shape)
-                part_ref[section, :, side, :, :, cols] = rows
+        below, above, middle = [
+            nn_dot(weights[which][:, lanes], x_ref[lanes, :]).astype(BF16)
+            for which, lanes in zip((0, 0, 1), (low, high, both))
+        ]
+        one, two = below[CHUNK:], above[CHUNK:]
+        rows = (
+            below[:CHUNK], above[:CHUNK], jnp.where(first, two, one),
+            middle[:CHUNK], middle[CHUNK:], jnp.where(first, one, two),
+        )
+        for i, x in enumerate(rows):
+            part_ref[i, :, :, :, cols] = x.reshape(shape)
 
     back(d_scores, bq_ref, slice(0, LANES))
     back(probs, bg_ref, slice(LANES, 2 * LANES))
@@ -220,7 +226,7 @@
         )(lo, hi, queries, d_context, *tokens, *tokens)
 
     parts = pl.BlockSpec(
-        (3, src, 2, tok, None, W, 2 * LANES), lambda b, g: (0, 0, 0, 0, b, 0, g)
+        (6, src, tok, None, W, 2 * LANES), lambda b, g: (0, 0, 0, b, 0, g)
     )
     return pl.pallas_call(
         grads_kernel,
@@ -231,7 +237,7 @@
         ],
         out_shape=[
             jax.ShapeDtypeStruct((2, 2, n_query, groups * LANES), F32),
-            jax.ShapeDtypeStruct((3, src, 2, tok, 2, W, 2 * groups * LANES), BF16),
+            jax.ShapeDtypeStruct((6, src, tok, 2, W, 2 * groups * LANES), BF16),
         ],
         scratch_shapes=[bias] + [operand] * 4,
         cost_estimate=pl.CostEstimate(
@@ -240,6 +246,45 @@
         name="banded_grads",
         **common,
     )(lo, hi, *stats, queries, d_context, *tokens, *tokens)
+
+
+TILE = 512
+
+
+def project_kernel(x_ref, wk_ref, wv_ref, out_ref):
+    n = pl.program_id(0)
+    half = pl.num_programs(0) // 2
+
+    @pl.when(n < half)
+    def _():
+        out_ref[...] = nn_dot(x_ref[...], wk_ref[...]).astype(BF16)
+
+    @pl.when(n >= half)
+    def _():
+        out_ref[...] = nn_dot(x_ref[...], wv_ref[...]).astype(BF16)
+
+
+def project_rows(x, key_weight, value_weight):
+    width = x.shape[1]
+    half = width // TILE
+    return pl.pallas_call(
+        project_kernel,
+        grid=(2 * half,),
+        in_specs=[
+            pl.BlockSpec(x.shape, lambda n: (0, 0)),
+            pl.BlockSpec((width, TILE), lambda n: (0, jnp.minimum(n, half - 1))),
+            pl.BlockSpec((width, TILE), lambda n: (0, jnp.maximum(n - half, 0))),
+        ],
+        out_specs=pl.BlockSpec((x.shape[0], TILE), lambda n: (0, n)),
+        out_shape=jax.ShapeDtypeStruct((x.shape[0], 2 * width), BF16),
+        compiler_params=pltpu.CompilerParams(dimension_semantics=("arbitrary",)),
+        cost_estimate=pl.CostEstimate(
+            flops=4 * x.shape[0] * width * width,
+            bytes_accessed=6 * x.shape[0] * width + 4 * width * width,
+            transcendentals=0,
+        ),
+        name="project_rows",
+    )(x, key_weight, value_weight)
 
 
 def flips(n_dev, bit):
@@ -351,12 +396,18 @@
 
     edge_kv = project(edge)
     up = [(i, i + 1) for i in range(n_dev - 1) if (i + 1) % src]
+    local = jnp.stack([edge[:, 0, :, 1], edge[:, 1, :, 0]], axis=2)
+    rows = [x.reshape(-1, width) for x in (edge[:, 0], edge[:, 1], local)]
+    rows = jnp.concatenate(rows, axis=0)
+    rows = jnp.pad(rows, ((0, rows.shape[0]), (0, 0)))
     low = Move(edge[:, 1, :, 1], up)
     high = Move(edge[:, 0, :, 0], [(target, source) for source, target in up])
-    middle, edge_kv, q_pair, g_pair, lo, hi, low.block, high.block = fence(
-        (middle, edge_kv, q_pair, g_pair, lo, hi, low.block, high.block)
-    )
-    middle_kv = beside([low, high], project, middle)
+    middle, edge_kv, q_pair, g_pair, lo, hi, rows, low.block, high.block = fence(
+        (middle, edge_kv, q_pair, g_pair, lo, hi, rows, low.block, high.block)
+    )
+    middle_kv = beside(
+        [low, high], project_rows, middle.reshape(-1, width), key_weight, value_weight
+    ).reshape(middle.shape[:-1] + (2 * width,))
     ext = jnp.stack([low.come, high.come], axis=1)
     ext_kv = project(ext)
     tokens = (edge_kv, middle_kv, ext_kv)
@@ -368,13 +419,16 @@
     )
     swap = Move(stats, flips(n_dev, bits - 1))
 
-    def all_sources(edge, middle, ext):
-        below = jnp.stack([ext[:, 0], edge[:, 1, :, 0]], axis=2)
-        above = jnp.stack([edge[:, 0, :, 1], ext[:, 1]], axis=2)
-        halo = jnp.stack([below, above], axis=1)
-        return jnp.concatenate([x.reshape(-1, width) for x in (edge, middle, halo)], axis=0)
-
-    sources = beside([gather, swap], all_sources, edge, middle, ext)
+    def fill(rows, middle, low, high):
+        late = (middle[:, 0], middle[:, 1], jnp.stack([low, high], axis=2))
+        at = rows.shape[0] // 2
+        for x in late:
+            x = x.reshape(-1, width)
+            rows = lax.dynamic_update_slice_in_dim(rows, x, at, 0)
+            at += x.shape[0]
+        return rows
+
+    sources = beside([gather, swap], fill, rows, middle, low.come, high.come)
 
     core = me & 1
     chips = [[2 * k + c for k in range(src)] for c in range(2)]

time: 266 us -> 267 us (level)
  waiting for transfers between devices: 79.9 us -> 62.9 us
  local copies, waits for them, and re-layouts: 25.4 us -> 35.1 us
  Pallas kernels: 32.1 us -> 40.8 us
  matrix products: 47.6 us -> 39.6 us
  other arithmetic: 27.1 us -> 32.5 us
    all_to_all x1, waiting for transfers between devices: 11 us -> 0.01 us  [shards(): lax.all_to_all(inner, 'tm', 0, 0, axis_index_groups=halves, tiled=True)]
    dot_general x4 -> x3, matrix products: 21.8 us -> 12.5 us  [nn_dot(): return jnp.dot(a, b, preferred_element_type=F32)]
    pallas_call x0 -> x1, Pallas kernels: none -> 8.65 us  [project_rows(): pl.pallas_call(project_kernel, grid=(2 * half,), in_specs=[pl.BlockSpec(x...]
    concatenate x1, other arithmetic: 5.51 us -> 11.5 us  [shards(): rows = jnp.concatenate(rows, axis=0)]
    ppermute x1, waiting for transfers between devices: 14.7 us -> 10.8 us  [shards(): two = lax.ppermute(letter, 'tm', [(b, a) for a, b in owner_two])]
    slice x0 -> x2, local copies, waits for them, and re-layouts: none -> 3.43 us  [the longest x1 1.72 us: fill(): late = (middle[:, 0], middle[:, 1], jnp.stack([low, high], axis=2))]
    dynamic_update_slice x0 -> x3, local copies, waits for them, and re-layouts: none -> 3.16 us  [fill(): rows = lax.dynamic_update_slice_in_dim(rows, x, at, 0)]
    ppermute x14, starting transfers between devices: 18.5 us -> 21.4 us  [beside(): lax.ppermute(away, 'tm', perm)]
  transfers between devices with their start and end apart: 20 -> 20, of which waited for: 8 -> 7; matrix products, arithmetic and copies ran while one was open for 28% -> 31% of each run, Pallas kernels for 8% -> 12%
where the time goes in v8:
time: 267 us; the launch traced here: 266 us
  waiting for transfers between devices  62.9 us (24%)
  starting transfers between devices  53.5 us (20%)
  Pallas kernels  40.8 us (15%)
  matrix products  39.6 us (15%)
  local copies, waits for them, and re-layouts  35.1 us (13%)
  other arithmetic  32.5 us (12%)
    all_to_all x2, waiting for transfers between devices, scatter(): lax.all_to_all(block, 'tm', 0, 0, axis_index_groups=chips, tiled=True)  43.6 us
    dot_general x4, matrix products, tn_dot(): lax.dot_general(a, b, (((0,), (0,)), ((), ())), preferred_element_type=F32)  25.5 us
    ppermute x14, starting transfers between devices, beside(): lax.ppermute(away, 'tm', perm)  21.4 us
    pallas_call x2, Pallas kernels, attention(): pl.pallas_call(grads_kernel, in_specs=[flat, flat, table, table, rows, ro...  19.7 us
    all_to_all x1, starting transfers between devices, shards(): lax.all_to_all(inner, 'tm', 0, 0, axis_index_groups=halves, tiled=True)  13.1 us
    dot_general x3, matrix products, nn_dot(): return jnp.dot(a, b, preferred_element_type=F32)  12.5 us
    pallas_call x1, Pallas kernels, attention(): pl.pallas_call(stats_kernel, in_specs=[flat, flat, rows, rows] + sections...  12.4 us
    concatenate x1, other arithmetic, shards(): rows = jnp.concatenate(rows, axis=0)  11.5 us
  transfers between devices with their start and end apart: 20, of which 7 were waited for; matrix products, arithmetic and copies ran while one was open for 31% of the time, Pallas kernels for 12%

profile of v8, /device:TPU:0, one launch (start us, length us, event | category | flops | bytes accessed | tf_op | source)
XLA Modules:
  0.0 265.6 jit_solution(14289122447620705342)
XLA Ops:
  0.6 3.6 %copy.21 = bf16[1024,2,1024]{2,0,1:T(8,128)(2,1)S(1)} copy(bf16[1024,2,1024]{2,1,0:T(2,128)(2,1)} %param.10) | data formatting | bytes 8388608 | tf_op args[0]
  6.5 5.3 %all-to-all-start = ((bf16[8,2,2,2,16,1024]{5,4,3,2,1,0:T(8,128)(2,1)}), bf16[8,2,2,2,16,1024]{5,4,3,2,1,0:T(8,128)(2,1)}, u32[]{:S(2)}, u32[]{:S(2)}) async-start(bf16[8,2,2,2,16,1024]{5,4,3,2,1,0:T(8,128)(2,1)} %maximum_bitcast_fusion), calls=%async_computation | async-start | bytes 4194304 | tf_op jit(solution)/shard_map/all_to_all | solution.py:371
  13.3 4.8 %collective-permute-start.1 = (bf16[144,1024]{1,0:T(8,128)(2,1)S(1)}, bf16[144,1024]{1,0:T(8,128)(2,1)S(1)}, u32[]{:S(2)}, u32[]{:S(2)}) collective-permute-start(bf16[144,1024]{1,0:T(8,128)(2,1)S(1)} %fusion.7), channel_id=1, source_target_pairs={{1,0},{3,1},{5,2},{7,3},{9,4},{11,5},{13,6},{15,7},{0,8},{2,9},{4,... | collective-permute-start | bytes 884744 | tf_op jit(solution)/shard_map/ppermute | solution.py:373
  18.1 5.5 %copy.24 = bf16[1024,2,1024]{2,0,1:T(8,128)(2,1)} copy(bf16[1024,2,1024]{2,1,0:T(2,128)(2,1)} %param.10) | data formatting | bytes 8388608 | tf_op jit(solution)/shard_map/optimization_barrier | solution.py:366
  23.6 1.7 fusion.21
  28.4 2.5 pad_maximum_fusion
  30.9 10.8 %collective-permute-done.1 = bf16[144,1024]{1,0:T(8,128)(2,1)S(1)} collective-permute-done((bf16[144,1024]{1,0:T(8,128)(2,1)S(1)}, bf16[144,1024]{1,0:T(8,128)(2,1)S(1)}, u32[]{:S(2)}, u32[]{:S(2)}) %collective-permute-start.1) | collective-permute-done | bytes 294944 | tf_op jit(solution)/shard_map/ppermute | solution.py:373
  41.7 13.1 %all-to-all-start.1 = ((bf16[8,2,2,2,16,1024]{5,4,3,2,1,0:T(8,128)(2,1)}), bf16[8,2,2,2,16,1024]{5,4,3,2,1,0:T(8,128)(2,1)}, u32[]{:S(2)}, u32[]{:S(2)}) async-start(bf16[8,2,2,2,16,1024]{5,4,3,2,1,0:T(8,128)(2,1)} %maximum_bitcast_fusion.1), calls=%async_computation.1 | async-start | bytes 4194304 | tf_op jit(solution)/shard_map/all_to_all | solution.py:376
  56.4 2.1 slice_bitcast_fusion.2
  58.5 2.1 slice_bitcast_fusion
  64.8 11.5 %fusion.4 = bf16[3072,1024]{1,0:T(8,128)(2,1)} fusion(bf16[512,1024]{1,0:T(8,128)(2,1)S(1)} %bitcast.144, bf16[512,1024]{1,0:T(8,128)(2,1)S(1)} %bitcast.146, bf16[512,1024]{1,0:T(8,128)(2,1)S(1)} %bitcast.145), kind=kLoop, calls=%fused_computation.5 | loop fusion | flops 31457280 | bytes 9437184 | tf_op jit(solution)/shard_map/concatenate | solution.py:401
  76.3 7.7 %convolution_convert_fusion = bf16[1024,2048]{1,0:T(8,128)(2,1)} fusion(bf16[1024,1024]{1,0:T(8,128)(2,1)} %bitcast.9, bf16[1024,2048]{1,0:T(8,128)(2,1)S(1)} %copy-done.1), kind=kOutput, calls=%fused_computation.7 | convolution fusion | flops 4297064448 | bytes 10485760 | tf_op jit(solution)/shard_map/dot_general | solution.py:31
  84.0 2.4 collective-permute-start.2
  88.6 8.6 %project_rows.1 = bf16[1024,2048]{1,0:T(8,128)(2,1)} custom-call(bf16[1024,1024]{1,0:T(8,128)(2,1)} %bitcast.22.x_ref, bf16[1024,1024]{1,0:T(8,128)(2,1)} %wk_ref, bf16[1024,1024]{1,0:T(8,128)(2,1)} %wv_ref), custom_call_target="tpu_custom_call" | custom-call | flops 4294967296 | bytes 10485760 | tf_op jit(solution)/shard_map/project_rows/pallas_call | solution.py:270
  97.5 1.9 copy-done.2
  99.5 3.7 %convolution_convert_fusion.1 = bf16[512,2048]{1,0:T(8,128)(2,1)} fusion(bf16[512,1024]{1,0:T(8,128)(2,1)S(1)} %bitcast.164, bf16[1024,2048]{1,0:T(8,128)(2,1)S(1)} %copy-done.2), kind=kOutput, calls=%fused_computation.8 | convolution fusion | flops 2148532224 | bytes 7340032 | tf_op jit(solution)/shard_map/dot_general | solution.py:31
  104.2 12.4 %softmax_stats.1.one_ref = f32[2,4,3,256]{3,2,1,0:T(4,128)} custom-call(s32[2,1,256]{2,1,0:T(1,128)} %tile.15.lo_ref, s32[2,1,256]{2,1,0:T(1,128)} %tile.17.hi_ref, bf16[2,64,1024]{2,1,0:T(8,128)(2,1)} %get-tuple-element.164.q_ref, bf16[2,64,1024]{2,1,0:T(8,128)(2,1)} %bitcast.141, bf16[8,2,2,2,16,2048]{5,4,3,2,1,0:T(8,128)(2,1)} %bitcast.115, ...), custom_call_target="tpu_custom_call" | custom-call | flops 2147483648 | bytes 12582912 | tf_op jit(solution)/shard_map/softmax_stats/pallas_call | solution.py:215
  118.4 3.8 %collective-permute-start.5 = (bf16[2,64,1024]{2,1,0:T(8,128)(2,1)S(1)}, bf16[2,64,1024]{2,1,0:T(8,128)(2,1)S(1)}, u32[]{:S(2)}, u32[]{:S(2)}) collective-permute-start(bf16[2,64,1024]{2,1,0:T(8,128)(2,1)S(1)} %maximum_select_fusion.6), channel_id=1, source_target_pairs={{0,4},{1,5},{2,6},{3,7},{4,0},{5,1},{6,2},{7,3},{8,12},{9,13},{10,... | collective-permute-start | bytes 786440 | tf_op jit(solution)/shard_map/ppermute | solution.py:332
  122.2 2.9 %collective-permute-start.6 = (f32[2,4,3,256]{3,2,1,0:T(4,128)S(1)}, f32[2,4,3,256]{3,2,1,0:T(4,128)S(1)}, u32[]{:S(2)}, u32[]{:S(2)}) collective-permute-start(f32[2,4,3,256]{3,2,1,0:T(4,128)S(1)} %copy-done.14), channel_id=1, source_target_pairs={{0,8},{1,9},{2,10},{3,11},{4,12},{5,13},{6,14},{7,15},{8,0},{9,1},... | collective-permute-start | bytes 73736 | tf_op jit(solution)/shard_map/ppermute | solution.py:332
  132.0 9.9 %banded_grads.2 = (f32[2,2,64,512]{3,2,1,0:T(8,128)}, bf16[6,8,2,2,16,1024]{5,4,3,2,1,0:T(8,128)(2,1)}) custom-call(s32[2,1,256]{2,1,0:T(1,128)} %tile.15.lo_ref, s32[2,1,256]{2,1,0:T(1,128)} %tile.17.hi_ref, f32[2,4,3,256]{3,2,1,0:T(4,128)} %softmax_stats.1.one_ref, f32[2,4,3,256]{3,2,1,0:T(4,128)} %copy-done.18, ...), custom_call_target="tpu_custom_call" | custom-call | flops 3221225472 | bytes 12582912 | tf_op jit(solution)/shard_map/banded_grads/pallas_call | solution.py:231
  144.5 3.1 %collective-permute-start.9 = (f32[2,64,512]{2,1,0:T(8,128)S(1)}, f32[2,64,512]{2,1,0:T(8,128)S(1)}, u32[]{:S(2)}, u32[]{:S(2)}) collective-permute-start(f32[2,64,512]{2,1,0:T(8,128)S(1)} %get-tuple-element.156), channel_id=1, source_target_pairs={{0,1},{1,3},{2,5},{3,7},{4,9},{5,11},{6,13},{7,15},{8,0},{9,2},{10... | collective-permute-start | bytes 786440 | tf_op jit(solution)/shard_map/ppermute | solution.py:332
  147.6 10.7 %convolution_convert_fusion.3 = bf16[1024,1024]{1,0:T(8,128)(2,1)S(1)} fusion(bf16[3072,1024]{1,0:T(8,128)(2,1)} %constant_dynamic-update-slice_fusion, bf16[3072,1024]{1,0:T(8,128)(2,1)} %bitcast.176), kind=kOutput, calls=%fused_computation.16 | convolution fusion | flops 6443499520 | bytes 14680064 | tf_op jit(solution)/shard_map/dot_general | solution.py:23
  158.3 2.9 %collective-permute-done.9 = f32[2,64,512]{2,1,0:T(8,128)S(1)} collective-permute-done((f32[2,64,512]{2,1,0:T(8,128)S(1)}, f32[2,64,512]{2,1,0:T(8,128)S(1)}, u32[]{:S(2)}, u32[]{:S(2)}) %collective-permute-start.9) | collective-permute-done | bytes 262176 | tf_op jit(solution)/shard_map/ppermute | solution.py:332
  161.6 2.6 collective-permute-done.11
  165.6 9.9 %banded_grads.3 = (f32[2,2,64,512]{3,2,1,0:T(8,128)}, bf16[6,8,2,2,16,1024]{5,4,3,2,1,0:T(8,128)(2,1)}) custom-call(s32[2,1,256]{2,1,0:T(1,128)} %tile.15.lo_ref, s32[2,1,256]{2,1,0:T(1,128)} %tile.17.hi_ref, f32[2,4,3,256]{3,2,1,0:T(4,128)} %softmax_stats.1.one_ref, f32[2,4,3,256]{3,2,1,0:T(4,128)} %copy-done.18, ...), custom_call_target="tpu_custom_call" | custom-call | flops 3221225472 | bytes 12582912 | tf_op jit(solution)/shard_map/banded_grads/pallas_call | solution.py:231
  177.3 3.2 %collective-permute-start.13 = (f32[2,64,512]{2,1,0:T(8,128)S(1)}, f32[2,64,512]{2,1,0:T(8,128)S(1)}, u32[]{:S(2)}, u32[]{:S(2)}) collective-permute-start(f32[2,64,512]{2,1,0:T(8,128)S(1)} %get-tuple-element.173), channel_id=1, source_target_pairs={{0,1},{1,3},{2,5},{3,7},{4,9},{5,11},{6,13},{7,15},{8,0},{9,2},{10... | collective-permute-start | bytes 786440 | tf_op jit(solution)/shard_map/ppermute | solution.py:332
  180.4 11.7 %convolution_convert_fusion.2 = bf16[1024,1024]{1,0:T(8,128)(2,1)} fusion(bf16[3072,1024]{1,0:T(8,128)(2,1)} %constant_dynamic-update-slice_fusion, bf16[3072,1024]{1,0:T(8,128)(2,1)} %bitcast.175), kind=kOutput, calls=%fused_computation.15 | convolution fusion | flops 6443499520 | bytes 14680064 | tf_op jit(solution)/shard_map/dot_general | solution.py:23
  192.1 4.3 %all-to-all-start.2 = ((bf16[8,64,1024]{2,1,0:T(8,128)(2,1)}), bf16[8,64,1024]{2,1,0:T(8,128)(2,1)}, u32[]{:S(2)}, u32[]{:S(2)}) async-start(bf16[8,64,1024]{2,1,0:T(8,128)(2,1)} %add_convert_fusion.1), calls=%async_computation.2 | async-start | bytes 2097152 | tf_op jit(solution)/shard_map/all_to_all | solution.py:443
  200.1 2.4 collective-permute-done.15
  203.0 19.9 %all-to-all-done.2 = bf16[8,64,1024]{2,1,0:T(8,128)(2,1)} async-done(((bf16[8,64,1024]{2,1,0:T(8,128)(2,1)}), bf16[8,64,1024]{2,1,0:T(8,128)(2,1)}, u32[]{:S(2)}, u32[]{:S(2)}) %all-to-all-start.2) | async-done | bytes 1048608 | tf_op jit(solution)/shard_map/all_to_all | solution.py:443
  224.2 4.1 %all-to-all-start.3 = ((bf16[8,64,1280]{2,1,0:T(8,128)(2,1)}), bf16[8,64,1280]{2,1,0:T(8,128)(2,1)S(1)}, u32[]{:S(2)}, u32[]{:S(2)}) async-start(bf16[8,64,1280]{2,1,0:T(8,128)(2,1)} %pad_maximum_fusion.1), calls=%async_computation.3 | async-start | bytes 2621440 | tf_op jit(solution)/shard_map/all_to_all | solution.py:443
  236.4 23.7 %all-to-all-done.3 = bf16[8,64,1280]{2,1,0:T(8,128)(2,1)S(1)} async-done(((bf16[8,64,1280]{2,1,0:T(8,128)(2,1)}), bf16[8,64,1280]{2,1,0:T(8,128)(2,1)S(1)}, u32[]{:S(2)}, u32[]{:S(2)}) %all-to-all-start.3) | async-done | bytes 1310752 | tf_op jit(solution)/shard_map/all_to_all | solution.py:443
  (133 shorter events, 49.7 us)
Async XLA Ops:
  0.6 60.9 %copy-start = (bf16[1024,1024]{1,0:T(8,128)(2,1)S(1)}, bf16[1024,1024]{1,0:T(8,128)(2,1)}, u32[]{:S(2)}) copy-start(bf16[1024,1024]{1,0:T(8,128)(2,1)} %param.14) | copy-start | bytes 6291460
  4.9 6.9 %copy-start.19 = (s32[64]{0:T(128)S(1)}, s32[64]{0:T(128)}, u32[]{:S(2)}) copy-start(s32[64]{0:T(128)} %param.15) | copy-start | bytes 772
  4.9 6.9 %copy-start.20 = (s32[64]{0:T(128)S(1)}, s32[64]{0:T(128)}, u32[]{:S(2)}) copy-start(s32[64]{0:T(128)} %param.16) | copy-start | bytes 772
  4.9 6.9 %copy-start.7 = (bf16[64,1024]{1,0:T(8,128)(2,1)S(1)}, bf16[64,1024]{1,0:T(8,128)(2,1)}, u32[]{:S(2)}) copy-start(bf16[64,1024]{1,0:T(8,128)(2,1)} %param.17) | copy-start | bytes 393220
  4.9 7.6 %copy-start.17 = (bf16[64,1024]{1,0:T(8,128)(2,1)S(1)}, bf16[64,1024]{1,0:T(8,128)(2,1)}, u32[]{:S(2)}) copy-start(bf16[64,1024]{1,0:T(8,128)(2,1)} %param.11) | copy-start | bytes 393220
  6.5 35.2 %all-to-all-start = ((bf16[8,2,2,2,16,1024]{5,4,3,2,1,0:T(8,128)(2,1)}), bf16[8,2,2,2,16,1024]{5,4,3,2,1,0:T(8,128)(2,1)}, u32[]{:S(2)}, u32[]{:S(2)}) async-start(bf16[8,2,2,2,16,1024]{5,4,3,2,1,0:T(8,128)(2,1)} %maximum_bitcast_fusion), calls=%async_computation | async-start | bytes 4194304 | tf_op jit(solution)/shard_map/all_to_all | solution.py:371
  12.6 18.3 %collective-permute-start = (bf16[144,1024]{1,0:T(8,128)(2,1)S(1)}, bf16[144,1024]{1,0:T(8,128)(2,1)S(1)}, u32[]{:S(2)}, u32[]{:S(2)}) collective-permute-start(bf16[144,1024]{1,0:T(8,128)(2,1)S(1)} %fusion.7), channel_id=1, source_target_pairs={{0,0},{2,1},{4,2},{6,3},{8,4},{10,5},{12,6},{14,7},{1,8},{3,9},{5,... | collective-permute-start | bytes 884744 | tf_op jit(solution)/shard_map/ppermute | solution.py:372
  13.3 28.4 %collective-permute-start.1 = (bf16[144,1024]{1,0:T(8,128)(2,1)S(1)}, bf16[144,1024]{1,0:T(8,128)(2,1)S(1)}, u32[]{:S(2)}, u32[]{:S(2)}) collective-permute-start(bf16[144,1024]{1,0:T(8,128)(2,1)S(1)} %fusion.7), channel_id=1, source_target_pairs={{1,0},{3,1},{5,2},{7,3},{9,4},{11,5},{13,6},{15,7},{0,8},{2,9},{4,... | collective-permute-start | bytes 884744 | tf_op jit(solution)/shard_map/ppermute | solution.py:373
  41.7 42.2 %all-to-all-start.1 = ((bf16[8,2,2,2,16,1024]{5,4,3,2,1,0:T(8,128)(2,1)}), bf16[8,2,2,2,16,1024]{5,4,3,2,1,0:T(8,128)(2,1)}, u32[]{:S(2)}, u32[]{:S(2)}) async-start(bf16[8,2,2,2,16,1024]{5,4,3,2,1,0:T(8,128)(2,1)} %maximum_bitcast_fusion.1), calls=%async_computation.1 | async-start | bytes 4194304 | tf_op jit(solution)/shard_map/all_to_all | solution.py:376
  64.8 11.5 %copy-start.1 = (bf16[1024,2048]{1,0:T(8,128)(2,1)S(1)}, bf16[1024,2048]{1,0:T(8,128)(2,1)}, u32[]{:S(2)}) copy-start(bf16[1024,2048]{1,0:T(8,128)(2,1)} %pad_maximum_fusion) | copy-start | bytes 12582916
  84.0 13.3 %collective-permute-start.2 = (bf16[8,2,16,1024]{3,2,1,0:T(8,128)(2,1)}, bf16[8,2,16,1024]{3,2,1,0:T(8,128)(2,1)S(1)}, u32[]{:S(2)}, u32[]{:S(2)}) collective-permute-start(bf16[8,2,16,1024]{3,2,1,0:T(8,128)(2,1)} %get-tuple-element.116), channel_id=1, source_target_pairs={{0,1},{1,2},{2,3},{3,4},{4,5},{5,6},{6,7},{8,9},{9,10},{10,11},{11... | collective-permute-start | bytes 1572872 | tf_op jit(solution)/shard_map/ppermute | solution.py:332
  86.4 10.9 %collective-permute-start.3 = (bf16[8,2,16,1024]{3,2,1,0:T(8,128)(2,1)}, bf16[8,2,16,1024]{3,2,1,0:T(8,128)(2,1)S(1)}, u32[]{:S(2)}, u32[]{:S(2)}) collective-permute-start(bf16[8,2,16,1024]{3,2,1,0:T(8,128)(2,1)} %get-tuple-element.117), channel_id=1, source_target_pairs={{1,0},{2,1},{3,2},{4,3},{5,4},{6,5},{7,6},{9,8},{10,9},{11,10},{12... | collective-permute-start | bytes 1572872 | tf_op jit(solution)/shard_map/ppermute | solution.py:332
  103.2 13.5 %copy-start.12 = (bf16[1,64,1024]{2,1,0:T(8,128)(2,1)S(1)}, bf16[1,64,1024]{2,1,0:T(8,128)(2,1)}, u32[]{:S(2)}) copy-start(bf16[1,64,1024]{2,1,0:T(8,128)(2,1)} %fusion.43) | copy-start | bytes 393220
  103.2 13.5 %collective-permute-start.4 = (bf16[64,1024]{1,0:T(8,128)(2,1)S(1)}, bf16[64,1024]{1,0:T(8,128)(2,1)S(1)}, u32[]{:S(2)}, u32[]{:S(2)}) collective-permute-start(bf16[64,1024]{1,0:T(8,128)(2,1)S(1)} %copy-done.11), channel_id=1, source_target_pairs={{0,8},{1,9},{2,10},{3,11},{4,12},{5,13},{6,14},{7,15},{8,0},{9,1},... | collective-permute-start | bytes 393224 | tf_op jit(solution)/shard_map/ppermute | solution.py:332
  116.6 5.6 %copy-start.14 = (f32[2,4,3,256]{3,2,1,0:T(4,128)S(1)}, f32[2,4,3,256]{3,2,1,0:T(4,128)}, u32[]{:S(2)}) copy-start(f32[2,4,3,256]{3,2,1,0:T(4,128)} %softmax_stats.1.one_ref) | copy-start | bytes 73732
  118.4 11.0 %collective-permute-start.5 = (bf16[2,64,1024]{2,1,0:T(8,128)(2,1)S(1)}, bf16[2,64,1024]{2,1,0:T(8,128)(2,1)S(1)}, u32[]{:S(2)}, u32[]{:S(2)}) collective-permute-start(bf16[2,64,1024]{2,1,0:T(8,128)(2,1)S(1)} %maximum_select_fusion.6), channel_id=1, source_target_pairs={{0,4},{1,5},{2,6},{3,7},{4,0},{5,1},{6,2},{7,3},{8,12},{9,13},{10,... | collective-permute-start | bytes 786440 | tf_op jit(solution)/shard_map/ppermute | solution.py:332
  122.2 7.1 %collective-permute-start.6 = (f32[2,4,3,256]{3,2,1,0:T(4,128)S(1)}, f32[2,4,3,256]{3,2,1,0:T(4,128)S(1)}, u32[]{:S(2)}, u32[]{:S(2)}) collective-permute-start(f32[2,4,3,256]{3,2,1,0:T(4,128)S(1)} %copy-done.14), channel_id=1, source_target_pairs={{0,8},{1,9},{2,10},{3,11},{4,12},{5,13},{6,14},{7,15},{8,0},{9,1},... | collective-permute-start | bytes 73736 | tf_op jit(solution)/shard_map/ppermute | solution.py:332
  129.4 12.6 %copy-start.3 = (bf16[2,64,1024]{2,1,0:T(8,128)(2,1)}, bf16[2,64,1024]{2,1,0:T(8,128)(2,1)S(1)}, u32[]{:S(2)}) copy-start(bf16[2,64,1024]{2,1,0:T(8,128)(2,1)S(1)} %collective-permute-done.5) | copy-start | bytes 786436
  130.2 12.3 %collective-permute-start.7 = (bf16[2,2,64,1024]{3,2,0,1:T(8,128)(2,1)}, bf16[2,2,64,1024]{3,2,0,1:T(8,128)(2,1)S(1)}, u32[]{:S(2)}, u32[]{:S(2)}) collective-permute-start(bf16[2,2,64,1024]{3,2,0,1:T(8,128)(2,1)} %maximum_select_fusion.3), channel_id=1, source_target_pairs={{0,2},{1,3},{2,0},{3,1},{4,6},{5,7},{6,4},{7,5},{8,10},{9,11},{10,... | collective-permute-start | bytes 1572872 | tf_op jit(solution)/shard_map/ppermute | solution.py:332
  142.5 15.8 %copy-start.4 = (bf16[2,2,64,1024]{3,2,0,1:T(8,128)(2,1)}, bf16[2,2,64,1024]{3,2,0,1:T(8,128)(2,1)S(1)}, u32[]{:S(2)}) copy-start(bf16[2,2,64,1024]{3,2,0,1:T(8,128)(2,1)S(1)} %collective-permute-done.7) | copy-start | bytes 1572868
  143.8 17.4 %collective-permute-start.10 = (bf16[2,2,2,64,1024]{4,3,0,1,2:T(8,128)(2,1)S(1)}, bf16[2,2,2,64,1024]{4,3,0,1,2:T(8,128)(2,1)S(1)}, u32[]{:S(2)}, u32[]{:S(2)}) collective-permute-start(bf16[2,2,2,64,1024]{4,3,0,1,2:T(8,128)(2,1)S(1)} %maximum_select_fusion), channel_id=1, source_target_pairs={{0,1},{1,0},{2,3},{3,2},{4,5},{5,4},{6,7},{7,6},{8,9},{9,8},{10,11... | collective-permute-start | bytes 3145736 | tf_op jit(solution)/shard_map/ppermute | solution.py:332
  143.9 14.5 %collective-permute-start.8 = (f32[2,64,512]{2,1,0:T(8,128)S(1)}, f32[2,64,512]{2,1,0:T(8,128)S(1)}, u32[]{:S(2)}, u32[]{:S(2)}) collective-permute-start(f32[2,64,512]{2,1,0:T(8,128)S(1)} %get-tuple-element.155), channel_id=1, source_target_pairs={{0,0},{1,2},{2,4},{3,6},{4,8},{5,10},{6,12},{7,14},{8,1},{9,3},{10... | collective-permute-start | bytes 786440 | tf_op jit(solution)/shard_map/ppermute | solution.py:332
  144.5 16.7 %collective-permute-start.9 = (f32[2,64,512]{2,1,0:T(8,128)S(1)}, f32[2,64,512]{2,1,0:T(8,128)S(1)}, u32[]{:S(2)}, u32[]{:S(2)}) collective-permute-start(f32[2,64,512]{2,1,0:T(8,128)S(1)} %get-tuple-element.156), channel_id=1, source_target_pairs={{0,1},{1,3},{2,5},{3,7},{4,9},{5,11},{6,13},{7,15},{8,0},{9,2},{10... | collective-permute-start | bytes 786440 | tf_op jit(solution)/shard_map/ppermute | solution.py:332
  161.4 2.7 %collective-permute-start.11 = (bf16[8,64,1024]{2,1,0:T(8,128)(2,1)S(1)}, bf16[8,64,1024]{2,1,0:T(8,128)(2,1)S(1)}, u32[]{:S(2)}, u32[]{:S(2)}) collective-permute-start(bf16[8,64,1024]{2,1,0:T(8,128)(2,1)S(1)} %get-tuple-element.160), channel_id=1, source_target_pairs={{0,1},{1,0},{2,3},{3,2},{4,5},{5,4},{6,7},{7,6},{8,9},{9,8},{10,11... | collective-permute-start | bytes 3145736 | tf_op jit(solution)/shard_map/ppermute | solution.py:332
  176.6 19.8 %collective-permute-start.12 = (f32[2,64,512]{2,1,0:T(8,128)S(1)}, f32[2,64,512]{2,1,0:T(8,128)S(1)}, u32[]{:S(2)}, u32[]{:S(2)}) collective-permute-start(f32[2,64,512]{2,1,0:T(8,128)S(1)} %get-tuple-element.172), channel_id=1, source_target_pairs={{0,0},{1,2},{2,4},{3,6},{4,8},{5,10},{6,12},{7,14},{8,1},{9,3},{10... | collective-permute-start | bytes 786440 | tf_op jit(solution)/shard_map/ppermute | solution.py:332
  177.3 19.1 %collective-permute-start.13 = (f32[2,64,512]{2,1,0:T(8,128)S(1)}, f32[2,64,512]{2,1,0:T(8,128)S(1)}, u32[]{:S(2)}, u32[]{:S(2)}) collective-permute-start(f32[2,64,512]{2,1,0:T(8,128)S(1)} %get-tuple-element.173), channel_id=1, source_target_pairs={{0,1},{1,3},{2,5},{3,7},{4,9},{5,11},{6,13},{7,15},{8,0},{9,2},{10... | collective-permute-start | bytes 786440 | tf_op jit(solution)/shard_map/ppermute | solution.py:332
  192.1 30.8 %all-to-all-start.2 = ((bf16[8,64,1024]{2,1,0:T(8,128)(2,1)}), bf16[8,64,1024]{2,1,0:T(8,128)(2,1)}, u32[]{:S(2)}, u32[]{:S(2)}) async-start(bf16[8,64,1024]{2,1,0:T(8,128)(2,1)} %add_convert_fusion.1), calls=%async_computation.2 | async-start | bytes 2097152 | tf_op jit(solution)/shard_map/all_to_all | solution.py:443
  198.8 3.7 %collective-permute-start.14 = (bf16[8,64,1024]{2,1,0:T(8,128)(2,1)S(1)}, bf16[8,64,1024]{2,1,0:T(8,128)(2,1)S(1)}, u32[]{:S(2)}, u32[]{:S(2)}) collective-permute-start(bf16[8,64,1024]{2,1,0:T(8,128)(2,1)S(1)} %get-tuple-element.181), channel_id=1, source_target_pairs={{0,1},{1,0},{2,3},{3,2},{4,5},{5,4},{6,7},{7,6},{8,9},{9,8},{10,11... | collective-permute-start | bytes 3145736 | tf_op jit(solution)/shard_map/ppermute | solution.py:332
  200.0 2.5 collective-permute-start.15
  224.2 35.9 %all-to-all-start.3 = ((bf16[8,64,1280]{2,1,0:T(8,128)(2,1)}), bf16[8,64,1280]{2,1,0:T(8,128)(2,1)S(1)}, u32[]{:S(2)}, u32[]{:S(2)}) async-start(bf16[8,64,1280]{2,1,0:T(8,128)(2,1)} %pad_maximum_fusion.1), calls=%async_computation.3 | async-start | bytes 2621440 | tf_op jit(solution)/shard_map/all_to_all | solution.py:443
  260.1 4.1 %copy-start.15 = (f32[64,256]{1,0:T(8,128)S(1)}, f32[64,256]{1,0:T(8,128)}, u32[]{:S(2)}) copy-start(f32[64,256]{1,0:T(8,128)} %get-tuple-element.216) | copy-start | bytes 196612
  260.1 4.1 %copy-start.16 = (f32[64,256]{1,0:T(8,128)S(1)}, f32[64,256]{1,0:T(8,128)}, u32[]{:S(2)}) copy-start(f32[64,256]{1,0:T(8,128)} %get-tuple-element.217) | copy-start | bytes 196612
  (9 other events, 23.2 us)

commit v9 on v8

--- a/solution.py
+++ b/solution.py
@@ -291,6 +291,13 @@
     return [(i, i ^ (1 << bit)) for i in range(n_dev)]
 
 
+def place(rows, blocks, at):
+    for x in blocks:
+        rows = lax.dynamic_update_slice_in_dim(rows, x, at, 0)
+        at += x.shape[0]
+    return rows
+
+
 class Gather:
     def __init__(self, block, bits):
         self.block = block
@@ -397,9 +404,9 @@
     edge_kv = project(edge)
     up = [(i, i + 1) for i in range(n_dev - 1) if (i + 1) % src]
     local = jnp.stack([edge[:, 0, :, 1], edge[:, 1, :, 0]], axis=2)
-    rows = [x.reshape(-1, width) for x in (edge[:, 0], edge[:, 1], local)]
-    rows = jnp.concatenate(rows, axis=0)
-    rows = jnp.pad(rows, ((0, rows.shape[0]), (0, 0)))
+    early = [x.reshape(-1, width) for x in (edge[:, 0], edge[:, 1], local)]
+    n_early = sum(x.shape[0] for x in early)
+    rows = place(jnp.zeros((2 * n_early, width), BF16), early, 0)
     low = Move(edge[:, 1, :, 1], up)
     high = Move(edge[:, 0, :, 0], [(target, source) for source, target in up])
     middle, edge_kv, q_pair, g_pair, lo, hi, rows, low.block, high.block = fence(
@@ -421,12 +428,7 @@
 
     def fill(rows, middle, low, high):
         late = (middle[:, 0], middle[:, 1], jnp.stack([low, high], axis=2))
-        at = rows.shape[0] // 2
-        for x in late:
-            x = x.reshape(-1, width)
-            rows = lax.dynamic_update_slice_in_dim(rows, x, at, 0)
-            at += x.shape[0]
-        return rows
+        return place(rows, [x.reshape(-1, width) for x in late], n_early)
 
     sources = beside([gather, swap], fill, rows, middle, low.come, high.come)
 

time: 267 us -> 262 us (0.981)
  other arithmetic: 32.5 us -> 21 us
  waiting for transfers between devices: 62.9 us -> 67.9 us
  local copies, waits for them, and re-layouts: 35.1 us -> 37.8 us
    concatenate x1 -> x0, other arithmetic: 11.5 us -> none  [shards(): rows = jnp.concatenate(rows, axis=0)]
    dynamic_update_slice x3 -> x6, local copies, waits for them, and re-layouts: 3.16 us -> 8.82 us  [place(): rows = lax.dynamic_update_slice_in_dim(rows, x, at, 0)]
    ppermute x1, waiting for transfers between devices: 10.8 us -> 14.7 us  [shards(): two = lax.ppermute(letter, 'tm', [(b, a) for a, b in owner_two])]
    unnamed x45 -> x47, local copies, waits for them, and re-layouts: 6.77 us -> 7.14 us
  transfers between devices with their start and end apart: 20 -> 20, of which waited for: 7 -> 8; matrix products, arithmetic and copies ran while one was open for 31% -> 28% of each run, Pallas kernels for 12% -> 12%
where the time goes in v9:
time: 262 us; the launch traced here: 260 us
  waiting for transfers between devices  67.9 us (26%)
  starting transfers between devices  53.3 us (20%)
  Pallas kernels  40.9 us (16%)
  matrix products  38.3 us (15%)
  local copies, waits for them, and re-layouts  37.8 us (14%)
  other arithmetic  21 us (8%)
    all_to_all x2, waiting for transfers between devices, scatter(): lax.all_to_all(block, 'tm', 0, 0, axis_index_groups=chips, tiled=True)  43.3 us
    dot_general x4, matrix products, tn_dot(): lax.dot_general(a, b, (((0,), (0,)), ((), ())), preferred_element_type=F32)  24.3 us
    ppermute x14, starting transfers between devices, beside(): lax.ppermute(away, 'tm', perm)  21.1 us
    pallas_call x2, Pallas kernels, attention(): pl.pallas_call(grads_kernel, in_specs=[flat, flat, table, table, rows, ro...  19.8 us
    ppermute x1, waiting for transfers between devices, shards(): two = lax.ppermute(letter, 'tm', [(b, a) for a, b in owner_two])  14.7 us
    all_to_all x1, starting transfers between devices, shards(): lax.all_to_all(inner, 'tm', 0, 0, axis_index_groups=halves, tiled=True)  12.8 us
    dot_general x3, matrix products, nn_dot(): return jnp.dot(a, b, preferred_element_type=F32)  12.5 us
    pallas_call x1, Pallas kernels, attention(): pl.pallas_call(stats_kernel, in_specs=[flat, flat, rows, rows] + sections...  12.4 us
  transfers between devices with their start and end apart: 20, of which 8 were waited for; matrix products, arithmetic and copies ran while one was open for 28% of the time, Pallas kernels for 12%

profile of v9, /device:TPU:0, one launch (start us, length us, event | category | flops | bytes accessed | tf_op | source)
XLA Modules:
  0.0 260.4 jit_solution(5993407582809141429)
XLA Ops:
  0.6 3.6 %copy.21 = bf16[1024,2,1024]{2,0,1:T(8,128)(2,1)S(1)} copy(bf16[1024,2,1024]{2,1,0:T(2,128)(2,1)} %param.10) | data formatting | bytes 8388608 | tf_op args[0]
  6.5 5.4 %all-to-all-start = ((bf16[8,2,2,2,16,1024]{5,4,3,2,1,0:T(8,128)(2,1)}), bf16[8,2,2,2,16,1024]{5,4,3,2,1,0:T(8,128)(2,1)}, u32[]{:S(2)}, u32[]{:S(2)}) async-start(bf16[8,2,2,2,16,1024]{5,4,3,2,1,0:T(8,128)(2,1)} %maximum_bitcast_fusion), calls=%async_computation | async-start | bytes 4194304 | tf_op jit(solution)/shard_map/all_to_all | solution.py:378
  12.8 4.8 %collective-permute-start.1 = (bf16[144,1024]{1,0:T(8,128)(2,1)S(1)}, bf16[144,1024]{1,0:T(8,128)(2,1)S(1)}, u32[]{:S(2)}, u32[]{:S(2)}) collective-permute-start(bf16[144,1024]{1,0:T(8,128)(2,1)S(1)} %fusion.2), channel_id=1, source_target_pairs={{1,0},{3,1},{5,2},{7,3},{9,4},{11,5},{13,6},{15,7},{0,8},{2,9},{4,... | collective-permute-start | bytes 884744 | tf_op jit(solution)/shard_map/ppermute | solution.py:380
  17.6 3.5 %copy.24 = bf16[1024,2,1024]{2,0,1:T(8,128)(2,1)S(1)} copy(bf16[1024,2,1024]{2,1,0:T(2,128)(2,1)} %param.10) | data formatting | bytes 8388608 | tf_op jit(solution)/shard_map/optimization_barrier | solution.py:373
  24.7 2.4 pad_maximum_fusion
  27.1 14.7 %collective-permute-done.1 = bf16[144,1024]{1,0:T(8,128)(2,1)S(1)} collective-permute-done((bf16[144,1024]{1,0:T(8,128)(2,1)S(1)}, bf16[144,1024]{1,0:T(8,128)(2,1)S(1)}, u32[]{:S(2)}, u32[]{:S(2)}) %collective-permute-start.1) | collective-permute-done | bytes 294944 | tf_op jit(solution)/shard_map/ppermute | solution.py:380
  41.8 12.8 %all-to-all-start.1 = ((bf16[8,2,2,2,16,1024]{5,4,3,2,1,0:T(8,128)(2,1)}), bf16[8,2,2,2,16,1024]{5,4,3,2,1,0:T(8,128)(2,1)}, u32[]{:S(2)}, u32[]{:S(2)}) async-start(bf16[8,2,2,2,16,1024]{5,4,3,2,1,0:T(8,128)(2,1)} %maximum_bitcast_fusion.1), calls=%async_computation.1 | async-start | bytes 4194304 | tf_op jit(solution)/shard_map/all_to_all | solution.py:383
  56.9 2.1 slice_bitcast_fusion.2
  59.0 2.1 slice_bitcast_fusion
  61.3 1.8 fusion.19
  63.1 3.5 %dynamic_update_slice.18 = bf16[3072,1024]{1,0:T(8,128)(2,1)} pad(bf16[512,1024]{1,0:T(8,128)(2,1)S(1)} %bitcast.151, bf16[]{:T(256)} %constant.86.clone.1), padding=0_2560x0_0 | pad | bytes 7340034 | tf_op jit(solution)/shard_map/dynamic_update_slice | solution.py:296
  71.1 7.7 %convolution_convert_fusion = bf16[1024,2048]{1,0:T(8,128)(2,1)} fusion(bf16[1024,1024]{1,0:T(8,128)(2,1)} %bitcast.9, bf16[1024,2048]{1,0:T(8,128)(2,1)S(1)} %copy-done.1), kind=kOutput, calls=%fused_computation.1 | convolution fusion | flops 4297064448 | bytes 10485760 | tf_op jit(solution)/shard_map/dot_general | solution.py:31
  84.1 8.7 %project_rows.1 = bf16[1024,2048]{1,0:T(8,128)(2,1)} custom-call(bf16[1024,1024]{1,0:T(8,128)(2,1)} %bitcast.22.x_ref, bf16[1024,1024]{1,0:T(8,128)(2,1)} %wk_ref, bf16[1024,1024]{1,0:T(8,128)(2,1)} %wv_ref), custom_call_target="tpu_custom_call" | custom-call | flops 4294967296 | bytes 10485760 | tf_op jit(solution)/shard_map/project_rows/pallas_call | solution.py:270
  93.1 1.9 copy-done.2
  95.0 3.7 %convolution_convert_fusion.1 = bf16[512,2048]{1,0:T(8,128)(2,1)} fusion(bf16[512,1024]{1,0:T(8,128)(2,1)S(1)} %bitcast.164, bf16[1024,2048]{1,0:T(8,128)(2,1)S(1)} %copy-done.2), kind=kOutput, calls=%fused_computation.2 | convolution fusion | flops 2148532224 | bytes 7340032 | tf_op jit(solution)/shard_map/dot_general | solution.py:31
  99.2 12.4 %softmax_stats.1.one_ref = f32[2,4,3,256]{3,2,1,0:T(4,128)} custom-call(s32[2,1,256]{2,1,0:T(1,128)} %tile.15.lo_ref, s32[2,1,256]{2,1,0:T(1,128)} %tile.17.hi_ref, bf16[2,64,1024]{2,1,0:T(8,128)(2,1)} %get-tuple-element.164.q_ref, bf16[2,64,1024]{2,1,0:T(8,128)(2,1)} %bitcast.141, bf16[8,2,2,2,16,2048]{5,4,3,2,1,0:T(8,128)(2,1)} %bitcast.115, ...), custom_call_target="tpu_custom_call" | custom-call | flops 2147483648 | bytes 12582912 | tf_op jit(solution)/shard_map/softmax_stats/pallas_call | solution.py:215
  111.6 1.7 fusion.18
  113.3 4.8 %collective-permute-start.5 = (bf16[2,64,1024]{2,1,0:T(8,128)(2,1)S(1)}, bf16[2,64,1024]{2,1,0:T(8,128)(2,1)S(1)}, u32[]{:S(2)}, u32[]{:S(2)}) collective-permute-start(bf16[2,64,1024]{2,1,0:T(8,128)(2,1)S(1)} %maximum_select_fusion.6), channel_id=1, source_target_pairs={{0,4},{1,5},{2,6},{3,7},{4,0},{5,1},{6,2},{7,3},{8,12},{9,13},{10,... | collective-permute-start | bytes 786440 | tf_op jit(solution)/shard_map/ppermute | solution.py:339
  118.1 2.9 %collective-permute-start.6 = (f32[2,4,3,256]{3,2,1,0:T(4,128)S(1)}, f32[2,4,3,256]{3,2,1,0:T(4,128)S(1)}, u32[]{:S(2)}, u32[]{:S(2)}) collective-permute-start(f32[2,4,3,256]{3,2,1,0:T(4,128)S(1)} %copy-done.15), channel_id=1, source_target_pairs={{0,8},{1,9},{2,10},{3,11},{4,12},{5,13},{6,14},{7,15},{8,0},{9,1},... | collective-permute-start | bytes 73736 | tf_op jit(solution)/shard_map/ppermute | solution.py:339
  128.0 9.9 %banded_grads.2 = (f32[2,2,64,512]{3,2,1,0:T(8,128)}, bf16[6,8,2,2,16,1024]{5,4,3,2,1,0:T(8,128)(2,1)}) custom-call(s32[2,1,256]{2,1,0:T(1,128)} %tile.15.lo_ref, s32[2,1,256]{2,1,0:T(1,128)} %tile.17.hi_ref, f32[2,4,3,256]{3,2,1,0:T(4,128)} %softmax_stats.1.one_ref, f32[2,4,3,256]{3,2,1,0:T(4,128)} %copy-done.19, ...), custom_call_target="tpu_custom_call" | custom-call | flops 3221225472 | bytes 12582912 | tf_op jit(solution)/shard_map/banded_grads/pallas_call | solution.py:231
  140.4 3.2 %collective-permute-start.9 = (f32[2,64,512]{2,1,0:T(8,128)S(1)}, f32[2,64,512]{2,1,0:T(8,128)S(1)}, u32[]{:S(2)}, u32[]{:S(2)}) collective-permute-start(f32[2,64,512]{2,1,0:T(8,128)S(1)} %get-tuple-element.156), channel_id=1, source_target_pairs={{0,1},{1,3},{2,5},{3,7},{4,9},{5,11},{6,13},{7,15},{8,0},{9,2},{10... | collective-permute-start | bytes 786440 | tf_op jit(solution)/shard_map/ppermute | solution.py:339
  143.6 10.7 %convolution_convert_fusion.3 = bf16[1024,1024]{1,0:T(8,128)(2,1)S(1)} fusion(bf16[3072,1024]{1,0:T(8,128)(2,1)} %constant_dynamic-update-slice_fusion, bf16[3072,1024]{1,0:T(8,128)(2,1)} %bitcast.176), kind=kOutput, calls=%fused_computation.10 | convolution fusion | flops 6443499520 | bytes 14680064 | tf_op jit(solution)/shard_map/dot_general | solution.py:23
  154.3 2.7 %collective-permute-done.9 = f32[2,64,512]{2,1,0:T(8,128)S(1)} collective-permute-done((f32[2,64,512]{2,1,0:T(8,128)S(1)}, f32[2,64,512]{2,1,0:T(8,128)S(1)}, u32[]{:S(2)}, u32[]{:S(2)}) %collective-permute-start.9) | collective-permute-done | bytes 262176 | tf_op jit(solution)/shard_map/ppermute | solution.py:339
  157.3 2.6 collective-permute-done.11
  161.4 9.9 %banded_grads.3 = (f32[2,2,64,512]{3,2,1,0:T(8,128)}, bf16[6,8,2,2,16,1024]{5,4,3,2,1,0:T(8,128)(2,1)}) custom-call(s32[2,1,256]{2,1,0:T(1,128)} %tile.15.lo_ref, s32[2,1,256]{2,1,0:T(1,128)} %tile.17.hi_ref, f32[2,4,3,256]{3,2,1,0:T(4,128)} %softmax_stats.1.one_ref, f32[2,4,3,256]{3,2,1,0:T(4,128)} %copy-done.19, ...), custom_call_target="tpu_custom_call" | custom-call | flops 3221225472 | bytes 12582912 | tf_op jit(solution)/shard_map/banded_grads/pallas_call | solution.py:231
  173.0 3.3 %collective-permute-start.13 = (f32[2,64,512]{2,1,0:T(8,128)S(1)}, f32[2,64,512]{2,1,0:T(8,128)S(1)}, u32[]{:S(2)}, u32[]{:S(2)}) collective-permute-start(f32[2,64,512]{2,1,0:T(8,128)S(1)} %get-tuple-element.173), channel_id=1, source_target_pairs={{0,1},{1,3},{2,5},{3,7},{4,9},{5,11},{6,13},{7,15},{8,0},{9,2},{10... | collective-permute-start | bytes 786440 | tf_op jit(solution)/shard_map/ppermute | solution.py:339
  176.3 11.7 %convolution_convert_fusion.2 = bf16[1024,1024]{1,0:T(8,128)(2,1)} fusion(bf16[3072,1024]{1,0:T(8,128)(2,1)} %constant_dynamic-update-slice_fusion, bf16[3072,1024]{1,0:T(8,128)(2,1)} %bitcast.175), kind=kOutput, calls=%fused_computation.9 | convolution fusion | flops 6443499520 | bytes 14680064 | tf_op jit(solution)/shard_map/dot_general | solution.py:23
  188.0 4.2 %all-to-all-start.2 = ((bf16[8,64,1024]{2,1,0:T(8,128)(2,1)}), bf16[8,64,1024]{2,1,0:T(8,128)(2,1)}, u32[]{:S(2)}, u32[]{:S(2)}) async-start(bf16[8,64,1024]{2,1,0:T(8,128)(2,1)} %add_convert_fusion.1), calls=%async_computation.2 | async-start | bytes 2097152 | tf_op jit(solution)/shard_map/all_to_all | solution.py:445
  196.1 2.4 collective-permute-done.15
  199.0 19.8 %all-to-all-done.2 = bf16[8,64,1024]{2,1,0:T(8,128)(2,1)} async-done(((bf16[8,64,1024]{2,1,0:T(8,128)(2,1)}), bf16[8,64,1024]{2,1,0:T(8,128)(2,1)}, u32[]{:S(2)}, u32[]{:S(2)}) %all-to-all-start.2) | async-done | bytes 1048608 | tf_op jit(solution)/shard_map/all_to_all | solution.py:445
  220.1 4.3 %all-to-all-start.3 = ((bf16[8,64,1280]{2,1,0:T(8,128)(2,1)}), bf16[8,64,1280]{2,1,0:T(8,128)(2,1)S(1)}, u32[]{:S(2)}, u32[]{:S(2)}) async-start(bf16[8,64,1280]{2,1,0:T(8,128)(2,1)} %pad_maximum_fusion.1), calls=%async_computation.3 | async-start | bytes 2621440 | tf_op jit(solution)/shard_map/all_to_all | solution.py:445
  232.5 23.5 %all-to-all-done.3 = bf16[8,64,1280]{2,1,0:T(8,128)(2,1)S(1)} async-done(((bf16[8,64,1280]{2,1,0:T(8,128)(2,1)}), bf16[8,64,1280]{2,1,0:T(8,128)(2,1)S(1)}, u32[]{:S(2)}, u32[]{:S(2)}) %all-to-all-start.3) | async-done | bytes 1310752 | tf_op jit(solution)/shard_map/all_to_all | solution.py:445
  (137 shorter events, 50.6 us)
Async XLA Ops:
  0.6 68.9 %copy-start = (bf16[1024,1024]{1,0:T(8,128)(2,1)S(1)}, bf16[1024,1024]{1,0:T(8,128)(2,1)}, u32[]{:S(2)}) copy-start(bf16[1024,1024]{1,0:T(8,128)(2,1)} %param.14) | copy-start | bytes 6291460
  6.5 5.4 %copy-start.20 = (s32[64]{0:T(128)S(1)}, s32[64]{0:T(128)}, u32[]{:S(2)}) copy-start(s32[64]{0:T(128)} %param.15) | copy-start | bytes 772
  6.5 5.5 %copy-start.21 = (s32[64]{0:T(128)S(1)}, s32[64]{0:T(128)}, u32[]{:S(2)}) copy-start(s32[64]{0:T(128)} %param.16) | copy-start | bytes 772
  6.5 5.5 %copy-start.8 = (bf16[64,1024]{1,0:T(8,128)(2,1)S(1)}, bf16[64,1024]{1,0:T(8,128)(2,1)}, u32[]{:S(2)}) copy-start(bf16[64,1024]{1,0:T(8,128)(2,1)} %param.17) | copy-start | bytes 393220
  6.5 5.6 %copy-start.18 = (bf16[64,1024]{1,0:T(8,128)(2,1)S(1)}, bf16[64,1024]{1,0:T(8,128)(2,1)}, u32[]{:S(2)}) copy-start(bf16[64,1024]{1,0:T(8,128)(2,1)} %param.11) | copy-start | bytes 393220
  6.5 35.4 %all-to-all-start = ((bf16[8,2,2,2,16,1024]{5,4,3,2,1,0:T(8,128)(2,1)}), bf16[8,2,2,2,16,1024]{5,4,3,2,1,0:T(8,128)(2,1)}, u32[]{:S(2)}, u32[]{:S(2)}) async-start(bf16[8,2,2,2,16,1024]{5,4,3,2,1,0:T(8,128)(2,1)} %maximum_bitcast_fusion), calls=%async_computation | async-start | bytes 4194304 | tf_op jit(solution)/shard_map/all_to_all | solution.py:378
  12.1 15.1 %collective-permute-start = (bf16[144,1024]{1,0:T(8,128)(2,1)S(1)}, bf16[144,1024]{1,0:T(8,128)(2,1)S(1)}, u32[]{:S(2)}, u32[]{:S(2)}) collective-permute-start(bf16[144,1024]{1,0:T(8,128)(2,1)S(1)} %fusion.2), channel_id=1, source_target_pairs={{0,0},{2,1},{4,2},{6,3},{8,4},{10,5},{12,6},{14,7},{1,8},{3,9},{5,... | collective-permute-start | bytes 884744 | tf_op jit(solution)/shard_map/ppermute | solution.py:379
  12.8 29.1 %collective-permute-start.1 = (bf16[144,1024]{1,0:T(8,128)(2,1)S(1)}, bf16[144,1024]{1,0:T(8,128)(2,1)S(1)}, u32[]{:S(2)}, u32[]{:S(2)}) collective-permute-start(bf16[144,1024]{1,0:T(8,128)(2,1)S(1)} %fusion.2), channel_id=1, source_target_pairs={{1,0},{3,1},{5,2},{7,3},{9,4},{11,5},{13,6},{15,7},{0,8},{2,9},{4,... | collective-permute-start | bytes 884744 | tf_op jit(solution)/shard_map/ppermute | solution.py:380
  41.8 38.6 %all-to-all-start.1 = ((bf16[8,2,2,2,16,1024]{5,4,3,2,1,0:T(8,128)(2,1)}), bf16[8,2,2,2,16,1024]{5,4,3,2,1,0:T(8,128)(2,1)}, u32[]{:S(2)}, u32[]{:S(2)}) async-start(bf16[8,2,2,2,16,1024]{5,4,3,2,1,0:T(8,128)(2,1)} %maximum_bitcast_fusion.1), calls=%async_computation.1 | async-start | bytes 4194304 | tf_op jit(solution)/shard_map/all_to_all | solution.py:383
  67.7 3.3 %copy-start.1 = (bf16[1024,2048]{1,0:T(8,128)(2,1)S(1)}, bf16[1024,2048]{1,0:T(8,128)(2,1)}, u32[]{:S(2)}) copy-start(bf16[1024,2048]{1,0:T(8,128)(2,1)} %pad_maximum_fusion) | copy-start | bytes 12582916
  80.4 12.4 %collective-permute-start.2 = (bf16[8,2,16,1024]{3,2,1,0:T(8,128)(2,1)}, bf16[8,2,16,1024]{3,2,1,0:T(8,128)(2,1)S(1)}, u32[]{:S(2)}, u32[]{:S(2)}) collective-permute-start(bf16[8,2,16,1024]{3,2,1,0:T(8,128)(2,1)} %get-tuple-element.116), channel_id=1, source_target_pairs={{0,1},{1,2},{2,3},{3,4},{4,5},{5,6},{6,7},{8,9},{9,10},{10,11},{11... | collective-permute-start | bytes 1572872 | tf_op jit(solution)/shard_map/ppermute | solution.py:339
  81.9 10.9 %collective-permute-start.3 = (bf16[8,2,16,1024]{3,2,1,0:T(8,128)(2,1)}, bf16[8,2,16,1024]{3,2,1,0:T(8,128)(2,1)S(1)}, u32[]{:S(2)}, u32[]{:S(2)}) collective-permute-start(bf16[8,2,16,1024]{3,2,1,0:T(8,128)(2,1)} %get-tuple-element.117), channel_id=1, source_target_pairs={{1,0},{2,1},{3,2},{4,3},{5,4},{6,5},{7,6},{9,8},{10,9},{11,10},{12... | collective-permute-start | bytes 1572872 | tf_op jit(solution)/shard_map/ppermute | solution.py:339
  95.0 3.7 %copy-start.12 = (bf16[64,1024]{1,0:T(8,128)(2,1)S(1)}, bf16[64,1024]{1,0:T(8,128)(2,1)}, u32[]{:S(2)}) copy-start(bf16[64,1024]{1,0:T(8,128)(2,1)} %copy-done.11) | copy-start | bytes 393220
  98.7 12.9 %copy-start.13 = (bf16[1,64,1024]{2,1,0:T(8,128)(2,1)S(1)}, bf16[1,64,1024]{2,1,0:T(8,128)(2,1)}, u32[]{:S(2)}) copy-start(bf16[1,64,1024]{2,1,0:T(8,128)(2,1)} %fusion.38) | copy-start | bytes 393220
  98.7 12.8 %collective-permute-start.4 = (bf16[64,1024]{1,0:T(8,128)(2,1)S(1)}, bf16[64,1024]{1,0:T(8,128)(2,1)S(1)}, u32[]{:S(2)}, u32[]{:S(2)}) collective-permute-start(bf16[64,1024]{1,0:T(8,128)(2,1)S(1)} %copy-done.12), channel_id=1, source_target_pairs={{0,8},{1,9},{2,10},{3,11},{4,12},{5,13},{6,14},{7,15},{8,0},{9,1},... | collective-permute-start | bytes 393224 | tf_op jit(solution)/shard_map/ppermute | solution.py:339
  111.6 6.5 %copy-start.15 = (f32[2,4,3,256]{3,2,1,0:T(4,128)S(1)}, f32[2,4,3,256]{3,2,1,0:T(4,128)}, u32[]{:S(2)}) copy-start(f32[2,4,3,256]{3,2,1,0:T(4,128)} %softmax_stats.1.one_ref) | copy-start | bytes 73732
  113.3 11.9 %collective-permute-start.5 = (bf16[2,64,1024]{2,1,0:T(8,128)(2,1)S(1)}, bf16[2,64,1024]{2,1,0:T(8,128)(2,1)S(1)}, u32[]{:S(2)}, u32[]{:S(2)}) collective-permute-start(bf16[2,64,1024]{2,1,0:T(8,128)(2,1)S(1)} %maximum_select_fusion.6), channel_id=1, source_target_pairs={{0,4},{1,5},{2,6},{3,7},{4,0},{5,1},{6,2},{7,3},{8,12},{9,13},{10,... | collective-permute-start | bytes 786440 | tf_op jit(solution)/shard_map/ppermute | solution.py:339
  118.1 7.2 %collective-permute-start.6 = (f32[2,4,3,256]{3,2,1,0:T(4,128)S(1)}, f32[2,4,3,256]{3,2,1,0:T(4,128)S(1)}, u32[]{:S(2)}, u32[]{:S(2)}) collective-permute-start(f32[2,4,3,256]{3,2,1,0:T(4,128)S(1)} %copy-done.15), channel_id=1, source_target_pairs={{0,8},{1,9},{2,10},{3,11},{4,12},{5,13},{6,14},{7,15},{8,0},{9,1},... | collective-permute-start | bytes 73736 | tf_op jit(solution)/shard_map/ppermute | solution.py:339
  125.3 12.6 %copy-start.4 = (bf16[2,64,1024]{2,1,0:T(8,128)(2,1)}, bf16[2,64,1024]{2,1,0:T(8,128)(2,1)S(1)}, u32[]{:S(2)}) copy-start(bf16[2,64,1024]{2,1,0:T(8,128)(2,1)S(1)} %collective-permute-done.5) | copy-start | bytes 786436
  126.2 12.2 %collective-permute-start.7 = (bf16[2,2,64,1024]{3,2,0,1:T(8,128)(2,1)}, bf16[2,2,64,1024]{3,2,0,1:T(8,128)(2,1)S(1)}, u32[]{:S(2)}, u32[]{:S(2)}) collective-permute-start(bf16[2,2,64,1024]{3,2,0,1:T(8,128)(2,1)} %maximum_select_fusion.3), channel_id=1, source_target_pairs={{0,2},{1,3},{2,0},{3,1},{4,6},{5,7},{6,4},{7,5},{8,10},{9,11},{10,... | collective-permute-start | bytes 1572872 | tf_op jit(solution)/shard_map/ppermute | solution.py:339
  138.3 15.9 %copy-start.5 = (bf16[2,2,64,1024]{3,2,0,1:T(8,128)(2,1)}, bf16[2,2,64,1024]{3,2,0,1:T(8,128)(2,1)S(1)}, u32[]{:S(2)}) copy-start(bf16[2,2,64,1024]{3,2,0,1:T(8,128)(2,1)S(1)} %collective-permute-done.7) | copy-start | bytes 1572868
  139.6 17.3 %collective-permute-start.10 = (bf16[2,2,2,64,1024]{4,3,0,1,2:T(8,128)(2,1)S(1)}, bf16[2,2,2,64,1024]{4,3,0,1,2:T(8,128)(2,1)S(1)}, u32[]{:S(2)}, u32[]{:S(2)}) collective-permute-start(bf16[2,2,2,64,1024]{4,3,0,1,2:T(8,128)(2,1)S(1)} %maximum_select_fusion), channel_id=1, source_target_pairs={{0,1},{1,0},{2,3},{3,2},{4,5},{5,4},{6,7},{7,6},{8,9},{9,8},{10,11... | collective-permute-start | bytes 3145736 | tf_op jit(solution)/shard_map/ppermute | solution.py:339
  139.7 14.6 %collective-permute-start.8 = (f32[2,64,512]{2,1,0:T(8,128)S(1)}, f32[2,64,512]{2,1,0:T(8,128)S(1)}, u32[]{:S(2)}, u32[]{:S(2)}) collective-permute-start(f32[2,64,512]{2,1,0:T(8,128)S(1)} %get-tuple-element.155), channel_id=1, source_target_pairs={{0,0},{1,2},{2,4},{3,6},{4,8},{5,10},{6,12},{7,14},{8,1},{9,3},{10... | collective-permute-start | bytes 786440 | tf_op jit(solution)/shard_map/ppermute | solution.py:339
  140.4 16.6 %collective-permute-start.9 = (f32[2,64,512]{2,1,0:T(8,128)S(1)}, f32[2,64,512]{2,1,0:T(8,128)S(1)}, u32[]{:S(2)}, u32[]{:S(2)}) collective-permute-start(f32[2,64,512]{2,1,0:T(8,128)S(1)} %get-tuple-element.156), channel_id=1, source_target_pairs={{0,1},{1,3},{2,5},{3,7},{4,9},{5,11},{6,13},{7,15},{8,0},{9,2},{10... | collective-permute-start | bytes 786440 | tf_op jit(solution)/shard_map/ppermute | solution.py:339
  157.2 2.7 %collective-permute-start.11 = (bf16[8,64,1024]{2,1,0:T(8,128)(2,1)S(1)}, bf16[8,64,1024]{2,1,0:T(8,128)(2,1)S(1)}, u32[]{:S(2)}, u32[]{:S(2)}) collective-permute-start(bf16[8,64,1024]{2,1,0:T(8,128)(2,1)S(1)} %get-tuple-element.160), channel_id=1, source_target_pairs={{0,1},{1,0},{2,3},{3,2},{4,5},{5,4},{6,7},{7,6},{8,9},{9,8},{10,11... | collective-permute-start | bytes 3145736 | tf_op jit(solution)/shard_map/ppermute | solution.py:339
  172.3 19.9 %collective-permute-start.12 = (f32[2,64,512]{2,1,0:T(8,128)S(1)}, f32[2,64,512]{2,1,0:T(8,128)S(1)}, u32[]{:S(2)}, u32[]{:S(2)}) collective-permute-start(f32[2,64,512]{2,1,0:T(8,128)S(1)} %get-tuple-element.172), channel_id=1, source_target_pairs={{0,0},{1,2},{2,4},{3,6},{4,8},{5,10},{6,12},{7,14},{8,1},{9,3},{10... | collective-permute-start | bytes 786440 | tf_op jit(solution)/shard_map/ppermute | solution.py:339
  173.0 19.3 %collective-permute-start.13 = (f32[2,64,512]{2,1,0:T(8,128)S(1)}, f32[2,64,512]{2,1,0:T(8,128)S(1)}, u32[]{:S(2)}, u32[]{:S(2)}) collective-permute-start(f32[2,64,512]{2,1,0:T(8,128)S(1)} %get-tuple-element.173), channel_id=1, source_target_pairs={{0,1},{1,3},{2,5},{3,7},{4,9},{5,11},{6,13},{7,15},{8,0},{9,2},{10... | collective-permute-start | bytes 786440 | tf_op jit(solution)/shard_map/ppermute | solution.py:339
  188.0 30.9 %all-to-all-start.2 = ((bf16[8,64,1024]{2,1,0:T(8,128)(2,1)}), bf16[8,64,1024]{2,1,0:T(8,128)(2,1)}, u32[]{:S(2)}, u32[]{:S(2)}) async-start(bf16[8,64,1024]{2,1,0:T(8,128)(2,1)} %add_convert_fusion.1), calls=%async_computation.2 | async-start | bytes 2097152 | tf_op jit(solution)/shard_map/all_to_all | solution.py:445
  194.7 3.8 %collective-permute-start.14 = (bf16[8,64,1024]{2,1,0:T(8,128)(2,1)S(1)}, bf16[8,64,1024]{2,1,0:T(8,128)(2,1)S(1)}, u32[]{:S(2)}, u32[]{:S(2)}) collective-permute-start(bf16[8,64,1024]{2,1,0:T(8,128)(2,1)S(1)} %get-tuple-element.181), channel_id=1, source_target_pairs={{0,1},{1,0},{2,3},{3,2},{4,5},{5,4},{6,7},{7,6},{8,9},{9,8},{10,11... | collective-permute-start | bytes 3145736 | tf_op jit(solution)/shard_map/ppermute | solution.py:339
  196.0 2.5 collective-permute-start.15
  220.1 36.0 %all-to-all-start.3 = ((bf16[8,64,1280]{2,1,0:T(8,128)(2,1)}), bf16[8,64,1280]{2,1,0:T(8,128)(2,1)S(1)}, u32[]{:S(2)}, u32[]{:S(2)}) async-start(bf16[8,64,1280]{2,1,0:T(8,128)(2,1)} %pad_maximum_fusion.1), calls=%async_computation.3 | async-start | bytes 2621440 | tf_op jit(solution)/shard_map/all_to_all | solution.py:445
  224.3 3.8 %copy-start.10 = (bf16[2,2,2,64,1024]{4,3,0,1,2:T(8,128)(2,1)S(1)}, bf16[2,2,2,64,1024]{4,3,0,1,2:T(8,128)(2,1)}, u32[]{:S(2)}) copy-start(bf16[2,2,2,64,1024]{4,3,0,1,2:T(8,128)(2,1)} %copy-done.9) | copy-start | bytes 3145732
  (10 other events, 20.9 us)

commit v10 on v9

--- a/solution.py
+++ b/solution.py
@@ -439,7 +439,7 @@
         rows = term.reshape(src, 2, -1, term.shape[1])
         away = lax.dynamic_index_in_dim(rows, 1 - core, 1, keepdims=False)
         keep = lax.dynamic_index_in_dim(rows, core, 1, keepdims=False)
-        return Move(away, flips(n_dev, 0)), keep
+        return add(keep, lax.ppermute(away, "tm", flips(n_dev, 0)))
 
     def scatter(block):
         return lax.all_to_all(block, "tm", 0, 0, axis_index_groups=chips, tiled=True)
@@ -457,12 +457,16 @@
     def weigh(g):
         return tn_dot(sources, g.reshape(sources.shape[0], -1)).astype(BF16)
 
+    def weigh_and_meet(g):
+        term = weigh(g)
+        return meet(term)
+
     def assemble(*parts):
         sums = [(a + b).astype(BF16) for a, b in zip(parts[::2], parts[1::2])]
         return jnp.concatenate(sums, axis=2)
 
     trades, shares, ready, start = [], [], None, 0
-    for call, groups in enumerate(SPLIT):
+    for groups in SPLIT:
         work = functools.partial(attention, start, groups, lo, hi, (swap.block, swap.come))
         start += groups
         if ready is not None:
@@ -471,19 +475,15 @@
         partial, grads = beside([gather], work, q_pair, g_pair, tokens)
         trade = half_context(partial)
         trades += trade
-        term = beside(trade + [gather], weigh, grads)
+        sent = beside(trade + [gather], weigh_and_meet, grads)
         if ready is not None:
             shares.append(share)
-        if call < len(SPLIT) - 1:
-            away, keep = meet(term)
-            keep = beside([away, gather], lambda x: x, keep)
-            ready = add(keep, away.come)
+        ready = sent
 
     context, d_query = assemble(*[move.come for move in trades])
-    away, keep = meet(term)
     partner = Move(context, flips(n_dev, 0))
-    keep, context = beside([away, partner], lambda *x: x, keep, context)
-    ready, shares = fence((add(keep, away.come), shares))
+    context = beside([partner], lambda x: x, context)
+    ready, shares = fence((ready, shares))
 
     columns = jnp.concatenate(
         [x.reshape(n_query, src, -1).swapaxes(0, 1) for x in (context, partner.come)], axis=2

time: 262 us -> 283 us (1.080)
  waiting for transfers between devices: 67.9 us -> 77.3 us
  other arithmetic: 21 us -> 27.4 us
  local copies, waits for them, and re-layouts: 37.8 us -> 43.9 us
    ppermute x14 -> x12, waiting for transfers between devices: 8.13 us -> 35.9 us  [beside(): lax.ppermute(away, 'tm', perm)]
    all_to_all x2, waiting for transfers between devices: 43.3 us -> 23.8 us  [scatter(): lax.all_to_all(block, 'tm', 0, 0, axis_index_groups=chips, tiled=True)]
    ppermute x0 -> x2, starting transfers between devices: none -> 4.82 us  [meet(): return add(keep, lax.ppermute(away, 'tm', flips(n_dev, 0)))]
    convert_element_type x2, other arithmetic: 1.88 us -> 6.03 us  [add(): return (x.astype(F32) + y.astype(F32)).astype(BF16)]
    unnamed x47 -> x53, local copies, waits for them, and re-layouts: 7.14 us -> 11.2 us
    ppermute x14 -> x12, starting transfers between devices: 21.1 us -> 17.3 us  [beside(): lax.ppermute(away, 'tm', perm)]
  transfers between devices with their start and end apart: 20 -> 20, of which waited for: 8 -> 8; matrix products, arithmetic and copies ran while one was open for 28% -> 19% of each run, Pallas kernels for 12% -> 11%
where the time goes in v10:
time: 283 us; the launch traced here: 281 us
  waiting for transfers between devices  77.3 us (27%)
  starting transfers between devices  53.4 us (19%)
  local copies, waits for them, and re-layouts  43.9 us (16%)
  Pallas kernels  40.8 us (14%)
  matrix products  37.3 us (13%)
  other arithmetic  27.4 us (10%)
    ppermute x12, waiting for transfers between devices, beside(): lax.ppermute(away, 'tm', perm)  35.9 us
    all_to_all x2, waiting for transfers between devices, scatter(): lax.all_to_all(block, 'tm', 0, 0, axis_index_groups=chips, tiled=True)  23.8 us
    dot_general x4, matrix products, tn_dot(): lax.dot_general(a, b, (((0,), (0,)), ((), ())), preferred_element_type=F32)  23.3 us
    pallas_call x2, Pallas kernels, attention(): pl.pallas_call(grads_kernel, in_specs=[flat, flat, table, table, rows, ro...  19.7 us
    ppermute x12, starting transfers between devices, beside(): lax.ppermute(away, 'tm', perm)  17.3 us
    ppermute x1, waiting for transfers between devices, shards(): two = lax.ppermute(letter, 'tm', [(b, a) for a, b in owner_two])  14.7 us
    all_to_all x1, starting transfers between devices, shards(): lax.all_to_all(inner, 'tm', 0, 0, axis_index_groups=halves, tiled=True)  12.8 us
    dot_general x3, matrix products, nn_dot(): return jnp.dot(a, b, preferred_element_type=F32)  12.5 us
  transfers between devices with their start and end apart: 20, of which 8 were waited for; matrix products, arithmetic and copies ran while one was open for 19% of the time, Pallas kernels for 11%

profile of v10, /device:TPU:0, one launch (start us, length us, event | category | flops | bytes accessed | tf_op | source)
XLA Modules:
  0.0 281.4 jit_solution(7898728115847601561)
XLA Ops:
  0.6 3.6 %copy.21 = bf16[1024,2,1024]{2,0,1:T(8,128)(2,1)S(1)} copy(bf16[1024,2,1024]{2,1,0:T(2,128)(2,1)} %param.10) | data formatting | bytes 8388608 | tf_op args[0]
  6.5 5.4 %all-to-all-start = ((bf16[8,2,2,2,16,1024]{5,4,3,2,1,0:T(8,128)(2,1)}), bf16[8,2,2,2,16,1024]{5,4,3,2,1,0:T(8,128)(2,1)}, u32[]{:S(2)}, u32[]{:S(2)}) async-start(bf16[8,2,2,2,16,1024]{5,4,3,2,1,0:T(8,128)(2,1)} %maximum_bitcast_fusion), calls=%async_computation | async-start | bytes 4194304 | tf_op jit(solution)/shard_map/all_to_all | solution.py:378
  12.8 4.8 %collective-permute-start.1 = (bf16[144,1024]{1,0:T(8,128)(2,1)S(1)}, bf16[144,1024]{1,0:T(8,128)(2,1)S(1)}, u32[]{:S(2)}, u32[]{:S(2)}) collective-permute-start(bf16[144,1024]{1,0:T(8,128)(2,1)S(1)} %fusion.4), channel_id=1, source_target_pairs={{1,0},{3,1},{5,2},{7,3},{9,4},{11,5},{13,6},{15,7},{0,8},{2,9},{4,... | collective-permute-start | bytes 884744 | tf_op jit(solution)/shard_map/ppermute | solution.py:380
  17.6 3.5 %copy.24 = bf16[1024,2,1024]{2,0,1:T(8,128)(2,1)S(1)} copy(bf16[1024,2,1024]{2,1,0:T(2,128)(2,1)} %param.10) | data formatting | bytes 8388608 | tf_op jit(solution)/shard_map/optimization_barrier | solution.py:373
  24.7 2.4 pad_maximum_fusion
  27.2 14.7 %collective-permute-done.1 = bf16[144,1024]{1,0:T(8,128)(2,1)S(1)} collective-permute-done((bf16[144,1024]{1,0:T(8,128)(2,1)S(1)}, bf16[144,1024]{1,0:T(8,128)(2,1)S(1)}, u32[]{:S(2)}, u32[]{:S(2)}) %collective-permute-start.1) | collective-permute-done | bytes 294944 | tf_op jit(solution)/shard_map/ppermute | solution.py:380
  41.8 12.8 %all-to-all-start.1 = ((bf16[8,2,2,2,16,1024]{5,4,3,2,1,0:T(8,128)(2,1)}), bf16[8,2,2,2,16,1024]{5,4,3,2,1,0:T(8,128)(2,1)}, u32[]{:S(2)}, u32[]{:S(2)}) async-start(bf16[8,2,2,2,16,1024]{5,4,3,2,1,0:T(8,128)(2,1)} %maximum_bitcast_fusion.1), calls=%async_computation.1 | async-start | bytes 4194304 | tf_op jit(solution)/shard_map/all_to_all | solution.py:383
  57.0 2.1 slice_bitcast_fusion.2
  59.1 2.1 slice_bitcast_fusion
  63.3 3.5 %dynamic_update_slice.18 = bf16[3072,1024]{1,0:T(8,128)(2,1)} pad(bf16[512,1024]{1,0:T(8,128)(2,1)S(1)} %bitcast.159, bf16[]{:T(256)} %constant.86.clone.1), padding=0_2560x0_0 | pad | bytes 7340034 | tf_op jit(solution)/shard_map/dynamic_update_slice | solution.py:296
  71.2 7.7 %convolution_convert_fusion = bf16[1024,2048]{1,0:T(8,128)(2,1)} fusion(bf16[1024,1024]{1,0:T(8,128)(2,1)} %bitcast.9, bf16[1024,2048]{1,0:T(8,128)(2,1)S(1)} %copy-done.3), kind=kOutput, calls=%fused_computation.1 | convolution fusion | flops 4297064448 | bytes 10485760 | tf_op jit(solution)/shard_map/dot_general | solution.py:31
  84.1 8.7 %project_rows.1 = bf16[1024,2048]{1,0:T(8,128)(2,1)} custom-call(bf16[1024,1024]{1,0:T(8,128)(2,1)} %bitcast.22.x_ref, bf16[1024,1024]{1,0:T(8,128)(2,1)} %wk_ref, bf16[1024,1024]{1,0:T(8,128)(2,1)} %wv_ref), custom_call_target="tpu_custom_call" | custom-call | flops 4294967296 | bytes 10485760 | tf_op jit(solution)/shard_map/project_rows/pallas_call | solution.py:270
  93.1 1.9 copy-done.4
  95.0 3.7 %convolution_convert_fusion.1 = bf16[512,2048]{1,0:T(8,128)(2,1)} fusion(bf16[512,1024]{1,0:T(8,128)(2,1)S(1)} %bitcast.173, bf16[1024,2048]{1,0:T(8,128)(2,1)S(1)} %copy-done.4), kind=kOutput, calls=%fused_computation.2 | convolution fusion | flops 2148532224 | bytes 7340032 | tf_op jit(solution)/shard_map/dot_general | solution.py:31
  99.3 12.4 %softmax_stats.1.one_ref = f32[2,4,3,256]{3,2,1,0:T(4,128)} custom-call(s32[2,1,256]{2,1,0:T(1,128)} %tile.15.lo_ref, s32[2,1,256]{2,1,0:T(1,128)} %tile.17.hi_ref, bf16[2,64,1024]{2,1,0:T(8,128)(2,1)} %get-tuple-element.154.q_ref, bf16[2,64,1024]{2,1,0:T(8,128)(2,1)} %bitcast.149, bf16[8,2,2,2,16,2048]{5,4,3,2,1,0:T(8,128)(2,1)} %bitcast.123, ...), custom_call_target="tpu_custom_call" | custom-call | flops 2147483648 | bytes 12582912 | tf_op jit(solution)/shard_map/softmax_stats/pallas_call | solution.py:215
  113.5 4.6 %collective-permute-start.5 = (bf16[2,64,1024]{2,1,0:T(8,128)(2,1)S(1)}, bf16[2,64,1024]{2,1,0:T(8,128)(2,1)S(1)}, u32[]{:S(2)}, u32[]{:S(2)}) collective-permute-start(bf16[2,64,1024]{2,1,0:T(8,128)(2,1)S(1)} %maximum_select_fusion.6), channel_id=1, source_target_pairs={{0,4},{1,5},{2,6},{3,7},{4,0},{5,1},{6,2},{7,3},{8,12},{9,13},{10,... | collective-permute-start | bytes 786440 | tf_op jit(solution)/shard_map/ppermute | solution.py:339
  118.1 2.9 %collective-permute-start.6 = (f32[2,4,3,256]{3,2,1,0:T(4,128)S(1)}, f32[2,4,3,256]{3,2,1,0:T(4,128)S(1)}, u32[]{:S(2)}, u32[]{:S(2)}) collective-permute-start(f32[2,4,3,256]{3,2,1,0:T(4,128)S(1)} %copy-done.17), channel_id=1, source_target_pairs={{0,8},{1,9},{2,10},{3,11},{4,12},{5,13},{6,14},{7,15},{8,0},{9,1},... | collective-permute-start | bytes 73736 | tf_op jit(solution)/shard_map/ppermute | solution.py:339
  128.0 9.9 %banded_grads.2 = (f32[2,2,64,512]{3,2,1,0:T(8,128)}, bf16[6,8,2,2,16,1024]{5,4,3,2,1,0:T(8,128)(2,1)}) custom-call(s32[2,1,256]{2,1,0:T(1,128)} %tile.15.lo_ref, s32[2,1,256]{2,1,0:T(1,128)} %tile.17.hi_ref, f32[2,4,3,256]{3,2,1,0:T(4,128)} %softmax_stats.1.one_ref, f32[2,4,3,256]{3,2,1,0:T(4,128)} %copy-done.23, ...), custom_call_target="tpu_custom_call" | custom-call | flops 3221225472 | bytes 12582912 | tf_op jit(solution)/shard_map/banded_grads/pallas_call | solution.py:231
  141.3 10.7 %convolution_convert_fusion.3 = bf16[1024,1024]{1,0:T(8,128)(2,1)S(1)} fusion(bf16[3072,1024]{1,0:T(8,128)(2,1)} %constant_dynamic-update-slice_fusion, bf16[3072,1024]{1,0:T(8,128)(2,1)} %bitcast.182), kind=kOutput, calls=%fused_computation.12 | convolution fusion | flops 6443499520 | bytes 14680064 | tf_op jit(solution)/shard_map/dot_general | solution.py:23
  156.3 3.0 %fusion.1 = bf16[8,64,1024]{2,1,0:T(8,128)(2,1)} fusion(bf16[8,64,1024]{2,1,0:T(8,128)(2,1)} %collective-permute-done.8, bf16[8,2,64,1024]{3,2,1,0:T(8,128)(2,1)} %bitcast.168, s32[]{:T(128)S(6)} %select_n.130), kind=kLoop, calls=%fused_computation.8 | loop fusion | flops 2097152 | bytes 3145732 | tf_op jit(solution)/shard_map/convert_element_type | solution.py:448
  159.3 4.5 %collective-permute-done.10 = f32[2,64,512]{2,1,0:T(8,128)S(1)} collective-permute-done((f32[2,64,512]{2,1,0:T(8,128)}, f32[2,64,512]{2,1,0:T(8,128)S(1)}, u32[]{:S(2)}, u32[]{:S(2)}) %collective-permute-start.10) | collective-permute-done | bytes 262176 | tf_op jit(solution)/shard_map/ppermute | solution.py:339
  165.3 9.8 %banded_grads.3 = (f32[2,2,64,512]{3,2,1,0:T(8,128)}, bf16[6,8,2,2,16,1024]{5,4,3,2,1,0:T(8,128)(2,1)}) custom-call(s32[2,1,256]{2,1,0:T(1,128)} %tile.15.lo_ref, s32[2,1,256]{2,1,0:T(1,128)} %tile.17.hi_ref, f32[2,4,3,256]{3,2,1,0:T(4,128)} %softmax_stats.1.one_ref, f32[2,4,3,256]{3,2,1,0:T(4,128)} %copy-done.23, ...), custom_call_target="tpu_custom_call" | custom-call | flops 3221225472 | bytes 12582912 | tf_op jit(solution)/shard_map/banded_grads/pallas_call | solution.py:231
  176.9 10.7 %convolution_convert_fusion.2 = bf16[1024,1024]{1,0:T(8,128)(2,1)S(1)} fusion(bf16[3072,1024]{1,0:T(8,128)(2,1)} %constant_dynamic-update-slice_fusion, bf16[3072,1024]{1,0:T(8,128)(2,1)} %bitcast.181), kind=kOutput, calls=%fused_computation.11 | convolution fusion | flops 6443499520 | bytes 14680064 | tf_op jit(solution)/shard_map/dot_general | solution.py:23
  190.0 4.7 %collective-permute-start.12 = (bf16[8,64,1024]{2,1,0:T(8,128)(2,1)}, bf16[8,64,1024]{2,1,0:T(8,128)(2,1)}, u32[]{:S(2)}, u32[]{:S(2)}) collective-permute-start(bf16[8,64,1024]{2,1,0:T(8,128)(2,1)} %dynamic-slice_bitcast_fusion), channel_id=1, source_target_pairs={{0,1},{1,0},{2,3},{3,2},{4,5},{5,4},{6,7},{7,6},{8,9},{9,8},{10,11... | collective-permute-start | bytes 3145736 | tf_op jit(solution)/shard_map/ppermute | solution.py:442
  194.8 4.1 %all-to-all-start.2 = ((bf16[8,64,1024]{2,1,0:T(8,128)(2,1)}), bf16[8,64,1024]{2,1,0:T(8,128)(2,1)S(1)}, u32[]{:S(2)}, u32[]{:S(2)}) async-start(bf16[8,64,1024]{2,1,0:T(8,128)(2,1)} %fusion.1), calls=%async_computation.2 | async-start | bytes 2097152 | tf_op jit(solution)/shard_map/all_to_all | solution.py:445
  200.4 2.5 collective-permute-start.14
  204.0 3.0 %fusion = bf16[8,64,1024]{2,1,0:T(8,128)(2,1)} fusion(bf16[8,64,1024]{2,1,0:T(8,128)(2,1)} %collective-permute-done.12, bf16[8,2,64,1024]{3,2,1,0:T(8,128)(2,1)} %bitcast.166, s32[]{:T(128)S(6)} %select_n.130), kind=kLoop, calls=%fused_computation.6 | loop fusion | flops 2097152 | bytes 3145732 | tf_op jit(solution)/shard_map/convert_element_type | solution.py:448
  207.0 29.5 %collective-permute-done.14 = f32[2,64,512]{2,1,0:T(8,128)S(1)} collective-permute-done((f32[2,64,512]{2,1,0:T(8,128)S(1)}, f32[2,64,512]{2,1,0:T(8,128)S(1)}, u32[]{:S(2)}, u32[]{:S(2)}) %collective-permute-start.14) | collective-permute-done | bytes 262176 | tf_op jit(solution)/shard_map/ppermute | solution.py:339
  238.7 2.8 %pad_maximum_fusion.1 = bf16[8,64,1280]{2,1,0:T(8,128)(2,1)} fusion(bf16[8,64,128]{2,1,0:T(8,128)(2,1)S(1)} %bitcast_bitcast_fusion, bf16[8,64,128]{2,1,0:T(8,128)(2,1)S(1)} %bitcast_bitcast_fusion.1, bf16[8,64,1024]{2,1,0:T(8,128)(2,1)} %fusion), kind=kLoop, calls=%fused_computation.13 | loop fusion | flops 3932160 | bytes 2621440 | tf_op jit(solution)/shard_map/concatenate | solution.py:492
  241.5 3.6 %all-to-all-start.3 = ((bf16[8,64,1280]{2,1,0:T(8,128)(2,1)}), bf16[8,64,1280]{2,1,0:T(8,128)(2,1)S(1)}, u32[]{:S(2)}, u32[]{:S(2)}) async-start(bf16[8,64,1280]{2,1,0:T(8,128)(2,1)} %pad_maximum_fusion.1), calls=%async_computation.3 | async-start | bytes 2621440 | tf_op jit(solution)/shard_map/all_to_all | solution.py:445
  248.8 2.4 copy.37
  253.2 23.8 %all-to-all-done.3 = bf16[8,64,1280]{2,1,0:T(8,128)(2,1)S(1)} async-done(((bf16[8,64,1280]{2,1,0:T(8,128)(2,1)}), bf16[8,64,1280]{2,1,0:T(8,128)(2,1)S(1)}, u32[]{:S(2)}, u32[]{:S(2)}) %all-to-all-start.3) | async-done | bytes 1310752 | tf_op jit(solution)/shard_map/all_to_all | solution.py:445
  (143 shorter events, 58.3 us)
Async XLA Ops:
  0.6 69.0 %copy-start = (bf16[1024,1024]{1,0:T(8,128)(2,1)S(1)}, bf16[1024,1024]{1,0:T(8,128)(2,1)}, u32[]{:S(2)}) copy-start(bf16[1024,1024]{1,0:T(8,128)(2,1)} %param.14) | copy-start | bytes 6291460
  6.5 5.4 %copy-start.24 = (s32[64]{0:T(128)S(1)}, s32[64]{0:T(128)}, u32[]{:S(2)}) copy-start(s32[64]{0:T(128)} %param.15) | copy-start | bytes 772
  6.5 5.5 %copy-start.25 = (s32[64]{0:T(128)S(1)}, s32[64]{0:T(128)}, u32[]{:S(2)}) copy-start(s32[64]{0:T(128)} %param.16) | copy-start | bytes 772
  6.5 5.5 %copy-start.12 = (bf16[64,1024]{1,0:T(8,128)(2,1)S(1)}, bf16[64,1024]{1,0:T(8,128)(2,1)}, u32[]{:S(2)}) copy-start(bf16[64,1024]{1,0:T(8,128)(2,1)} %param.17) | copy-start | bytes 393220
  6.5 5.6 %copy-start.22 = (bf16[64,1024]{1,0:T(8,128)(2,1)S(1)}, bf16[64,1024]{1,0:T(8,128)(2,1)}, u32[]{:S(2)}) copy-start(bf16[64,1024]{1,0:T(8,128)(2,1)} %param.11) | copy-start | bytes 393220
  6.5 35.4 %all-to-all-start = ((bf16[8,2,2,2,16,1024]{5,4,3,2,1,0:T(8,128)(2,1)}), bf16[8,2,2,2,16,1024]{5,4,3,2,1,0:T(8,128)(2,1)}, u32[]{:S(2)}, u32[]{:S(2)}) async-start(bf16[8,2,2,2,16,1024]{5,4,3,2,1,0:T(8,128)(2,1)} %maximum_bitcast_fusion), calls=%async_computation | async-start | bytes 4194304 | tf_op jit(solution)/shard_map/all_to_all | solution.py:378
  12.1 15.1 %collective-permute-start = (bf16[144,1024]{1,0:T(8,128)(2,1)S(1)}, bf16[144,1024]{1,0:T(8,128)(2,1)S(1)}, u32[]{:S(2)}, u32[]{:S(2)}) collective-permute-start(bf16[144,1024]{1,0:T(8,128)(2,1)S(1)} %fusion.4), channel_id=1, source_target_pairs={{0,0},{2,1},{4,2},{6,3},{8,4},{10,5},{12,6},{14,7},{1,8},{3,9},{5,... | collective-permute-start | bytes 884744 | tf_op jit(solution)/shard_map/ppermute | solution.py:379
  12.8 29.1 %collective-permute-start.1 = (bf16[144,1024]{1,0:T(8,128)(2,1)S(1)}, bf16[144,1024]{1,0:T(8,128)(2,1)S(1)}, u32[]{:S(2)}, u32[]{:S(2)}) collective-permute-start(bf16[144,1024]{1,0:T(8,128)(2,1)S(1)} %fusion.4), channel_id=1, source_target_pairs={{1,0},{3,1},{5,2},{7,3},{9,4},{11,5},{13,6},{15,7},{0,8},{2,9},{4,... | collective-permute-start | bytes 884744 | tf_op jit(solution)/shard_map/ppermute | solution.py:380
  41.8 38.6 %all-to-all-start.1 = ((bf16[8,2,2,2,16,1024]{5,4,3,2,1,0:T(8,128)(2,1)}), bf16[8,2,2,2,16,1024]{5,4,3,2,1,0:T(8,128)(2,1)}, u32[]{:S(2)}, u32[]{:S(2)}) async-start(bf16[8,2,2,2,16,1024]{5,4,3,2,1,0:T(8,128)(2,1)} %maximum_bitcast_fusion.1), calls=%async_computation.1 | async-start | bytes 4194304 | tf_op jit(solution)/shard_map/all_to_all | solution.py:383
  67.9 3.3 %copy-start.3 = (bf16[1024,2048]{1,0:T(8,128)(2,1)S(1)}, bf16[1024,2048]{1,0:T(8,128)(2,1)}, u32[]{:S(2)}) copy-start(bf16[1024,2048]{1,0:T(8,128)(2,1)} %pad_maximum_fusion) | copy-start | bytes 12582916
  80.4 12.4 %collective-permute-start.2 = (bf16[8,2,16,1024]{3,2,1,0:T(8,128)(2,1)}, bf16[8,2,16,1024]{3,2,1,0:T(8,128)(2,1)S(1)}, u32[]{:S(2)}, u32[]{:S(2)}) collective-permute-start(bf16[8,2,16,1024]{3,2,1,0:T(8,128)(2,1)} %get-tuple-element.108), channel_id=1, source_target_pairs={{0,1},{1,2},{2,3},{3,4},{4,5},{5,6},{6,7},{8,9},{9,10},{10,11},{11... | collective-permute-start | bytes 1572872 | tf_op jit(solution)/shard_map/ppermute | solution.py:339
  81.9 10.9 %collective-permute-start.3 = (bf16[8,2,16,1024]{3,2,1,0:T(8,128)(2,1)}, bf16[8,2,16,1024]{3,2,1,0:T(8,128)(2,1)S(1)}, u32[]{:S(2)}, u32[]{:S(2)}) collective-permute-start(bf16[8,2,16,1024]{3,2,1,0:T(8,128)(2,1)} %get-tuple-element.109), channel_id=1, source_target_pairs={{1,0},{2,1},{3,2},{4,3},{5,4},{6,5},{7,6},{9,8},{10,9},{11,10},{12... | collective-permute-start | bytes 1572872 | tf_op jit(solution)/shard_map/ppermute | solution.py:339
  95.0 3.7 %copy-start.14 = (bf16[64,1024]{1,0:T(8,128)(2,1)S(1)}, bf16[64,1024]{1,0:T(8,128)(2,1)}, u32[]{:S(2)}) copy-start(bf16[64,1024]{1,0:T(8,128)(2,1)} %copy-done.13) | copy-start | bytes 393220
  98.7 13.0 %copy-start.15 = (bf16[1,64,1024]{2,1,0:T(8,128)(2,1)S(1)}, bf16[1,64,1024]{2,1,0:T(8,128)(2,1)}, u32[]{:S(2)}) copy-start(bf16[1,64,1024]{2,1,0:T(8,128)(2,1)} %fusion.40) | copy-start | bytes 393220
  98.7 13.0 %collective-permute-start.4 = (bf16[64,1024]{1,0:T(8,128)(2,1)S(1)}, bf16[64,1024]{1,0:T(8,128)(2,1)S(1)}, u32[]{:S(2)}, u32[]{:S(2)}) collective-permute-start(bf16[64,1024]{1,0:T(8,128)(2,1)S(1)} %copy-done.14), channel_id=1, source_target_pairs={{0,8},{1,9},{2,10},{3,11},{4,12},{5,13},{6,14},{7,15},{8,0},{9,1},... | collective-permute-start | bytes 393224 | tf_op jit(solution)/shard_map/ppermute | solution.py:339
  111.7 6.4 %copy-start.17 = (f32[2,4,3,256]{3,2,1,0:T(4,128)S(1)}, f32[2,4,3,256]{3,2,1,0:T(4,128)}, u32[]{:S(2)}) copy-start(f32[2,4,3,256]{3,2,1,0:T(4,128)} %softmax_stats.1.one_ref) | copy-start | bytes 73732
  113.5 11.8 %collective-permute-start.5 = (bf16[2,64,1024]{2,1,0:T(8,128)(2,1)S(1)}, bf16[2,64,1024]{2,1,0:T(8,128)(2,1)S(1)}, u32[]{:S(2)}, u32[]{:S(2)}) collective-permute-start(bf16[2,64,1024]{2,1,0:T(8,128)(2,1)S(1)} %maximum_select_fusion.6), channel_id=1, source_target_pairs={{0,4},{1,5},{2,6},{3,7},{4,0},{5,1},{6,2},{7,3},{8,12},{9,13},{10,... | collective-permute-start | bytes 786440 | tf_op jit(solution)/shard_map/ppermute | solution.py:339
  118.1 7.2 %collective-permute-start.6 = (f32[2,4,3,256]{3,2,1,0:T(4,128)S(1)}, f32[2,4,3,256]{3,2,1,0:T(4,128)S(1)}, u32[]{:S(2)}, u32[]{:S(2)}) collective-permute-start(f32[2,4,3,256]{3,2,1,0:T(4,128)S(1)} %copy-done.17), channel_id=1, source_target_pairs={{0,8},{1,9},{2,10},{3,11},{4,12},{5,13},{6,14},{7,15},{8,0},{9,1},... | collective-permute-start | bytes 73736 | tf_op jit(solution)/shard_map/ppermute | solution.py:339
  125.3 12.6 %copy-start.6 = (bf16[2,64,1024]{2,1,0:T(8,128)(2,1)}, bf16[2,64,1024]{2,1,0:T(8,128)(2,1)S(1)}, u32[]{:S(2)}) copy-start(bf16[2,64,1024]{2,1,0:T(8,128)(2,1)S(1)} %collective-permute-done.5) | copy-start | bytes 786436
  126.2 12.2 %collective-permute-start.7 = (bf16[2,2,64,1024]{3,2,0,1:T(8,128)(2,1)}, bf16[2,2,64,1024]{3,2,0,1:T(8,128)(2,1)S(1)}, u32[]{:S(2)}, u32[]{:S(2)}) collective-permute-start(bf16[2,2,64,1024]{3,2,0,1:T(8,128)(2,1)} %maximum_select_fusion.3), channel_id=1, source_target_pairs={{0,2},{1,3},{2,0},{3,1},{4,6},{5,7},{6,4},{7,5},{8,10},{9,11},{10,... | collective-permute-start | bytes 1572872 | tf_op jit(solution)/shard_map/ppermute | solution.py:339
  138.4 13.6 %copy-start.7 = (bf16[2,2,64,1024]{3,2,0,1:T(8,128)(2,1)}, bf16[2,2,64,1024]{3,2,0,1:T(8,128)(2,1)S(1)}, u32[]{:S(2)}) copy-start(bf16[2,2,64,1024]{3,2,0,1:T(8,128)(2,1)S(1)} %collective-permute-done.7) | copy-start | bytes 1572868
  153.4 2.9 %collective-permute-start.8 = (bf16[8,64,1024]{2,1,0:T(8,128)(2,1)S(1)}, bf16[8,64,1024]{2,1,0:T(8,128)(2,1)}, u32[]{:S(2)}, u32[]{:S(2)}) collective-permute-start(bf16[8,64,1024]{2,1,0:T(8,128)(2,1)S(1)} %dynamic-slice_bitcast_fusion.1), channel_id=1, source_target_pairs={{0,1},{1,0},{2,3},{3,2},{4,5},{5,4},{6,7},{7,6},{8,9},{9,8},{10,11... | collective-permute-start | bytes 3145736 | tf_op jit(solution)/shard_map/ppermute | solution.py:442
  153.5 11.8 %collective-permute-start.11 = (bf16[2,2,2,64,1024]{4,3,0,1,2:T(8,128)(2,1)}, bf16[2,2,2,64,1024]{4,3,0,1,2:T(8,128)(2,1)}, u32[]{:S(2)}, u32[]{:S(2)}) collective-permute-start(bf16[2,2,2,64,1024]{4,3,0,1,2:T(8,128)(2,1)} %maximum_select_fusion), channel_id=1, source_target_pairs={{0,1},{1,0},{2,3},{3,2},{4,5},{5,4},{6,7},{7,6},{8,9},{9,8},{10,11... | collective-permute-start | bytes 3145736 | tf_op jit(solution)/shard_map/ppermute | solution.py:339
  154.0 9.9 %collective-permute-start.10 = (f32[2,64,512]{2,1,0:T(8,128)}, f32[2,64,512]{2,1,0:T(8,128)S(1)}, u32[]{:S(2)}, u32[]{:S(2)}) collective-permute-start(f32[2,64,512]{2,1,0:T(8,128)} %get-tuple-element.148), channel_id=1, source_target_pairs={{0,1},{1,3},{2,5},{3,7},{4,9},{5,11},{6,13},{7,15},{8,0},{9,2},{10... | collective-permute-start | bytes 786440 | tf_op jit(solution)/shard_map/ppermute | solution.py:339
  154.1 9.8 %collective-permute-start.9 = (f32[2,64,512]{2,1,0:T(8,128)S(1)}, f32[2,64,512]{2,1,0:T(8,128)S(1)}, u32[]{:S(2)}, u32[]{:S(2)}) collective-permute-start(f32[2,64,512]{2,1,0:T(8,128)S(1)} %get-tuple-element.147), channel_id=1, source_target_pairs={{0,0},{1,2},{2,4},{3,6},{4,8},{5,10},{6,12},{7,14},{8,1},{9,3},{10... | collective-permute-start | bytes 786440 | tf_op jit(solution)/shard_map/ppermute | solution.py:339
  190.0 14.0 %collective-permute-start.12 = (bf16[8,64,1024]{2,1,0:T(8,128)(2,1)}, bf16[8,64,1024]{2,1,0:T(8,128)(2,1)}, u32[]{:S(2)}, u32[]{:S(2)}) collective-permute-start(bf16[8,64,1024]{2,1,0:T(8,128)(2,1)} %dynamic-slice_bitcast_fusion), channel_id=1, source_target_pairs={{0,1},{1,0},{2,3},{3,2},{4,5},{5,4},{6,7},{7,6},{8,9},{9,8},{10,11... | collective-permute-start | bytes 3145736 | tf_op jit(solution)/shard_map/ppermute | solution.py:442
  194.8 43.9 %all-to-all-start.2 = ((bf16[8,64,1024]{2,1,0:T(8,128)(2,1)}), bf16[8,64,1024]{2,1,0:T(8,128)(2,1)S(1)}, u32[]{:S(2)}, u32[]{:S(2)}) async-start(bf16[8,64,1024]{2,1,0:T(8,128)(2,1)} %fusion.1), calls=%async_computation.2 | async-start | bytes 2097152 | tf_op jit(solution)/shard_map/all_to_all | solution.py:445
  198.8 8.2 %collective-permute-start.13 = (f32[2,64,512]{2,1,0:T(8,128)}, f32[2,64,512]{2,1,0:T(8,128)S(1)}, u32[]{:S(2)}, u32[]{:S(2)}) collective-permute-start(f32[2,64,512]{2,1,0:T(8,128)} %get-tuple-element.162), channel_id=1, source_target_pairs={{0,0},{1,2},{2,4},{3,6},{4,8},{5,10},{6,12},{7,14},{8,1},{9,3},{10... | collective-permute-start | bytes 786440 | tf_op jit(solution)/shard_map/ppermute | solution.py:339
  200.4 36.1 %collective-permute-start.14 = (f32[2,64,512]{2,1,0:T(8,128)S(1)}, f32[2,64,512]{2,1,0:T(8,128)S(1)}, u32[]{:S(2)}, u32[]{:S(2)}) collective-permute-start(f32[2,64,512]{2,1,0:T(8,128)S(1)} %get-tuple-element.163), channel_id=1, source_target_pairs={{0,1},{1,3},{2,5},{3,7},{4,9},{5,11},{6,13},{7,15},{8,0},{9,2},{10... | collective-permute-start | bytes 786440 | tf_op jit(solution)/shard_map/ppermute | solution.py:339
  237.2 1.3 collective-permute-start.15
  241.5 35.5 %all-to-all-start.3 = ((bf16[8,64,1280]{2,1,0:T(8,128)(2,1)}), bf16[8,64,1280]{2,1,0:T(8,128)(2,1)S(1)}, u32[]{:S(2)}, u32[]{:S(2)}) async-start(bf16[8,64,1280]{2,1,0:T(8,128)(2,1)} %pad_maximum_fusion.1), calls=%async_computation.3 | async-start | bytes 2621440 | tf_op jit(solution)/shard_map/all_to_all | solution.py:445
  248.8 3.5 %copy-start.2 = (bf16[8,64,1024]{2,1,0:T(8,128)(2,1)S(1)}, bf16[8,64,1024]{2,1,0:T(8,128)(2,1)}, u32[]{:S(2)}) copy-start(bf16[8,64,1024]{2,1,0:T(8,128)(2,1)} %copy-done.1) | copy-start | bytes 3145732
  (14 other events, 24.9 us)
